TPU v7x, 32 devices: a whole 2x2x4 slice. The times are simulated.
32 devices in a mesh: dp: 2 (over x), gr: 4 (over z), gc: 4 (over y, core).
Axes of the slice: x: 2, y: 2, z: 4, core: 2. Of those that a mesh axis runs over, the one named last changes fastest.
Arguments:
- tokens: bfloat16 [16384, 768], P(('dp', 'gr', 'gc')), may hold values from -6 to 6
- teacher: bfloat16 [16384, 768], P(('dp', 'gr', 'gc')), may hold values from -15 to 15
- pass_embed: bfloat16 [768], P('gr'), may hold values from -0.119628906 to 0.119628906
- ln1_gain: bfloat16 [768], P('gr'), may hold values from 0.25 to 1.75
- ln1_bias: bfloat16 [768], P('gr'), may hold values from -0.119628906 to 0.119628906
- qkv_weight: bfloat16 [768, 2304], P('gr', 'gc'), may hold values from -0.21875 to 0.21875
- out_weight: bfloat16 [768, 768], P('gc', 'gr'), may hold values from -1.75 to 1.75
- out_bias: bfloat16 [768], P('gr'), may hold values from -0.8984375 to 0.8984375
- ln2_gain: bfloat16 [768], P('gr'), may hold values from 0.25 to 1.75
- ln2_bias: bfloat16 [768], P('gr'), may hold values from -0.8984375 to 0.8984375
- fc1_weight: bfloat16 [768, 3072], P('gr', 'gc'), may hold values from -0.3125 to 0.3125
- fc1_bias: bfloat16 [3072], P('gc'), may hold values from -2 to 2
- fc2_weight: bfloat16 [768, 3072], P('gr', 'gc'), may hold values from -0.109375 to 0.109375
- fc2_bias: bfloat16 [768], P('gr'), may hold values from -0.8984375 to 0.8984375
- cont_group: int32 [64], P(('dp', 'gr')), may hold values from 0 to 3, as said below
- token_count: int32 [1], replicated, may hold values from 8192 to 16384
Outputs:
- output: bfloat16 [16384, 768], P(('dp', 'gr', 'gc'))
- loss: float32 [1], replicated
- input_grad: float32 [16384, 768], P(('dp', 'gr', 'gc'))
- pass_embed_grad: float32 [768], P('gr')
- ln1_gain_grad: float32 [768], P('gr')
- ln1_bias_grad: float32 [768], P('gr')
- qkv_weight_grad: float32 [768, 2304], P('gr', 'gc')
- out_weight_grad: float32 [768, 768], P('gc', 'gr')
- out_bias_grad: float32 [768], P('gr')
- ln2_gain_grad: float32 [768], P('gr')
- ln2_bias_grad: float32 [768], P('gr')
- fc1_weight_grad: float32 [768, 3072], P('gr', 'gc')
- fc1_bias_grad: float32 [3072], P('gc')
- fc2_weight_grad: float32 [768, 3072], P('gr', 'gc')
- fc2_bias_grad: float32 [768], P('gr')
Inputs may be any that keep to these rules, and one draw needn't show every extreme that they name: `cont_group`: continuation k names a group of index k // 32 of dp by its place among that index's 4 groups; each place is named by exactly 8 of that index's continuations.
All inputs are finite; a program needn't handle non-finite values.
Results may differ from a plain program's by a relative error of at most 0.025.
Values may be sent and summed in bfloat16 or wider, within the bound.
A program may use at most 192 MiB of HBM per device.

v0:
```python
from functools import partial
import math

import jax
import jax.numpy as jnp
from jax import lax
from jax.sharding import PartitionSpec as P

D = 768
HD = 64
P_SIZE = 1024
CL = 128
GPS = 1
SHARD = 2048


eps = 1e-05
negative = -1e30


def as_sent(array):

    def short(part):
        return part.astype(jnp.bfloat16) if part.dtype == jnp.float32 else part

    return jax.tree.map(short, array)


def feature_sums(values):
    return lax.psum(values, "gr")


def small_total(values):
    return lax.psum(values, ("dp", "gr", "gc"))


def data_total(values):
    return jax.tree.map(lambda part: part.astype(jnp.float32), lax.psum(as_sent(values), "dp"))


def layer_norm(hidden, gain, shift):
    feature_count = hidden.shape[1] * lax.axis_size("gr")
    center = feature_sums(jnp.sum(hidden, axis=1)) / feature_count
    offset = hidden - center[:, None]
    spread = feature_sums(jnp.sum(offset * offset, axis=1)) / feature_count
    factor = lax.rsqrt(spread + eps)
    unit_rows = offset * factor[:, None]
    return (unit_rows * gain + shift, unit_rows, factor)


def layer_norm_back(grad_out, gain, unit_rows, factor):
    feature_count = grad_out.shape[1] * lax.axis_size("gr")
    grad_unit = grad_out * gain
    first, second = feature_sums(
        (jnp.sum(grad_unit, axis=1), jnp.sum(grad_unit * unit_rows, axis=1))
    )
    grad_in = factor[:, None] * (
        grad_unit - first[:, None] / feature_count - unit_rows * (second[:, None] / feature_count)
    )
    return (grad_in, jnp.sum(grad_out * unit_rows, axis=0), jnp.sum(grad_out, axis=0))


def spread_columns(values):
    return lax.all_gather(values, "gc", axis=0, tiled=True)


def reduce_rows(whole, weight, row_count, transpose):

    def term(row_start, count):
        if transpose:
            return lax.dot_general(
                whole, weight, (((1,), (1,)), ((), ())), preferred_element_type=jnp.float32
            )
        return jnp.dot(whole, weight, preferred_element_type=jnp.float32)

    return lax.psum_scatter(
        term(jnp.int32(0), lax.axis_size("gr") * row_count).astype(jnp.bfloat16),
        "gr",
        scatter_dimension=0,
        tiled=True,
    ).astype(jnp.float32)


def sum_columns(partial_rows):
    return lax.psum_scatter(
        partial_rows.astype(jnp.bfloat16), "gc", scatter_dimension=0, tiled=True
    ).astype(jnp.float32)


def fold_rows(values, step_fn, init):
    return step_fn(
        init,
        jax.tree.map(lambda part: lax.all_gather(part, "gr", axis=0, tiled=True), as_sent(values)),
        jnp.int32(0),
    )


def product_step(weight, transpose, carried, row_piece, row_start):
    if transpose:
        term = lax.dot_general(
            row_piece, weight, (((1,), (1,)), ((), ())), preferred_element_type=jnp.float32
        )
    else:
        term = jnp.dot(row_piece, weight, preferred_element_type=jnp.float32)
    return lax.dynamic_update_slice_in_dim(carried, term, row_start, 0)


def project_rows(values, weight, transpose):
    rows_all = values.shape[0] * lax.axis_size("gr")
    out_cols = weight.shape[0] if transpose else weight.shape[1]
    partial_rows = fold_rows(
        values,
        partial(product_step, weight, transpose),
        jnp.zeros((rows_all, out_cols), jnp.float32),
    )
    return sum_columns(partial_rows)


def weight_step(kept, carried, row_piece, row_start):
    return lax.dot_general(
        row_piece, kept, (((0,), (0,)), ((), ())), preferred_element_type=jnp.float32
    )


def weight_step_swapped(kept, carried, row_piece, row_start):
    kept_rows = lax.dynamic_slice_in_dim(kept, row_start, row_piece.shape[0], 0)
    return carried + lax.dot_general(
        kept_rows, row_piece, (((0,), (0,)), ((), ())), preferred_element_type=jnp.float32
    )


def input_step(kept, weight, carried, row_piece, row_start):
    grad_w = lax.dot_general(
        kept, row_piece, (((0,), (0,)), ((), ())), preferred_element_type=jnp.float32
    )
    term = lax.dot_general(
        row_piece, weight, (((1,), (1,)), ((), ())), preferred_element_type=jnp.float32
    )
    return (grad_w, term)


def input_bias_step(kept, weight, carried, row_piece, row_start):
    grad_w, grad_b, partial_rows = carried
    grad_w, partial_rows = input_step(kept, weight, (grad_w, partial_rows), row_piece, row_start)
    return (grad_w, jnp.sum(row_piece, axis=0, dtype=jnp.float32), partial_rows)


def near_mask(size):
    positions = jnp.arange(size)
    return positions[None, :] <= positions[:, None]


def prompt_pass(queries, key_rows, value_rows, block_rows, score_scale):
    length = queries.shape[0]
    columns = jnp.arange(length)

    def one_block(block_index):
        row_start = block_index * block_rows
        query_part = lax.dynamic_slice_in_dim(queries, row_start, block_rows, 0)
        scores = (
            jnp.einsum("qhd,khd->hqk", query_part, key_rows, preferred_element_type=jnp.float32)
            * score_scale
        )
        allowed = columns[None, :] <= (row_start + jnp.arange(block_rows))[:, None]
        scores = jnp.where(allowed[None], scores, negative)
        row_max = jnp.max(scores, axis=2, keepdims=True)
        weights = jnp.exp(scores - row_max)
        totals = jnp.sum(weights, axis=2, keepdims=True)
        prob_low = (weights / totals).astype(jnp.bfloat16)
        mixture = jnp.einsum(
            "hqk,khd->qhd", prob_low, value_rows, preferred_element_type=jnp.float32
        )
        return (mixture, row_max[:, :, 0] + jnp.log(totals[:, :, 0]))

    mixture, logsum = lax.map(one_block, jnp.arange(length // block_rows))
    return (mixture.reshape(queries.shape), logsum)


def prompt_back(queries, key_rows, value_rows, grad_mix, logsum, block_rows, score_scale):
    length = queries.shape[0]
    columns = jnp.arange(length)

    def one_block(carried, block_index):
        grad_keys, grad_values = carried
        row_start = block_index * block_rows
        query_part = lax.dynamic_slice_in_dim(queries, row_start, block_rows, 0)
        grad_part = lax.dynamic_slice_in_dim(grad_mix, row_start, block_rows, 0)
        scores = (
            jnp.einsum("qhd,khd->hqk", query_part, key_rows, preferred_element_type=jnp.float32)
            * score_scale
        )
        allowed = columns[None, :] <= (row_start + jnp.arange(block_rows))[:, None]
        prob_rows = jnp.where(allowed[None], jnp.exp(scores - logsum[block_index][:, :, None]), 0.0)
        grad_prob = jnp.einsum(
            "qhd,khd->hqk", grad_part, value_rows, preferred_element_type=jnp.float32
        )
        inner = jnp.sum(prob_rows * grad_prob, axis=2, keepdims=True)
        grad_scores = (prob_rows * (grad_prob - inner) * score_scale).astype(jnp.bfloat16)
        grad_query = jnp.einsum(
            "hqk,khd->qhd", grad_scores, key_rows, preferred_element_type=jnp.float32
        )
        grad_keys = grad_keys + jnp.einsum(
            "hqk,qhd->khd", grad_scores, query_part, preferred_element_type=jnp.float32
        )
        grad_values = grad_values + jnp.einsum(
            "hqk,qhd->khd",
            prob_rows.astype(jnp.bfloat16),
            grad_part,
            preferred_element_type=jnp.float32,
        )
        return ((grad_keys, grad_values), grad_query)

    zero_rows = jnp.zeros(key_rows.shape, jnp.float32)
    (grad_keys, grad_values), grad_query = lax.scan(
        one_block, (zero_rows, zero_rows), jnp.arange(length // block_rows)
    )
    return (grad_query.reshape(queries.shape), grad_keys, grad_values)


def cont_scores(queries, far_keys, near_keys, score_scale):
    far_scores = (
        jnp.einsum("bqhd,bkhd->bhqk", queries, far_keys, preferred_element_type=jnp.float32)
        * score_scale
    )
    near_scores = (
        jnp.einsum("bqhd,bkhd->bhqk", queries, near_keys, preferred_element_type=jnp.float32)
        * score_scale
    )
    near_scores = jnp.where(near_mask(queries.shape[1])[None, None], near_scores, negative)
    return (far_scores, near_scores)


def cont_pass(queries, far_keys, far_values, near_keys, near_values, score_scale):
    far_scores, near_scores = cont_scores(queries, far_keys, near_keys, score_scale)
    row_max = jnp.maximum(
        jnp.max(far_scores, axis=3, keepdims=True), jnp.max(near_scores, axis=3, keepdims=True)
    )
    far_weights = jnp.exp(far_scores - row_max)
    near_weights = jnp.exp(near_scores - row_max)
    totals = jnp.sum(far_weights, axis=3, keepdims=True) + jnp.sum(
        near_weights, axis=3, keepdims=True
    )
    mixture = jnp.einsum(
        "bhqk,bkhd->bqhd",
        (far_weights / totals).astype(jnp.bfloat16),
        far_values,
        preferred_element_type=jnp.float32,
    )
    mixture = mixture + jnp.einsum(
        "bhqk,bkhd->bqhd",
        (near_weights / totals).astype(jnp.bfloat16),
        near_values,
        preferred_element_type=jnp.float32,
    )
    return (mixture, row_max[..., 0] + jnp.log(totals[..., 0]))


def cont_back(queries, far_keys, far_values, near_keys, near_values, grad_mix, logsum, score_scale):
    far_scores, near_scores = cont_scores(queries, far_keys, near_keys, score_scale)
    far_prob = jnp.exp(far_scores - logsum[..., None])
    near_prob = jnp.where(
        near_mask(queries.shape[1])[None, None], jnp.exp(near_scores - logsum[..., None]), 0.0
    )
    far_grad = jnp.einsum(
        "bqhd,bkhd->bhqk", grad_mix, far_values, preferred_element_type=jnp.float32
    )
    near_grad = jnp.einsum(
        "bqhd,bkhd->bhqk", grad_mix, near_values, preferred_element_type=jnp.float32
    )
    inner = jnp.sum(far_prob * far_grad, axis=3, keepdims=True) + jnp.sum(
        near_prob * near_grad, axis=3, keepdims=True
    )
    far_step = (far_prob * (far_grad - inner) * score_scale).astype(jnp.bfloat16)
    near_step = (near_prob * (near_grad - inner) * score_scale).astype(jnp.bfloat16)
    grad_query = jnp.einsum(
        "bhqk,bkhd->bqhd", far_step, far_keys, preferred_element_type=jnp.float32
    )
    grad_query = grad_query + jnp.einsum(
        "bhqk,bkhd->bqhd", near_step, near_keys, preferred_element_type=jnp.float32
    )
    grad_far_keys = jnp.einsum(
        "bhqk,bqhd->bkhd", far_step, queries, preferred_element_type=jnp.float32
    )
    grad_far_values = jnp.einsum(
        "bhqk,bqhd->bkhd",
        far_prob.astype(jnp.bfloat16),
        grad_mix,
        preferred_element_type=jnp.float32,
    )
    grad_near_keys = jnp.einsum(
        "bhqk,bqhd->bkhd", near_step, queries, preferred_element_type=jnp.float32
    )
    grad_near_values = jnp.einsum(
        "bhqk,bqhd->bkhd",
        near_prob.astype(jnp.bfloat16),
        grad_mix,
        preferred_element_type=jnp.float32,
    )
    return (grad_query, grad_far_keys, grad_far_values, grad_near_keys, grad_near_values)


def arrange(qkv_low, cont_group):
    head_cols = qkv_low.reshape(qkv_low.shape[0], -1, 3, HD)
    prompt_rows = GPS * P_SIZE
    conts = head_cols[prompt_rows:].reshape(-1, CL, head_cols.shape[1], 3, HD)
    group_width = math.gcd(conts.shape[0], max(1, 512 // CL))
    conts = conts.reshape(-1, group_width, CL, head_cols.shape[1], 3, HD)
    owner_blocks = cont_group.reshape(-1, group_width)
    prompt_heads = head_cols[:prompt_rows].reshape(GPS, P_SIZE, head_cols.shape[1], 3, HD)
    return (head_cols, prompt_heads, conts, owner_blocks)


def attend(qkv_low, cont_group, score_scale):
    head_cols, prompt_heads, conts, owner_blocks = arrange(qkv_low, cont_group)
    local_heads = head_cols.shape[1]
    prompt_rows = GPS * P_SIZE
    own_pairs = head_cols[:prompt_rows, :, 1:].reshape(prompt_rows, local_heads * 2 * HD)
    every_pair = lax.all_gather(own_pairs, "gr", axis=0, tiled=True)
    far_table = every_pair.reshape(-1, P_SIZE, local_heads, 2, HD)
    block_rows = min(512, P_SIZE)

    def prompt_group(group_rows):
        return prompt_pass(
            group_rows[:, :, 0], group_rows[:, :, 1], group_rows[:, :, 2], block_rows, score_scale
        )

    prompt_mix, prompt_sum = lax.map(prompt_group, prompt_heads)

    def cont_block(item_pack):
        cont_part, group_ids = item_pack
        far_rows = far_table[group_ids]
        return cont_pass(
            cont_part[:, :, :, 0],
            far_rows[:, :, :, 0],
            far_rows[:, :, :, 1],
            cont_part[:, :, :, 1],
            cont_part[:, :, :, 2],
            score_scale,
        )

    cont_mix, cont_sum = lax.map(cont_block, (conts, owner_blocks))
    mixture = jnp.concatenate(
        [prompt_mix.reshape(prompt_rows, local_heads * HD), cont_mix.reshape(-1, local_heads * HD)],
        axis=0,
    )
    return (mixture, (far_table, prompt_sum, cont_sum))


def attend_back(qkv_low, cont_group, saved, grad_mix_low, score_scale):
    far_table, prompt_sum, cont_sum = saved
    head_cols, prompt_heads, conts, owner_blocks = arrange(qkv_low, cont_group)
    local_heads = head_cols.shape[1]
    prompt_rows = GPS * P_SIZE
    block_rows = min(512, P_SIZE)
    prompt_grad = grad_mix_low[:prompt_rows].reshape(GPS, P_SIZE, local_heads, HD)
    cont_grad = grad_mix_low[prompt_rows:].reshape(
        conts.shape[0], conts.shape[1], CL, local_heads, HD
    )

    def prompt_group(item_pack):
        group_rows, grad_rows, logsum = item_pack
        return prompt_back(
            group_rows[:, :, 0],
            group_rows[:, :, 1],
            group_rows[:, :, 2],
            grad_rows,
            logsum,
            block_rows,
            score_scale,
        )

    grad_pq, grad_pk, grad_pv = lax.map(prompt_group, (prompt_heads, prompt_grad, prompt_sum))

    def cont_block(carried, item_pack):
        cont_part, group_ids, grad_rows, logsum = item_pack
        far_rows = far_table[group_ids]
        grad_q, grad_fk, grad_fv, grad_nk, grad_nv = cont_back(
            cont_part[:, :, :, 0],
            far_rows[:, :, :, 0],
            far_rows[:, :, :, 1],
            cont_part[:, :, :, 1],
            cont_part[:, :, :, 2],
            grad_rows,
            logsum,
            score_scale,
        )
        carried = carried.at[group_ids].add(jnp.stack([grad_fk, grad_fv], axis=3))
        return (carried, jnp.stack([grad_q, grad_nk, grad_nv], axis=3))

    far_grads, cont_grads = lax.scan(
        cont_block,
        jnp.zeros(far_table.shape, jnp.float32),
        (conts, owner_blocks, cont_grad, cont_sum),
    )
    returned = lax.psum_scatter(
        far_grads.reshape(-1, local_heads * 2 * HD).astype(jnp.bfloat16),
        "gr",
        scatter_dimension=0,
        tiled=True,
    ).astype(jnp.float32)
    returned = returned.reshape(GPS, P_SIZE, local_heads, 2, HD)
    prompt_grads = jnp.stack(
        [grad_pq, grad_pk + returned[:, :, :, 0], grad_pv + returned[:, :, :, 1]], axis=3
    )
    return jnp.concatenate(
        [prompt_grads.reshape(prompt_rows, -1), cont_grads.reshape(-1, local_heads * 3 * HD)],
        axis=0,
    )


def grid_layer(
    tokens,
    teacher,
    pass_embed,
    ln1_gain,
    ln1_bias,
    qkv_weight,
    out_weight,
    out_bias,
    ln2_gain,
    ln2_bias,
    fc1_weight,
    fc1_bias,
    fc2_weight,
    fc2_bias,
    cont_group,
    token_count,
):
    score_scale = 1.0 / math.sqrt(HD)
    tokens_grid, teacher_grid = (
        lax.all_to_all(tokens, "gr", split_axis=1, concat_axis=0, tiled=True),
        lax.all_to_all(teacher, "gr", split_axis=1, concat_axis=0, tiled=True),
    )
    gain_one = ln1_gain.astype(jnp.float32)
    gain_two = ln2_gain.astype(jnp.float32)
    hidden = tokens_grid.astype(jnp.float32) + pass_embed.astype(jnp.float32)
    normed_one, unit_one, factor_one = layer_norm(hidden, gain_one, ln1_bias.astype(jnp.float32))
    spread_one = spread_columns(normed_one.astype(jnp.bfloat16))
    qkv_low = reduce_rows(spread_one, qkv_weight, SHARD, False).astype(jnp.bfloat16)
    mixture, saved = attend(qkv_low, cont_group, score_scale)
    mixture_low = mixture.astype(jnp.bfloat16)
    hidden_two = hidden + (
        project_rows(mixture_low, out_weight, False) + out_bias.astype(jnp.float32)
    )
    normed_two, unit_two, factor_two = layer_norm(
        hidden_two, gain_two, ln2_bias.astype(jnp.float32)
    )
    spread_two = spread_columns(normed_two.astype(jnp.bfloat16))
    pre_act = reduce_rows(spread_two, fc1_weight, SHARD, False) + fc1_bias.astype(jnp.float32)
    active, gelu_back = jax.vjp(partial(jax.nn.gelu, approximate=True), pre_act)
    active_low = active.astype(jnp.bfloat16)
    final = hidden_two + (project_rows(active_low, fc2_weight, True) + fc2_bias.astype(jnp.float32))
    grad_final = final - teacher_grid.astype(jnp.float32)
    grad_branch = spread_columns(grad_final.astype(jnp.bfloat16))
    grad_fc2_bias = jnp.sum(grad_branch, axis=0, dtype=jnp.float32)
    grad_active = reduce_rows(grad_branch, fc2_weight, SHARD, False)
    grad_fc2 = fold_rows(
        active_low,
        partial(weight_step_swapped, grad_branch),
        jnp.zeros(fc2_weight.shape, jnp.float32),
    )
    (grad_pre,) = gelu_back(grad_active)
    rows_all = spread_two.shape[0]
    start_up = (
        jnp.zeros(fc1_weight.shape, jnp.float32),
        jnp.zeros(fc1_bias.shape, jnp.float32),
        jnp.zeros((rows_all, fc1_weight.shape[0]), jnp.float32),
    )
    grad_fc1, grad_fc1_bias, partial_two = fold_rows(
        grad_pre.astype(jnp.bfloat16), partial(input_bias_step, spread_two, fc1_weight), start_up
    )
    grad_normed_two = sum_columns(partial_two)
    grad_norm_two, grad_gain_two, grad_shift_two = layer_norm_back(
        grad_normed_two, gain_two, unit_two, factor_two
    )
    grad_hidden_two = grad_final + grad_norm_two
    grad_attended = spread_columns(grad_hidden_two.astype(jnp.bfloat16))
    grad_out_bias = jnp.sum(grad_attended, axis=0, dtype=jnp.float32)
    grad_mixture = reduce_rows(grad_attended, out_weight, SHARD, True)
    grad_out = fold_rows(
        mixture_low, partial(weight_step, grad_attended), jnp.zeros(out_weight.shape, jnp.float32)
    )
    grad_qkv = attend_back(
        qkv_low, cont_group, saved, grad_mixture.astype(jnp.bfloat16), score_scale
    )
    start_qkv = (
        jnp.zeros(qkv_weight.shape, jnp.float32),
        jnp.zeros((rows_all, qkv_weight.shape[0]), jnp.float32),
    )
    grad_qkv_weight, partial_one = fold_rows(
        grad_qkv.astype(jnp.bfloat16), partial(input_step, spread_one, qkv_weight), start_qkv
    )
    grad_qkv_weight, grad_out, grad_out_bias, grad_fc1, grad_fc1_bias, grad_fc2, grad_fc2_bias = (
        data_total(
            (
                grad_qkv_weight,
                grad_out,
                grad_out_bias,
                grad_fc1,
                grad_fc1_bias,
                grad_fc2,
                grad_fc2_bias,
            )
        )
    )
    grad_normed_one = sum_columns(partial_one)
    grad_norm_one, grad_gain_one, grad_shift_one = layer_norm_back(
        grad_normed_one, gain_one, unit_one, factor_one
    )
    input_grad = grad_hidden_two + grad_norm_one
    row_place = lax.axis_index("gr")
    vectors = jnp.stack(
        [jnp.sum(input_grad, axis=0), grad_gain_one, grad_shift_one, grad_gain_two, grad_shift_two]
    )
    padded = lax.dynamic_update_slice_in_dim(
        jnp.zeros((vectors.shape[0], lax.axis_size("gr"), vectors.shape[1]), jnp.float32),
        vectors[:, None],
        row_place,
        1,
    )
    summed, squared = small_total((padded, jnp.sum(grad_final * grad_final)))
    own = lax.dynamic_index_in_dim(summed, row_place, 1, keepdims=False)
    loss = (squared / (D * token_count[0].astype(jnp.float32))).reshape(1)
    final_rows, input_rows = (
        lax.all_to_all(
            final.astype(jnp.bfloat16), "gr", split_axis=0, concat_axis=1, tiled=True
        ).astype(final.dtype),
        lax.all_to_all(
            input_grad.astype(jnp.bfloat16), "gr", split_axis=0, concat_axis=1, tiled=True
        ).astype(input_grad.dtype),
    )
    return (
        final_rows.astype(jnp.bfloat16),
        loss,
        input_rows,
        own[0],
        own[1],
        own[2],
        grad_qkv_weight,
        grad_out,
        grad_out_bias,
        own[3],
        own[4],
        grad_fc1,
        grad_fc1_bias,
        grad_fc2,
        grad_fc2_bias,
    )


def on_device(
    tokens,
    teacher,
    pass_embed,
    ln1_gain,
    ln1_bias,
    qkv_weight,
    out_weight,
    out_bias,
    ln2_gain,
    ln2_bias,
    fc1_weight,
    fc1_bias,
    fc2_weight,
    fc2_bias,
    cont_group,
    token_count,
):
    return grid_layer(
        tokens,
        teacher,
        pass_embed,
        ln1_gain,
        ln1_bias,
        qkv_weight,
        out_weight,
        out_bias,
        ln2_gain,
        ln2_bias,
        fc1_weight,
        fc1_bias,
        fc2_weight,
        fc2_bias,
        cont_group,
        token_count,
    )


def solution(mesh):
    in_specs = (
        P(("dp", "gr", "gc"), None),
        P(("dp", "gr", "gc"), None),
        P("gr"),
        P("gr"),
        P("gr"),
        P("gr", "gc"),
        P("gc", "gr"),
        P("gr"),
        P("gr"),
        P("gr"),
        P("gr", "gc"),
        P("gc"),
        P("gr", "gc"),
        P("gr"),
        P(("dp", "gr")),
        P(),
    )
    out_specs = (
        P(("dp", "gr", "gc"), None),
        P(),
        P(("dp", "gr", "gc"), None),
        P("gr"),
        P("gr"),
        P("gr"),
        P("gr", "gc"),
        P("gc", "gr"),
        P("gr"),
        P("gr"),
        P("gr"),
        P("gr", "gc"),
        P("gc"),
        P("gr", "gc"),
        P("gr"),
    )
    return jax.shard_map(
        on_device, mesh=mesh, in_specs=in_specs, out_specs=out_specs, check_vma=False
    )
```

profile of v0, /device:TPU:0, one launch (start us, length us, event | category | flops | bytes accessed | tf_op | source)
XLA Modules:
  0.0 2206.1 jit_solution(17885552895020646739)
XLA Ops:
  9.6 6.3 all-to-all-start
  16.0 20.0 all-to-all-done
  36.2 10.0 psum.119
  46.6 9.2 psum.120
  58.7 27.6 %all-gather.10.cloned.1.call-done = bf16[8192,192]{0,1:T(8,128)(2,1)} async-done(((bf16[2048,192]{0,1:T(8,128)(2,1)}), bf16[8192,192]{0,1:T(8,128)(2,1)}) %all-gather.10.cloned.1.call-update) | async-done | bytes 3145744 | tf_op jit(solution)/shard_map/all_gather | solution.py:64
  86.4 8.2 convolution_convert_fusion.2
  95.9 160.2 %reduce-scatter.10.cloned.1.call-done = bf16[2048,576]{0,1:T(8,128)(2,1)} async-done(((bf16[8192,576]{0,1:T(8,128)(2,1)}), bf16[2048,576]{0,1:T(8,128)(2,1)}) %reduce-scatter.10.cloned.1.call-update) | async-done | bytes 2359312 | tf_op jit(solution)/shard_map/reduce_scatter | solution.py:76
  259.9 14.1 while.74
  279.3 43.4 %all-gather.12.cloned.1.call-done = bf16[4096,384]{0,1:T(8,128)(2,1)} async-done(((bf16[1024,384]{0,1:T(8,128)(2,1)}), bf16[4096,384]{0,1:T(8,128)(2,1)}) %all-gather.12.cloned.1.call-update) | async-done | bytes 3145744 | tf_op jit(solution)/shard_map/all_gather | solution.py:318
  322.8 6.2 reshape.386
  331.8 30.1 %while.72 = (s32[]{:T(128)}, bf16[2,4,128,3,64]{2,4,3,1,0:T(8,128)(2,1)}, f32[2,4,3,128]{3,2,1,0:T(4,128)}, s32[2,4]{1,0:T(2,128)}, bf16[4,1024,3,2,64]{1,4,3,2,...) while((s32[]{:T(128)}, bf16[2,4,128,3,64]{2,4,3,1,0:T(8,128)(2,1)}, ...), condition=%wide.region_14.15_spmd, body=%wide.region_9.0_spmd.sunk | while | flops 468827648 | bytes 55208240 | solution.py:341
  368.4 62.0 %all-gather.14.cloned.1.call-done = bf16[8192,192]{0,1:T(8,128)(2,1)} async-done(((bf16[2048,192]{0,1:T(8,128)(2,1)}), bf16[8192,192]{0,1:T(8,128)(2,1)}) %all-gather.14.cloned.1.call-update) | async-done | bytes 3145744 | tf_op jit(solution)/shard_map/all_gather | solution.py:93
  430.4 4.6 convolution_convert_fusion.7
  437.4 34.4 %reduce-scatter.12.cloned.1.call-done = bf16[2048,192]{0,1:T(8,128)(2,1)} async-done(((bf16[8192,192]{0,1:T(8,128)(2,1)}), bf16[2048,192]{0,1:T(8,128)(2,1)}) %reduce-scatter.12.cloned.1.call-update) | async-done | bytes 786448 | tf_op jit(solution)/shard_map/reduce_scatter | solution.py:85
  475.0 12.4 psum.121
  489.7 9.1 psum.122
  502.2 27.3 %all-gather.16.cloned.1.call-done = bf16[8192,192]{0,1:T(8,128)(2,1)} async-done(((bf16[2048,192]{0,1:T(8,128)(2,1)}), bf16[8192,192]{0,1:T(8,128)(2,1)}) %all-gather.16.cloned.1.call-update) | async-done | bytes 3145744 | tf_op jit(solution)/shard_map/all_gather | solution.py:64
  529.5 9.9 convolution_convert_fusion.1
  540.8 210.7 %reduce-scatter.14.cloned.1.call-done = bf16[2048,768]{1,0:T(8,128)(2,1)} async-done(((bf16[8192,768]{1,0:T(8,128)(2,1)}), bf16[2048,768]{1,0:T(8,128)(2,1)}) %reduce-scatter.14.cloned.1.call-update) | async-done | bytes 3145744 | tf_op jit(solution)/shard_map/reduce_scatter | solution.py:76
  751.5 5.0 multiply_convert_fusion.3
  756.6 219.3 %all-gather.18.cloned.1.call-done = bf16[8192,768]{1,0:T(8,128)(2,1)} async-done(((bf16[2048,768]{1,0:T(8,128)(2,1)}), bf16[8192,768]{1,0:T(8,128)(2,1)}) %all-gather.18.cloned.1.call-update) | async-done | bytes 12582928 | tf_op jit(solution)/shard_map/all_gather | solution.py:93
  975.9 10.5 convolution_convert_fusion.5
  988.8 4.2 all-to-all-start.2
  994.3 19.4 all-to-all-done.2
  1016.4 6.5 reduce-scatter.16.cloned.1.call-done
  1022.8 4.3 fusion.162
  1027.6 28.2 %all-gather.20.cloned.1.call-done = bf16[8192,192]{0,1:T(8,128)(2,1)} async-done(((bf16[2048,192]{0,1:T(8,128)(2,1)}), bf16[8192,192]{0,1:T(8,128)(2,1)}) %all-gather.20.cloned.1.call-update) | async-done | bytes 3145744 | tf_op jit(solution)/shard_map/all_gather | solution.py:64
  1055.8 9.9 convolution_convert_fusion
  1065.8 211.9 %reduce-scatter.18.cloned.1.call-done = bf16[2048,768]{1,0:T(8,128)(2,1)} async-done(((bf16[8192,768]{1,0:T(8,128)(2,1)}), bf16[2048,768]{1,0:T(8,128)(2,1)}) %reduce-scatter.18.cloned.1.call-update) | async-done | bytes 3145744 | tf_op jit(solution)/shard_map/reduce_scatter | solution.py:76
  1277.8 8.1 fusion.120
  1285.9 219.4 %all-gather.22.cloned.1.call-done = bf16[8192,768]{1,0:T(8,128)(2,1)} async-done(((bf16[2048,768]{1,0:T(8,128)(2,1)}), bf16[8192,768]{1,0:T(8,128)(2,1)}) %all-gather.22.cloned.1.call-update) | async-done | bytes 12582928 | tf_op jit(solution)/shard_map/all_gather | solution.py:93
  1505.3 10.5 convolution_convert_fusion.4
  1515.8 36.2 %reduce-scatter.20.cloned.1.call-done = bf16[2048,192]{0,1:T(8,128)(2,1)} async-done(((bf16[8192,192]{0,1:T(8,128)(2,1)}), bf16[2048,192]{0,1:T(8,128)(2,1)}) %reduce-scatter.20.cloned.1.call-update) | async-done | bytes 786448 | tf_op jit(solution)/shard_map/reduce_scatter | solution.py:85
  1555.1 18.7 all-reduce.2
  1573.8 3.5 fusion.159
  1577.4 25.9 %all-gather.24.cloned.1.call-done = bf16[8192,192]{0,1:T(8,128)(2,1)} async-done(((bf16[2048,192]{0,1:T(8,128)(2,1)}), bf16[8192,192]{0,1:T(8,128)(2,1)}) %all-gather.24.cloned.1.call-update) | async-done | bytes 3145744 | tf_op jit(solution)/shard_map/all_gather | solution.py:64
  1603.3 4.6 convolution_convert_fusion.6
  1607.9 60.4 %reduce-scatter.22.cloned.1.call-done = bf16[2048,192]{0,1:T(8,128)(2,1)} async-done(((bf16[8192,192]{0,1:T(8,128)(2,1)}), bf16[2048,192]{0,1:T(8,128)(2,1)}) %reduce-scatter.22.cloned.1.call-update) | async-done | bytes 786448 | tf_op jit(solution)/shard_map/reduce_scatter | solution.py:76
  1672.3 3.5 broadcast_in_dim.149
  1675.8 82.7 %while.73 = (s32[]{:T(128)}, f32[4,1024,3,2,64]{1,4,3,2,0:T(8,128)}, bf16[2,4,128,3,3,64]{2,5,3,1,4,0:T(8,128)(2,1)}, s32[2,4]{1,0:T(2,128)}, bf16[2,4,128,3,3,6...) while((s32[]{:T(128)}, ...), condition=%wide.region_38.39_spmd, body=%wide.region_34.38_spmd.sunk | while | flops 1160199680 | bytes 151509424 | solution.py:390
  1698.6 3.3 copy.122
  1701.9 13.4 scatter_fusion
  1743.2 13.4 scatter_fusion
  1768.6 79.6 %while.75 = (s32[]{:T(128)}, f32[1024,3,64]{0,2,1:T(8,128)}, f32[1024,3,64]{0,2,1:T(8,128)}, bf16[2,512,3,64]{1,3,2,0:T(8,128)(2,1)S(1)}, s32[2]{0:T(128)S(1)}, ...) while((s32[]{:T(128)}, f32[1024,3,64]{0,2,1:T(8,128)}, ...), condition=%wide.region_33.34_spmd.clone, body=%wide.region_31.33_spmd.clone.sunk | while | flops 1048843776 | bytes 109371744 | solution.py:214
  1777.3 3.7 fusion.274
  1781.0 12.9 fusion.278
  1793.9 14.6 fusion.276
  1816.9 3.7 fusion.274
  1820.6 12.9 fusion.278
  1833.5 14.7 fusion.276
  1857.3 166.5 %all-gather.26.cloned.1.call-done = bf16[8192,576]{0,1:T(8,128)(2,1)} async-done(((bf16[2048,576]{0,1:T(8,128)(2,1)}), bf16[8192,576]{0,1:T(8,128)(2,1)}) %all-gather.26.cloned.1.call-update) | async-done | bytes 9437200 | tf_op jit(solution)/shard_map/all_gather | solution.py:93
  2023.7 8.0 convolution_convert_fusion.3
  2034.0 4.2 all-to-all-start.1
  2038.3 8.4 convolution_convert_fusion.8
  2046.7 8.6 convolution_convert_fusion.9
  2057.0 11.0 reduce-scatter.26.cloned.1.call-done
  2070.1 18.7 all-reduce.1
  2088.9 4.8 fusion.160
  2094.7 4.2 all-to-all-start.3
  2099.2 9.0 convolution_convert_fusion.10
  2111.7 6.8 reduce_sum.237
  2119.0 5.1 all-reduce.3
  2125.9 21.0 all-reduce.7.cloned.1.call-done
  2154.2 39.9 %all-reduce = (f32[]{:T(128)}, f32[5,4,192]{2,1,0:T(4,128)S(1)}) all-reduce(f32[]{:T(128)} %get-tuple-element.433, f32[5,4,192]{2,1,0:T(4,128)S(1)} %dynamic_update_slice.38), channel_id=1, replica_groups=mesh['dp'=2,'gr'=4,'gc'=4] {'dp','gr','gc'}, use_global_device_ids=true, to_apply=%region_23.24 | all-reduce | flops 3841 | bytes 30728 | tf_op jit(solution)/shard_map/psum | solution.py:34
  (399 shorter events, 200.5 us)
Async XLA Ops:
  7.2 968.8 %copy-start = (bf16[192,768]{1,0:T(8,128)(2,1)S(1)}, bf16[192,768]{1,0:T(8,128)(2,1)}, u32[]{:S(2)}) copy-start(bf16[192,768]{1,0:T(8,128)(2,1)} %param.36) | copy-start | bytes 884740
  7.2 8.7 copy-start.64
  7.2 8.7 copy-start.65
  7.2 8.7 copy-start.66
  9.6 26.4 %all-to-all-start = ((bf16[512,4,192]{0,2,1:T(8,128)(2,1)}), bf16[512,4,192]{0,2,1:T(8,128)(2,1)S(1)}, u32[]{:S(2)}, u32[]{:S(2)}) async-start(bf16[512,4,192]{0,2,1:T(8,128)(2,1)} %bitcast.32), calls=%async_computation | async-start | bytes 1572864 | tf_op jit(solution)/shard_map/all_to_all | solution.py:431
  15.9 70.5 %all-gather.10.cloned.1.call-start = ((), (), s32[]{:S(2)}) async-start(), calls=%async_computation.13 | async-start | bytes 3932160 | tf_op jit(solution)/shard_map/all_gather | solution.py:64
  15.9 40.3 %copy-start.55 = (f32[192]{0:T(256)}, f32[192]{0:T(256)S(1)}, u32[]{:S(2)}) copy-start(f32[192]{0:T(256)S(1)} %convert_element_type.210) | copy-start | bytes 2308
  15.9 40.3 %copy-start.60 = (f32[192]{0:T(256)}, f32[192]{0:T(256)S(1)}, u32[]{:S(2)}) copy-start(f32[192]{0:T(256)S(1)} %convert_element_type.212) | copy-start | bytes 2308
  46.2 10.0 copy-start.44
  56.0 30.3 %copy-start.32 = (bf16[192,576]{1,0:T(8,128)(2,1)S(1)}, bf16[192,576]{1,0:T(8,128)(2,1)}, u32[]{:S(2)}) copy-start(bf16[192,576]{1,0:T(8,128)(2,1)} %param.29) | copy-start | bytes 663556
  58.7 197.4 %reduce-scatter.10.cloned.1.call-start = ((), (), s32[]{:S(2)}) async-start(), calls=%async_computation.14 | async-start | bytes 11796480 | tf_op jit(solution)/shard_map/reduce_scatter | solution.py:76
  94.6 228.2 %all-gather.12.cloned.1.call-start = ((), (), s32[]{:S(2)}) async-start(), calls=%async_computation.15 | async-start | bytes 3932160 | tf_op jit(solution)/shard_map/all_gather | solution.py:318
  258.3 172.1 %all-gather.14.cloned.1.call-start = ((), (), s32[]{:S(2)}) async-start(), calls=%async_computation.16 | async-start | bytes 3932160 | tf_op jit(solution)/shard_map/all_gather | solution.py:93
  362.0 68.5 %copy-start.36 = (bf16[192,192]{1,0:T(8,128)(2,1)S(1)}, bf16[192,192]{1,0:T(8,128)(2,1)}, u32[]{:S(2)}) copy-start(bf16[192,192]{1,0:T(8,128)(2,1)} %param.30) | copy-start | bytes 221188
  368.1 103.7 %reduce-scatter.12.cloned.1.call-start = ((), (), s32[]{:S(2)}) async-start(), calls=%async_computation.17 | async-start | bytes 3932160 | tf_op jit(solution)/shard_map/reduce_scatter | solution.py:85
  435.0 36.8 %copy-start.56 = (f32[192]{0:T(256)S(1)}, f32[192]{0:T(256)}, u32[]{:S(2)}) copy-start(f32[192]{0:T(256)} %copy-done.55) | copy-start | bytes 2308
  435.0 94.5 %all-gather.16.cloned.1.call-start = ((), (), s32[]{:S(2)}) async-start(), calls=%async_computation.18 | async-start | bytes 3932160 | tf_op jit(solution)/shard_map/all_gather | solution.py:64
  488.1 1085.7 %copy-start.40 = (f32[2048]{0:T(1024)}, f32[2048]{0:T(1024)S(1)}, u32[]{:S(2)}) copy-start(f32[2048]{0:T(1024)S(1)} %broadcast_multiply_fusion.4) | copy-start | bytes 24580
  499.5 1074.3 %copy-start.42 = (f32[2048]{0:T(1024)}, f32[2048]{0:T(1024)S(1)}, u32[]{:S(2)}) copy-start(f32[2048]{0:T(1024)S(1)} %add_rsqrt_fusion) | copy-start | bytes 24580
  502.2 249.3 %reduce-scatter.14.cloned.1.call-start = ((), (), s32[]{:S(2)}) async-start(), calls=%async_computation.19 | async-start | bytes 15728640 | tf_op jit(solution)/shard_map/reduce_scatter | solution.py:76
  539.5 436.5 %all-gather.18.cloned.1.call-start = ((), (), s32[]{:S(2)}) async-start(), calls=%async_computation.20 | async-start | bytes 15728640 | tf_op jit(solution)/shard_map/all_gather | solution.py:93
  756.5 266.3 %reduce-scatter.16.cloned.1.call-start = ((), (), s32[]{:S(2)}) async-start(), calls=%async_computation.21 | async-start | bytes 3932160 | tf_op jit(solution)/shard_map/reduce_scatter | solution.py:85
  988.8 24.9 %all-to-all-start.2 = ((bf16[512,4,192]{0,2,1:T(8,128)(2,1)}), bf16[512,4,192]{0,2,1:T(8,128)(2,1)}, u32[]{:S(2)}, u32[]{:S(2)}) async-start(bf16[512,4,192]{0,2,1:T(8,128)(2,1)} %bitcast.416), calls=%async_computation.6 | async-start | bytes 1572864 | tf_op jit(solution)/shard_map/all_to_all | solution.py:432
  993.0 62.8 %all-gather.20.cloned.1.call-start = ((), (), s32[]{:S(2)}) async-start(), calls=%async_computation.22 | async-start | bytes 3932160 | tf_op jit(solution)/shard_map/all_gather | solution.py:64
  1027.2 250.6 %reduce-scatter.18.cloned.1.call-start = ((), (), s32[]{:S(2)}) async-start(), calls=%async_computation.23 | async-start | bytes 15728640 | tf_op jit(solution)/shard_map/reduce_scatter | solution.py:76
  1065.8 212.0 %copy-start.54 = (f32[768]{0:T(1024)S(1)}, f32[768]{0:T(1024)}, u32[]{:S(2)}) copy-start(f32[768]{0:T(1024)} %convert_element_type.224) | copy-start | bytes 9220
  1065.8 439.5 %all-gather.22.cloned.1.call-start = ((), (), s32[]{:S(2)}) async-start(), calls=%async_computation.24 | async-start | bytes 15728640 | tf_op jit(solution)/shard_map/all_gather | solution.py:93
  1285.8 219.4 %copy-start.39 = (bf16[192,768]{1,0:T(8,128)(2,1)S(1)}, bf16[192,768]{1,0:T(8,128)(2,1)}, u32[]{:S(2)}) copy-start(bf16[192,768]{1,0:T(8,128)(2,1)} %param.34) | copy-start | bytes 884740
  1285.9 266.2 %reduce-scatter.20.cloned.1.call-start = ((), (), s32[]{:S(2)}) async-start(), calls=%async_computation.25 | async-start | bytes 3932160 | tf_op jit(solution)/shard_map/reduce_scatter | solution.py:85
  1515.8 36.3 %copy-start.58 = (f32[192]{0:T(256)S(1)}, f32[192]{0:T(256)}, u32[]{:S(2)}) copy-start(f32[192]{0:T(256)} %convert_element_type.219) | copy-start | bytes 2308
  1515.8 87.5 %all-gather.24.cloned.1.call-start = ((), (), s32[]{:S(2)}) async-start(), calls=%async_computation.26 | async-start | bytes 3932160 | tf_op jit(solution)/shard_map/all_gather | solution.py:64
  1573.8 34.0 %copy-start.50 = (f32[2048]{0:T(1024)}, f32[2048]{0:T(1024)S(1)}, u32[]{:S(2)}) copy-start(f32[2048]{0:T(1024)S(1)} %get-tuple-element.446) | copy-start | bytes 24580
  1573.8 34.0 %copy-start.52 = (f32[2048]{0:T(1024)}, f32[2048]{0:T(1024)S(1)}, u32[]{:S(2)}) copy-start(f32[2048]{0:T(1024)S(1)} %get-tuple-element.447) | copy-start | bytes 24580
  1577.3 91.0 %reduce-scatter.22.cloned.1.call-start = ((), (), s32[]{:S(2)}) async-start(), calls=%async_computation.27 | async-start | bytes 3932160 | tf_op jit(solution)/shard_map/reduce_scatter | solution.py:76
  1607.9 244.1 %reduce-scatter.24.cloned.1.call-start = ((), (), s32[]{:S(2)}) async-start(), calls=%async_computation.28 | async-start | bytes 3932160 | tf_op jit(solution)/shard_map/reduce_scatter | solution.py:395
  1701.9 13.4 copy-start.18
  1743.2 13.4 copy-start.18
  1767.3 256.4 %all-gather.26.cloned.1.call-start = ((), (), s32[]{:S(2)}) async-start(), calls=%async_computation.29 | async-start | bytes 11796480 | tf_op jit(solution)/shard_map/all_gather | solution.py:93
  1855.2 168.6 %copy-start.33 = (bf16[192,576]{1,0:T(8,128)(2,1)S(1)}, bf16[192,576]{1,0:T(8,128)(2,1)}, u32[]{:S(2)}) copy-start(bf16[192,576]{1,0:T(8,128)(2,1)} %param.29) | copy-start | bytes 663556
  1856.8 211.2 %reduce-scatter.26.cloned.1.call-start = ((), (), s32[]{:S(2)}) async-start(), calls=%async_computation.30 | async-start | bytes 3932160 | tf_op jit(solution)/shard_map/reduce_scatter | solution.py:85
  2031.8 6.5 copy-start.19
  2034.0 60.7 %all-to-all-start.1 = ((bf16[4,512,192]{1,2,0:T(8,128)(2,1)}), bf16[4,512,192]{1,2,0:T(8,128)(2,1)}, u32[]{:S(2)}, u32[]{:S(2)}) async-start(bf16[4,512,192]{1,2,0:T(8,128)(2,1)} %bitcast.415), calls=%async_computation.5 | async-start | bytes 1572864 | tf_op jit(solution)/shard_map/all_to_all | solution.py:525
  2038.3 8.4 copy-start.29
  2046.7 8.6 copy-start.25
  2046.7 8.6 copy-start.28
  2055.3 12.8 copy-start.15
  2055.3 12.8 copy-start.45
  2055.3 12.8 copy-start.47
  2055.3 12.8 copy-start.57
  2055.3 12.8 copy-start.61
  2055.4 33.5 %copy-start.41 = (f32[2048]{0:T(1024)S(1)}, f32[2048]{0:T(1024)}, u32[]{:S(2)}) copy-start(f32[2048]{0:T(1024)} %copy-done.40) | copy-start | bytes 24580
  2055.4 33.5 %copy-start.43 = (f32[2048]{0:T(1024)S(1)}, f32[2048]{0:T(1024)}, u32[]{:S(2)}) copy-start(f32[2048]{0:T(1024)} %copy-done.42) | copy-start | bytes 24580
  2055.4 33.5 %copy-start.51 = (f32[2048]{0:T(1024)S(1)}, f32[2048]{0:T(1024)}, u32[]{:S(2)}) copy-start(f32[2048]{0:T(1024)} %copy-done.50) | copy-start | bytes 24580
  2055.4 33.5 %copy-start.53 = (f32[2048]{0:T(1024)S(1)}, f32[2048]{0:T(1024)}, u32[]{:S(2)}) copy-start(f32[2048]{0:T(1024)} %copy-done.52) | copy-start | bytes 24580
  2055.4 33.5 %copy-start.59 = (f32[192]{0:T(256)S(1)}, f32[192]{0:T(256)}, u32[]{:S(2)}) copy-start(f32[192]{0:T(256)} %convert_element_type.219) | copy-start | bytes 2308
  2057.0 31.9 %copy-start.11 = (f32[2048,192]{0,1:T(8,128)S(1)}, f32[2048,192]{0,1:T(8,128)}, u32[]{:S(2)}) copy-start(f32[2048,192]{0,1:T(8,128)} %get-tuple-element.419) | copy-start | bytes 4718596
  2094.7 100.6 %all-to-all-start.3 = ((bf16[4,512,192]{1,2,0:T(8,128)(2,1)}), bf16[4,512,192]{1,2,0:T(8,128)(2,1)}, u32[]{:S(2)}, u32[]{:S(2)}) async-start(bf16[4,512,192]{1,2,0:T(8,128)(2,1)} %bitcast.296), calls=%async_computation.12 | async-start | bytes 1572864 | tf_op jit(solution)/shard_map/all_to_all | solution.py:528
  2098.9 48.0 %all-reduce.7.cloned.1.call-start = ((), (), s32[]{:S(2)}) async-start(), calls=%async_computation.31 | async-start | bytes 1867776 | tf_op jit(solution)/shard_map/psum | solution.py:38
  2099.2 12.0 copy-start.20
  2111.7 6.8 copy-start.26
  2118.5 35.6 %copy-start.62 = (f32[192]{0:T(256)S(1)}, f32[192]{0:T(256)}, u32[]{:S(2)}) copy-start(f32[192]{0:T(256)} %get-tuple-element.331) | copy-start | bytes 2308
  2118.5 35.6 %copy-start.63 = (f32[192]{0:T(256)S(1)}, f32[192]{0:T(256)}, u32[]{:S(2)}) copy-start(f32[192]{0:T(256)} %get-tuple-element.335) | copy-start | bytes 2308
  2119.0 34.9 %copy-start.27 = (f32[2048,192]{0,1:T(8,128)S(1)}, f32[2048,192]{0,1:T(8,128)}, u32[]{:S(2)}) copy-start(f32[2048,192]{0,1:T(8,128)} %get-tuple-element.415) | copy-start | bytes 4718596
  2153.9 44.4 %copy-start.1 = (bf16[192,768]{1,0:T(8,128)(2,1)S(1)}, bf16[192,768]{1,0:T(8,128)(2,1)}, u32[]{:S(2)}) copy-start(bf16[192,768]{1,0:T(8,128)(2,1)} %param.36) | copy-start | bytes 884740
  (45 other events, 80.2 us)
Sparse Core Ops, SparseCore 0:
  58.8 27.5 all-gather.9
  94.7 161.2 reduce-scatter.9
  258.4 64.2 all-gather.11
  368.3 62.1 all-gather.13
  435.1 36.6 reduce-scatter.11
  502.3 27.1 all-gather.15
  539.6 211.8 reduce-scatter.13
  756.7 219.2 all-gather.17
  986.6 36.1 reduce-scatter.15
  1027.3 28.5 all-gather.19
  1065.9 211.8 reduce-scatter.17
  1286.0 219.2 all-gather.21
  1515.9 36.1 reduce-scatter.19
  1577.4 25.7 all-gather.23
  1608.0 60.2 reduce-scatter.21
  1767.4 60.3 reduce-scatter.23
  1857.0 166.7 all-gather.25
  2031.9 36.1 reduce-scatter.25
  2108.4 38.5 all-reduce.6
where the time goes:
time: 2210 us
  waiting for transfers between devices  1610 us (73%)
  matrix products  208 us (9%)
  other arithmetic  123 us (6%)
  blocking collectives  123 us (6%)
  local copies, waits for them, and re-layouts  94.9 us (4%)
    all_gather x4, waiting for transfers between devices, fold_rows(): lax.all_gather(part, 'gr', axis=0, tiled=True)  667 us
    reduce_scatter x4, waiting for transfers between devices, reduce_rows(): lax.psum_scatter(term(jnp.int32(0), lax.axis_size('gr') * row_count).asty...  643 us
    all_gather x4, waiting for transfers between devices, spread_columns(): return lax.all_gather(values, 'gc', axis=0, tiled=True)  109 us
    reduce_scatter x4, waiting for transfers between devices, sum_columns(): lax.psum_scatter(partial_rows.astype(jnp.bfloat16), 'gc', scatter_dimensi...  88.1 us
    psum x6, blocking collectives, feature_sums(): return lax.psum(values, 'gr')  78.2 us
  transfers between devices with their start and end apart: 23, of which 20 were waited for; matrix products, arithmetic and copies ran while one was open for 7% of the time, Pallas kernels for 0%

commit v1 on v0

v1 whole, which is shorter than its diff:
```python
from functools import partial

import jax
import jax.numpy as jnp
from jax import lax
from jax.experimental import pallas as pl
from jax.experimental.pallas import tpu as pltpu
from jax.sharding import PartitionSpec as P

D = 768
HD = 64
FF = 3072
P_SIZE = 1024
CL = 128
QROWS = 512
eps = 1e-05
negative = -1e30
BF = jnp.bfloat16
F32 = jnp.float32


def nt(a, b):
    return lax.dot_general(a, b, (((1,), (1,)), ((), ())), preferred_element_type=F32)


def nn(a, b):
    return lax.dot_general(a, b, (((1,), (0,)), ((), ())), preferred_element_type=F32)


def tn(a, b):
    return lax.dot_general(a, b, (((0,), (0,)), ((), ())), preferred_element_type=F32)


def att_fwd_kernel(grp_ref, z_ref, q_ref, kvo_ref, kvp_ref, o_ref, lse_ref):
    j = pl.program_id(1)
    row0 = pl.multiple_of(grp_ref[j] * P_SIZE, P_SIZE)
    z = z_ref[0]
    lane = lax.broadcasted_iota(jnp.int32, (CL, 128), 1)
    low = lane < 64
    zero = jnp.zeros((CL, 128), BF)
    q = q_ref[...]
    q_parts = (jnp.where(low, zero, q), jnp.where(low, q, zero))

    @pl.when(z >= 2)
    def _():
        row = lax.broadcasted_iota(jnp.int32, (CL, CL), 0)
        near_ok = lax.broadcasted_iota(jnp.int32, (CL, CL), 1) <= row
        mixes, sums = [], []
        for h in range(2):
            cols = slice(128 * h, 128 * h + 128)
            kv = kvp_ref[pl.ds(row0, P_SIZE), cols]
            kvo = kvo_ref[:, cols]
            far = nt(q_parts[h], kv)
            near = jnp.where(near_ok, nt(q_parts[h], kvo), negative)
            top = jnp.maximum(
                jnp.max(far, axis=1, keepdims=True), jnp.max(near, axis=1, keepdims=True)
            )
            far = jnp.exp(far - top)
            near = jnp.exp(near - top)
            total = jnp.sum(far, axis=1, keepdims=True) + jnp.sum(near, axis=1, keepdims=True)
            mix = nn(far.astype(BF), kv) + nn(near.astype(BF), kvo)
            mixes.append(mix / total)
            sums.append(jnp.broadcast_to(top + jnp.log(total), (CL, 128)))
        o_ref[...] = jnp.where(low, mixes[0], mixes[1]).astype(BF)
        lse_ref[...] = jnp.where(low, sums[0], sums[1])

    @pl.when(z < 2)
    def _():
        limit = z * QROWS + (j % (QROWS // CL)) * CL
        row = lax.broadcasted_iota(jnp.int32, (CL, P_SIZE), 0)
        key = lax.broadcasted_iota(jnp.int32, (CL, P_SIZE), 1)
        allowed = key - row <= limit
        mixes, sums = [], []
        for h in range(2):
            cols = slice(128 * h, 128 * h + 128)
            kv = kvp_ref[pl.ds(row0, P_SIZE), cols]
            far = jnp.where(allowed, nt(q_parts[h], kv), negative)
            top = jnp.max(far, axis=1, keepdims=True)
            far = jnp.exp(far - top)
            total = jnp.sum(far, axis=1, keepdims=True)
            mix = nn(far.astype(BF), kv)
            mixes.append(mix / total)
            sums.append(jnp.broadcast_to(top + jnp.log(total), (CL, 128)))
        o_ref[...] = jnp.where(low, mixes[0], mixes[1]).astype(BF)
        lse_ref[...] = jnp.where(low, sums[0], sums[1])


def attend(grp, z, q, kvo, kvp):
    rows = q.shape[0]
    pairs = q.shape[1] // 128
    groups_rows = kvp.shape[0]
    return pl.pallas_call(
        att_fwd_kernel,
        name="att_fwd",
        grid_spec=pltpu.PrefetchScalarGridSpec(
            num_scalar_prefetch=2,
            grid=(pairs, rows // CL),
            in_specs=[
                pl.BlockSpec((CL, 128), lambda p, j, *_: (j, p)),
                pl.BlockSpec((CL, 256), lambda p, j, *_: (j, p)),
                pl.BlockSpec((groups_rows, 256), lambda p, j, *_: (0, p)),
            ],
            out_specs=[
                pl.BlockSpec((CL, 128), lambda p, j, *_: (j, p)),
                pl.BlockSpec((CL, 128), lambda p, j, *_: (j, p)),
            ],
        ),
        out_shape=[
            jax.ShapeDtypeStruct((rows, pairs * 128), BF),
            jax.ShapeDtypeStruct((rows, pairs * 128), F32),
        ],
        compiler_params=pltpu.CompilerParams(vmem_limit_bytes=40 << 20),
        cost_estimate=pl.CostEstimate(
            flops=4 * rows * P_SIZE * 128 * pairs * 2,
            bytes_accessed=groups_rows * 512 * pairs,
            transcendentals=rows * P_SIZE * pairs * 2,
        ),
    )(grp, z, q, kvo, kvp)


def att_bwd_kernel(
    grp_ref, z_ref, q_ref, gm_ref, lse_ref, kvo_ref, kvp_ref, dq_ref, dkvo_ref, dkvp_ref, acc
):
    j = pl.program_id(1)
    row0 = pl.multiple_of(grp_ref[j] * P_SIZE, P_SIZE)
    z = z_ref[0]
    low = lax.broadcasted_iota(jnp.int32, (CL, 128), 1) < 64
    zero = jnp.zeros((CL, 128), BF)
    q = q_ref[...]
    gm = gm_ref[...]
    stacks = (
        jnp.concatenate([jnp.where(low, zero, q), jnp.where(low, gm, zero)], axis=0),
        jnp.concatenate([jnp.where(low, q, zero), jnp.where(low, zero, gm)], axis=0),
    )

    @pl.when(j == 0)
    def _():
        acc[...] = jnp.zeros_like(acc)

    @pl.when(z >= 2)
    def _():
        row = lax.broadcasted_iota(jnp.int32, (CL, CL), 0)
        near_ok = row <= lax.broadcasted_iota(jnp.int32, (CL, CL), 1)
        dqs = []
        for h in range(2):
            cols = slice(128 * h, 128 * h + 128)
            kv = kvp_ref[pl.ds(row0, P_SIZE), cols]
            kvo = kvo_ref[:, cols]
            lse = lse_ref[0, 0, h : h + 1, :]
            far = nt(kv, stacks[h])
            near = nt(kvo, stacks[h])
            pf = jnp.exp(far[:, :CL] - lse)
            pn = jnp.where(near_ok, jnp.exp(near[:, :CL] - lse), 0.0)
            df = far[:, CL:]
            dn = near[:, CL:]
            inner = jnp.sum(pf * df, axis=0, keepdims=True) + jnp.sum(
                pn * dn, axis=0, keepdims=True
            )
            sf = (pf * (df - inner)).astype(BF)
            sn = (pn * (dn - inner)).astype(BF)
            acc[pl.ds(row0, P_SIZE), cols] += nn(
                jnp.concatenate([sf, pf.astype(BF)], axis=1), stacks[h]
            )
            dkvo_ref[:, cols] = nn(
                jnp.concatenate([sn, pn.astype(BF)], axis=1), stacks[h]
            ).astype(BF)
            dqs.append(tn(sf, kv) + tn(sn, kvo))
        dq_ref[...] = (jnp.where(low, dqs[1], dqs[0]) * 0.125).astype(BF)

    @pl.when(z < 2)
    def _():
        limit = z * QROWS + (j % (QROWS // CL)) * CL
        key = lax.broadcasted_iota(jnp.int32, (P_SIZE, CL), 0)
        row = lax.broadcasted_iota(jnp.int32, (P_SIZE, CL), 1)
        allowed = key - row <= limit
        dqs = []
        for h in range(2):
            cols = slice(128 * h, 128 * h + 128)
            kv = kvp_ref[pl.ds(row0, P_SIZE), cols]
            lse = lse_ref[0, 0, h : h + 1, :]
            far = nt(kv, stacks[h])
            pf = jnp.where(allowed, jnp.exp(far[:, :CL] - lse), 0.0)
            df = far[:, CL:]
            inner = jnp.sum(pf * df, axis=0, keepdims=True)
            sf = (pf * (df - inner)).astype(BF)
            acc[pl.ds(row0, P_SIZE), cols] += nn(
                jnp.concatenate([sf, pf.astype(BF)], axis=1), stacks[h]
            )
            dqs.append(tn(sf, kv))
        dkvo_ref[...] = jnp.zeros_like(dkvo_ref)
        dq_ref[...] = (jnp.where(low, dqs[1], dqs[0]) * 0.125).astype(BF)

    @pl.when(j == pl.num_programs(1) - 1)
    def _():
        dkvp_ref[...] = acc[...].astype(BF)


def attend_back(grp, z, q, gm, lse, kvo, kvp):
    rows = q.shape[0]
    pairs = q.shape[1] // 128
    groups_rows = kvp.shape[0]
    return pl.pallas_call(
        att_bwd_kernel,
        name="att_bwd",
        grid_spec=pltpu.PrefetchScalarGridSpec(
            num_scalar_prefetch=2,
            grid=(pairs, rows // CL),
            in_specs=[
                pl.BlockSpec((CL, 128), lambda p, j, *_: (j, p)),
                pl.BlockSpec((CL, 128), lambda p, j, *_: (j, p)),
                pl.BlockSpec((1, 1, 2, 128), lambda p, j, *_: (p, j, 0, 0)),
                pl.BlockSpec((CL, 256), lambda p, j, *_: (j, p)),
                pl.BlockSpec((groups_rows, 256), lambda p, j, *_: (0, p)),
            ],
            out_specs=[
                pl.BlockSpec((CL, 128), lambda p, j, *_: (j, p)),
                pl.BlockSpec((CL, 256), lambda p, j, *_: (j, p)),
                pl.BlockSpec((groups_rows, 256), lambda p, j, *_: (0, p)),
            ],
            scratch_shapes=[pltpu.VMEM((groups_rows, 256), F32)],
        ),
        out_shape=[
            jax.ShapeDtypeStruct((rows, pairs * 128), BF),
            jax.ShapeDtypeStruct((rows, pairs * 256), BF),
            jax.ShapeDtypeStruct((groups_rows, pairs * 256), BF),
        ],
        compiler_params=pltpu.CompilerParams(vmem_limit_bytes=48 << 20),
        cost_estimate=pl.CostEstimate(
            flops=10 * rows * P_SIZE * 128 * pairs * 2,
            bytes_accessed=groups_rows * 1024 * pairs,
            transcendentals=rows * P_SIZE * pairs * 2,
        ),
    )(grp, z, q, gm, lse, kvo, kvp)


def norm(hidden, gain, shift):
    center = jnp.mean(hidden, axis=1, keepdims=True)
    offset = hidden - center
    factor = lax.rsqrt(jnp.mean(offset * offset, axis=1, keepdims=True) + eps)
    unit = offset * factor
    return unit * gain + shift, unit, factor


def norm_back(grad, gain, unit, factor):
    grad_unit = grad * gain
    first = jnp.mean(grad_unit, axis=1, keepdims=True)
    second = jnp.mean(grad_unit * unit, axis=1, keepdims=True)
    grad_in = factor * (grad_unit - first - unit * second)
    return grad_in, jnp.sum(grad * unit, axis=0), jnp.sum(grad, axis=0)


def head_layout(blocks):
    chunks = blocks.transpose(1, 0, 2).reshape(D, 6, 3, HD)
    q_list, kv_list = [], []
    for pair in range(3):
        a, b = 2 * pair, 2 * pair + 1
        q_list += [chunks[:, b, 0], chunks[:, a, 0]]
        kv_list += [chunks[:, a, 2], chunks[:, a, 1], chunks[:, b, 1], chunks[:, b, 2]]
    return jnp.concatenate(q_list, axis=1), jnp.concatenate(kv_list, axis=1)


def head_layout_back(grad_q, grad_kv):
    qc = grad_q.reshape(D, 3, 2, HD)
    kc = grad_kv.reshape(D, 3, 4, HD)
    pieces = []
    for pair in range(3):
        pieces += [qc[:, pair, 1], kc[:, pair, 1], kc[:, pair, 0]]
        pieces += [qc[:, pair, 0], kc[:, pair, 2], kc[:, pair, 3]]
    whole = jnp.concatenate(pieces, axis=1)
    return whole.reshape(D, 2, 576).transpose(1, 0, 2)


def on_device(
    tokens,
    teacher,
    pass_embed,
    ln1_gain,
    ln1_bias,
    qkv_weight,
    out_weight,
    out_bias,
    ln2_gain,
    ln2_bias,
    fc1_weight,
    fc1_bias,
    fc2_weight,
    fc2_bias,
    cont_group,
    token_count,
):
    n_gr = lax.axis_size("gr")
    n_gc = lax.axis_size("gc")
    z = lax.axis_index("gr")
    g = lax.axis_index("gc")
    c = g % 2
    y = g // 2
    swap_core = [(i, i ^ 1) for i in range(n_gc)]
    swap_y = [(i, i ^ 2) for i in range(n_gc)]

    vectors = jnp.stack(
        [pass_embed, ln1_gain, ln1_bias, out_bias, ln2_gain, ln2_bias, fc2_bias]
    )
    vectors = lax.all_gather(vectors, "gr", axis=1, tiled=True).astype(F32)
    embed, gain1, shift1, b_out, gain2, shift2, b_down = [vectors[i] for i in range(7)]
    b_up = lax.all_gather(fc1_bias, "gc", axis=0, tiled=True).astype(F32)
    owners = lax.all_gather(cont_group, "gr", axis=0, tiled=True)
    owners = owners.reshape(n_gc, 2, 4)
    mine = lax.dynamic_slice(owners, (2 * y, jnp.maximum(z - 2, 0), 0), (2, 1, 4)).reshape(8)
    own_groups = jnp.repeat(2 * y + jnp.arange(2), 4)
    grp = jnp.where(z < 2, own_groups, mine).astype(jnp.int32)
    z_arr = z.astype(jnp.int32).reshape(1)

    hidden = tokens.astype(F32) + embed
    normed1, unit1, factor1 = norm(hidden, gain1, shift1)
    n1 = normed1.astype(BF)

    w_other = lax.ppermute(qkv_weight, "gc", swap_y)
    w_pair = jnp.where(y == 0, jnp.stack([qkv_weight, w_other]), jnp.stack([w_other, qkv_weight]))
    w_qkv = lax.all_gather(w_pair, "gr", axis=1, tiled=True)
    w_q, w_kv = head_layout(w_qkv)

    n1_other = lax.ppermute(n1, "gc", swap_core)
    n1_chip = jnp.where(
        c == 0, jnp.concatenate([n1, n1_other]), jnp.concatenate([n1_other, n1])
    )
    n1_col = lax.all_gather(n1, "gr", axis=0, tiled=True)[:P_SIZE]
    n1_prompt = lax.all_gather(n1_col, "gc", axis=0, tiled=True)

    w_out = lax.all_gather(out_weight, ("gc", "gr"))
    w_up = lax.all_gather(fc1_weight, ("gc", "gr")).reshape(n_gc, D, FF // n_gc)
    w_down = lax.all_gather(fc2_weight, ("gc", "gr")).reshape(n_gc, D, FF // n_gc)
    w_out = w_out.reshape(n_gc, n_gr, 192, 192).transpose(0, 2, 1, 3).reshape(D, D)

    kvp = nn(n1_prompt, w_kv).astype(BF)
    kvo = nn(n1_chip, w_kv).astype(BF)
    q = (nn(n1_chip, w_q) * 0.125).astype(BF)
    mixed_heads, lse = attend(grp, z_arr, q, kvo, kvp)
    lse_rows = lse[:, ::64].reshape(8, CL, 3, 2).transpose(2, 0, 3, 1)

    halves = mixed_heads.reshape(2, QROWS, 2, 192)
    keep = lax.dynamic_index_in_dim(halves, c, 0, keepdims=False)
    give = lax.dynamic_index_in_dim(halves, 1 - c, 0, keepdims=False)
    take = lax.ppermute(give, "gc", swap_core)
    mixed = jnp.where(c == 0, jnp.stack([keep, take], axis=2), jnp.stack([take, keep], axis=2))
    mixed = mixed.reshape(QROWS, D)

    hidden2 = hidden + nn(mixed, w_out) + b_out
    normed2, unit2, factor2 = norm(hidden2, gain2, shift2)
    n2 = normed2.astype(BF)
    pre = lax.dot_general(n2, w_up, (((1,), (1,)), ((), ())), preferred_element_type=F32)
    pre = pre.reshape(QROWS, FF) + b_up
    active, gelu_back = jax.vjp(partial(jax.nn.gelu, approximate=True), pre)
    act = active.astype(BF)
    act_blocks = act.reshape(QROWS, n_gc, FF // n_gc)
    final = (
        hidden2
        + lax.dot_general(
            act_blocks, w_down, (((1, 2), (0, 2)), ((), ())), preferred_element_type=F32
        )
        + b_down
    )
    grad_final = final - teacher.astype(F32)
    squared = jnp.sum(grad_final * grad_final)
    gb = grad_final.astype(BF)
    grad_b_down = jnp.sum(gb, axis=0, dtype=F32)
    grad_active = lax.dot_general(
        gb, w_down, (((1,), (1,)), ((), ())), preferred_element_type=F32
    ).reshape(QROWS, FF)
    grad_w_down = jnp.einsum("td,tgf->gdf", gb, act_blocks, preferred_element_type=F32)
    (grad_pre,) = gelu_back(grad_active)
    gp = grad_pre.astype(BF)
    gp_blocks = gp.reshape(QROWS, n_gc, FF // n_gc)
    grad_b_up = jnp.sum(gp, axis=0, dtype=F32)
    grad_w_up = jnp.einsum("td,tgf->gdf", n2, gp_blocks, preferred_element_type=F32)
    grad_n2 = lax.dot_general(
        gp_blocks, w_up, (((1, 2), (0, 2)), ((), ())), preferred_element_type=F32
    )
    back2, grad_gain2, grad_shift2 = norm_back(grad_n2, gain2, unit2, factor2)
    grad_h2 = grad_final + back2
    ga = grad_h2.astype(BF)
    grad_b_out = jnp.sum(ga, axis=0, dtype=F32)
    grad_w_out = tn(mixed, ga)
    gm = nt(ga, w_out).astype(BF)

    gm_blocks = gm.reshape(QROWS, 2, 2, 192)
    gm_keep = lax.dynamic_index_in_dim(gm_blocks, c, 2, keepdims=False)
    gm_give = lax.dynamic_index_in_dim(gm_blocks, 1 - c, 2, keepdims=False)
    gm_take = lax.ppermute(gm_give, "gc", swap_core)
    gm_chip = jnp.where(c == 0, jnp.stack([gm_keep, gm_take]), jnp.stack([gm_take, gm_keep]))
    gm_chip = gm_chip.reshape(2 * QROWS, 384)

    def scatter16(blocks):
        part = lax.psum_scatter(
            blocks.astype(BF), ("gc", "gr"), scatter_dimension=0, tiled=True
        )
        return lax.psum(part, "dp").astype(F32)

    out_w_down = scatter16(grad_w_down.reshape(n_gc * n_gr * 192, 768))
    out_w_up = scatter16(grad_w_up.reshape(n_gc * n_gr * 192, 768))
    out_w_out = scatter16(
        grad_w_out.reshape(n_gc, 192, n_gr, 192).transpose(0, 2, 1, 3).reshape(-1, 192)
    )

    dq, dkvo, dkvp = attend_back(grp, z_arr, q, gm_chip, lse_rows, kvo, kvp)

    part_prompt = nt(dkvp, w_kv).astype(BF)
    back_prompt = lax.psum_scatter(part_prompt, "gc", scatter_dimension=0, tiled=True)
    back_prompt = lax.psum_scatter(
        jnp.concatenate([back_prompt, jnp.zeros_like(back_prompt)]),
        "gr",
        scatter_dimension=0,
        tiled=True,
    ).astype(F32)
    part_chip = (nt(dq, w_q) + nt(dkvo, w_kv)).reshape(2, QROWS, D)
    part_keep = lax.dynamic_index_in_dim(part_chip, c, 0, keepdims=False)
    part_give = lax.dynamic_index_in_dim(part_chip, 1 - c, 0, keepdims=False)
    part_take = lax.ppermute(part_give.astype(BF), "gc", swap_core).astype(F32)
    grad_n1 = part_keep + part_take + back_prompt

    grad_kv = tn(n1_prompt, dkvp) + tn(n1_chip, dkvo)
    grad_q = tn(n1_chip, dq)
    grad_qkv = head_layout_back(grad_q, grad_kv)
    qkv_keep = lax.dynamic_index_in_dim(grad_qkv, y, 0, keepdims=False)
    qkv_give = lax.dynamic_index_in_dim(grad_qkv, 1 - y, 0, keepdims=False)
    qkv_take = lax.ppermute(qkv_give.astype(BF), "gc", swap_y).astype(F32)
    out_w_qkv = lax.psum_scatter(
        (qkv_keep + qkv_take).astype(BF), "gr", scatter_dimension=0, tiled=True
    )
    out_w_qkv = lax.psum(out_w_qkv, "dp").astype(F32)

    back1, grad_gain1, grad_shift1 = norm_back(grad_n1, gain1, unit1, factor1)
    input_grad = grad_h2 + back1
    sums = jnp.concatenate(
        [
            jnp.sum(input_grad, axis=0),
            grad_gain1,
            grad_shift1,
            grad_gain2,
            grad_shift2,
            grad_b_out,
            grad_b_down,
            grad_b_up,
            jnp.broadcast_to(squared, (128,)),
        ]
    )
    sums = lax.psum(sums, ("dp", "gr", "gc"))
    loss = (sums[-1] / (D * token_count[0].astype(F32))).reshape(1)
    rows = sums[: 7 * D].reshape(7, n_gr, D // n_gr)
    rows = lax.dynamic_index_in_dim(rows, z, 1, keepdims=False)
    up = lax.dynamic_index_in_dim(
        sums[7 * D : 7 * D + FF].reshape(n_gc, FF // n_gc), g, 0, keepdims=False
    )
    return (
        final.astype(BF),
        loss,
        input_grad,
        rows[0],
        rows[1],
        rows[2],
        out_w_qkv,
        out_w_out,
        rows[5],
        rows[3],
        rows[4],
        out_w_up,
        up,
        out_w_down,
        rows[6],
    )


def solution(mesh):
    rows = P(("dp", "gr", "gc"), None)
    in_specs = (
        rows,
        rows,
        P("gr"),
        P("gr"),
        P("gr"),
        P("gr", "gc"),
        P("gc", "gr"),
        P("gr"),
        P("gr"),
        P("gr"),
        P("gr", "gc"),
        P("gc"),
        P("gr", "gc"),
        P("gr"),
        P(("dp", "gr")),
        P(),
    )
    out_specs = (
        rows,
        P(),
        rows,
        P("gr"),
        P("gr"),
        P("gr"),
        P("gr", "gc"),
        P("gc", "gr"),
        P("gr"),
        P("gr"),
        P("gr"),
        P("gr", "gc"),
        P("gc"),
        P("gr", "gc"),
        P("gr"),
    )
    return jax.shard_map(
        on_device, mesh=mesh, in_specs=in_specs, out_specs=out_specs, check_vma=False
    )
```

time: 2210 us -> 947 us (0.43)
  waiting for transfers between devices: 1610 us -> 611 us
  matrix products: 208 us -> 74.2 us
  other arithmetic: 123 us -> 21.3 us
  Pallas kernels: 0 us -> 67.9 us
  blocking collectives: 123 us -> 69.2 us
    all_gather x9 -> x6, waiting for transfers between devices: 820 us -> 215 us  [the longest x1 56.9 us: on_device(): n1_col = lax.all_gather(n1, 'gr', axis=0, tiled=True)[:P_SIZE]]
    reduce_scatter x9 -> x5, waiting for transfers between devices: 731 us -> 335 us  [the longest x3 218 us: scatter16(): lax.psum_scatter(blocks.astype(BF), ('gc', 'gr'), scatter_dimension=0, ti...]
    dot_general x54 -> x18, matrix products: 208 us -> 74.2 us  [the longest x4 13.8 us: nt(): lax.dot_general(a, b, (((1,), (1,)), ((), ())), preferred_element_type=F32)]
    psum x8 -> x1, blocking collectives: 123 us -> 40.6 us  [on_device(): sums = lax.psum(sums, ('dp', 'gr', 'gc'))]
    pallas_call x0 -> x2, Pallas kernels: none -> 67.9 us  [the longest x1 43.7 us: attend_back(): pl.pallas_call(att_bwd_kernel, name='att_bwd', grid_spec=pltpu.PrefetchSc...]
    convert_element_type x28 -> x6, other arithmetic: 51 us -> 7.9 us  [the longest x3 4.37 us: scatter16(): return lax.psum(part, 'dp').astype(F32)]
    all_to_all x4 -> x0, waiting for transfers between devices: 39.4 us -> none  [the longest x1 20 us: grid_layer(): lax.all_to_all(tokens, 'gr', split_axis=1, concat_axis=0, tiled=True)]
    scatter-add x2 -> x0, other arithmetic: 26.8 us -> none  [cont_block(): carried = carried.at[group_ids].add(jnp.stack([grad_fk, grad_fv], axis=3))]
  transfers between devices with their start and end apart: 23 -> 19, of which waited for: 20 -> 14; matrix products, arithmetic and copies ran while one was open for 7% -> 10% of each run, Pallas kernels for 0% -> 3%
where the time goes in v1:
time: 947 us; the launch traced here: 943 us
  waiting for transfers between devices  611 us (65%)
  local copies, waits for them, and re-layouts  77.6 us (8%)
  matrix products  74.2 us (8%)
  blocking collectives  69.2 us (7%)
  Pallas kernels  67.9 us (7%)
  other arithmetic  21.3 us (2%)
  between operations  18.4 us (2%)
    reduce_scatter x3, waiting for transfers between devices, scatter16(): lax.psum_scatter(blocks.astype(BF), ('gc', 'gr'), scatter_dimension=0, ti...  218 us
    reduce_scatter x1, waiting for transfers between devices, on_device(): lax.psum_scatter(part_prompt, 'gc', scatter_dimension=0, tiled=True)  59.7 us
    reduce_scatter x1, waiting for transfers between devices, on_device(): lax.psum_scatter(jnp.concatenate([back_prompt, jnp.zeros_like(back_prompt...  57.3 us
    all_gather x1, waiting for transfers between devices, on_device(): n1_col = lax.all_gather(n1, 'gr', axis=0, tiled=True)[:P_SIZE]  56.9 us
    all_gather x1, waiting for transfers between devices, on_device(): lax.all_gather(fc2_weight, ('gc', 'gr')).reshape(n_gc, D, FF // n_gc)  47.5 us
    all_gather x1, waiting for transfers between devices, on_device(): w_up = lax.all_gather(fc1_weight, ('gc', 'gr')).reshape(n_gc, D, FF // n_gc)  44 us
    pallas_call x1, Pallas kernels, attend_back(): pl.pallas_call(att_bwd_kernel, name='att_bwd', grid_spec=pltpu.PrefetchSc...  43.7 us
    psum x1, blocking collectives, on_device(): sums = lax.psum(sums, ('dp', 'gr', 'gc'))  40.6 us
  transfers between devices with their start and end apart: 19, of which 14 were waited for; matrix products, arithmetic and copies ran while one was open for 10% of the time, Pallas kernels for 3%

profile of v1, /device:TPU:0, one launch (start us, length us, event | category | flops | bytes accessed | tf_op | source)
XLA Modules:
  0.0 943.0 jit_solution(5322700956216169703)
XLA Ops:
  11.9 14.8 %all-gather.3 = bf16[4,192,7]{1,2,0:T(8,128)(2,1)S(1)} all-gather(bf16[1,192,7]{1,2,0:T(8,128)(2,1)S(1)} %bitcast.375), channel_id=1, replica_groups=mesh['dp'=2,'gr'=4,'gc'=4] {'gr'}, dimensions={0}, use_global_device_ids=true | all-gather | bytes 13440 | tf_op jit(solution)/shard_map/all_gather | solution.py:303
  27.5 1.4 fusion.30
  28.9 1.5 multiply_reduce_fusion.5
  30.4 1.3 add_convert_fusion.1
  31.8 1.6 collective-permute-start.1
  33.3 4.7 collective-permute-done.1
  38.2 1.3 copy.116
  39.5 56.9 %all-gather.14.cloned.1.call-done = bf16[2048,768]{1,0:T(8,128)(2,1)} async-done(((bf16[512,768]{1,0:T(8,128)(2,1)}), bf16[2048,768]{1,0:T(8,128)(2,1)}) %all-gather.14.cloned.1.call-update) | async-done | bytes 3145744 | tf_op jit(solution)/shard_map/all_gather | solution.py:326
  96.4 2.7 slice.248
  102.6 8.5 all-reduce.2
  111.4 29.4 %all-gather.12.cloned.1.call-done = bf16[2,768,576]{2,0,1:T(2,128)(2,1)} async-done(((bf16[2,192,576]{2,0,1:T(2,128)(2,1)}), bf16[2,768,576]{2,0,1:T(2,128)(2,1)}) %all-gather.12.cloned.1.call-update) | async-done | bytes 1769488 | tf_op jit(solution)/shard_map/all_gather | solution.py:319
  140.9 5.7 copy.117
  148.3 2.6 convolution_convert_fusion.3.kvo_ref
  150.9 36.7 %all-gather.16.cloned.1.call-done = bf16[4096,768]{1,0:T(8,128)(2,1)} async-done(((bf16[1024,768]{1,0:T(8,128)(2,1)}), bf16[4096,768]{1,0:T(8,128)(2,1)}) %all-gather.16.cloned.1.call-update) | async-done | bytes 6291472 | tf_op jit(solution)/shard_map/all_gather | solution.py:327
  187.6 7.7 convolution_convert_fusion.1.kvp_ref
  195.3 24.2 %att_fwd.1 = (bf16[1024,384]{1,0:T(8,128)(2,1)S(1)}, f32[1024,384]{1,0:T(8,128)S(1)}) custom-call(s32[8]{0:T(128)S(1)} %broadcast_select_fusion.grp_ref, s32[1]{0:T(128)} %bitcast.4.z_ref, bf16[1024,384]{1,0:T(8,128)(2,1)S(1)} %multiply_convert_fusion.1.q_ref, bf16[1024,768]{1,0:T(8,128)(2,1)S(1)} %copy-done.3, ...), custom_call_target="tpu_custom_call" | custom-call | flops 3221225472 | bytes 6291456 | tf_op jit(solution)/shard_map/att_fwd/pallas_call | solution.py:92
  220.8 2.6 reshape.197
  223.3 2.5 constant_dynamic-slice_fusion.9
  226.2 5.3 all-gather.4
  232.2 3.8 copy.175
  236.0 4.0 reshape.199
  240.0 44.0 %all-gather.20.cloned.1.call-done = bf16[3072,768]{1,0:T(8,128)(2,1)} async-done(((bf16[192,768]{1,0:T(8,128)(2,1)}), bf16[3072,768]{1,0:T(8,128)(2,1)}) %all-gather.20.cloned.1.call-update) | async-done | bytes 4718608 | tf_op jit(solution)/shard_map/all_gather | solution.py:330
  284.0 6.6 copy.120
  290.6 47.5 %all-gather.22.cloned.1.call-done = bf16[3072,768]{1,0:T(8,128)(2,1)} async-done(((bf16[192,768]{1,0:T(8,128)(2,1)}), bf16[3072,768]{1,0:T(8,128)(2,1)}) %all-gather.22.cloned.1.call-update) | async-done | bytes 4718608 | tf_op jit(solution)/shard_map/all_gather | solution.py:331
  338.1 6.7 copy.122
  344.9 1.4 maximum_select_fusion.1
  348.5 5.7 multiply_convert_fusion
  354.2 3.3 convert_reduce_fusion.1
  357.6 9.3 convert_reduce_fusion
  366.9 3.5 fusion.27
  370.4 2.6 convert_bitcast_fusion
  374.2 1.7 convolution_convert_fusion.4
  375.9 1.4 copy.124
  378.4 3.7 slice.198
  385.1 1.4 copy-done.4
  386.5 43.7 %att_bwd.1 = (bf16[1024,384]{1,0:T(8,128)(2,1)S(1)}, bf16[1024,768]{1,0:T(8,128)(2,1)S(1)}, bf16[4096,768]{1,0:T(8,128)(2,1)}) custom-call(s32[8]{0:T(128)S(1)} %broadcast_select_fusion.grp_ref, s32[1]{0:T(128)} %bitcast.4.z_ref, bf16[1024,384]{1,0:T(8,128)(2,1)S(1)} %multiply_convert_fusion.1.q_ref, bf16[1024,384]{1,0:T(8,128)(2,1)S(1)} %reshape.235.gm_ref, ...), custom_call_target="tpu_custom_call" | custom-call | flops 8053063680 | bytes 12582912 | tf_op jit(solution)/shard_map/att_bwd/pallas_call | solution.py:202
  431.1 2.4 copy-done.55
  433.5 9.0 fusion.87
  442.5 1.6 convolution_add_fusion.1
  444.5 1.7 copy-done.17
  446.9 21.3 %collective-permute-done.5 = bf16[768,576]{0,1:T(8,128)(2,1)S(1)} collective-permute-done((bf16[768,576]{0,1:T(8,128)(2,1)S(1)}, bf16[768,576]{0,1:T(8,128)(2,1)S(1)}, u32[]{:S(2)}, u32[]{:S(2)}) %collective-permute-start.5) | collective-permute-done | bytes 884768 | tf_op jit(solution)/shard_map/ppermute | solution.py:425
  468.2 1.7 fusion.25
  469.9 1.4 copy.141
  472.3 2.2 convolution_convert_fusion.2
  474.6 1.3 copy-done.12
  476.0 6.4 fusion.18
  483.5 6.2 fusion.15
  491.1 9.7 %convolution_convert_fusion = bf16[4096,768]{1,0:T(8,128)(2,1)} fusion(bf16[4096,768]{1,0:T(8,128)(2,1)} %get-tuple-element.24, bf16[768,768]{0,1:T(8,128)(2,1)S(1)} %copy-done.38), kind=kOutput, calls=%fused_computation.2 | convolution fusion | flops 4834983936 | bytes 13762560 | tf_op jit(solution)/shard_map/dot_general | solution.py:23
  502.0 1.8 copy.142
  503.8 60.3 %reduce-scatter.13.cloned.1.call-done = bf16[192,192]{1,0:T(8,128)(2,1)} async-done(((bf16[3072,192]{1,0:T(8,128)(2,1)}), bf16[192,192]{1,0:T(8,128)(2,1)}) %reduce-scatter.13.cloned.1.call-update) | async-done | bytes 73744 | tf_op jit(solution)/shard_map/reduce_scatter | solution.py:393
  564.1 78.5 %reduce-scatter.15.cloned.1.call-done = bf16[192,768]{1,0:T(8,128)(2,1)} async-done(((bf16[3072,768]{1,0:T(8,128)(2,1)}), bf16[192,768]{1,0:T(8,128)(2,1)}) %reduce-scatter.15.cloned.1.call-update) | async-done | bytes 294928 | tf_op jit(solution)/shard_map/reduce_scatter | solution.py:393
  642.7 78.8 %reduce-scatter.17.cloned.1.call-done = bf16[192,768]{1,0:T(8,128)(2,1)} async-done(((bf16[3072,768]{1,0:T(8,128)(2,1)}), bf16[192,768]{1,0:T(8,128)(2,1)}) %reduce-scatter.17.cloned.1.call-update) | async-done | bytes 294928 | tf_op jit(solution)/shard_map/reduce_scatter | solution.py:393
  721.7 59.7 %reduce-scatter.9.cloned.1.call-done = bf16[1024,768]{1,0:T(8,128)(2,1)} async-done(((bf16[4096,768]{1,0:T(8,128)(2,1)}), bf16[1024,768]{1,0:T(8,128)(2,1)}) %reduce-scatter.9.cloned.1.call-update) | async-done | bytes 1572880 | tf_op jit(solution)/shard_map/reduce_scatter | solution.py:407
  781.5 3.2 concatenate.25
  784.7 1.4 copy-done.2
  786.1 1.4 fusion.86
  788.5 1.7 copy-done.8
  791.1 32.6 %all-reduce.6.cloned.1.call-done = (bf16[192,576]{0,1:T(8,128)(2,1)}, bf16[192,192]{1,0:T(8,128)(2,1)}, bf16[192,768]{1,0:T(8,128)(2,1)}, bf16[192,768]{1,0:T(8,128)(2,1)}) async-done(((bf16[192,576]{0,1:T(8,128)(2,1)}, bf16[192,192]{1,0:T(8,128)(2,1)}, bf16[192,768]{1,0:T(8,128)(2,1)}, bf16[192,768]{1,0:T(8,128)(2,1)}), (bf16[192,576]{0,1:T(8,128)(2,1)}, bf16[192,192]{1,0:T(8,128)(2,1)}, ...) | async-done | bytes 884752 | tf_op jit(solution)/shard_map/psum | solution.py:429
  823.7 1.9 convert_element_type.160
  825.6 1.8 convert_element_type.164
  829.0 57.3 %reduce-scatter.11.cloned.1.call-done = bf16[512,768]{1,0:T(8,128)(2,1)} async-done(((bf16[2048,768]{1,0:T(8,128)(2,1)}), bf16[512,768]{1,0:T(8,128)(2,1)}) %reduce-scatter.11.cloned.1.call-update) | async-done | bytes 786448 | tf_op jit(solution)/shard_map/reduce_scatter | solution.py:408
  886.3 2.9 multiply_reduce_fusion.1
  889.3 1.8 fusion.83
  891.9 40.6 %psum.35 = f32[8576]{0:T(1024)S(1)} all-reduce(f32[8576]{0:T(1024)S(1)} %constant_dynamic-update-slice_fusion.2), channel_id=1, replica_groups=mesh['dp'=2,'gr'=4,'gc'=4] {'dp','gr','gc'}, use_global_device_ids=true, to_apply=%region_19.20 | all-reduce | flops 8576 | bytes 68608 | tf_op jit(solution)/shard_map/psum | solution.py:446
  (261 shorter events, 32.2 us)
Async XLA Ops:
  7.2 23.2 %copy-start.5 = (bf16[512,768]{1,0:T(8,128)(2,1)S(1)}, bf16[512,768]{1,0:T(8,128)(2,1)}, u32[]{:S(2)}) copy-start(bf16[512,768]{1,0:T(8,128)(2,1)} %param.16) | copy-start | bytes 2359300
  7.2 89.2 %all-gather.14.cloned.1.call-start = ((), (), s32[]{:S(2)}) async-start(), calls=%async_computation.7 | async-start | bytes 3932160 | tf_op jit(solution)/shard_map/all_gather | solution.py:326
  28.8 2.9 copy-start.25
  30.4 7.8 copy-start.27
  31.7 109.2 %all-gather.12.cloned.1.call-start = ((), (), s32[]{:S(2)}) async-start(), calls=%async_computation.6 | async-start | bytes 2457600 | tf_op jit(solution)/shard_map/all_gather | solution.py:319
  31.8 6.3 collective-permute-start.1
  39.5 148.1 %all-gather.16.cloned.1.call-start = ((), (), s32[]{:S(2)}) async-start(), calls=%async_computation.8 | async-start | bytes 7864320 | tf_op jit(solution)/shard_map/all_gather | solution.py:327
  99.1 1.8 copy-start.14
  99.1 1.9 copy-start.52
  99.1 3.2 copy-start.49
  99.1 133.0 %all-gather.18.cloned.1.call-start = ((), (), s32[]{:S(2)}) async-start(), calls=%async_computation.14 | async-start | bytes 1671168 | tf_op jit(solution)/shard_map/all_gather | solution.py:329
  99.7 184.3 %all-gather.20.cloned.1.call-start = ((), (), s32[]{:S(2)}) async-start(), calls=%async_computation.15 | async-start | bytes 5013504 | tf_op jit(solution)/shard_map/all_gather | solution.py:330
  100.3 237.8 %all-gather.22.cloned.1.call-start = ((), (), s32[]{:S(2)}) async-start(), calls=%async_computation.16 | async-start | bytes 5013504 | tf_op jit(solution)/shard_map/all_gather | solution.py:331
  100.9 401.1 %reduce-scatter.19.cloned.1.call-start = ((), (), s32[]{:S(2)}) async-start(), calls=%async_computation.17 | async-start | bytes 1228800
  100.9 45.9 %collective-permute-start = (bf16[512,768]{1,0:T(8,128)(2,1)S(1)}, bf16[512,768]{1,0:T(8,128)(2,1)S(1)}, u32[]{:S(2)}, u32[]{:S(2)}) collective-permute-start(bf16[512,768]{1,0:T(8,128)(2,1)S(1)} %copy-done.14), channel_id=1, source_target_pairs={{0,1},{1,0},{2,3},{3,2},{4,5},{5,4},{6,7},{7,6},{8,9},{9,8},{10,11... | collective-permute-start | bytes 2359304 | tf_op jit(solution)/shard_map/ppermute | solution.py:322
  187.6 7.7 copy-start.3
  195.3 24.3 %copy-start = (bf16[4096,768]{1,0:T(8,128)(2,1)}, bf16[4096,768]{1,0:T(8,128)(2,1)S(1)}, u32[]{:S(2)}) copy-start(bf16[4096,768]{1,0:T(8,128)(2,1)S(1)} %convolution_convert_fusion.1.kvp_ref) | copy-start | bytes 18874372
  223.3 2.9 copy-start.46
  225.9 119.0 %collective-permute-start.2 = (bf16[512,2,192]{0,2,1:T(8,128)(2,1)S(1)}, bf16[512,2,192]{0,2,1:T(8,128)(2,1)}, u32[]{:S(2)}, u32[]{:S(2)}) collective-permute-start(bf16[512,2,192]{0,2,1:T(8,128)(2,1)S(1)} %bitcast.369), channel_id=1, source_target_pairs={{0,1},{1,0},{2,3},{3,2},{4,5},{5,4},{6,7},{7,6},{8,9},{9,8},{10,11... | collective-permute-start | bytes 1179656 | tf_op jit(solution)/shard_map/ppermute | solution.py:343
  338.1 6.7 copy-start.16
  344.8 1.7 copy-start.18
  344.8 1.7 copy-start.42
  344.9 3.3 slice-start.6
  346.6 1.7 slice-start.7
  347.5 22.9 %copy-start.11 = (f32[512,768]{1,0:T(8,128)}, f32[512,768]{1,0:T(8,128)S(1)}, u32[]{:S(2)}) copy-start(f32[512,768]{1,0:T(8,128)S(1)} %get-tuple-element.140) | copy-start | bytes 4718596
  347.6 22.8 %copy-start.29 = (f32[512]{0:T(512)}, f32[512]{0:T(512)S(1)}, u32[]{:S(2)}) copy-start(f32[512]{0:T(512)S(1)} %broadcast_multiply_fusion.4) | copy-start | bytes 6148
  347.6 6.6 slice-start.2
  347.6 9.9 %slice-start.4 = ((s8[4718592]{0:T(1024)(128)(4,1)}), s8[4194304]{0:T(1024)(128)(4,1)S(1)}, s32[]{:S(2)}) async-start(s8[4718592]{0:T(1024)(128)(4,1)} %bitcast.336), calls=%async_computation.23 | async-start | bytes 8388608
  347.9 22.5 %copy-start.35 = (f32[512]{0:T(512)}, f32[512]{0:T(512)S(1)}, u32[]{:S(2)}) copy-start(f32[512]{0:T(512)S(1)} %add_rsqrt_fusion) | copy-start | bytes 6148
  348.5 5.7 slice-start.3
  348.5 5.7 copy-start.21
  348.5 5.7 copy-start.41
  348.5 9.0 slice-start.5
  354.2 3.3 copy-start.50
  354.2 12.7 %slice-start = ((s8[4718592]{0:T(1024)(128)(4,1)}), s8[4194304]{0:T(1024)(128)(4,1)S(1)}, s32[]{:S(2)}) async-start(s8[4718592]{0:T(1024)(128)(4,1)} %bitcast.327), calls=%async_computation.19 | async-start | bytes 8388608
  357.5 9.3 copy-start.53
  357.5 9.3 slice-start.1
  366.9 3.5 copy-start.51
  378.2 4.2 collective-permute-start.3
  386.5 43.7 %copy-start.15 = (bf16[512,768]{1,0:T(8,128)(2,1)S(1)}, bf16[512,768]{1,0:T(8,128)(2,1)}, u32[]{:S(2)}) copy-start(bf16[512,768]{1,0:T(8,128)(2,1)} %add_convert_fusion.1) | copy-start | bytes 2359300
  386.5 43.7 %copy-start.48 = (bf16[512,768]{1,0:T(8,128)(2,1)S(1)}, bf16[512,768]{1,0:T(8,128)(2,1)}, u32[]{:S(2)}) copy-start(bf16[512,768]{1,0:T(8,128)(2,1)} %copy-done.47) | copy-start | bytes 2359300
  430.1 12.4 %copy-start.1 = (bf16[1024,768]{1,0:T(8,128)(2,1)}, bf16[1024,768]{1,0:T(8,128)(2,1)S(1)}, u32[]{:S(2)}) copy-start(bf16[1024,768]{1,0:T(8,128)(2,1)S(1)} %get-tuple-element.23) | copy-start | bytes 4718596
  430.1 3.4 copy-start.55
  444.5 1.7 copy-start.17
  446.3 21.9 %collective-permute-start.5 = (bf16[768,576]{0,1:T(8,128)(2,1)S(1)}, bf16[768,576]{0,1:T(8,128)(2,1)S(1)}, u32[]{:S(2)}, u32[]{:S(2)}) collective-permute-start(bf16[768,576]{0,1:T(8,128)(2,1)S(1)} %fusion.35), channel_id=1, source_target_pairs={{0,2},{1,3},{2,0},{3,1},{4,6},{5,7},{6,4},{7,5},{8,10},{9,11},{10,... | collective-permute-start | bytes 2654216 | tf_op jit(solution)/shard_map/ppermute | solution.py:425
  471.2 92.9 %reduce-scatter.13.cloned.1.call-start = ((), (), s32[]{:S(2)}) async-start(), calls=%async_computation.11 | async-start | bytes 1671168 | tf_op jit(solution)/shard_map/reduce_scatter | solution.py:393
  472.3 2.3 copy-start.32
  472.3 2.3 copy-start.40
  474.6 168.1 %reduce-scatter.15.cloned.1.call-start = ((), (), s32[]{:S(2)}) async-start(), calls=%async_computation.12 | async-start | bytes 5013504 | tf_op jit(solution)/shard_map/reduce_scatter | solution.py:393
  482.4 239.0 %reduce-scatter.17.cloned.1.call-start = ((), (), s32[]{:S(2)}) async-start(), calls=%async_computation.13 | async-start | bytes 5013504 | tf_op jit(solution)/shard_map/reduce_scatter | solution.py:393
  489.8 291.7 %reduce-scatter.9.cloned.1.call-start = ((), (), s32[]{:S(2)}) async-start(), calls=%async_computation.9 | async-start | bytes 7864320 | tf_op jit(solution)/shard_map/reduce_scatter | solution.py:407
  500.8 322.9 %all-reduce.6.cloned.1.call-start = ((), (), s32[]{:S(2)}) async-start(), calls=%async_computation.18 | async-start | bytes 1966080 | tf_op jit(solution)/shard_map/psum | solution.py:429
  721.5 164.8 %reduce-scatter.11.cloned.1.call-start = ((), (), s32[]{:S(2)}) async-start(), calls=%async_computation.10 | async-start | bytes 3932160 | tf_op jit(solution)/shard_map/reduce_scatter | solution.py:408
  788.5 1.7 copy-start.8
  790.3 96.0 %copy-start.7 = (bf16[512,768]{1,0:T(8,128)(2,1)S(1)}, bf16[512,768]{1,0:T(8,128)(2,1)}, u32[]{:S(2)}) copy-start(bf16[512,768]{1,0:T(8,128)(2,1)} %param.16) | copy-start | bytes 2359300
  790.3 96.0 %copy-start.28 = (f32[512]{0:T(512)S(1)}, f32[512]{0:T(512)}, u32[]{:S(2)}) copy-start(f32[512]{0:T(512)} %copy-done.27) | copy-start | bytes 6148
  790.3 38.7 %collective-permute-start.4 = (bf16[512,768]{1,0:T(8,128)(2,1)S(1)}, bf16[512,768]{1,0:T(8,128)(2,1)}, u32[]{:S(2)}, u32[]{:S(2)}) collective-permute-start(bf16[512,768]{1,0:T(8,128)(2,1)S(1)} %fusion.36), channel_id=1, source_target_pairs={{0,1},{1,0},{2,3},{3,2},{4,5},{5,4},{6,7},{7,6},{8,9},{9,8},{10,11... | collective-permute-start | bytes 2359304 | tf_op jit(solution)/shard_map/ppermute | solution.py:417
  823.7 3.7 copy-start.24
  823.7 4.6 copy-start.26
  829.0 60.3 %copy-start.10 = (f32[512,768]{1,0:T(8,128)S(1)}, f32[512,768]{1,0:T(8,128)}, u32[]{:S(2)}) copy-start(f32[512,768]{1,0:T(8,128)} %copy-done.9) | copy-start | bytes 4718596
  889.3 1.9 copy-start.45
  889.3 1.9 copy-start.44
  889.3 1.9 copy-start.43
  889.3 1.9 copy-start.33
  (19 other events, 23.7 us)
Sparse Core Ops, SparseCore 0:
  31.8 64.5 all-gather.13
  98.5 42.2 all-gather.11
  142.4 45.1 all-gather.15
  189.8 39.7 all-gather.17
  231.7 52.2 all-gather.19
  286.1 51.9 all-gather.21
  471.4 30.5 reduce-scatter.18
  506.1 57.9 reduce-scatter.12
  568.0 74.6 reduce-scatter.14
  646.9 74.5 reduce-scatter.16
  724.0 57.3 reduce-scatter.8
  784.5 39.1 all-reduce.5
  826.0 60.2 reduce-scatter.10

commit v2 on v1

--- a/solution.py
+++ b/solution.py
@@ -233,6 +233,195 @@
     )(grp, z, q, gm, lse, kvo, kvp)
 
 
+MESH = pl.DeviceIdType.MESH
+
+
+def places():
+    x = lax.axis_index("dp")
+    z = lax.axis_index("gr")
+    g = lax.axis_index("gc")
+    return x, z, g, g // 2, g % 2
+
+
+def greet(partners):
+    barrier = pltpu.get_barrier_semaphore()
+    for partner in partners:
+        pl.semaphore_signal(barrier, inc=1, device_id=partner, device_id_type=MESH)
+    pl.semaphore_wait(barrier, len(partners))
+
+
+def all_partners():
+    x, z, g, y, c = places()
+    by_z = [{"gr": lax.rem(z + step, 4)} for step in (1, 2, 3)]
+    return [{"gc": g ^ 1}, {"gc": g ^ 2}, {"dp": x ^ 1}] + by_z
+
+
+def send(src, dst, sems, slot, target):
+    return pltpu.make_async_remote_copy(
+        src_ref=src,
+        dst_ref=dst,
+        send_sem=sems[0].at[slot],
+        recv_sem=sems[1].at[slot],
+        device_id=target,
+        device_id_type=MESH,
+    )
+
+
+def add_into(dst, left, right):
+    dst[...] = (left[...].astype(F32) + right[...].astype(F32)).astype(dst.dtype)
+
+
+RS_SLOTS = 10
+
+
+def rs_steps(grads, outs, bufs, sems, sem_own, base):
+    own, ra, rb0, rb1, rc0, rc1, sc, rd, re = bufs
+    x, z, g, y, c = places()
+    sib, over_y, over_x = {"gc": g ^ 1}, {"gc": g ^ 2}, {"dp": x ^ 1}
+    rows = grads.shape[2]
+    q = rows // 4
+    mine0 = pl.ds(pl.multiple_of(q * x, 16), q)
+    other0 = pl.ds(pl.multiple_of(q * (1 - x), 16), q)
+    mine1 = pl.ds(pl.multiple_of(2 * q + q * x, 16), q)
+    other1 = pl.ds(pl.multiple_of(2 * q + q * (1 - x), 16), q)
+    first = pl.ds(0, 2 * q)
+
+    def slot(i):
+        return base * RS_SLOTS + i
+
+    loads = [
+        pltpu.make_async_copy(grads.at[2 * i + c], own.at[i], sem_own.at[2 * base + i])
+        for i in range(2)
+    ]
+    hop_a = [send(grads.at[2 * i + 1 - c], ra.at[i], sems, slot(i), sib) for i in range(2)]
+    hop_b0 = send(own.at[1 - y, :, first], rb0, sems, slot(2), over_y)
+    hop_b1 = send(own.at[:, :, other1], rb1, sems, slot(3), over_x)
+    hop_c0 = send(own.at[y, :, other0], rc0, sems, slot(4), over_x)
+    hop_c1 = send(own.at[1 - y, :, mine1], rc1, sems, slot(5), over_y)
+    hop_z = [
+        send(
+            sc.at[lax.rem(z + step, 4)],
+            rd.at[step - 1],
+            sems,
+            slot(5 + step),
+            {"gr": lax.rem(z + step, 4)},
+        )
+        for step in (1, 2, 3)
+    ]
+    hop_d = send(sc.at[z], re, sems, slot(9), over_x)
+
+    def start():
+        for copy in loads + hop_a:
+            copy.start()
+
+    def after_a():
+        for copy in loads + hop_a:
+            copy.wait()
+
+        @pl.loop(0, 8)
+        def _(i):
+            add_into(own.at[i // 4, i % 4], own.at[i // 4, i % 4], ra.at[i // 4, i % 4])
+
+        hop_b0.start()
+        hop_b1.start()
+
+    def after_b():
+        hop_b0.wait()
+        hop_b1.wait()
+
+        @pl.loop(0, 4)
+        def _(i):
+            add_into(own.at[y, i, first], own.at[y, i, first], rb0.at[i])
+            add_into(own.at[0, i, mine1], own.at[0, i, mine1], rb1.at[0, i])
+            add_into(own.at[1, i, mine1], own.at[1, i, mine1], rb1.at[1, i])
+
+        hop_c0.start()
+        hop_c1.start()
+
+    def after_c():
+        hop_c0.wait()
+        hop_c1.wait()
+
+        @pl.loop(0, 4)
+        def _(i):
+            add_into(sc.at[i, pl.ds(0, q)], own.at[y, i, mine0], rc0.at[i])
+            add_into(sc.at[i, pl.ds(q, q)], own.at[y, i, mine1], rc1.at[i])
+
+        for copy in hop_z:
+            copy.start()
+
+    def after_z():
+        for copy in hop_z:
+            copy.wait()
+        total = sc[z].astype(F32)
+        for i in range(3):
+            total = total + rd[i].astype(F32)
+        sc[z] = total.astype(BF)
+        hop_d.start()
+
+    def finish():
+        hop_d.wait()
+        outs[mine0] = sc[z, pl.ds(0, q)].astype(F32)
+        outs[mine1] = sc[z, pl.ds(q, q)].astype(F32)
+        outs[other0] = re[pl.ds(0, q)].astype(F32)
+        outs[other1] = re[pl.ds(q, q)].astype(F32)
+
+    return [start, after_a, after_b, after_c, after_z, finish]
+
+
+def rs_scratch(shape):
+    _, n_gr, rows, cols = shape
+    q = rows // 4
+    return [
+        pltpu.VMEM((2, n_gr, rows, cols), BF),
+        pltpu.VMEM((2, n_gr, rows, cols), BF),
+        pltpu.VMEM((n_gr, 2 * q, cols), BF),
+        pltpu.VMEM((2, n_gr, q, cols), BF),
+        pltpu.VMEM((n_gr, q, cols), BF),
+        pltpu.VMEM((n_gr, q, cols), BF),
+        pltpu.VMEM((n_gr, 2 * q, cols), BF),
+        pltpu.VMEM((3, 2 * q, cols), BF),
+        pltpu.VMEM((2 * q, cols), BF),
+    ]
+
+
+def scatter_kernel(count, *refs):
+    grads, outs = refs[:count], refs[count : 2 * count]
+    bufs = refs[2 * count : 2 * count + 9 * count]
+    send_sem, recv_sem, sem_own = refs[11 * count :]
+    greet(all_partners())
+    steps = [
+        rs_steps(grads[k], outs[k], bufs[9 * k : 9 * k + 9], (send_sem, recv_sem), sem_own, k)
+        for k in range(count)
+    ]
+    for stage in range(len(steps[0])):
+        for k in range(count):
+            steps[k][stage]()
+
+
+def scatter_grads(grads, collective_id):
+    count = len(grads)
+    scratch = []
+    for grad in grads:
+        scratch += rs_scratch(grad.shape)
+    return pl.pallas_call(
+        partial(scatter_kernel, count),
+        name="scatter_grads",
+        in_specs=[pl.BlockSpec(memory_space=pl.ANY)] * count,
+        out_specs=[pl.BlockSpec(memory_space=pltpu.VMEM)] * count,
+        out_shape=[jax.ShapeDtypeStruct(grad.shape[2:], F32) for grad in grads],
+        scratch_shapes=scratch
+        + [
+            pltpu.SemaphoreType.DMA((RS_SLOTS * count,)),
+            pltpu.SemaphoreType.DMA((RS_SLOTS * count,)),
+            pltpu.SemaphoreType.DMA((2 * count,)),
+        ],
+        compiler_params=pltpu.CompilerParams(
+            collective_id=collective_id, has_side_effects=True, vmem_limit_bytes=50 << 20
+        ),
+    )(*grads)
+
+
 def norm(hidden, gain, shift):
     center = jnp.mean(hidden, axis=1, keepdims=True)
     offset = hidden - center
@@ -288,6 +477,7 @@
     cont_group,
     token_count,
 ):
+    n_dp = lax.axis_size("dp")
     n_gr = lax.axis_size("gr")
     n_gc = lax.axis_size("gc")
     z = lax.axis_index("gr")
@@ -391,15 +581,22 @@
 
     def scatter16(blocks):
         part = lax.psum_scatter(
-            blocks.astype(BF), ("gc", "gr"), scatter_dimension=0, tiled=True
+            blocks.astype(BF).reshape(n_gc * n_gr * blocks.shape[2], -1),
+            ("gc", "gr"),
+            scatter_dimension=0,
+            tiled=True,
         )
         return lax.psum(part, "dp").astype(F32)
 
-    out_w_down = scatter16(grad_w_down.reshape(n_gc * n_gr * 192, 768))
-    out_w_up = scatter16(grad_w_up.reshape(n_gc * n_gr * 192, 768))
-    out_w_out = scatter16(
-        grad_w_out.reshape(n_gc, 192, n_gr, 192).transpose(0, 2, 1, 3).reshape(-1, 192)
-    )
+    weight_grads = [
+        grad_w_down.astype(BF).reshape(n_gc, n_gr, 192, 768),
+        grad_w_up.astype(BF).reshape(n_gc, n_gr, 192, 768),
+        grad_w_out.astype(BF).reshape(n_gc, 192, n_gr, 192).transpose(0, 2, 1, 3),
+    ]
+    if n_dp == 2:
+        out_w_down, out_w_up, out_w_out = scatter_grads(weight_grads, 3)
+    else:
+        out_w_down, out_w_up, out_w_out = [scatter16(grad) for grad in weight_grads]
 
     dq, dkvo, dkvp = attend_back(grp, z_arr, q, gm_chip, lse_rows, kvo, kvp)
 

time: 947 us -> 749 us (0.79)
  waiting for transfers between devices: 611 us -> 321 us
  Pallas kernels: 67.9 us -> 163 us
    reduce_scatter x3 -> x0, waiting for transfers between devices: 218 us -> none  [scatter16(): lax.psum_scatter(blocks.astype(BF), ('gc', 'gr'), scatter_dimension=0, ti...]
    pallas_call x0 -> x1, Pallas kernels: none -> 95 us  [scatter_grads(): pl.pallas_call(partial(scatter_kernel, count), name='scatter_grads', in_s...]
    reduce_scatter x1, waiting for transfers between devices: 57.3 us -> 0.01 us  [on_device(): lax.psum_scatter(jnp.concatenate([back_prompt, jnp.zeros_like(back_prompt...]
    psum x1, waiting for transfers between devices: 32.6 us -> 0.02 us  [on_device(): out_w_qkv = lax.psum(out_w_qkv, 'dp').astype(F32)]
    unnamed x14 -> x11, waiting for transfers between devices: 2.92 us -> 22.6 us
    unnamed x174 -> x175, local copies, waits for them, and re-layouts: 21 us -> 21.7 us
  transfers between devices with their start and end apart: 19 -> 16, of which waited for: 14 -> 9; matrix products, arithmetic and copies ran while one was open for 10% -> 12% of each run, Pallas kernels for 3% -> 16%
where the time goes in v2:
time: 749 us; the launch traced here: 745 us
  waiting for transfers between devices  321 us (43%)
  Pallas kernels  163 us (22%)
  local copies, waits for them, and re-layouts  79.7 us (11%)
  matrix products  73 us (10%)
  blocking collectives  69 us (9%)
  between operations  18.8 us (3%)
  other arithmetic  16.9 us (2%)
    pallas_call x1, Pallas kernels, scatter_grads(): pl.pallas_call(partial(scatter_kernel, count), name='scatter_grads', in_s...  95 us
    reduce_scatter x1, waiting for transfers between devices, on_device(): lax.psum_scatter(part_prompt, 'gc', scatter_dimension=0, tiled=True)  57.8 us
    all_gather x1, waiting for transfers between devices, on_device(): n1_col = lax.all_gather(n1, 'gr', axis=0, tiled=True)[:P_SIZE]  56.9 us
    all_gather x1, waiting for transfers between devices, on_device(): lax.all_gather(fc2_weight, ('gc', 'gr')).reshape(n_gc, D, FF // n_gc)  47.5 us
    all_gather x1, waiting for transfers between devices, on_device(): w_up = lax.all_gather(fc1_weight, ('gc', 'gr')).reshape(n_gc, D, FF // n_gc)  44 us
    pallas_call x1, Pallas kernels, attend_back(): pl.pallas_call(att_bwd_kernel, name='att_bwd', grid_spec=pltpu.PrefetchSc...  43.7 us
    psum x1, blocking collectives, on_device(): sums = lax.psum(sums, ('dp', 'gr', 'gc'))  40.3 us
    all_gather x1, waiting for transfers between devices, on_device(): n1_prompt = lax.all_gather(n1_col, 'gc', axis=0, tiled=True)  36.7 us
  transfers between devices with their start and end apart: 16, of which 9 were waited for; matrix products, arithmetic and copies ran while one was open for 12% of the time, Pallas kernels for 16%

profile of v2, /device:TPU:0, one launch (start us, length us, event | category | flops | bytes accessed | tf_op | source)
XLA Modules:
  0.0 744.6 jit_solution(5925226732607066532)
XLA Ops:
  11.9 14.8 %all-gather.3 = bf16[4,192,7]{1,2,0:T(8,128)(2,1)S(1)} all-gather(bf16[1,192,7]{1,2,0:T(8,128)(2,1)S(1)} %bitcast.360), channel_id=1, replica_groups=mesh['dp'=2,'gr'=4,'gc'=4] {'gr'}, dimensions={0}, use_global_device_ids=true | all-gather | bytes 13440 | tf_op jit(solution)/shard_map/all_gather | solution.py:493
  27.5 1.4 fusion.30
  28.9 1.5 multiply_reduce_fusion.5
  30.4 1.3 add_convert_fusion.1
  31.8 1.6 collective-permute-start.1
  33.4 4.7 collective-permute-done.1
  38.2 1.3 copy.112
  39.5 56.9 %all-gather.14.cloned.1.call-done = bf16[2048,768]{1,0:T(8,128)(2,1)} async-done(((bf16[512,768]{1,0:T(8,128)(2,1)}), bf16[2048,768]{1,0:T(8,128)(2,1)}) %all-gather.14.cloned.1.call-update) | async-done | bytes 3145744 | tf_op jit(solution)/shard_map/all_gather | solution.py:516
  96.4 2.7 slice.248
  102.6 8.5 %all-reduce.2 = s32[4,2,4]{2,1,0:T(2,128)S(1)} all-reduce(s32[4,2,4]{2,1,0:T(2,128)S(1)} %reshape.193), channel_id=1, replica_groups=mesh['dp'=2,'gr'=4,'gc'=4] {'gr'}, use_global_device_ids=true, to_apply=%add.1 | all-reduce | flops 32 | bytes 256
  111.4 29.5 %all-gather.12.cloned.1.call-done = bf16[2,768,576]{2,0,1:T(2,128)(2,1)} async-done(((bf16[2,192,576]{2,0,1:T(2,128)(2,1)}), bf16[2,768,576]{2,0,1:T(2,128)(2,1)}) %all-gather.12.cloned.1.call-update) | async-done | bytes 1769488 | tf_op jit(solution)/shard_map/all_gather | solution.py:509
  140.9 5.7 copy.113
  146.9 1.0 multiply_convert_fusion.1.q_ref
  148.3 2.6 convolution_convert_fusion.2.kvo_ref
  151.0 36.7 %all-gather.16.cloned.1.call-done = bf16[4096,768]{1,0:T(8,128)(2,1)} async-done(((bf16[1024,768]{1,0:T(8,128)(2,1)}), bf16[4096,768]{1,0:T(8,128)(2,1)}) %all-gather.16.cloned.1.call-update) | async-done | bytes 6291472 | tf_op jit(solution)/shard_map/all_gather | solution.py:517
  187.7 7.7 %convolution_convert_fusion.1.kvp_ref = bf16[4096,768]{1,0:T(8,128)(2,1)S(1)} fusion(bf16[4096,768]{1,0:T(8,128)(2,1)} %all-gather.16.cloned.1.call-done, bf16[768,768]{0,1:T(8,128)(2,1)} %copy-done.34), kind=kOutput, calls=%fused_computation.3 | convolution fusion | flops 4834983936 | bytes 13762560 | tf_op jit(solution)/shard_map/dot_general | solution.py:27
  195.4 24.2 %att_fwd.1 = (bf16[1024,384]{1,0:T(8,128)(2,1)S(1)}, f32[1024,384]{1,0:T(8,128)S(1)}) custom-call(s32[8]{0:T(128)S(1)} %broadcast_select_fusion.grp_ref, s32[1]{0:T(128)} %bitcast.4.z_ref, bf16[1024,384]{1,0:T(8,128)(2,1)S(1)} %multiply_convert_fusion.1.q_ref, bf16[1024,768]{1,0:T(8,128)(2,1)S(1)} %copy-done.3, ...), custom_call_target="tpu_custom_call" | custom-call | flops 3221225472 | bytes 6291456 | tf_op jit(solution)/shard_map/att_fwd/pallas_call | solution.py:92
  219.6 1.2 copy.114
  220.8 2.6 reshape.197
  223.4 2.5 constant_dynamic-slice_fusion.9
  226.3 5.3 all-gather.4
  232.3 3.8 copy.172
  236.0 4.0 reshape.199
  240.1 44.0 %all-gather.20.cloned.1.call-done = bf16[3072,768]{1,0:T(8,128)(2,1)} async-done(((bf16[192,768]{1,0:T(8,128)(2,1)}), bf16[3072,768]{1,0:T(8,128)(2,1)}) %all-gather.20.cloned.1.call-update) | async-done | bytes 4718608 | tf_op jit(solution)/shard_map/all_gather | solution.py:520
  284.0 6.6 copy.116
  290.7 47.5 %all-gather.22.cloned.1.call-done = bf16[3072,768]{1,0:T(8,128)(2,1)} async-done(((bf16[192,768]{1,0:T(8,128)(2,1)}), bf16[3072,768]{1,0:T(8,128)(2,1)}) %all-gather.22.cloned.1.call-update) | async-done | bytes 4718608 | tf_op jit(solution)/shard_map/all_gather | solution.py:521
  338.2 6.6 copy.118
  344.8 1.3 copy.174
  346.2 1.4 maximum_select_fusion.1
  349.5 5.7 multiply_convert_fusion
  355.2 3.3 convert_reduce_fusion.1
  358.5 9.5 %convert_reduce_fusion = (f32[3072]{0:T(1024)}, bf16[512,3072]{1,0:T(8,128)(2,1)S(1)}) fusion(f32[512,3072]{1,0:T(8,128)} %get-tuple-element.143, f32[3072]{0:T(1024)S(1)} %bitcast.362, bf16[512,768]{1,0:T(8,128)(2,1)S(1)} %get-tuple-element.109, bf16[3072,768]{1,0:T(8,128)(2,1)S(1)} %bitcast.323), kind=kOutput, calls=%fused_computation.11 | convolution fusion | flops 2452091904 | bytes 14966784 | tf_op jit(solution)/shard_map/dot_general | solution.py:556
  368.0 3.5 fusion.27
  371.6 2.5 convert_reduce_fusion.2
  374.0 1.2 copy-done.8
  375.2 1.7 convolution_convert_fusion.4
  376.9 1.4 copy.120
  379.4 3.7 slice.198
  383.4 1.3 maximum_select_fusion.2
  386.1 1.4 copy-done.4
  387.5 43.7 %att_bwd.1 = (bf16[1024,384]{1,0:T(8,128)(2,1)S(1)}, bf16[1024,768]{1,0:T(8,128)(2,1)S(1)}, bf16[4096,768]{1,0:T(8,128)(2,1)}) custom-call(s32[8]{0:T(128)S(1)} %broadcast_select_fusion.grp_ref, s32[1]{0:T(128)} %bitcast.4.z_ref, bf16[1024,384]{1,0:T(8,128)(2,1)S(1)} %multiply_convert_fusion.1.q_ref, bf16[1024,384]{1,0:T(8,128)(2,1)S(1)} %reshape.236.gm_ref, ...), custom_call_target="tpu_custom_call" | custom-call | flops 8053063680 | bytes 12582912 | tf_op jit(solution)/shard_map/att_bwd/pallas_call | solution.py:202
  432.2 2.4 copy-done.54
  434.6 8.8 %fusion.88 = f32[768,768]{0,1:T(8,128)S(1)} fusion(bf16[4096,768]{1,0:T(8,128)(2,1)} %all-gather.16.cloned.1.call-done, bf16[4096,768]{1,0:T(8,128)(2,1)S(1)} %copy-done.54), kind=kOutput, calls=%fused_computation.200 | convolution fusion | flops 4831838208 | bytes 14942208 | tf_op jit(solution)/shard_map/dot_general | solution.py:31
  443.3 1.6 convolution_add_fusion.1
  445.3 1.7 copy-done.18
  447.8 21.3 %collective-permute-done.5 = bf16[768,576]{0,1:T(8,128)(2,1)S(1)} collective-permute-done((bf16[768,576]{0,1:T(8,128)(2,1)S(1)}, bf16[768,576]{0,1:T(8,128)(2,1)S(1)}, u32[]{:S(2)}, u32[]{:S(2)}) %collective-permute-start.5) | collective-permute-done | bytes 884768 | tf_op jit(solution)/shard_map/ppermute | solution.py:622
  469.0 1.7 fusion.25
  470.7 1.4 copy.136
  472.2 9.7 %convolution_convert_fusion = bf16[4096,768]{1,0:T(8,128)(2,1)} fusion(bf16[4096,768]{1,0:T(8,128)(2,1)} %get-tuple-element.27, bf16[768,768]{0,1:T(8,128)(2,1)S(1)} %copy-done.35), kind=kOutput, calls=%fused_computation.2 | convolution fusion | flops 4834983936 | bytes 13762560 | tf_op jit(solution)/shard_map/dot_general | solution.py:23
  481.9 20.9 %reduce-scatter.10.cloned.1.call-done = bf16[192,576]{1,0:T(8,128)(2,1)} async-done(((bf16[768,576]{1,0:T(8,128)(2,1)}), bf16[192,576]{1,0:T(8,128)(2,1)}) %reduce-scatter.10.cloned.1.call-update) | async-done | bytes 221200
  502.8 1.8 copy.137
  504.7 57.8 %reduce-scatter.6.cloned.1.call-done = bf16[1024,768]{1,0:T(8,128)(2,1)} async-done(((bf16[4096,768]{1,0:T(8,128)(2,1)}), bf16[1024,768]{1,0:T(8,128)(2,1)}) %reduce-scatter.6.cloned.1.call-update) | async-done | bytes 1572880 | tf_op jit(solution)/shard_map/reduce_scatter | solution.py:604
  562.6 3.4 concatenate.25
  567.1 6.3 fusion.15
  573.4 1.4 fusion.87
  575.9 1.7 copy-done.11
  579.2 1.4 reshape.213
  580.9 1.1 copy-done.13
  582.1 6.5 fusion.18
  588.6 95.0 %scatter_grads.1 = (f32[192,768]{1,0:T(8,128)S(1)}, f32[192,768]{1,0:T(8,128)S(1)}, f32[192,192]{1,0:T(8,128)S(1)}) custom-call(bf16[4,4,192,768]{3,2,1,0:T(8,128)(2,1)} %bitcast.327, bf16[4,4,192,768]{3,2,1,0:T(8,128)(2,1)} %bitcast.328, bf16[4,4,192,192]{3,2,1,0:T(8,128)(2,1)S(1)} %bitcast.296), custom_call_target="tpu_custom_call" | custom-call | tf_op jit(solution)/shard_map/scatter_grads/pallas_call | solution.py:407
  683.6 1.9 copy.130
  685.5 3.1 multiply_reduce_fusion.1
  688.7 1.8 fusion.84
  691.3 40.3 %psum.14 = f32[8576]{0:T(1024)S(1)} all-reduce(f32[8576]{0:T(1024)S(1)} %constant_dynamic-update-slice_fusion.2), channel_id=1, replica_groups=mesh['dp'=2,'gr'=4,'gc'=4] {'dp','gr','gc'}, use_global_device_ids=true, to_apply=%region_19.20 | all-reduce | flops 8576 | bytes 68608 | tf_op jit(solution)/shard_map/psum | solution.py:643
  (252 shorter events, 25.3 us)
Async XLA Ops:
  7.2 23.2 %copy-start.5 = (bf16[512,768]{1,0:T(8,128)(2,1)S(1)}, bf16[512,768]{1,0:T(8,128)(2,1)}, u32[]{:S(2)}) copy-start(bf16[512,768]{1,0:T(8,128)(2,1)} %param.16) | copy-start | bytes 2359300
  7.2 89.2 %all-gather.14.cloned.1.call-start = ((), (), s32[]{:S(2)}) async-start(), calls=%async_computation.4 | async-start | bytes 3932160 | tf_op jit(solution)/shard_map/all_gather | solution.py:516
  28.8 2.9 copy-start.23
  30.4 7.8 %copy-start.25 = (f32[512]{0:T(512)}, f32[512]{0:T(512)S(1)}, u32[]{:S(2)}) copy-start(f32[512]{0:T(512)S(1)} %add_rsqrt_fusion.1) | copy-start | bytes 6148
  31.7 109.2 %all-gather.12.cloned.1.call-start = ((), (), s32[]{:S(2)}) async-start(), calls=%async_computation.3 | async-start | bytes 2457600 | tf_op jit(solution)/shard_map/all_gather | solution.py:509
  31.8 6.3 collective-permute-start.1
  39.5 148.2 %all-gather.16.cloned.1.call-start = ((), (), s32[]{:S(2)}) async-start(), calls=%async_computation.5 | async-start | bytes 7864320 | tf_op jit(solution)/shard_map/all_gather | solution.py:517
  99.1 1.8 copy-start.16
  99.1 1.9 copy-start.51
  99.1 3.2 copy-start.48
  99.1 133.1 %all-gather.18.cloned.1.call-start = ((), (), s32[]{:S(2)}) async-start(), calls=%async_computation.9 | async-start | bytes 1671168 | tf_op jit(solution)/shard_map/all_gather | solution.py:519
  99.7 184.3 %all-gather.20.cloned.1.call-start = ((), (), s32[]{:S(2)}) async-start(), calls=%async_computation.10 | async-start | bytes 5013504 | tf_op jit(solution)/shard_map/all_gather | solution.py:520
  100.3 237.9 %all-gather.22.cloned.1.call-start = ((), (), s32[]{:S(2)}) async-start(), calls=%async_computation.11 | async-start | bytes 5013504 | tf_op jit(solution)/shard_map/all_gather | solution.py:521
  100.9 402.0 %reduce-scatter.10.cloned.1.call-start = ((), (), s32[]{:S(2)}) async-start(), calls=%async_computation.12 | async-start | bytes 1228800
  100.9 46.0 %collective-permute-start = (bf16[512,768]{1,0:T(8,128)(2,1)S(1)}, bf16[512,768]{1,0:T(8,128)(2,1)S(1)}, u32[]{:S(2)}, u32[]{:S(2)}) collective-permute-start(bf16[512,768]{1,0:T(8,128)(2,1)S(1)} %copy-done.16), channel_id=1, source_target_pairs={{0,1},{1,0},{2,3},{3,2},{4,5},{5,4},{6,7},{7,6},{8,9},{9,8},{10,11... | collective-permute-start | bytes 2359304 | tf_op jit(solution)/shard_map/ppermute | solution.py:512
  146.9 1.4 copy-start.46
  187.7 7.7 %copy-start.3 = (bf16[1024,768]{1,0:T(8,128)(2,1)S(1)}, bf16[1024,768]{1,0:T(8,128)(2,1)}, u32[]{:S(2)}) copy-start(bf16[1024,768]{1,0:T(8,128)(2,1)} %convolution_convert_fusion.2.kvo_ref) | copy-start | bytes 4718596
  195.4 24.3 %copy-start = (bf16[4096,768]{1,0:T(8,128)(2,1)}, bf16[4096,768]{1,0:T(8,128)(2,1)S(1)}, u32[]{:S(2)}) copy-start(bf16[4096,768]{1,0:T(8,128)(2,1)S(1)} %convolution_convert_fusion.1.kvp_ref) | copy-start | bytes 18874372
  223.4 2.9 copy-start.45
  226.0 120.2 %collective-permute-start.2 = (bf16[512,2,192]{0,2,1:T(8,128)(2,1)S(1)}, bf16[512,2,192]{0,2,1:T(8,128)(2,1)}, u32[]{:S(2)}, u32[]{:S(2)}) collective-permute-start(bf16[512,2,192]{0,2,1:T(8,128)(2,1)S(1)} %bitcast.354), channel_id=1, source_target_pairs={{0,1},{1,0},{2,3},{3,2},{4,5},{5,4},{6,7},{7,6},{8,9},{9,8},{10,11... | collective-permute-start | bytes 1179656 | tf_op jit(solution)/shard_map/ppermute | solution.py:533
  344.8 2.8 copy-start.6
  344.8 2.8 copy-start.19
  344.8 2.8 copy-start.41
  346.2 2.8 slice-start.6
  347.6 1.5 slice-start.7
  348.6 23.0 %copy-start.12 = (f32[512,768]{1,0:T(8,128)}, f32[512,768]{1,0:T(8,128)S(1)}, u32[]{:S(2)}) copy-start(f32[512,768]{1,0:T(8,128)S(1)} %get-tuple-element.141) | copy-start | bytes 4718596
  348.6 22.9 %copy-start.27 = (f32[512]{0:T(512)}, f32[512]{0:T(512)S(1)}, u32[]{:S(2)}) copy-start(f32[512]{0:T(512)S(1)} %broadcast_multiply_fusion.4) | copy-start | bytes 6148
  348.6 6.5 slice-start.2
  348.6 9.8 %slice-start.4 = ((s8[4718592]{0:T(1024)(128)(4,1)}), s8[4194304]{0:T(1024)(128)(4,1)S(1)}, s32[]{:S(2)}) async-start(s8[4718592]{0:T(1024)(128)(4,1)} %bitcast.321), calls=%async_computation.17 | async-start | bytes 8388608
  349.0 22.6 %copy-start.36 = (f32[512]{0:T(512)}, f32[512]{0:T(512)S(1)}, u32[]{:S(2)}) copy-start(f32[512]{0:T(512)S(1)} %add_rsqrt_fusion) | copy-start | bytes 6148
  349.4 5.7 slice-start.3
  349.4 5.7 copy-start.22
  349.4 5.7 copy-start.40
  349.4 9.0 %slice-start.5 = ((s8[4718592]{0:T(1024)(128)(4,1)}), s8[524288]{0:T(1024)(128)(4,1)S(1)}, s32[]{:S(2)}) async-start(s8[4718592]{0:T(1024)(128)(4,1)} %bitcast.321), calls=%async_computation.18 | async-start | bytes 1048576
  355.1 3.3 copy-start.50
  355.1 12.9 %slice-start = ((s8[4718592]{0:T(1024)(128)(4,1)}), s8[4194304]{0:T(1024)(128)(4,1)S(1)}, s32[]{:S(2)}) async-start(s8[4718592]{0:T(1024)(128)(4,1)} %bitcast.314), calls=%async_computation.13 | async-start | bytes 8388608
  358.5 9.5 %copy-start.52 = (bf16[512,768]{1,0:T(8,128)(2,1)}, bf16[512,768]{1,0:T(8,128)(2,1)S(1)}, u32[]{:S(2)}) copy-start(bf16[512,768]{1,0:T(8,128)(2,1)S(1)} %get-tuple-element.109) | copy-start | bytes 2359300
  358.5 9.5 %slice-start.1 = ((s8[4718592]{0:T(1024)(128)(4,1)}), s8[524288]{0:T(1024)(128)(4,1)S(1)}, s32[]{:S(2)}) async-start(s8[4718592]{0:T(1024)(128)(4,1)} %bitcast.314), calls=%async_computation.14 | async-start | bytes 1048576
  368.0 3.5 copy-start.49
  379.2 4.2 collective-permute-start.3
  387.5 43.7 %copy-start.17 = (bf16[512,768]{1,0:T(8,128)(2,1)S(1)}, bf16[512,768]{1,0:T(8,128)(2,1)}, u32[]{:S(2)}) copy-start(bf16[512,768]{1,0:T(8,128)(2,1)} %add_convert_fusion.1) | copy-start | bytes 2359300
  387.5 43.7 %copy-start.47 = (bf16[512,768]{1,0:T(8,128)(2,1)S(1)}, bf16[512,768]{1,0:T(8,128)(2,1)}, u32[]{:S(2)}) copy-start(bf16[512,768]{1,0:T(8,128)(2,1)} %copy-done.46) | copy-start | bytes 2359300
  431.2 12.1 %copy-start.1 = (bf16[1024,768]{1,0:T(8,128)(2,1)}, bf16[1024,768]{1,0:T(8,128)(2,1)S(1)}, u32[]{:S(2)}) copy-start(bf16[1024,768]{1,0:T(8,128)(2,1)S(1)} %get-tuple-element.26) | copy-start | bytes 4718596
  431.2 3.4 copy-start.54
  445.3 1.7 copy-start.18
  447.2 21.9 %collective-permute-start.5 = (bf16[768,576]{0,1:T(8,128)(2,1)S(1)}, bf16[768,576]{0,1:T(8,128)(2,1)S(1)}, u32[]{:S(2)}, u32[]{:S(2)}) collective-permute-start(bf16[768,576]{0,1:T(8,128)(2,1)S(1)} %fusion.35), channel_id=1, source_target_pairs={{0,2},{1,3},{2,0},{3,1},{4,6},{5,7},{6,4},{7,5},{8,10},{9,11},{10,... | collective-permute-start | bytes 2654216 | tf_op jit(solution)/shard_map/ppermute | solution.py:622
  470.7 1.4 copy-start.35
  472.1 90.5 %reduce-scatter.6.cloned.1.call-start = ((), (), s32[]{:S(2)}) async-start(), calls=%async_computation.6 | async-start | bytes 7864320 | tf_op jit(solution)/shard_map/reduce_scatter | solution.py:604
  481.9 201.7 %all-reduce.5.cloned.1.call-start = ((), (), s32[]{:S(2)}) async-start(), calls=%async_computation.8 | async-start | bytes 589824 | tf_op jit(solution)/shard_map/psum | solution.py:626
  504.7 180.8 %reduce-scatter.8.cloned.1.call-start = ((), (), s32[]{:S(2)}) async-start(), calls=%async_computation.7 | async-start | bytes 3932160 | tf_op jit(solution)/shard_map/reduce_scatter | solution.py:605
  567.1 6.4 copy-start.2
  574.8 2.9 copy-start.15
  575.8 1.7 copy-start.11
  575.8 2.6 copy-start.9
  577.6 107.9 %collective-permute-start.4 = (bf16[512,768]{1,0:T(8,128)(2,1)S(1)}, bf16[512,768]{1,0:T(8,128)(2,1)}, u32[]{:S(2)}, u32[]{:S(2)}) collective-permute-start(bf16[512,768]{1,0:T(8,128)(2,1)S(1)} %fusion.36), channel_id=1, source_target_pairs={{0,1},{1,0},{2,3},{3,2},{4,5},{5,4},{6,7},{7,6},{8,9},{9,8},{10,11... | collective-permute-start | bytes 2359304 | tf_op jit(solution)/shard_map/ppermute | solution.py:614
  588.6 96.9 %copy-start.7 = (bf16[512,768]{1,0:T(8,128)(2,1)S(1)}, bf16[512,768]{1,0:T(8,128)(2,1)}, u32[]{:S(2)}) copy-start(bf16[512,768]{1,0:T(8,128)(2,1)} %param.16) | copy-start | bytes 2359300
  588.6 96.9 %copy-start.26 = (f32[512]{0:T(512)S(1)}, f32[512]{0:T(512)}, u32[]{:S(2)}) copy-start(f32[512]{0:T(512)} %copy-done.25) | copy-start | bytes 6148
  685.5 3.1 copy-start.10
  688.6 1.9 copy-start.24
  688.6 1.9 copy-start.44
  688.6 1.9 copy-start.43
  688.6 1.9 copy-start.31
  688.6 1.9 copy-start.42
  688.6 1.9 copy-start.32
  (15 other events, 17.8 us)
Sparse Core Ops, SparseCore 0:
  31.8 64.5 all-gather.13
  98.5 42.3 all-gather.11
  142.5 45.1 all-gather.15
  189.8 39.7 all-gather.17
  231.7 52.2 all-gather.19
  286.2 51.9 all-gather.21
  472.2 30.5 reduce-scatter.9
  505.5 56.9 reduce-scatter.5
  565.4 23.6 all-reduce.4
  591.2 74.6 reduce-scatter.7

commit v3 on v2

--- a/solution.py
+++ b/solution.py
@@ -252,15 +252,15 @@
 
 def all_partners():
     x, z, g, y, c = places()
-    by_z = [{"gr": lax.rem(z + step, 4)} for step in (1, 2, 3)]
+    by_z = [{"gr": z ^ step} for step in (1, 2, 3)]
     return [{"gc": g ^ 1}, {"gc": g ^ 2}, {"dp": x ^ 1}] + by_z
 
 
-def send(src, dst, sems, slot, target):
+def send(src, dst, sems, slot, target, send_slot=None):
     return pltpu.make_async_remote_copy(
         src_ref=src,
         dst_ref=dst,
-        send_sem=sems[0].at[slot],
+        send_sem=sems[0].at[slot if send_slot is None else send_slot],
         recv_sem=sems[1].at[slot],
         device_id=target,
         device_id_type=MESH,
@@ -300,11 +300,11 @@
     hop_c1 = send(own.at[1 - y, :, mine1], rc1, sems, slot(5), over_y)
     hop_z = [
         send(
-            sc.at[lax.rem(z + step, 4)],
+            sc.at[z ^ step],
             rd.at[step - 1],
             sems,
             slot(5 + step),
-            {"gr": lax.rem(z + step, 4)},
+            {"gr": z ^ step},
         )
         for step in (1, 2, 3)
     ]
@@ -420,6 +420,487 @@
             collective_id=collective_id, has_side_effects=True, vmem_limit_bytes=50 << 20
         ),
     )(*grads)
+
+
+def norm_rows(hidden, gain, shift):
+    center = jnp.mean(hidden, axis=1, keepdims=True)
+    offset = hidden - center
+    factor = lax.rsqrt(jnp.mean(offset * offset, axis=1, keepdims=True) + eps)
+    return offset * factor * gain + shift
+
+
+CHUNKS = 4
+
+
+def start_kernel(
+    tokens,
+    vec,
+    bup,
+    own,
+    wq,
+    prompts,
+    chip,
+    wpair,
+    vec_out,
+    bup_out,
+    own_out,
+    n1,
+    vec_in,
+    z_sems,
+    y_sems,
+    d_sems,
+    w_sems,
+    s_sems,
+    l_sems,
+):
+    x, z, g, y, c = places()
+    sib, over_y, over_x = {"gc": g ^ 1}, {"gc": g ^ 2}, {"dp": x ^ 1}
+    greet(all_partners() + [{"gc": g ^ 3}])
+    half_rows = wq.shape[0] // 2
+    my_half = pl.ds(pl.multiple_of(x * half_rows, 16), half_rows)
+
+    small = []
+    for s in (1, 2, 3):
+        to = {"gr": z ^ s}
+        small.append(send(vec, vec_in.at[s], s_sems, s, to))
+        small.append(send(own, own_out.at[z], s_sems, 3 + s, to))
+        small.append(send(bup, bup_out.at[g], s_sems, 6 + s, {"gc": g ^ s}))
+    for copy in small:
+        copy.start()
+    own_out[z] = own[...]
+    bup_out[g] = bup[...]
+
+    w_local = pltpu.make_async_copy(wq.at[my_half], wpair.at[y, z, my_half], l_sems.at[0])
+    w_local.start()
+    w_gr = [
+        send(wq.at[my_half], wpair.at[y, z, my_half], w_sems, s, {"gr": z ^ s}) for s in (1, 2, 3)
+    ]
+    for copy in w_gr:
+        copy.start()
+
+    def w_step(s):
+        block = z ^ s
+        piece = wpair.at[y, block, my_half]
+        across = wpair.at[1 - y, block, my_half]
+        return (
+            send(piece, piece, w_sems, 4 + s, over_y),
+            send(piece, piece, w_sems, 8 + s, over_x),
+            send(across, across, w_sems, 12 + s, over_x),
+        )
+
+    for copy in small[0::3]:
+        copy.wait_recv()
+    total = vec[...]
+    for s in (1, 2, 3):
+        total = total + vec_in[s]
+    vec_out[...] = total
+
+    @pl.loop(0, QROWS // 128)
+    def _(i):
+        rows = pl.ds(pl.multiple_of(i * 128, 128), 128)
+        hidden = tokens[rows].astype(F32) + vec_out[0:1]
+        n1[rows] = norm_rows(hidden, vec_out[1:2], vec_out[2:3]).astype(BF)
+
+    to_chip = pltpu.make_async_copy(n1, chip.at[c], l_sems.at[1])
+    to_chip.start()
+    chip_send = send(n1, chip.at[c], s_sems, 10, sib)
+    chip_send.start()
+    is_prompt = z < 2
+
+    @pl.when(is_prompt)
+    def _():
+        local = pltpu.make_async_copy(n1, prompts.at[g, z], l_sems.at[2])
+        local.start()
+        local.wait()
+
+    w_local.wait()
+    for copy in w_step(0)[:2]:
+        copy.start()
+
+    rows = QROWS // CHUNKS
+
+    def item(column, half, k):
+        return prompts.at[column, half, pl.ds(k * rows, rows)]
+
+    def copies(half, k):
+        mine = item(g, half, k)
+        across = item(g ^ 2, half, k)
+        n = half * CHUNKS + k
+        return {
+            "up": send(mine, mine, z_sems, n, {"gr": jnp.minimum(z + 1, 3)}),
+            "down": send(
+                mine, mine, z_sems, n, {"gr": jnp.maximum(z - 1, 0)}, 2 * CHUNKS + k
+            ),
+            "y": send(mine, mine, y_sems, n, over_y),
+            "core": send(mine, mine, d_sems, n, sib),
+            "core2": send(across, across, d_sems, 2 * CHUNKS + n, sib),
+        }
+
+    first = jnp.where(z == 0, 0, 1)
+
+    def forward(step):
+        half = first if step < CHUNKS else 1 - first
+        k = step % CHUNKS
+        moves = copies(half, k)
+
+        @pl.when(half != z)
+        def _():
+            moves["up"].wait_recv()
+
+        @pl.when(jnp.logical_and(z < 3, half <= z))
+        def _():
+            moves["up"].start()
+
+        @pl.when(jnp.logical_and(z == 1, half == 1))
+        def _():
+            moves["down"].start()
+
+        moves["y"].start()
+        moves["core"].start()
+
+    def across(step):
+        half = first if step < CHUNKS else 1 - first
+        moves = copies(half, step % CHUNKS)
+        moves["y"].wait_recv()
+        moves["core2"].start()
+
+    for step in range(2 * CHUNKS):
+        forward(step)
+        if step >= 2:
+            across(step - 2)
+        if step in (1, 2, 3):
+            w_gr[step - 1].wait_recv()
+            one, two, _ = w_step(step)
+            one.start()
+            two.start()
+        if step in (4, 5, 6, 7):
+            one, _, three = w_step(step - 4)
+            one.wait_recv()
+            three.start()
+    across(2 * CHUNKS - 2)
+    across(2 * CHUNKS - 1)
+
+    for step in range(2 * CHUNKS):
+        half = first if step < CHUNKS else 1 - first
+        moves = copies(half, step % CHUNKS)
+        moves["core"].wait_recv()
+        moves["core2"].wait_recv()
+        moves["y"].wait_send()
+        moves["core"].wait_send()
+        moves["core2"].wait_send()
+
+        @pl.when(jnp.logical_and(z < 3, half <= z))
+        def _():
+            moves["up"].wait_send()
+
+        @pl.when(jnp.logical_and(z == 1, half == 1))
+        def _():
+            moves["down"].wait_send()
+
+    for copy in w_gr:
+        copy.wait_send()
+    for s in range(4):
+        one, two, three = w_step(s)
+        one.wait_send()
+        two.wait()
+        three.wait()
+    for i, copy in enumerate(small):
+        if i % 3 == 0:
+            copy.wait_send()
+        else:
+            copy.wait()
+    to_chip.wait()
+    chip_send.wait()
+
+
+def start_exchange(tokens, vec, bup, own, wq, collective_id):
+    any_space = pl.BlockSpec(memory_space=pl.ANY)
+    vmem = pl.BlockSpec(memory_space=pltpu.VMEM)
+
+    def dma(count):
+        return pltpu.SemaphoreType.DMA((count,))
+
+    def pair(count, extra=0):
+        return dma(count + extra), dma(count)
+
+    z_pair, y_pair, d_pair = pair(2 * CHUNKS, CHUNKS), pair(2 * CHUNKS), pair(4 * CHUNKS)
+    w_pair, s_pair = pair(16), pair(11)
+
+    def body(*refs):
+        main, sems = refs[:13], refs[13:]
+        start_kernel(*main, sems[0:2], sems[2:4], sems[4:6], sems[6:8], sems[8:10], sems[10])
+
+    return pl.pallas_call(
+        body,
+        name="start_exchange",
+        in_specs=[vmem, vmem, vmem, vmem, any_space],
+        out_specs=[any_space, any_space, any_space, vmem, vmem, vmem],
+        out_shape=[
+            jax.ShapeDtypeStruct((4, 2, QROWS, D), BF),
+            jax.ShapeDtypeStruct((2, QROWS, D), BF),
+            jax.ShapeDtypeStruct((2, 4) + wq.shape, BF),
+            jax.ShapeDtypeStruct(vec.shape, F32),
+            jax.ShapeDtypeStruct((4,) + bup.shape, F32),
+            jax.ShapeDtypeStruct((4,) + own.shape, jnp.int32),
+        ],
+        scratch_shapes=[pltpu.VMEM((QROWS, D), BF), pltpu.VMEM((4,) + vec.shape, F32)]
+        + [*z_pair, *y_pair, *d_pair, *w_pair, *s_pair, dma(3)],
+        compiler_params=pltpu.CompilerParams(
+            collective_id=collective_id, has_side_effects=True, vmem_limit_bytes=32 << 20
+        ),
+    )(tokens, vec, bup, own, wq)
+
+
+GATHER_SLOTS = 36
+
+
+def gather_steps(blocks, wholes, sems, l_sems):
+    x, z, g, y, c = places()
+    sib, over_y, over_x = {"gc": g ^ 1}, {"gc": g ^ 2}, {"dp": x ^ 1}
+    steps = []
+
+    def plan(a):
+        block, whole = blocks[a], wholes[a]
+        rows = block.shape[0]
+        q = rows // 4
+        half = pl.ds(pl.multiple_of(x * 2 * q, 16), 2 * q)
+        qa = pl.ds(pl.multiple_of(x * 2 * q, 16), q)
+        qb = pl.ds(pl.multiple_of(x * 2 * q + q, 16), q)
+        base = a * GATHER_SLOTS
+        local = pltpu.make_async_copy(block.at[half], whole.at[g, z, half], l_sems.at[a])
+        by_gr = [
+            send(block.at[half], whole.at[g, z, half], sems, base + s, {"gr": z ^ s})
+            for s in (1, 2, 3)
+        ]
+
+        def moves(s):
+            o = base + 4 + 8 * s
+            mine, far = whole.at[g, z ^ s], whole.at[g ^ 2, z ^ s]
+            return {
+                "ay": send(mine.at[qa], mine.at[qa], sems, o, over_y),
+                "ax": send(mine.at[qa], mine.at[qa], sems, o + 1, over_x),
+                "afx": send(far.at[qa], far.at[qa], sems, o + 2, over_x),
+                "bx": send(mine.at[qb], mine.at[qb], sems, o + 3, over_x),
+                "by": send(mine.at[qb], mine.at[qb], sems, o + 4, over_y),
+                "bfy": send(
+                    mine.at[pl.ds(pl.multiple_of((1 - x) * 2 * q + q, 16), q)],
+                    mine.at[pl.ds(pl.multiple_of((1 - x) * 2 * q + q, 16), q)],
+                    sems,
+                    o + 5,
+                    over_y,
+                ),
+                "c1": send(mine, mine, sems, o + 6, sib),
+                "c2": send(far, far, sems, o + 7, sib),
+            }
+
+        return local, by_gr, moves
+
+    plans = [plan(a) for a in range(len(blocks))]
+
+    def begin():
+        for local, by_gr, _ in plans:
+            local.start()
+            for copy in by_gr:
+                copy.start()
+        for local, _, _ in plans:
+            local.wait()
+
+    def first(a, s):
+        def run():
+            _, by_gr, moves = plans[a]
+            if s:
+                by_gr[s - 1].wait_recv()
+            m = moves(s)
+            for name in ("ay", "bx", "ax", "by"):
+                m[name].start()
+
+        return run
+
+    def second(a, s):
+        def run():
+            m = plans[a][2](s)
+            m["ay"].wait_recv()
+            m["afx"].start()
+            m["bx"].wait_recv()
+            m["bfy"].start()
+
+        return run
+
+    def third(a, s):
+        def run():
+            m = plans[a][2](s)
+            for name in ("ax", "afx", "by", "bfy"):
+                m[name].wait_recv()
+            m["c1"].start()
+            m["c2"].start()
+
+        return run
+
+    def finish():
+        for _, by_gr, moves in plans:
+            for copy in by_gr:
+                copy.wait_send()
+            for s in range(4):
+                m = moves(s)
+                m["c1"].wait_recv()
+                m["c2"].wait_recv()
+                for copy in m.values():
+                    copy.wait_send()
+
+    order = [(a, s) for a in range(len(blocks)) for s in range(4)]
+    steps = [begin]
+    n = len(order)
+    for i in range(n + 4):
+        part = []
+        if i < n:
+            part.append(first(*order[i]))
+        if 2 <= i < n + 2:
+            part.append(second(*order[i - 2]))
+        if i >= 4:
+            part.append(third(*order[i - 4]))
+        steps.append(partial(lambda fs: [f() for f in fs], part))
+    steps.append(finish)
+    return steps
+
+
+def att_gather_kernel(count, grp_ref, q_ref, kvo_ref, kvp_ref, *refs):
+    blocks = refs[:count]
+    mixed, lse_ref = refs[count : count + 2]
+    wholes = refs[count + 2 : 2 * count + 2]
+    mix, sems_s, sems_r, l_sems, m_send, m_recv, m_local = refs[2 * count + 2 :]
+    p, j = pl.program_id(0), pl.program_id(1)
+    step = p * pl.num_programs(1) + j
+    x, z, g, y, c = places()
+
+    hooks = gather_steps(blocks, wholes, (sems_s, sems_r), l_sems)
+
+    @pl.when(step == 0)
+    def _():
+        greet(all_partners())
+
+    last = len(hooks) - 1
+    for i, hook in enumerate(hooks):
+        when = i * 23 // last
+        if i == last:
+            continue
+
+        @pl.when(step == when)
+        def _():
+            hook()
+
+    group = grp_ref[j]
+    low = lax.broadcasted_iota(jnp.int32, (CL, 128), 1) < 64
+    zero = jnp.zeros((CL, 128), BF)
+    q = q_ref[...]
+    q_parts = (jnp.where(low, zero, q), jnp.where(low, q, zero))
+
+    def store(mixes, sums):
+        mix[p, j // 4, pl.ds(pl.multiple_of((j % 4) * CL, CL), CL)] = jnp.where(
+            low, mixes[0], mixes[1]
+        ).astype(BF)
+        flat = jnp.where(low, sums[0], sums[1]).T
+        lse_ref[0, 0, 0:1] = flat[0:1]
+        lse_ref[0, 0, 1:2] = flat[64:65]
+
+    @pl.when(z >= 2)
+    def _():
+        row = lax.broadcasted_iota(jnp.int32, (CL, CL), 0)
+        near_ok = lax.broadcasted_iota(jnp.int32, (CL, CL), 1) <= row
+        mixes, sums = [], []
+        for h in range(2):
+            cols = slice(128 * h, 128 * h + 128)
+            kv = kvp_ref[group, :, cols]
+            kvo = kvo_ref[:, cols]
+            far = nt(q_parts[h], kv)
+            near = jnp.where(near_ok, nt(q_parts[h], kvo), negative)
+            top = jnp.maximum(
+                jnp.max(far, axis=1, keepdims=True), jnp.max(near, axis=1, keepdims=True)
+            )
+            far = jnp.exp(far - top)
+            near = jnp.exp(near - top)
+            total = jnp.sum(far, axis=1, keepdims=True) + jnp.sum(near, axis=1, keepdims=True)
+            mixes.append((nn(far.astype(BF), kv) + nn(near.astype(BF), kvo)) / total)
+            sums.append(jnp.broadcast_to(top + jnp.log(total), (CL, 128)))
+        store(mixes, sums)
+
+    @pl.when(z < 2)
+    def _():
+        limit = z * QROWS + (j % (QROWS // CL)) * CL
+        row = lax.broadcasted_iota(jnp.int32, (CL, P_SIZE), 0)
+        key = lax.broadcasted_iota(jnp.int32, (CL, P_SIZE), 1)
+        allowed = key - row <= limit
+        mixes, sums = [], []
+        for h in range(2):
+            cols = slice(128 * h, 128 * h + 128)
+            kv = kvp_ref[group, :, cols]
+            far = jnp.where(allowed, nt(q_parts[h], kv), negative)
+            top = jnp.max(far, axis=1, keepdims=True)
+            far = jnp.exp(far - top)
+            total = jnp.sum(far, axis=1, keepdims=True)
+            mixes.append(nn(far.astype(BF), kv) / total)
+            sums.append(jnp.broadcast_to(top + jnp.log(total), (CL, 128)))
+        store(mixes, sums)
+
+    def exchange(i):
+        cols = pl.ds(128 * i, 128)
+        return (
+            pltpu.make_async_copy(mix.at[i, c], mixed.at[c, :, cols], m_local.at[i]),
+            send(mix.at[i, 1 - c], mixed.at[c, :, cols], (m_send, m_recv), i, {"gc": g ^ 1}),
+        )
+
+    for i in range(3):
+
+        @pl.when(step == 8 * i + 7)
+        def _():
+            for copy in exchange(i):
+                copy.start()
+
+    @pl.when(step == 23)
+    def _():
+        hooks[last]()
+        for i in range(3):
+            for copy in exchange(i):
+                copy.wait()
+
+
+def attend_gather(grp, q, kvo, kvp, blocks, collective_id):
+    rows = q.shape[0]
+    count = len(blocks)
+    any_space = pl.BlockSpec(memory_space=pl.ANY)
+    slots = GATHER_SLOTS * count
+    return pl.pallas_call(
+        partial(att_gather_kernel, count),
+        name="attend_gather",
+        grid_spec=pltpu.PrefetchScalarGridSpec(
+            num_scalar_prefetch=1,
+            grid=(3, rows // CL),
+            in_specs=[
+                pl.BlockSpec((CL, 128), lambda p, j, *_: (j, p)),
+                pl.BlockSpec((CL, 256), lambda p, j, *_: (j, p)),
+                pl.BlockSpec((4, P_SIZE, 256), lambda p, j, *_: (0, 0, p)),
+            ]
+            + [any_space] * count,
+            out_specs=[any_space, pl.BlockSpec((1, 1, 2, 128), lambda p, j, *_: (p, j, 0, 0))]
+            + [any_space] * count,
+            scratch_shapes=[
+                pltpu.VMEM((3, 2, QROWS, 128), BF),
+                pltpu.SemaphoreType.DMA((slots,)),
+                pltpu.SemaphoreType.DMA((slots,)),
+                pltpu.SemaphoreType.DMA((count,)),
+                pltpu.SemaphoreType.DMA((3,)),
+                pltpu.SemaphoreType.DMA((3,)),
+                pltpu.SemaphoreType.DMA((3,)),
+            ],
+        ),
+        out_shape=[
+            jax.ShapeDtypeStruct((2, QROWS, 384), BF),
+            jax.ShapeDtypeStruct((3, rows // CL, 2, 128), F32),
+        ]
+        + [jax.ShapeDtypeStruct((4, 4) + block.shape, BF) for block in blocks],
+        compiler_params=pltpu.CompilerParams(
+            collective_id=collective_id, has_side_effects=True, vmem_limit_bytes=40 << 20
+        ),
+    )(grp, q, kvo, kvp.reshape(4, P_SIZE, kvp.shape[1]), *blocks)
 
 
 def norm(hidden, gain, shift):
@@ -487,14 +968,27 @@
     swap_core = [(i, i ^ 1) for i in range(n_gc)]
     swap_y = [(i, i ^ 2) for i in range(n_gc)]
 
-    vectors = jnp.stack(
-        [pass_embed, ln1_gain, ln1_bias, out_bias, ln2_gain, ln2_bias, fc2_bias]
-    )
-    vectors = lax.all_gather(vectors, "gr", axis=1, tiled=True).astype(F32)
+    packed = jnp.stack(
+        [pass_embed, ln1_gain, ln1_bias, out_bias, ln2_gain, ln2_bias, fc2_bias, fc2_bias]
+    ).astype(F32)
+    if n_dp == 2:
+        vec = lax.dynamic_update_slice(jnp.zeros((8, D), F32), packed, (0, z * packed.shape[1]))
+        bup = jnp.broadcast_to(fc1_bias.astype(F32), (8, fc1_bias.shape[0]))
+        own = jnp.broadcast_to(jnp.pad(cont_group, (0, 120)), (8, 128))
+        n1_prompt, n1_chip, w_pair, vectors, b_up, owners = start_exchange(
+            tokens, vec, bup, own, qkv_weight, 1
+        )
+        n1_prompt = n1_prompt.reshape(4 * P_SIZE, D)
+        n1_chip = n1_chip.reshape(2 * QROWS, D)
+        w_qkv = w_pair.reshape(2, D, 576)
+        b_up = b_up[:, 0].reshape(FF)
+        owners = owners[:, 0, :8]
+    else:
+        vectors = lax.all_gather(packed, "gr", axis=1, tiled=True)
+        b_up = lax.all_gather(fc1_bias, "gc", axis=0, tiled=True).astype(F32)
+        owners = lax.all_gather(cont_group, "gr", axis=0, tiled=True)
     embed, gain1, shift1, b_out, gain2, shift2, b_down = [vectors[i] for i in range(7)]
-    b_up = lax.all_gather(fc1_bias, "gc", axis=0, tiled=True).astype(F32)
-    owners = lax.all_gather(cont_group, "gr", axis=0, tiled=True)
-    owners = owners.reshape(n_gc, 2, 4)
+    owners = owners.reshape(4, 2, 4)
     mine = lax.dynamic_slice(owners, (2 * y, jnp.maximum(z - 2, 0), 0), (2, 1, 4)).reshape(8)
     own_groups = jnp.repeat(2 * y + jnp.arange(2), 4)
     grp = jnp.where(z < 2, own_groups, mine).astype(jnp.int32)
@@ -504,37 +998,46 @@
     normed1, unit1, factor1 = norm(hidden, gain1, shift1)
     n1 = normed1.astype(BF)
 
-    w_other = lax.ppermute(qkv_weight, "gc", swap_y)
-    w_pair = jnp.where(y == 0, jnp.stack([qkv_weight, w_other]), jnp.stack([w_other, qkv_weight]))
-    w_qkv = lax.all_gather(w_pair, "gr", axis=1, tiled=True)
+    if n_dp != 2:
+        w_other = lax.ppermute(qkv_weight, "gc", swap_y)
+        w_pair = jnp.where(
+            y == 0, jnp.stack([qkv_weight, w_other]), jnp.stack([w_other, qkv_weight])
+        )
+        w_qkv = lax.all_gather(w_pair, "gr", axis=1, tiled=True)
+        n1_other = lax.ppermute(n1, "gc", swap_core)
+        n1_chip = jnp.where(
+            c == 0, jnp.concatenate([n1, n1_other]), jnp.concatenate([n1_other, n1])
+        )
+        n1_col = lax.all_gather(n1, "gr", axis=0, tiled=True)[:P_SIZE]
+        n1_prompt = lax.all_gather(n1_col, "gc", axis=0, tiled=True)
     w_q, w_kv = head_layout(w_qkv)
-
-    n1_other = lax.ppermute(n1, "gc", swap_core)
-    n1_chip = jnp.where(
-        c == 0, jnp.concatenate([n1, n1_other]), jnp.concatenate([n1_other, n1])
-    )
-    n1_col = lax.all_gather(n1, "gr", axis=0, tiled=True)[:P_SIZE]
-    n1_prompt = lax.all_gather(n1_col, "gc", axis=0, tiled=True)
-
-    w_out = lax.all_gather(out_weight, ("gc", "gr"))
-    w_up = lax.all_gather(fc1_weight, ("gc", "gr")).reshape(n_gc, D, FF // n_gc)
-    w_down = lax.all_gather(fc2_weight, ("gc", "gr")).reshape(n_gc, D, FF // n_gc)
-    w_out = w_out.reshape(n_gc, n_gr, 192, 192).transpose(0, 2, 1, 3).reshape(D, D)
 
     kvp = nn(n1_prompt, w_kv).astype(BF)
     kvo = nn(n1_chip, w_kv).astype(BF)
     q = (nn(n1_chip, w_q) * 0.125).astype(BF)
-    mixed_heads, lse = attend(grp, z_arr, q, kvo, kvp)
-    lse_rows = lse[:, ::64].reshape(8, CL, 3, 2).transpose(2, 0, 3, 1)
-
-    halves = mixed_heads.reshape(2, QROWS, 2, 192)
-    keep = lax.dynamic_index_in_dim(halves, c, 0, keepdims=False)
-    give = lax.dynamic_index_in_dim(halves, 1 - c, 0, keepdims=False)
-    take = lax.ppermute(give, "gc", swap_core)
-    mixed = jnp.where(c == 0, jnp.stack([keep, take], axis=2), jnp.stack([take, keep], axis=2))
-    mixed = mixed.reshape(QROWS, D)
-
-    hidden2 = hidden + nn(mixed, w_out) + b_out
+    if n_dp == 2:
+        mixed, lse_rows, w_out, w_up, w_down = attend_gather(
+            grp, q, kvo, kvp, [out_weight, fc1_weight, fc2_weight], 2
+        )
+    else:
+        w_out = lax.all_gather(out_weight, ("gc", "gr"))
+        w_up = lax.all_gather(fc1_weight, ("gc", "gr"))
+        w_down = lax.all_gather(fc2_weight, ("gc", "gr"))
+        mixed_heads, lse = attend(grp, z_arr, q, kvo, kvp)
+        lse_rows = lse[:, ::64].reshape(8, CL, 3, 2).transpose(2, 0, 3, 1)
+        halves = mixed_heads.reshape(2, QROWS, 384)
+        keep = lax.dynamic_index_in_dim(halves, c, 0, keepdims=False)
+        give = lax.dynamic_index_in_dim(halves, 1 - c, 0, keepdims=False)
+        take = lax.ppermute(give, "gc", swap_core)
+        mixed = jnp.where(c == 0, jnp.stack([keep, take]), jnp.stack([take, keep]))
+    w_up = w_up.reshape(n_gc, D, FF // n_gc)
+    w_down = w_down.reshape(n_gc, D, FF // n_gc)
+    w_out = w_out.reshape(2, 2, n_gr, 192, 192).transpose(1, 0, 3, 2, 4).reshape(2, 384, D)
+
+    attended = lax.dot_general(
+        mixed, w_out, (((0, 2), (0, 1)), ((), ())), preferred_element_type=F32
+    )
+    hidden2 = hidden + attended + b_out
     normed2, unit2, factor2 = norm(hidden2, gain2, shift2)
     n2 = normed2.astype(BF)
     pre = lax.dot_general(n2, w_up, (((1,), (1,)), ((), ())), preferred_element_type=F32)
@@ -569,12 +1072,11 @@
     grad_h2 = grad_final + back2
     ga = grad_h2.astype(BF)
     grad_b_out = jnp.sum(ga, axis=0, dtype=F32)
-    grad_w_out = tn(mixed, ga)
-    gm = nt(ga, w_out).astype(BF)
-
-    gm_blocks = gm.reshape(QROWS, 2, 2, 192)
-    gm_keep = lax.dynamic_index_in_dim(gm_blocks, c, 2, keepdims=False)
-    gm_give = lax.dynamic_index_in_dim(gm_blocks, 1 - c, 2, keepdims=False)
+    grad_w_out = jnp.einsum("ctk,tn->ckn", mixed, ga, preferred_element_type=F32)
+    gm = jnp.einsum("tn,ckn->ctk", ga, w_out, preferred_element_type=F32).astype(BF)
+
+    gm_keep = lax.dynamic_index_in_dim(gm, c, 0, keepdims=False)
+    gm_give = lax.dynamic_index_in_dim(gm, 1 - c, 0, keepdims=False)
     gm_take = lax.ppermute(gm_give, "gc", swap_core)
     gm_chip = jnp.where(c == 0, jnp.stack([gm_keep, gm_take]), jnp.stack([gm_take, gm_keep]))
     gm_chip = gm_chip.reshape(2 * QROWS, 384)
@@ -591,7 +1093,10 @@
     weight_grads = [
         grad_w_down.astype(BF).reshape(n_gc, n_gr, 192, 768),
         grad_w_up.astype(BF).reshape(n_gc, n_gr, 192, 768),
-        grad_w_out.astype(BF).reshape(n_gc, 192, n_gr, 192).transpose(0, 2, 1, 3),
+        grad_w_out.astype(BF)
+        .reshape(2, 2, 192, n_gr, 192)
+        .transpose(1, 0, 3, 2, 4)
+        .reshape(n_gc, n_gr, 192, 192),
     ]
     if n_dp == 2:
         out_w_down, out_w_up, out_w_out = scatter_grads(weight_grads, 3)

time: 749 us -> 638 us (0.85)
  waiting for transfers between devices: 321 us -> 102 us
  Pallas kernels: 163 us -> 288 us
  blocking collectives: 69 us -> 40.5 us
  local copies, waits for them, and re-layouts: 79.7 us -> 87.2 us
    all_gather x6 -> x0, waiting for transfers between devices: 215 us -> none  [the longest x1 56.9 us: on_device(): n1_col = lax.all_gather(n1, 'gr', axis=0, tiled=True)[:P_SIZE]]
    pallas_call x1 -> x2, Pallas kernels: 24.2 us -> 138 us  [the longest x1 79.9 us: attend_gather(): pl.pallas_call(partial(att_gather_kernel, count), name='attend_gather', g...]
    all_gather x2 -> x0, blocking collectives: 20.1 us -> none  [the longest x1 14.8 us: on_device(): vectors = lax.all_gather(vectors, 'gr', axis=1, tiled=True).astype(F32)]
    unnamed x175 -> x162, local copies, waits for them, and re-layouts: 21.7 us -> 41.5 us
    reshape x7 -> x6, local copies, waits for them, and re-layouts: 12.1 us -> 24.2 us  [the longest x1 6.92 us: on_device(): w_up = w_up.reshape(n_gc, D, FF // n_gc)]
    dot_general x2 -> x1, local copies, waits for them, and re-layouts: 13.3 us -> 1.19 us  [tn(): lax.dot_general(a, b, (((0,), (0,)), ((), ())), preferred_element_type=F32)]
    pallas_call x1, Pallas kernels: 43.7 us -> 53.3 us  [attend_back(): pl.pallas_call(att_bwd_kernel, name='att_bwd', grid_spec=pltpu.PrefetchSc...]
    unnamed x1 -> x0, blocking collectives: 8.51 us -> none
  transfers between devices with their start and end apart: 16 -> 7, of which waited for: 9 -> 4; matrix products, arithmetic and copies ran while one was open for 12% -> 6% of each run, Pallas kernels for 16% -> 16%
where the time goes in v3:
time: 638 us; the launch traced here: 627 us
  Pallas kernels  288 us (45%)
  waiting for transfers between devices  102 us (16%)
  local copies, waits for them, and re-layouts  87.2 us (14%)
  matrix products  78 us (12%)
  blocking collectives  40.5 us (6%)
  between operations  17.5 us (3%)
  other arithmetic  11.9 us (2%)
    pallas_call x1, Pallas kernels, scatter_grads(): pl.pallas_call(partial(scatter_kernel, count), name='scatter_grads', in_s...  97.2 us
    pallas_call x1, Pallas kernels, attend_gather(): pl.pallas_call(partial(att_gather_kernel, count), name='attend_gather', g...  79.9 us
    reduce_scatter x1, waiting for transfers between devices, on_device(): lax.psum_scatter(part_prompt, 'gc', scatter_dimension=0, tiled=True)  57.8 us
    pallas_call x1, Pallas kernels, start_exchange(): pl.pallas_call(body, name='start_exchange', in_specs=[vmem, vmem, vmem, v...  57.7 us
    pallas_call x1, Pallas kernels, attend_back(): pl.pallas_call(att_bwd_kernel, name='att_bwd', grid_spec=pltpu.PrefetchSc...  53.3 us
    unnamed x162, local copies, waits for them, and re-layouts  41.5 us
    psum x1, blocking collectives, on_device(): sums = lax.psum(sums, ('dp', 'gr', 'gc'))  40.5 us
    unnamed x5, waiting for transfers between devices  22.2 us
  transfers between devices with their start and end apart: 7, of which 4 were waited for; matrix products, arithmetic and copies ran while one was open for 6% of the time, Pallas kernels for 16%

profile of v3, /device:TPU:0, one launch (start us, length us, event | category | flops | bytes accessed | tf_op | source)
XLA Modules:
  0.0 627.2 jit_solution(4512655481680398344)
XLA Ops:
  14.0 1.1 copy-done
  15.1 0.9 copy-done.11
  16.1 57.7 %start_exchange.1 = (bf16[4,2,512,768]{3,2,1,0:T(8,128)(2,1)S(1)}, bf16[2,512,768]{2,1,0:T(8,128)(2,1)S(1)}, bf16[2,4,192,576]{3,2,1,0:T(8,128)(2,1)S(1)}, f32[8...) custom-call(bf16[512,768]{1,0:T(8,128)(2,1)S(1)} %copy-done, ...), custom_call_target="tpu_custom_call" | custom-call | tf_op jit(solution)/shard_map/start_exchange/pallas_call | solution.py:633
  75.1 2.7 copy-done.16
  77.7 1.1 copy-done.17
  78.9 2.4 copy.91
  86.6 1.0 fusion.66
  87.6 1.0 fusion.65
  88.6 1.0 fusion.64
  89.5 1.0 fusion.63
  90.5 1.0 fusion.62
  91.4 1.0 fusion.61
  92.4 10.5 %convolution_convert_fusion.1.kvp_ref = bf16[4096,768]{1,0:T(8,128)(2,1)} fusion(bf16[4096,768]{1,0:T(8,128)(2,1)} %bitcast.301, bf16[768,768]{0,1:T(8,128)(2,1)S(1)} %get-tuple-element.103), kind=kOutput, calls=%fused_computation.3 | convolution fusion | flops 4834983936 | bytes 13762560 | tf_op jit(solution)/shard_map/dot_general | solution.py:27
  102.9 1.4 convolution_convert_fusion.2.kvo_ref
  104.4 1.0 multiply_convert_fusion.1.q_ref
  105.8 1.0 copy-done.10
  106.8 79.9 %attend_gather.1 = (bf16[2,512,384]{2,1,0:T(8,128)(2,1)S(1)}, f32[3,8,2,128]{3,2,1,0:T(2,128)S(1)}, bf16[4,4,192,192]{3,2,1,0:T(8,128)(2,1)S(1)}, bf16[4,4,192,7...) custom-call(s32[8]{0:T(128)S(1)} %broadcast_select_fusion.grp_ref, bf16[1024,384]{1,0:T(8,128)(2,1)S(1)} %multiply_convert_fusion.1.q_ref, ...), custom_call_target="tpu_custom_call" | custom-call | tf_op jit(solution)/shard_map/attend_gather/pallas_call | solution.py:871
  186.7 2.1 copy-done.2
  188.8 1.1 copy-done.3
  190.6 6.9 %copy.93 = bf16[4,768,768]{1,2,0:T(8,128)(2,1)} copy(bf16[4,768,768]{2,1,0:T(8,128)(2,1)} %bitcast.293) | data formatting | bytes 9437184 | tf_op jit(solution)/shard_map/reshape | solution.py:1033
  197.5 3.8 copy.92
  201.3 4.1 reshape.185
  205.5 2.1 fusion.88
  207.7 1.2 copy-done.27
  209.1 0.9 slice.192
  210.0 6.9 %copy.95 = bf16[4,768,768]{1,2,0:T(8,128)(2,1)} copy(bf16[4,768,768]{2,1,0:T(8,128)(2,1)} %bitcast.322) | data formatting | bytes 9437184 | tf_op jit(solution)/shard_map/reshape | solution.py:1034
  217.0 6.8 %multiply_convert_fusion = (bf16[512,3072]{1,0:T(8,128)(2,1)S(1)}, f32[512,3072]{1,0:T(8,128)S(1)}) fusion(f32[3072]{0:T(1024)S(1)} %bitcast.346, bf16[3072,768]{1,0:T(8,128)(2,1)} %bitcast.326, f32[512,768]{1,0:T(8,128)} %copy-done.27, f32[768]{0:T(1024)S(1)} %get-tuple-element.89, f32[768]{0:T(1024)S(1)} %get-tuple-element.90, ...), kind=kOutput, calls=%fused_computation.12 | convolution fusion | flops 2433613824 | bytes 15751168 | tf_op jit(solution)/shard_map/dot_general | solution.py:1043
  223.9 3.3 convert_reduce_fusion.1
  227.3 7.2 %convert_reduce_fusion = (f32[3072]{0:T(1024)}, bf16[512,3072]{1,0:T(8,128)(2,1)S(1)}) fusion(f32[512,3072]{1,0:T(8,128)S(1)} %get-tuple-element.128, f32[3072]{0:T(1024)S(1)} %bitcast.347, bf16[512,768]{1,0:T(8,128)(2,1)S(1)} %get-tuple-element.96, bf16[3072,768]{1,0:T(8,128)(2,1)S(1)} %bitcast.327), kind=kOutput, calls=%fused_computation.11 | convolution fusion | flops 2452091904 | bytes 14966784 | tf_op jit(solution)/shard_map/dot_general | solution.py:1059
  234.5 3.5 fusion.27
  238.1 2.4 convert_reduce_fusion.2
  240.5 1.2 copy-done.24
  243.7 1.4 collective-permute-done
  245.8 1.5 maximum_select_fusion
  247.3 1.2 copy.97
  248.5 1.1 copy-done.7
  249.6 1.1 copy-done.8
  250.8 53.3 %att_bwd.1 = (bf16[1024,384]{1,0:T(8,128)(2,1)S(1)}, bf16[1024,768]{1,0:T(8,128)(2,1)S(1)}, bf16[4096,768]{1,0:T(8,128)(2,1)}) custom-call(s32[8]{0:T(128)S(1)} %broadcast_select_fusion.grp_ref, s32[1]{0:T(128)} %bitcast.37.z_ref, bf16[1024,384]{1,0:T(8,128)(2,1)S(1)} %copy-done.7, bf16[1024,384]{1,0:T(8,128)(2,1)S(1)} %bitcast.300, ...), custom_call_target="tpu_custom_call" | custom-call | flops 8053063680 | bytes 12582912 | tf_op jit(solution)/shard_map/att_bwd/pallas_call | solution.py:202
  304.0 10.7 %fusion.91 = f32[768,768]{0,1:T(8,128)} fusion(bf16[4096,768]{1,0:T(8,128)(2,1)} %bitcast.302, bf16[4096,768]{1,0:T(8,128)(2,1)} %get-tuple-element.45), kind=kOutput, calls=%fused_computation.192 | convolution fusion | flops 4831838208 | bytes 14942208 | tf_op jit(solution)/shard_map/dot_general | solution.py:31
  314.7 1.2 copy.98
  316.4 2.1 fusion.90
  318.8 1.5 convolution_add_fusion.1
  320.7 1.7 copy-done.31
  323.4 21.2 %collective-permute-done.2 = bf16[768,576]{0,1:T(8,128)(2,1)S(1)} collective-permute-done((bf16[768,576]{0,1:T(8,128)(2,1)S(1)}, bf16[768,576]{0,1:T(8,128)(2,1)S(1)}, u32[]{:S(2)}, u32[]{:S(2)}) %collective-permute-start.2) | collective-permute-done | bytes 884768 | tf_op jit(solution)/shard_map/ppermute | solution.py:1127
  344.6 1.7 fusion.25
  346.2 1.3 copy.112
  347.6 9.2 %convolution_convert_fusion = bf16[4096,768]{1,0:T(8,128)(2,1)} fusion(bf16[4096,768]{1,0:T(8,128)(2,1)} %get-tuple-element.45, bf16[768,768]{0,1:T(8,128)(2,1)} %copy-done.41), kind=kOutput, calls=%fused_computation.2 | convolution fusion | flops 4834983936 | bytes 13762560 | tf_op jit(solution)/shard_map/dot_general | solution.py:23
  356.9 22.1 %reduce-scatter.10.cloned.1.call-done = bf16[192,576]{1,0:T(8,128)(2,1)} async-done(((bf16[768,576]{1,0:T(8,128)(2,1)}), bf16[192,576]{1,0:T(8,128)(2,1)}) %reduce-scatter.10.cloned.1.call-update) | async-done | bytes 221200
  379.0 1.8 copy.113
  380.8 57.8 %reduce-scatter.6.cloned.1.call-done = bf16[1024,768]{1,0:T(8,128)(2,1)} async-done(((bf16[4096,768]{1,0:T(8,128)(2,1)}), bf16[1024,768]{1,0:T(8,128)(2,1)}) %reduce-scatter.6.cloned.1.call-update) | async-done | bytes 1572880 | tf_op jit(solution)/shard_map/reduce_scatter | solution.py:1109
  438.6 3.3 concatenate.17
  441.9 1.1 copy-done.5
  443.0 3.2 convolution_convert_fusion.3
  446.2 3.7 reshape.197
  450.2 1.6 copy-done.50
  451.9 5.7 fusion.15
  457.6 4.7 fusion.18
  462.3 97.2 %scatter_grads.1 = (f32[192,768]{1,0:T(8,128)S(1)}, f32[192,768]{1,0:T(8,128)S(1)}, f32[192,192]{1,0:T(8,128)S(1)}) custom-call(bf16[4,4,192,768]{3,2,1,0:T(8,128)(2,1)} %bitcast.328, bf16[4,4,192,768]{3,2,1,0:T(8,128)(2,1)} %bitcast.329, bf16[4,4,192,192]{3,2,1,0:T(8,128)(2,1)S(1)} %bitcast.292), custom_call_target="tpu_custom_call" | custom-call | tf_op jit(solution)/shard_map/scatter_grads/pallas_call | solution.py:407
  560.2 3.2 fusion.89
  563.4 1.0 convolution_add_fusion
  566.1 1.9 copy.105
  568.0 3.0 multiply_reduce_fusion.1
  571.1 1.8 fusion.86
  573.7 40.5 %psum.14 = f32[8576]{0:T(1024)S(1)} all-reduce(f32[8576]{0:T(1024)S(1)} %constant_dynamic-update-slice_fusion.2), channel_id=1, replica_groups=mesh['dp'=2,'gr'=4,'gc'=4] {'dp','gr','gc'}, use_global_device_ids=true, to_apply=%region_19.20 | all-reduce | flops 8576 | bytes 68608 | tf_op jit(solution)/shard_map/psum | solution.py:1148
  (204 shorter events, 26.7 us)
Async XLA Ops:
  7.2 371.8 %reduce-scatter.10.cloned.1.call-start = ((), (), s32[]{:S(2)}) async-start(), calls=%async_computation.6 | async-start | bytes 1228800
  14.0 1.1 copy-start
  15.1 0.9 copy-start.11
  75.1 2.7 copy-start.16
  77.7 1.1 copy-start.17
  92.4 10.5 %copy-start.41 = (bf16[768,768]{0,1:T(8,128)(2,1)}, bf16[768,768]{0,1:T(8,128)(2,1)S(1)}, u32[]{:S(2)}) copy-start(bf16[768,768]{0,1:T(8,128)(2,1)S(1)} %get-tuple-element.103) | copy-start | bytes 3538948
  92.4 11.9 %copy-start.33 = (bf16[768,384]{0,1:T(8,128)(2,1)}, bf16[768,384]{0,1:T(8,128)(2,1)S(1)}, u32[]{:S(2)}) copy-start(bf16[768,384]{0,1:T(8,128)(2,1)S(1)} %get-tuple-element.104) | copy-start | bytes 1769476
  92.4 10.5 %copy-start.18 = (bf16[2,512,768]{2,1,0:T(8,128)(2,1)S(1)}, bf16[2,512,768]{2,1,0:T(8,128)(2,1)}, u32[]{:S(2)}) copy-start(bf16[2,512,768]{2,1,0:T(8,128)(2,1)} %copy-done.17) | copy-start | bytes 4718596
  104.4 1.3 copy-start.53
  104.4 1.4 copy-start.9
  104.4 1.4 copy-start.12
  105.4 81.3 %copy-start.6 = (bf16[1024,384]{1,0:T(8,128)(2,1)}, bf16[1024,384]{1,0:T(8,128)(2,1)S(1)}, u32[]{:S(2)}) copy-start(bf16[1024,384]{1,0:T(8,128)(2,1)S(1)} %multiply_convert_fusion.1.q_ref) | copy-start | bytes 2359300
  105.8 1.0 copy-start.10
  186.7 2.1 copy-start.2
  188.8 1.1 copy-start.3
  190.6 14.9 %copy-start.4 = (bf16[2,512,384]{2,1,0:T(8,128)(2,1)}, bf16[2,512,384]{2,1,0:T(8,128)(2,1)S(1)}, u32[]{:S(2)}) copy-start(bf16[2,512,384]{2,1,0:T(8,128)(2,1)S(1)} %get-tuple-element.37) | copy-start | bytes 2359300
  201.3 4.1 copy-start.14
  201.3 4.2 copy-start.1
  205.5 11.5 %copy-start.47 = (f32[768]{0:T(1024)}, f32[768]{0:T(1024)S(1)}, u32[]{:S(2)}) copy-start(f32[768]{0:T(1024)S(1)} %get-tuple-element.89) | copy-start | bytes 9220
  205.5 32.6 %copy-start.38 = (f32[768]{0:T(1024)}, f32[768]{0:T(1024)S(1)}, u32[]{:S(2)}) copy-start(f32[768]{0:T(1024)S(1)} %get-tuple-element.90) | copy-start | bytes 9220
  207.6 1.2 copy-start.27
  209.1 28.9 %copy-start.42 = (f32[512]{0:T(512)}, f32[512]{0:T(512)S(1)}, u32[]{:S(2)}) copy-start(f32[512]{0:T(512)S(1)} %add_rsqrt_fusion.1) | copy-start | bytes 6148
  210.0 13.8 %slice-start.2 = ((s8[4718592]{0:T(1024)(128)(4,1)}), s8[524288]{0:T(1024)(128)(4,1)S(1)}, s32[]{:S(2)}) async-start(s8[4718592]{0:T(1024)(128)(4,1)} %bitcast.323), calls=%async_computation.9 | async-start | bytes 1048576
  217.0 6.9 %copy-start.28 = (f32[512,768]{1,0:T(8,128)S(1)}, f32[512,768]{1,0:T(8,128)}, u32[]{:S(2)}) copy-start(f32[512,768]{1,0:T(8,128)} %copy-done.27) | copy-start | bytes 4718596
  217.0 6.9 %slice-start.3 = ((s8[4718592]{0:T(1024)(128)(4,1)}), s8[4194304]{0:T(1024)(128)(4,1)S(1)}, s32[]{:S(2)}) async-start(s8[4718592]{0:T(1024)(128)(4,1)} %bitcast.323), calls=%async_computation.10 | async-start | bytes 8388608
  217.0 6.9 %copy-start.35 = (bf16[512,768]{1,0:T(8,128)(2,1)S(1)}, bf16[512,768]{1,0:T(8,128)(2,1)}, u32[]{:S(2)}) copy-start(bf16[512,768]{1,0:T(8,128)(2,1)} %param.17) | copy-start | bytes 2359300
  223.8 3.4 copy-start.49
  223.9 3.4 copy-start.30
  223.9 10.6 %slice-start = ((s8[4718592]{0:T(1024)(128)(4,1)}), s8[4194304]{0:T(1024)(128)(4,1)S(1)}, s32[]{:S(2)}) async-start(s8[4718592]{0:T(1024)(128)(4,1)} %bitcast.294), calls=%async_computation.7 | async-start | bytes 8388608
  227.2 7.3 %copy-start.55 = (bf16[512,768]{1,0:T(8,128)(2,1)}, bf16[512,768]{1,0:T(8,128)(2,1)S(1)}, u32[]{:S(2)}) copy-start(bf16[512,768]{1,0:T(8,128)(2,1)S(1)} %get-tuple-element.96) | copy-start | bytes 2359300
  227.3 7.2 %slice-start.1 = ((s8[4718592]{0:T(1024)(128)(4,1)}), s8[524288]{0:T(1024)(128)(4,1)S(1)}, s32[]{:S(2)}) async-start(s8[4718592]{0:T(1024)(128)(4,1)} %bitcast.294), calls=%async_computation.8 | async-start | bytes 1048576
  234.5 3.5 copy-start.51
  238.1 3.6 copy-start.32
  240.5 1.2 copy-start.24
  243.3 1.7 collective-permute-start
  245.1 0.7 copy-start.36
  245.8 2.7 copy-start.21
  248.5 1.1 copy-start.7
  249.6 1.1 copy-start.8
  304.0 10.7 %copy-start.22 = (bf16[1024,768]{1,0:T(8,128)(2,1)}, bf16[1024,768]{1,0:T(8,128)(2,1)S(1)}, u32[]{:S(2)}) copy-start(bf16[1024,768]{1,0:T(8,128)(2,1)S(1)} %get-tuple-element.44) | copy-start | bytes 4718596
  314.7 1.7 copy-start.19
  316.4 2.1 copy-start.23
  316.4 2.4 copy-start.54
  320.7 1.8 copy-start.31
  322.6 22.0 %collective-permute-start.2 = (bf16[768,576]{0,1:T(8,128)(2,1)S(1)}, bf16[768,576]{0,1:T(8,128)(2,1)S(1)}, u32[]{:S(2)}, u32[]{:S(2)}) collective-permute-start(bf16[768,576]{0,1:T(8,128)(2,1)S(1)} %fusion.36), channel_id=1, source_target_pairs={{0,2},{1,3},{2,0},{3,1},{4,6},{5,7},{6,4},{7,5},{8,10},{9,11},{10,... | collective-permute-start | bytes 2654216 | tf_op jit(solution)/shard_map/ppermute | solution.py:1127
  347.6 91.1 %reduce-scatter.6.cloned.1.call-start = ((), (), s32[]{:S(2)}) async-start(), calls=%async_computation.3 | async-start | bytes 7864320 | tf_op jit(solution)/shard_map/reduce_scatter | solution.py:1109
  356.8 209.2 %all-reduce.4.cloned.1.call-start = ((), (), s32[]{:S(2)}) async-start(), calls=%async_computation.5 | async-start | bytes 589824 | tf_op jit(solution)/shard_map/psum | solution.py:1131
  380.8 187.2 %reduce-scatter.8.cloned.1.call-start = ((), (), s32[]{:S(2)}) async-start(), calls=%async_computation.4 | async-start | bytes 3932160 | tf_op jit(solution)/shard_map/reduce_scatter | solution.py:1110
  441.9 1.1 copy-start.5
  449.9 1.9 copy-start.50
  451.8 5.7 copy-start.29
  451.8 5.7 copy-start.39
  451.8 5.7 copy-start.43
  451.8 5.7 copy-start.48
  451.9 5.7 copy-start.52
  560.2 3.2 copy-start.34
  564.4 1.6 copy-start.26
  564.5 3.4 collective-permute-start.1
  568.0 3.1 copy-start.25
  571.0 1.9 copy-start.46
  571.0 1.9 copy-start.45
  571.1 1.9 copy-start.37
  571.1 1.9 copy-start.44
  571.1 1.9 copy-start.40
  (3 other events, 1.9 us)
Sparse Core Ops, SparseCore 0:
  347.7 31.2 reduce-scatter.9
  381.6 56.9 reduce-scatter.5
  441.5 23.6 all-reduce.3
  467.3 74.0 reduce-scatter.7

commit v4 on v3

--- a/solution.py
+++ b/solution.py
@@ -271,10 +271,11 @@
     dst[...] = (left[...].astype(F32) + right[...].astype(F32)).astype(dst.dtype)
 
 
-RS_SLOTS = 10
-
-
-def rs_steps(grads, outs, bufs, sems, sem_own, base):
+RS_SLOTS = 28
+RS_ORDER = (3, 2, 1, 0)
+
+
+def rs_plan(grads, outs, bufs, sems, l_sems, base, paired):
     own, ra, rb0, rb1, rc0, rc1, sc, rd, re = bufs
     x, z, g, y, c = places()
     sib, over_y, over_x = {"gc": g ^ 1}, {"gc": g ^ 2}, {"dp": x ^ 1}
@@ -285,141 +286,320 @@
     mine1 = pl.ds(pl.multiple_of(2 * q + q * x, 16), q)
     other1 = pl.ds(pl.multiple_of(2 * q + q * (1 - x), 16), q)
     first = pl.ds(0, 2 * q)
-
-    def slot(i):
-        return base * RS_SLOTS + i
-
-    loads = [
-        pltpu.make_async_copy(grads.at[2 * i + c], own.at[i], sem_own.at[2 * base + i])
-        for i in range(2)
-    ]
-    hop_a = [send(grads.at[2 * i + 1 - c], ra.at[i], sems, slot(i), sib) for i in range(2)]
-    hop_b0 = send(own.at[1 - y, :, first], rb0, sems, slot(2), over_y)
-    hop_b1 = send(own.at[:, :, other1], rb1, sems, slot(3), over_x)
-    hop_c0 = send(own.at[y, :, other0], rc0, sems, slot(4), over_x)
-    hop_c1 = send(own.at[1 - y, :, mine1], rc1, sems, slot(5), over_y)
-    hop_z = [
-        send(
-            sc.at[z ^ step],
-            rd.at[step - 1],
-            sems,
-            slot(5 + step),
-            {"gr": z ^ step},
-        )
-        for step in (1, 2, 3)
-    ]
-    hop_d = send(sc.at[z], re, sems, slot(9), over_x)
-
-    def start():
-        for copy in loads + hop_a:
-            copy.start()
-
-    def after_a():
-        for copy in loads + hop_a:
-            copy.wait()
-
-        @pl.loop(0, 8)
-        def _(i):
-            add_into(own.at[i // 4, i % 4], own.at[i // 4, i % 4], ra.at[i // 4, i % 4])
-
-        hop_b0.start()
-        hop_b1.start()
-
-    def after_b():
-        hop_b0.wait()
-        hop_b1.wait()
-
-        @pl.loop(0, 4)
-        def _(i):
-            add_into(own.at[y, i, first], own.at[y, i, first], rb0.at[i])
-            add_into(own.at[0, i, mine1], own.at[0, i, mine1], rb1.at[0, i])
-            add_into(own.at[1, i, mine1], own.at[1, i, mine1], rb1.at[1, i])
-
-        hop_c0.start()
-        hop_c1.start()
-
-    def after_c():
-        hop_c0.wait()
-        hop_c1.wait()
-
-        @pl.loop(0, 4)
-        def _(i):
-            add_into(sc.at[i, pl.ds(0, q)], own.at[y, i, mine0], rc0.at[i])
-            add_into(sc.at[i, pl.ds(q, q)], own.at[y, i, mine1], rc1.at[i])
-
-        for copy in hop_z:
-            copy.start()
-
-    def after_z():
-        for copy in hop_z:
-            copy.wait()
-        total = sc[z].astype(F32)
+    slot = base * RS_SLOTS
+
+    def load(i, s):
+        source = grads.at[2 * i + c, z ^ s] if paired else grads.at[i, z ^ s]
+        return pltpu.make_async_copy(source, own.at[i, s], l_sems.at[8 * base + 2 * s + i])
+
+    def hop_a(i, s):
+        return send(grads.at[2 * i + 1 - c, z ^ s], ra.at[i, s], sems, slot + 6 * s + i, sib)
+
+    def hop_b0(s):
+        return send(own.at[1 - y, s, first], rb0.at[s], sems, slot + 6 * s + 2, over_y)
+
+    def hop_b1(s):
+        return send(own.at[:, s, other1], rb1.at[s], sems, slot + 6 * s + 3, over_x)
+
+    def hop_c0(s):
+        return send(own.at[y, s, other0], rc0.at[s], sems, slot + 6 * s + 4, over_x)
+
+    def hop_c1(s):
+        return send(own.at[1 - y, s, mine1], rc1.at[s], sems, slot + 6 * s + 5, over_y)
+
+    def hop_z(s):
+        return send(sc.at[s], rd.at[s - 1], sems, slot + 23 + s, {"gr": z ^ s})
+
+    def hop_d():
+        return send(sc.at[0], re, sems, slot + 27, over_x)
+
+    def begin(s):
+        for i in range(2):
+            load(i, s).start()
+            if paired:
+                hop_a(i, s).start()
+
+    def after_a(s):
+        for i in range(2):
+            load(i, s).wait()
+            if paired:
+                hop_a(i, s).wait()
+                add_into(own.at[i, s], own.at[i, s], ra.at[i, s])
+        hop_b0(s).start()
+        hop_b1(s).start()
+
+    def after_b(s):
+        hop_b0(s).wait()
+        hop_b1(s).wait()
+        add_into(own.at[y, s, first], own.at[y, s, first], rb0.at[s])
+        for i in range(2):
+            add_into(own.at[i, s, mine1], own.at[i, s, mine1], rb1.at[s, i])
+        hop_c0(s).start()
+        hop_c1(s).start()
+
+    def after_c(s):
+        hop_c0(s).wait()
+        hop_c1(s).wait()
+        add_into(sc.at[s, pl.ds(0, q)], own.at[y, s, mine0], rc0.at[s])
+        add_into(sc.at[s, pl.ds(q, q)], own.at[y, s, mine1], rc1.at[s])
+        if s:
+            hop_z(s).start()
+
+    def total():
+        for s in (1, 2, 3):
+            hop_z(s).wait()
+        whole = sc[0].astype(F32)
         for i in range(3):
-            total = total + rd[i].astype(F32)
-        sc[z] = total.astype(BF)
-        hop_d.start()
+            whole = whole + rd[i].astype(F32)
+        sc[0] = whole.astype(BF)
+        hop_d().start()
 
     def finish():
-        hop_d.wait()
-        outs[mine0] = sc[z, pl.ds(0, q)].astype(F32)
-        outs[mine1] = sc[z, pl.ds(q, q)].astype(F32)
+        hop_d().wait()
+        outs[mine0] = sc[0, pl.ds(0, q)].astype(F32)
+        outs[mine1] = sc[0, pl.ds(q, q)].astype(F32)
         outs[other0] = re[pl.ds(0, q)].astype(F32)
         outs[other1] = re[pl.ds(q, q)].astype(F32)
 
-    return [start, after_a, after_b, after_c, after_z, finish]
-
-
-def rs_scratch(shape):
-    _, n_gr, rows, cols = shape
+    return begin, after_a, after_b, after_c, total, finish
+
+
+def rs_steps(plans):
+    order = [(plan, s) for plan in plans for s in RS_ORDER]
+    n = len(order)
+    steps = [[partial(plan[0], s) for plan, s in order]]
+    for i in range(n + 10):
+        part = []
+        if i < n:
+            part.append(partial(order[i][0][1], order[i][1]))
+        if 2 <= i < n + 2:
+            part.append(partial(order[i - 2][0][2], order[i - 2][1]))
+        if 4 <= i < n + 4:
+            part.append(partial(order[i - 4][0][3], order[i - 4][1]))
+        if 7 <= i < n + 7 and (i - 7) % 4 == 3:
+            part.append(plans[(i - 7) // 4][4])
+        if 9 <= i < n + 9 and (i - 9) % 4 == 3:
+            part.append(plans[(i - 9) // 4][5])
+        if part:
+            steps.append(part)
+    return steps
+
+
+def rs_scratch(rows, cols, paired):
     q = rows // 4
     return [
-        pltpu.VMEM((2, n_gr, rows, cols), BF),
-        pltpu.VMEM((2, n_gr, rows, cols), BF),
-        pltpu.VMEM((n_gr, 2 * q, cols), BF),
-        pltpu.VMEM((2, n_gr, q, cols), BF),
-        pltpu.VMEM((n_gr, q, cols), BF),
-        pltpu.VMEM((n_gr, q, cols), BF),
-        pltpu.VMEM((n_gr, 2 * q, cols), BF),
+        pltpu.VMEM((2, 4, rows, cols), BF),
+        pltpu.VMEM((2, 4, rows, cols) if paired else (16, 128), BF),
+        pltpu.VMEM((4, 2 * q, cols), BF),
+        pltpu.VMEM((4, 2, q, cols), BF),
+        pltpu.VMEM((4, q, cols), BF),
+        pltpu.VMEM((4, q, cols), BF),
+        pltpu.VMEM((4, 2 * q, cols), BF),
         pltpu.VMEM((3, 2 * q, cols), BF),
         pltpu.VMEM((2 * q, cols), BF),
     ]
 
 
-def scatter_kernel(count, *refs):
-    grads, outs = refs[:count], refs[count : 2 * count]
-    bufs = refs[2 * count : 2 * count + 9 * count]
-    send_sem, recv_sem, sem_own = refs[11 * count :]
-    greet(all_partners())
-    steps = [
-        rs_steps(grads[k], outs[k], bufs[9 * k : 9 * k + 9], (send_sem, recv_sem), sem_own, k)
-        for k in range(count)
-    ]
-    for stage in range(len(steps[0])):
-        for k in range(count):
-            steps[k][stage]()
-
-
-def scatter_grads(grads, collective_id):
+def att_scatter_kernel(count, grp_ref, q_ref, lse_ref, kvo_ref, kvp_ref, gm, *refs):
+    grads = refs[:count]
+    dq_ref, dkvo_ref, dkv_ref = refs[count : count + 3]
+    outs = refs[count + 3 : 2 * count + 3]
+    rest = refs[2 * count + 3 :]
+    bufs, (gmx, sem_s, sem_r, l_sems, m_send, m_recv, m_local) = rest[: 9 * count], rest[9 * count :]
+    p, j = pl.program_id(0), pl.program_id(1)
+    step = p * pl.num_programs(1) + j
+    x, z, g, y, c = places()
+    hooks = rs_steps(
+        [
+            rs_plan(grads[k], outs[k], bufs[9 * k : 9 * k + 9], (sem_s, sem_r), l_sems, k, True)
+            for k in range(count)
+        ]
+    )
+
+    def exchange(i):
+        cols = pl.ds(128 * i, 128)
+        return (
+            pltpu.make_async_copy(gm.at[c, :, cols], gmx.at[i, c], m_local.at[i]),
+            send(gm.at[1 - c, :, cols], gmx.at[i, c], (m_send, m_recv), i, {"gc": g ^ 1}),
+        )
+
+    @pl.when(step == 0)
+    def _():
+        greet(all_partners())
+        for i in range(3):
+            for copy in exchange(i):
+                copy.start()
+        for hook in hooks[0]:
+            hook()
+        for copy in exchange(0):
+            copy.wait()
+
+    for i in (1, 2):
+
+        @pl.when(step == 8 * i)
+        def _():
+            for copy in exchange(i):
+                copy.wait()
+
+    last = len(hooks) - 1
+    for when in range(1, 23):
+        parts = [h for i in range(1, last) if i * 22 // (last - 1) == when for h in hooks[i]]
+        if parts:
+
+            @pl.when(step == when)
+            def _():
+                for hook in parts:
+                    hook()
+
+    group = grp_ref[j]
+    low = lax.broadcasted_iota(jnp.int32, (CL, 128), 1) < 64
+    zero = jnp.zeros((CL, 128), BF)
+    q = q_ref[...]
+    gmix = gmx[p, j // 4, pl.ds(pl.multiple_of((j % 4) * CL, CL), CL)]
+    stacks = (
+        jnp.concatenate([jnp.where(low, zero, q), jnp.where(low, gmix, zero)], axis=0),
+        jnp.concatenate([jnp.where(low, q, zero), jnp.where(low, zero, gmix)], axis=0),
+    )
+
+    @pl.when(z >= 2)
+    def _():
+        row = lax.broadcasted_iota(jnp.int32, (CL, CL), 0)
+        near_ok = row <= lax.broadcasted_iota(jnp.int32, (CL, CL), 1)
+        dqs = []
+        for h in range(2):
+            cols = slice(128 * h, 128 * h + 128)
+            kv = kvp_ref[group, :, cols]
+            kvo = kvo_ref[:, cols]
+            lse = lse_ref[0, 0, h : h + 1, :]
+            far = nt(kv, stacks[h])
+            near = nt(kvo, stacks[h])
+            pf = jnp.exp(far[:, :CL] - lse)
+            pn = jnp.where(near_ok, jnp.exp(near[:, :CL] - lse), 0.0)
+            df = far[:, CL:]
+            dn = near[:, CL:]
+            inner = jnp.sum(pf * df, axis=0, keepdims=True) + jnp.sum(
+                pn * dn, axis=0, keepdims=True
+            )
+            sf = (pf * (df - inner)).astype(BF)
+            sn = (pn * (dn - inner)).astype(BF)
+            dkv_ref[0, :, cols] = nn(
+                jnp.concatenate([sf, pf.astype(BF)], axis=1), stacks[h]
+            ).astype(BF)
+            dkvo_ref[:, cols] = nn(
+                jnp.concatenate([sn, pn.astype(BF)], axis=1), stacks[h]
+            ).astype(BF)
+            dqs.append(tn(sf, kv) + tn(sn, kvo))
+        dq_ref[...] = (jnp.where(low, dqs[1], dqs[0]) * 0.125).astype(BF)
+
+    @pl.when(z < 2)
+    def _():
+        limit = z * QROWS + (j % (QROWS // CL)) * CL
+        key = lax.broadcasted_iota(jnp.int32, (P_SIZE, CL), 0)
+        row = lax.broadcasted_iota(jnp.int32, (P_SIZE, CL), 1)
+        allowed = key - row <= limit
+        dqs = []
+        for h in range(2):
+            cols = slice(128 * h, 128 * h + 128)
+            kv = kvp_ref[group, :, cols]
+            lse = lse_ref[0, 0, h : h + 1, :]
+            far = nt(kv, stacks[h])
+            pf = jnp.where(allowed, jnp.exp(far[:, :CL] - lse), 0.0)
+            df = far[:, CL:]
+            inner = jnp.sum(pf * df, axis=0, keepdims=True)
+            sf = (pf * (df - inner)).astype(BF)
+            dkv_ref[0, :, cols] = nn(
+                jnp.concatenate([sf, pf.astype(BF)], axis=1), stacks[h]
+            ).astype(BF)
+            dqs.append(tn(sf, kv))
+        dkvo_ref[...] = jnp.zeros_like(dkvo_ref)
+        dq_ref[...] = (jnp.where(low, dqs[1], dqs[0]) * 0.125).astype(BF)
+
+    @pl.when(step == 23)
+    def _():
+        for hook in hooks[last]:
+            hook()
+
+
+def attend_back_scatter(grp, q, lse, kvo, kvp, gm, grads, collective_id):
+    rows = q.shape[0]
     count = len(grads)
+    any_space = pl.BlockSpec(memory_space=pl.ANY)
     scratch = []
     for grad in grads:
-        scratch += rs_scratch(grad.shape)
+        scratch += rs_scratch(grad.shape[2], grad.shape[3], True)
+    slots = RS_SLOTS * count
     return pl.pallas_call(
-        partial(scatter_kernel, count),
-        name="scatter_grads",
-        in_specs=[pl.BlockSpec(memory_space=pl.ANY)] * count,
-        out_specs=[pl.BlockSpec(memory_space=pltpu.VMEM)] * count,
-        out_shape=[jax.ShapeDtypeStruct(grad.shape[2:], F32) for grad in grads],
-        scratch_shapes=scratch
-        + [
-            pltpu.SemaphoreType.DMA((RS_SLOTS * count,)),
-            pltpu.SemaphoreType.DMA((RS_SLOTS * count,)),
-            pltpu.SemaphoreType.DMA((2 * count,)),
-        ],
+        partial(att_scatter_kernel, count),
+        name="attend_back_scatter",
+        grid_spec=pltpu.PrefetchScalarGridSpec(
+            num_scalar_prefetch=1,
+            grid=(3, rows // CL),
+            in_specs=[
+                pl.BlockSpec((CL, 128), lambda p, j, *_: (j, p)),
+                pl.BlockSpec((1, 1, 2, 128), lambda p, j, *_: (p, j, 0, 0)),
+                pl.BlockSpec((CL, 256), lambda p, j, *_: (j, p)),
+                pl.BlockSpec((4, P_SIZE, 256), lambda p, j, *_: (0, 0, p)),
+            ]
+            + [any_space] * (count + 1),
+            out_specs=[
+                pl.BlockSpec((CL, 128), lambda p, j, *_: (j, p)),
+                pl.BlockSpec((CL, 256), lambda p, j, *_: (j, p)),
+                pl.BlockSpec((1, P_SIZE, 256), lambda p, j, *_: (j, 0, p)),
+            ]
+            + [pl.BlockSpec(grad.shape[2:], lambda p, j, *_: (0, 0)) for grad in grads],
+            scratch_shapes=scratch
+            + [
+                pltpu.VMEM((3, 2, QROWS, 128), BF),
+                pltpu.SemaphoreType.DMA((slots,)),
+                pltpu.SemaphoreType.DMA((slots,)),
+                pltpu.SemaphoreType.DMA((8 * count,)),
+                pltpu.SemaphoreType.DMA((3,)),
+                pltpu.SemaphoreType.DMA((3,)),
+                pltpu.SemaphoreType.DMA((3,)),
+            ],
+        ),
+        out_shape=[
+            jax.ShapeDtypeStruct((rows, 384), BF),
+            jax.ShapeDtypeStruct((rows, 768), BF),
+            jax.ShapeDtypeStruct((8, P_SIZE, 768), BF),
+        ]
+        + [jax.ShapeDtypeStruct(grad.shape[2:], F32) for grad in grads],
         compiler_params=pltpu.CompilerParams(
-            collective_id=collective_id, has_side_effects=True, vmem_limit_bytes=50 << 20
+            collective_id=collective_id, has_side_effects=True, vmem_limit_bytes=56 << 20
         ),
-    )(*grads)
+    )(grp, q, lse, kvo, kvp.reshape(4, P_SIZE, kvp.shape[1]), gm, *grads)
+
+
+def fold_kernel(grp_ref, dkv_ref, w_ref, dkvp_ref, part_ref, acc):
+    acc[...] = jnp.zeros_like(acc)
+    for j in range(8):
+        acc[grp_ref[j]] += dkv_ref[j].astype(F32)
+    for k in range(4):
+        low = acc[k].astype(BF)
+        dkvp_ref[k] = low
+        part_ref[k] = nt(low, w_ref[...]).astype(BF)
+
+
+def fold_prompts(grp, dkv, w_kv):
+    tile = 128
+    block = pl.BlockSpec((4, tile, D), lambda i, *_: (0, i, 0))
+    shape = jax.ShapeDtypeStruct((4, P_SIZE, D), BF)
+    return pl.pallas_call(
+        fold_kernel,
+        name="fold_prompts",
+        grid_spec=pltpu.PrefetchScalarGridSpec(
+            num_scalar_prefetch=1,
+            grid=(P_SIZE // tile,),
+            in_specs=[
+                pl.BlockSpec((8, tile, D), lambda i, *_: (0, i, 0)),
+                pl.BlockSpec((D, D), lambda i, *_: (0, 0)),
+            ],
+            out_specs=[block, block],
+            scratch_shapes=[pltpu.VMEM((4, tile, D), F32)],
+        ),
+        out_shape=[shape, shape],
+        compiler_params=pltpu.CompilerParams(vmem_limit_bytes=40 << 20),
+    )(grp, dkv, w_kv)
 
 
 def norm_rows(hidden, gain, shift):
@@ -901,6 +1081,242 @@
             collective_id=collective_id, has_side_effects=True, vmem_limit_bytes=40 << 20
         ),
     )(grp, q, kvo, kvp.reshape(4, P_SIZE, kvp.shape[1]), *blocks)
+
+
+def tail_kernel(
+    part,
+    chip,
+    dw,
+    grad_h2,
+    tokens,
+    vec,
+    sums,
+    out,
+    sums_out,
+    dw_out,
+    own,
+    ra,
+    rb,
+    rz,
+    keep,
+    take,
+    gsum,
+    cur,
+    sb,
+    *rest,
+):
+    bufs, (sem_s, sem_r, l_sems, w_s, w_r, w_l) = rest[:9], rest[9:]
+    sems = (sem_s, sem_r)
+    x, z, g, y, c = places()
+    sib, over_y, over_x = {"gc": g ^ 1}, {"gc": g ^ 2}, {"dp": x ^ 1}
+    down = {"gr": jnp.maximum(z - 1, 0)}
+    far = z >= 2
+    greet(all_partners())
+    hooks = rs_steps([rs_plan(dw, dw_out, bufs, (w_s, w_r), w_l, 0, False)])
+    size = QROWS // CHUNKS
+    chunks = [(h, k) for h in range(2) for k in range(CHUNKS)]
+
+    def rows(k):
+        return pl.ds(k * size, size)
+
+    def index(side):
+        return 1 - y if side == 0 else y
+
+    def load(side, h, k):
+        i = index(side)
+        return pltpu.make_async_copy(
+            part.at[2 * i + c, h, rows(k)],
+            own.at[i, h, rows(k)],
+            l_sems.at[8 * side + CHUNKS * h + k],
+        )
+
+    def hop_a(side, h, k):
+        i = index(side)
+        return send(
+            part.at[2 * i + 1 - c, h, rows(k)],
+            ra.at[i, h, rows(k)],
+            sems,
+            8 * side + CHUNKS * h + k,
+            sib,
+        )
+
+    def hop_y(h, k):
+        return send(
+            own.at[1 - y, h, rows(k)], rb.at[h, rows(k)], sems, 16 + CHUNKS * h + k, over_y
+        )
+
+    def hop_z(h, k):
+        return send(own.at[y, h, rows(k)], rz.at[h, rows(k)], sems, 24 + CHUNKS * h + k, down)
+
+    hop_chip = send(chip.at[1 - c], take, sems, 32, sib)
+    load_chip = pltpu.make_async_copy(chip.at[c], keep, l_sems.at[16])
+
+    def fold(h, k, other):
+        add_into(own.at[y, h, rows(k)], own.at[y, h, rows(k)], other.at[rows(k)])
+
+    for h, k in chunks:
+
+        @pl.when(far)
+        def _():
+            load(0, h, k).start()
+            hop_a(0, h, k).start()
+
+        load(1, h, k).start()
+        hop_a(1, h, k).start()
+    hop_chip.start()
+    load_chip.start()
+    for hook in hooks[0]:
+        hook()
+
+    def stage1(h, k):
+        @pl.when(far)
+        def _():
+            load(0, h, k).wait()
+            hop_a(0, h, k).wait()
+            add_into(
+                own.at[1 - y, h, rows(k)], own.at[1 - y, h, rows(k)], ra.at[1 - y, h, rows(k)]
+            )
+            hop_y(h, k).start()
+
+        load(1, h, k).wait()
+        hop_a(1, h, k).wait()
+        fold(h, k, ra.at[y, h])
+
+    def stage2(h, k):
+        @pl.when(far)
+        def _():
+            hop_y(h, k).wait()
+            fold(h, k, rb.at[h])
+
+        @pl.when(z == 3)
+        def _():
+            hop_z(h, k).start()
+
+    def stage3(h, k):
+        @pl.when(z == 2)
+        def _():
+            hop_z(h, k).wait_recv()
+            fold(h, k, rz.at[h])
+            hop_z(h, k).start()
+
+    def stage4(h, k):
+        @pl.when(z == 1)
+        def _():
+            hop_z(h, k).wait_recv()
+            fold(h, k, rz.at[h])
+            if h == 0:
+                hop_z(h, k).start()
+
+    def stage5(h, k):
+        if h == 0:
+
+            @pl.when(z == 0)
+            def _():
+                hop_z(h, k).wait_recv()
+                fold(h, k, rz.at[h])
+
+    n = len(chunks)
+    stages = (stage1, stage2, stage3, stage4, stage5)
+    for i in range(max(n + 4, len(hooks) - 1)):
+        for lag, stage in enumerate(stages):
+            if 0 <= i - lag < n:
+                stage(*chunks[i - lag])
+        if i + 1 < len(hooks):
+            for hook in hooks[i + 1]:
+                hook()
+    for h, k in chunks:
+
+        @pl.when(z >= 2 if h else z >= 1)
+        def _():
+            hop_z(h, k).wait_send()
+
+    load_chip.wait()
+    hop_chip.wait()
+
+    @pl.loop(0, CHUNKS)
+    def _(k):
+        r = pl.ds(pl.multiple_of(k * size, size), size)
+        gsum[r] = keep[r].astype(F32) + take[r].astype(F32)
+
+    @pl.when(z < 2)
+    def _():
+        place = jnp.minimum(z, 1)
+
+        @pl.loop(0, CHUNKS)
+        def _(k):
+            r = pl.ds(pl.multiple_of(k * size, size), size)
+            gsum[r] += own[y, place, r].astype(F32)
+
+    cur[...] = sums[...]
+
+    @pl.loop(0, CHUNKS)
+    def _(k):
+        r = pl.ds(pl.multiple_of(k * size, size), size)
+        hidden = tokens[r].astype(F32) + vec[0:1]
+        center = jnp.mean(hidden, axis=1, keepdims=True)
+        offset = hidden - center
+        factor = lax.rsqrt(jnp.mean(offset * offset, axis=1, keepdims=True) + eps)
+        unit = offset * factor
+        grad = gsum[r]
+        scaled = grad * vec[1:2]
+        first = jnp.mean(scaled, axis=1, keepdims=True)
+        second = jnp.mean(scaled * unit, axis=1, keepdims=True)
+        total = grad_h2[r] + factor * (scaled - first - unit * second)
+        out[r] = total
+        cur[0:1] += jnp.sum(total, axis=0, keepdims=True)
+        cur[1:2] += jnp.sum(grad * unit, axis=0, keepdims=True)
+        cur[2:3] += jnp.sum(grad, axis=0, keepdims=True)
+
+    for i, target in enumerate((sib, over_y, over_x)):
+        hop = send(cur, sb.at[i], sems, 33 + i, target)
+        hop.start()
+        hop.wait()
+        cur[...] += sb[i]
+    hops = [send(cur, sb.at[2 + s], sems, 35 + s, {"gr": z ^ s}) for s in (1, 2, 3)]
+    for hop in hops:
+        hop.start()
+    for hop in hops:
+        hop.wait()
+    sums_out[...] = (cur[...] + sb[3]) + (sb[4] + sb[5])
+
+
+def tail_exchange(part, chip, dw, grad_h2, tokens, vec, sums, collective_id):
+    any_space = pl.BlockSpec(memory_space=pl.ANY)
+    vmem = pl.BlockSpec(memory_space=pltpu.VMEM)
+    return pl.pallas_call(
+        tail_kernel,
+        name="tail_exchange",
+        in_specs=[any_space, any_space, any_space, vmem, vmem, vmem, vmem],
+        out_specs=[vmem, vmem, vmem],
+        out_shape=[
+            jax.ShapeDtypeStruct((QROWS, D), F32),
+            jax.ShapeDtypeStruct(sums.shape, F32),
+            jax.ShapeDtypeStruct(dw.shape[2:], F32),
+        ],
+        scratch_shapes=[
+            pltpu.VMEM((2, 2, QROWS, D), BF),
+            pltpu.VMEM((2, 2, QROWS, D), BF),
+            pltpu.VMEM((2, QROWS, D), BF),
+            pltpu.VMEM((2, QROWS, D), BF),
+            pltpu.VMEM((QROWS, D), BF),
+            pltpu.VMEM((QROWS, D), BF),
+            pltpu.VMEM((QROWS, D), F32),
+            pltpu.VMEM(sums.shape, F32),
+            pltpu.VMEM((6,) + sums.shape, F32),
+        ]
+        + rs_scratch(dw.shape[2], dw.shape[3], False)
+        + [
+            pltpu.SemaphoreType.DMA((39,)),
+            pltpu.SemaphoreType.DMA((39,)),
+            pltpu.SemaphoreType.DMA((17,)),
+            pltpu.SemaphoreType.DMA((RS_SLOTS,)),
+            pltpu.SemaphoreType.DMA((RS_SLOTS,)),
+            pltpu.SemaphoreType.DMA((8,)),
+        ],
+        compiler_params=pltpu.CompilerParams(
+            collective_id=collective_id, has_side_effects=True, vmem_limit_bytes=48 << 20
+        ),
+    )(part, chip, dw, grad_h2, tokens, vec, sums)
 
 
 def norm(hidden, gain, shift):
@@ -1075,21 +1491,6 @@
     grad_w_out = jnp.einsum("ctk,tn->ckn", mixed, ga, preferred_element_type=F32)
     gm = jnp.einsum("tn,ckn->ctk", ga, w_out, preferred_element_type=F32).astype(BF)
 
-    gm_keep = lax.dynamic_index_in_dim(gm, c, 0, keepdims=False)
-    gm_give = lax.dynamic_index_in_dim(gm, 1 - c, 0, keepdims=False)
-    gm_take = lax.ppermute(gm_give, "gc", swap_core)
-    gm_chip = jnp.where(c == 0, jnp.stack([gm_keep, gm_take]), jnp.stack([gm_take, gm_keep]))
-    gm_chip = gm_chip.reshape(2 * QROWS, 384)
-
-    def scatter16(blocks):
-        part = lax.psum_scatter(
-            blocks.astype(BF).reshape(n_gc * n_gr * blocks.shape[2], -1),
-            ("gc", "gr"),
-            scatter_dimension=0,
-            tiled=True,
-        )
-        return lax.psum(part, "dp").astype(F32)
-
     weight_grads = [
         grad_w_down.astype(BF).reshape(n_gc, n_gr, 192, 768),
         grad_w_up.astype(BF).reshape(n_gc, n_gr, 192, 768),
@@ -1099,53 +1500,82 @@
         .reshape(n_gc, n_gr, 192, 192),
     ]
     if n_dp == 2:
-        out_w_down, out_w_up, out_w_out = scatter_grads(weight_grads, 3)
+        dq, dkvo, dkv, out_w_down, out_w_up, out_w_out = attend_back_scatter(
+            grp, q, lse_rows, kvo, kvp, gm, weight_grads, 3
+        )
+        dkvp, part_prompt = fold_prompts(grp, dkv, w_kv)
+        dkvp = dkvp.reshape(4 * P_SIZE, D)
+        part_prompt = part_prompt.reshape(4 * P_SIZE, D)
     else:
+        gm_keep = lax.dynamic_index_in_dim(gm, c, 0, keepdims=False)
+        gm_give = lax.dynamic_index_in_dim(gm, 1 - c, 0, keepdims=False)
+        gm_take = lax.ppermute(gm_give, "gc", swap_core)
+        gm_chip = jnp.where(c == 0, jnp.stack([gm_keep, gm_take]), jnp.stack([gm_take, gm_keep]))
+        gm_chip = gm_chip.reshape(2 * QROWS, 384)
+
+        def scatter16(blocks):
+            part = lax.psum_scatter(
+                blocks.reshape(n_gc * n_gr * blocks.shape[2], -1),
+                ("gc", "gr"),
+                scatter_dimension=0,
+                tiled=True,
+            )
+            return lax.psum(part, "dp").astype(F32)
+
         out_w_down, out_w_up, out_w_out = [scatter16(grad) for grad in weight_grads]
-
-    dq, dkvo, dkvp = attend_back(grp, z_arr, q, gm_chip, lse_rows, kvo, kvp)
-
-    part_prompt = nt(dkvp, w_kv).astype(BF)
-    back_prompt = lax.psum_scatter(part_prompt, "gc", scatter_dimension=0, tiled=True)
-    back_prompt = lax.psum_scatter(
-        jnp.concatenate([back_prompt, jnp.zeros_like(back_prompt)]),
-        "gr",
-        scatter_dimension=0,
-        tiled=True,
-    ).astype(F32)
+        dq, dkvo, dkvp = attend_back(grp, z_arr, q, gm_chip, lse_rows, kvo, kvp)
+        part_prompt = nt(dkvp, w_kv).astype(BF)
+
     part_chip = (nt(dq, w_q) + nt(dkvo, w_kv)).reshape(2, QROWS, D)
-    part_keep = lax.dynamic_index_in_dim(part_chip, c, 0, keepdims=False)
-    part_give = lax.dynamic_index_in_dim(part_chip, 1 - c, 0, keepdims=False)
-    part_take = lax.ppermute(part_give.astype(BF), "gc", swap_core).astype(F32)
-    grad_n1 = part_keep + part_take + back_prompt
-
     grad_kv = tn(n1_prompt, dkvp) + tn(n1_chip, dkvo)
     grad_q = tn(n1_chip, dq)
     grad_qkv = head_layout_back(grad_q, grad_kv)
-    qkv_keep = lax.dynamic_index_in_dim(grad_qkv, y, 0, keepdims=False)
-    qkv_give = lax.dynamic_index_in_dim(grad_qkv, 1 - y, 0, keepdims=False)
-    qkv_take = lax.ppermute(qkv_give.astype(BF), "gc", swap_y).astype(F32)
-    out_w_qkv = lax.psum_scatter(
-        (qkv_keep + qkv_take).astype(BF), "gr", scatter_dimension=0, tiled=True
-    )
-    out_w_qkv = lax.psum(out_w_qkv, "dp").astype(F32)
-
-    back1, grad_gain1, grad_shift1 = norm_back(grad_n1, gain1, unit1, factor1)
-    input_grad = grad_h2 + back1
-    sums = jnp.concatenate(
+    later_sums = jnp.concatenate(
         [
-            jnp.sum(input_grad, axis=0),
-            grad_gain1,
-            grad_shift1,
-            grad_gain2,
-            grad_shift2,
-            grad_b_out,
-            grad_b_down,
-            grad_b_up,
-            jnp.broadcast_to(squared, (128,)),
+            grad_gain2[None],
+            grad_shift2[None],
+            grad_b_out[None],
+            grad_b_down[None],
+            grad_b_up.reshape(4, D),
+            jnp.broadcast_to(squared, (1, D)),
+            jnp.zeros((4, D), F32),
         ]
     )
-    sums = lax.psum(sums, ("dp", "gr", "gc"))
+    if n_dp == 2:
+        input_grad, sums, out_w_qkv = tail_exchange(
+            part_prompt.reshape(4, 2, QROWS, D),
+            part_chip.astype(BF),
+            grad_qkv.astype(BF).reshape(2, 4, 192, 576),
+            grad_h2,
+            tokens,
+            vectors,
+            jnp.concatenate([jnp.zeros((3, D), F32), later_sums]),
+            4,
+        )
+    else:
+        back_prompt = lax.psum_scatter(part_prompt, "gc", scatter_dimension=0, tiled=True)
+        back_prompt = lax.psum_scatter(
+            jnp.concatenate([back_prompt, jnp.zeros_like(back_prompt)]),
+            "gr",
+            scatter_dimension=0,
+            tiled=True,
+        ).astype(F32)
+        part_keep = lax.dynamic_index_in_dim(part_chip, c, 0, keepdims=False)
+        part_give = lax.dynamic_index_in_dim(part_chip, 1 - c, 0, keepdims=False)
+        part_take = lax.ppermute(part_give.astype(BF), "gc", swap_core).astype(F32)
+        grad_n1 = part_keep + part_take + back_prompt
+        qkv_keep = lax.dynamic_index_in_dim(grad_qkv, y, 0, keepdims=False)
+        qkv_give = lax.dynamic_index_in_dim(grad_qkv, 1 - y, 0, keepdims=False)
+        qkv_take = lax.ppermute(qkv_give.astype(BF), "gc", swap_y).astype(F32)
+        out_w_qkv = lax.psum_scatter(
+            (qkv_keep + qkv_take).astype(BF), "gr", scatter_dimension=0, tiled=True
+        )
+        out_w_qkv = lax.psum(out_w_qkv, "dp").astype(F32)
+        back1, grad_gain1, grad_shift1 = norm_back(grad_n1, gain1, unit1, factor1)
+        input_grad = grad_h2 + back1
+        first_sums = jnp.stack([jnp.sum(input_grad, axis=0), grad_gain1, grad_shift1])
+        sums = lax.psum(jnp.concatenate([first_sums, later_sums]), ("dp", "gr", "gc"))
+    sums = sums[:12].reshape(12 * D)
     loss = (sums[-1] / (D * token_count[0].astype(F32))).reshape(1)
     rows = sums[: 7 * D].reshape(7, n_gr, D // n_gr)
     rows = lax.dynamic_index_in_dim(rows, z, 1, keepdims=False)

time: 638 us -> 504 us (0.79)
  waiting for transfers between devices: 102 us -> 0 us
  blocking collectives: 40.5 us -> 0 us
  Pallas kernels: 288 us -> 319 us
  between operations: 17.5 us -> 3.98 us
  local copies, waits for them, and re-layouts: 87.2 us -> 98 us
  other arithmetic: 11.9 us -> 2.81 us
    reduce_scatter x2 -> x0, waiting for transfers between devices: 57.8 us -> none  [the longest x1 57.8 us: on_device(): lax.psum_scatter(part_prompt, 'gc', scatter_dimension=0, tiled=True)]
    psum x1 -> x0, blocking collectives: 40.5 us -> none  [on_device(): sums = lax.psum(sums, ('dp', 'gr', 'gc'))]
    pallas_call x2 -> x3, Pallas kernels: 150 us -> 181 us  [the longest x1 84.6 us: tail_exchange(): pl.pallas_call(tail_kernel, name='tail_exchange', in_specs=[any_space, an...]
    ppermute x3 -> x0, waiting for transfers between devices: 22.6 us -> none  [the longest x1 21.2 us: on_device(): qkv_take = lax.ppermute(qkv_give.astype(BF), 'gc', swap_y).astype(F32)]
    unnamed x5 -> x0, waiting for transfers between devices: 22.2 us -> none
    dot_general x3 -> x2, matrix products: 13.4 us -> 2.39 us  [nt(): lax.dot_general(a, b, (((1,), (1,)), ((), ())), preferred_element_type=F32)]
    reshape x1, local copies, waits for them, and re-layouts: 6.92 us -> 17.8 us  [on_device(): w_up = w_up.reshape(n_gc, D, FF // n_gc)]
    unnamed x162 -> x155, local copies, waits for them, and re-layouts: 41.5 us -> 36.2 us
  transfers between devices with their start and end apart: 7 -> 0, of which waited for: 4 -> 0; matrix products, arithmetic and copies ran while one was open for 6% -> 0% of each run, Pallas kernels for 16% -> 0%
where the time goes in v4:
time: 504 us; the launch traced here: 498 us
  Pallas kernels  319 us (63%)
  local copies, waits for them, and re-layouts  98 us (19%)
  matrix products  74.4 us (15%)
    pallas_call x1, Pallas kernels, tail_exchange(): pl.pallas_call(tail_kernel, name='tail_exchange', in_specs=[any_space, an...  84.6 us
    pallas_call x1, Pallas kernels, attend_gather(): pl.pallas_call(partial(att_gather_kernel, count), name='attend_gather', g...  79.9 us
    pallas_call x1, Pallas kernels, attend_back_scatter(): pl.pallas_call(partial(att_scatter_kernel, count), name='attend_back_scat...  78.1 us
    pallas_call x1, Pallas kernels, start_exchange(): pl.pallas_call(body, name='start_exchange', in_specs=[vmem, vmem, vmem, v...  57.7 us
    unnamed x155, local copies, waits for them, and re-layouts  36.2 us
    pallas_call x1, Pallas kernels, fold_prompts(): pl.pallas_call(fold_kernel, name='fold_prompts', grid_spec=pltpu.Prefetch...  18.4 us
    reshape x1, local copies, waits for them, and re-layouts, on_device(): w_up = w_up.reshape(n_gc, D, FF // n_gc)  17.8 us
    dot_general x3, matrix products, nn(): lax.dot_general(a, b, (((1,), (0,)), ((), ())), preferred_element_type=F32)  14.1 us

profile of v4, /device:TPU:0, one launch (start us, length us, event | category | flops | bytes accessed | tf_op | source)
XLA Modules:
  0.0 497.9 jit_solution(17034560375979281199)
XLA Ops:
  5.6 0.7 broadcast_in_dim.38.refs_2_
  7.0 1.1 copy-done.4
  8.1 0.9 copy-done.14
  9.0 57.7 %start_exchange.1 = (bf16[4,2,512,768]{3,2,1,0:T(8,128)(2,1)S(1)}, bf16[2,512,768]{2,1,0:T(8,128)(2,1)S(1)}, bf16[2,4,192,576]{3,2,1,0:T(8,128)(2,1)S(1)}, f32[8...) custom-call(bf16[512,768]{1,0:T(8,128)(2,1)S(1)} %copy-done.4, ...), custom_call_target="tpu_custom_call" | custom-call | tf_op jit(solution)/shard_map/start_exchange/pallas_call | solution.py:813
  67.4 2.6 copy-done.22
  70.0 1.1 copy-done.24
  72.8 2.3 copy.43
  75.1 0.9 fusion.60
  76.0 0.9 fusion.59
  76.9 0.9 fusion.58
  77.8 0.9 fusion.57
  78.7 0.9 fusion.56
  79.6 0.9 fusion.55
  80.5 1.0 multiply_convert_fusion.1.q_ref
  81.5 0.7 copy-done.27
  83.5 0.8 copy.84
  84.4 0.8 copy.85
  85.2 0.8 copy.86
  86.0 0.8 copy.87
  86.8 0.8 copy.88
  87.6 2.4 concatenate.14.w_ref
  90.0 2.8 convolution_convert_fusion.1.kvo_ref
  92.9 10.3 %convolution_convert_fusion = bf16[4096,768]{1,0:T(8,128)(2,1)} fusion(bf16[4096,768]{1,0:T(8,128)(2,1)} %bitcast.248, bf16[768,768]{1,0:T(8,128)(2,1)S(1)} %concatenate.14.w_ref), kind=kOutput, calls=%fused_computation.2 | convolution fusion | flops 4834983936 | bytes 13762560 | tf_op jit(solution)/shard_map/dot_general | solution.py:27
  103.2 79.9 %attend_gather.1 = (bf16[2,512,384]{2,1,0:T(8,128)(2,1)S(1)}, f32[3,8,2,128]{3,2,1,0:T(2,128)S(1)}, bf16[4,4,192,192]{3,2,1,0:T(8,128)(2,1)S(1)}, bf16[4,4,192,7...) custom-call(s32[8]{0:T(128)S(1)} %broadcast_select_fusion.grp_ref, bf16[1024,384]{1,0:T(8,128)(2,1)S(1)} %multiply_convert_fusion.1.q_ref, ...), custom_call_target="tpu_custom_call" | custom-call | tf_op jit(solution)/shard_map/attend_gather/pallas_call | solution.py:1051
  183.2 2.2 copy-done.2
  186.0 2.4 copy.56
  188.4 4.1 reshape.166
  192.5 2.1 fusion.68
  194.7 1.2 copy-done.28
  196.1 1.5 slice.214
  197.6 17.8 %copy.57 = bf16[4,768,768]{1,2,0:T(8,128)(2,1)} copy(bf16[4,768,768]{2,1,0:T(8,128)(2,1)} %bitcast.241) | data formatting | bytes 9437184 | tf_op jit(solution)/shard_map/reshape | solution.py:1449
  215.5 8.0 %multiply_convert_fusion = (bf16[512,3072]{1,0:T(8,128)(2,1)S(1)}, f32[512,3072]{1,0:T(8,128)}) fusion(f32[3072]{0:T(1024)} %bitcast.299, bf16[3072,768]{1,0:T(8,128)(2,1)} %bitcast.269, f32[512,768]{1,0:T(8,128)S(1)} %copy-done.29, f32[768]{0:T(1024)S(1)} %get-tuple-element.64, f32[768]{0:T(1024)S(1)} %get-tuple-element.65, f32[512]{0:T(512)S(1)} %add_rsqrt_fusion, ...), kind=kOutput, calls=%fused_computation.11 | convolution fusion | flops 2433613824 | bytes 15751168 | tf_op jit(solution)/shard_map/dot_general | solution.py:1459
  223.5 8.2 %convert_reduce_fusion.1 = (f32[768]{0:T(1024)}, bf16[512,768]{1,0:T(8,128)(2,1)}, f32[512,768]{1,0:T(8,128)}) fusion(bf16[512,768]{1,0:T(8,128)(2,1)S(1)} %copy-done.37, f32[768]{0:T(1024)S(1)} %copy-done.45, f32[512,768]{1,0:T(8,128)S(1)} %copy-done.29, bf16[4,768,768]{2,1,0:T(8,128)(2,1)} %bitcast.266, bf16[64,4,8,768]{3,2,1,0:T(8,128)(2,1)S(1)} %bitcast.308), kind=kOutput, calls=%fused_computation.38 | convolution fusion | flops 2418670848 | bytes 12589056 | tf_op jit(solution)/shard_map/dot_general | solution.py:1466
  231.7 6.7 %copy.59 = bf16[4,768,768]{1,2,0:T(8,128)(2,1)} copy(bf16[4,768,768]{2,1,0:T(8,128)(2,1)} %bitcast.267) | data formatting | bytes 9437184 | tf_op jit(solution)/shard_map/reshape | solution.py:1450
  238.4 9.8 %convert_reduce_fusion = (f32[3072]{0:T(1024)}, bf16[512,3072]{1,0:T(8,128)(2,1)S(1)}) fusion(f32[512,3072]{1,0:T(8,128)} %get-tuple-element.98, f32[3072]{0:T(1024)S(1)} %bitcast.300, bf16[512,768]{1,0:T(8,128)(2,1)S(1)} %copy-done.54, bf16[3072,768]{1,0:T(8,128)(2,1)} %bitcast.268), kind=kOutput, calls=%fused_computation.10 | convolution fusion | flops 2452091904 | bytes 14966784 | tf_op jit(solution)/shard_map/dot_general | solution.py:1475
  248.3 3.5 fusion.25
  251.8 2.5 convert_reduce_fusion.2
  254.3 1.7 fusion.31.gm
  256.5 4.4 fusion.15
  260.9 4.8 fusion.18
  265.8 1.9 convolution_convert_fusion.2
  267.6 4.4 reshape.173
  272.0 2.9 copy.67
  274.9 78.1 %attend_back_scatter.1 = (bf16[1024,384]{1,0:T(8,128)(2,1)}, bf16[1024,768]{1,0:T(8,128)(2,1)}, bf16[8,1024,768]{2,1,0:T(8,128)(2,1)}, f32[192,768]{1,0:T(8,128)...) custom-call(s32[8]{0:T(128)} %copy-done.19, bf16[1024,384]{1,0:T(8,128)(2,1)} %copy-done.3, f32[3,8,2,128]{3,2,1,0:T(2,128)} %copy-done.18, ...), custom_call_target="tpu_custom_call" | custom-call | tf_op jit(solution)/shard_map/attend_back_scatter/pallas_call | solution.py:531
  353.0 18.4 %fold_prompts.1 = (bf16[4,1024,768]{2,1,0:T(8,128)(2,1)S(1)}, bf16[4,1024,768]{2,1,0:T(8,128)(2,1)S(1)}) custom-call(s32[8]{0:T(128)S(1)} %copy-done.20, bf16[8,1024,768]{2,1,0:T(8,128)(2,1)} %get-tuple-element.48.dkv_ref, bf16[768,768]{1,0:T(8,128)(2,1)S(1)} %concatenate.14.w_ref), custom_call_target="tpu_custom_call" | custom-call | tf_op jit(solution)/shard_map/fold_prompts/pallas_call | solution.py:587
  371.4 2.6 copy-done.23
  374.0 1.4 fusion.69
  375.5 1.2 copy-done.1
  376.7 1.0 add_convert_fusion
  377.7 2.3 copy.68
  380.0 2.4 convolution_convert_fusion.4
  382.4 9.4 %fusion.70 = f32[768,768]{0,1:T(8,128)S(1)} fusion(bf16[4096,768]{1,0:T(8,128)(2,1)} %bitcast.249, bf16[4096,768]{1,0:T(8,128)(2,1)} %bitcast.250), kind=kOutput, calls=%fused_computation.133 | convolution fusion | flops 4831838208 | bytes 14942208 | tf_op jit(solution)/shard_map/dot_general | solution.py:31
  391.8 1.5 add_convert_fusion.1
  393.7 1.2 copy-done.32
  394.9 4.0 copy.69
  399.9 1.1 copy-done.6
  401.0 84.6 %tail_exchange.1 = (f32[512,768]{1,0:T(8,128)S(1)}, f32[16,768]{1,0:T(8,128)S(1)}, f32[192,576]{1,0:T(8,128)S(1)}) custom-call(bf16[4,2,512,768]{3,2,1,0:T(8,128)(2,1)} %bitcast.239, bf16[2,512,768]{2,1,0:T(8,128)(2,1)S(1)} %bitcast.240, bf16[2,4,192,576]{3,2,1,0:T(8,128)(2,1)} %bitcast.257, f32[512,768]{1,0:T(8,128)S(1)} %get-tuple-element.73.grad_h2, ...), custom_call_target="tpu_custom_call" | custom-call | tf_op jit(solution)/shard_map/tail_exchange/pallas_call | solution.py:1286
  485.6 1.2 copy-done.7
  486.8 0.8 copy-done.10
  490.8 2.7 copy.142
  493.5 0.8 copy.143
  494.3 0.7 copy.144
  495.0 0.8 copy.145
  495.8 0.8 copy.146
  (172 shorter events, 13.6 us)
Async XLA Ops:
  7.0 1.1 copy-start.4
  8.1 0.9 copy-start.14
  66.8 0.6 copy-start.21
  67.4 2.6 copy-start.22
  70.0 1.1 copy-start.24
  71.8 0.6 copy-start.16
  72.4 143.1 %copy-start.43 = (f32[768]{0:T(1024)}, f32[768]{0:T(1024)S(1)}, u32[]{:S(2)}) copy-start(f32[768]{0:T(1024)S(1)} %get-tuple-element.64) | copy-start | bytes 9220
  72.8 30.4 %copy-start.19 = (s32[8]{0:T(128)}, s32[8]{0:T(128)S(1)}, u32[]{:S(2)}) copy-start(s32[8]{0:T(128)S(1)} %broadcast_select_fusion.grp_ref) | copy-start | bytes 100
  72.8 7.7 %copy-start.25 = (bf16[2,512,768]{2,1,0:T(8,128)(2,1)S(1)}, bf16[2,512,768]{2,1,0:T(8,128)(2,1)}, u32[]{:S(2)}) copy-start(bf16[2,512,768]{2,1,0:T(8,128)(2,1)} %copy-done.24) | copy-start | bytes 4718596
  80.5 1.0 copy-start.35
  80.5 1.7 copy-start.27
  82.2 21.0 %copy-start.3 = (bf16[1024,384]{1,0:T(8,128)(2,1)}, bf16[1024,384]{1,0:T(8,128)(2,1)S(1)}, u32[]{:S(2)}) copy-start(bf16[1024,384]{1,0:T(8,128)(2,1)S(1)} %multiply_convert_fusion.1.q_ref) | copy-start | bytes 2359300
  92.8 10.4 %copy-start = (bf16[1024,768]{1,0:T(8,128)(2,1)}, bf16[1024,768]{1,0:T(8,128)(2,1)S(1)}, u32[]{:S(2)}) copy-start(bf16[1024,768]{1,0:T(8,128)(2,1)S(1)} %convolution_convert_fusion.1.kvo_ref) | copy-start | bytes 4718596
  92.8 10.4 %copy-start.12 = (bf16[192,768]{1,0:T(8,128)(2,1)S(1)}, bf16[192,768]{1,0:T(8,128)(2,1)}, u32[]{:S(2)}) copy-start(bf16[192,768]{1,0:T(8,128)(2,1)} %refs_1_.1) | copy-start | bytes 884740
  92.8 10.3 %copy-start.13 = (bf16[192,768]{1,0:T(8,128)(2,1)S(1)}, bf16[192,768]{1,0:T(8,128)(2,1)}, u32[]{:S(2)}) copy-start(bf16[192,768]{1,0:T(8,128)(2,1)} %refs_2_.1) | copy-start | bytes 884740
  92.9 10.3 %copy-start.15 = (bf16[192,192]{1,0:T(8,128)(2,1)S(1)}, bf16[192,192]{1,0:T(8,128)(2,1)}, u32[]{:S(2)}) copy-start(bf16[192,192]{1,0:T(8,128)(2,1)} %refs_0_.3) | copy-start | bytes 221188
  183.2 2.2 copy-start.2
  185.4 0.6 copy-start.18
  186.0 6.5 %copy-start.8 = (bf16[2,512,384]{2,1,0:T(8,128)(2,1)}, bf16[2,512,384]{2,1,0:T(8,128)(2,1)S(1)}, u32[]{:S(2)}) copy-start(bf16[2,512,384]{2,1,0:T(8,128)(2,1)S(1)} %get-tuple-element.42) | copy-start | bytes 2359300
  188.4 4.1 copy-start.5
  188.4 4.1 copy-start.46
  194.6 1.2 copy-start.28
  197.6 17.8 %copy-start.29 = (f32[512,768]{1,0:T(8,128)S(1)}, f32[512,768]{1,0:T(8,128)}, u32[]{:S(2)}) copy-start(f32[512,768]{1,0:T(8,128)} %copy-done.28) | copy-start | bytes 4718596
  215.5 8.0 %copy-start.37 = (bf16[512,768]{1,0:T(8,128)(2,1)S(1)}, bf16[512,768]{1,0:T(8,128)(2,1)}, u32[]{:S(2)}) copy-start(bf16[512,768]{1,0:T(8,128)(2,1)} %param.17) | copy-start | bytes 2359300
  215.5 8.0 %copy-start.45 = (f32[768]{0:T(1024)S(1)}, f32[768]{0:T(1024)}, u32[]{:S(2)}) copy-start(f32[768]{0:T(1024)} %get-tuple-element.63) | copy-start | bytes 9220
  223.4 8.2 %copy-start.52 = (bf16[512,3072]{1,0:T(8,128)(2,1)}, bf16[512,3072]{1,0:T(8,128)(2,1)S(1)}, u32[]{:S(2)}) copy-start(bf16[512,3072]{1,0:T(8,128)(2,1)S(1)} %get-tuple-element.97) | copy-start | bytes 9437188
  231.7 6.7 %copy-start.42 = (f32[4,1,768]{2,1,0:T(1,128)S(1)}, f32[4,1,768]{2,1,0:T(1,128)}, u32[]{:S(2)}) copy-start(f32[4,1,768]{2,1,0:T(1,128)} %slice.214) | copy-start | bytes 36868
  231.7 6.7 %copy-start.54 = (bf16[512,768]{1,0:T(8,128)(2,1)S(1)}, bf16[512,768]{1,0:T(8,128)(2,1)}, u32[]{:S(2)}) copy-start(bf16[512,768]{1,0:T(8,128)(2,1)} %get-tuple-element.71) | copy-start | bytes 2359300
  231.7 16.6 %slice-start = ((s8[4718592]{0:T(1024)(128)(4,1)}), s8[524288]{0:T(1024)(128)(4,1)S(1)}, s32[]{:S(2)}) async-start(s8[4718592]{0:T(1024)(128)(4,1)} %bitcast.242), calls=%async_computation | async-start | bytes 1048576
  238.4 9.9 %slice-start.1 = ((s8[4718592]{0:T(1024)(128)(4,1)}), s8[4194304]{0:T(1024)(128)(4,1)S(1)}, s32[]{:S(2)}) async-start(s8[4718592]{0:T(1024)(128)(4,1)} %bitcast.242), calls=%async_computation.1 | async-start | bytes 8388608
  238.4 9.9 %copy-start.30 = (f32[512,768]{1,0:T(8,128)S(1)}, f32[512,768]{1,0:T(8,128)}, u32[]{:S(2)}) copy-start(f32[512,768]{1,0:T(8,128)} %copy-done.28) | copy-start | bytes 4718596
  248.3 3.6 copy-start.33
  251.8 2.5 copy-start.34
  251.8 4.2 copy-start.55
  254.3 2.2 copy-start.53
  256.5 4.4 copy-start.44
  260.9 4.9 copy-start.9
  274.9 78.1 %copy-start.20 = (s32[8]{0:T(128)S(1)}, s32[8]{0:T(128)}, u32[]{:S(2)}) copy-start(s32[8]{0:T(128)} %copy-done.19) | copy-start | bytes 100
  353.0 21.0 %copy-start.50 = (bf16[1024,768]{1,0:T(8,128)(2,1)S(1)}, bf16[1024,768]{1,0:T(8,128)(2,1)}, u32[]{:S(2)}) copy-start(bf16[1024,768]{1,0:T(8,128)(2,1)} %get-tuple-element.51) | copy-start | bytes 4718596
  371.4 2.6 copy-start.23
  374.0 2.7 copy-start.1
  374.0 2.7 copy-start.31
  374.0 2.7 copy-start.36
  382.4 9.4 %copy-start.26 = (bf16[2,512,768]{2,1,0:T(8,128)(2,1)S(1)}, bf16[2,512,768]{2,1,0:T(8,128)(2,1)}, u32[]{:S(2)}) copy-start(bf16[2,512,768]{2,1,0:T(8,128)(2,1)} %copy-done.24) | copy-start | bytes 4718596
  382.4 9.4 %copy-start.51 = (bf16[1024,768]{1,0:T(8,128)(2,1)S(1)}, bf16[1024,768]{1,0:T(8,128)(2,1)}, u32[]{:S(2)}) copy-start(bf16[1024,768]{1,0:T(8,128)(2,1)} %get-tuple-element.51) | copy-start | bytes 4718596
  393.6 1.3 copy-start.32
  394.9 4.0 copy-start.49
  394.9 4.0 copy-start.48
  394.9 4.0 copy-start.47
  394.9 4.1 copy-start.41
  394.9 4.9 copy-start.17
  399.9 1.1 copy-start.6
  485.6 1.2 copy-start.7
  486.8 0.8 copy-start.10
  487.6 6.0 %copy-start.11 = (f32[192,576]{1,0:T(8,128)S(1)}, f32[192,576]{1,0:T(8,128)}, u32[]{:S(2)}) copy-start(f32[192,576]{1,0:T(8,128)} %copy-done.10) | copy-start | bytes 1327108
  490.8 3.5 copy-start.40
  490.8 4.2 copy-start.39
  493.5 2.3 copy-start.38

commit v5 on v4

--- a/solution.py
+++ b/solution.py
@@ -1,4 +1,5 @@
 from functools import partial
+import math
 
 import jax
 import jax.numpy as jnp
@@ -570,20 +571,66 @@
     )(grp, q, lse, kvo, kvp.reshape(4, P_SIZE, kvp.shape[1]), gm, *grads)
 
 
-def fold_kernel(grp_ref, dkv_ref, w_ref, dkvp_ref, part_ref, acc):
+def fold_kernel(
+    grp_ref,
+    dkv_ref,
+    dkvo_ref,
+    dq_ref,
+    n1p_ref,
+    n1c_ref,
+    w_q,
+    w_kv,
+    part_ref,
+    chip_ref,
+    dw_ref,
+    acc,
+    wkt,
+    wqt,
+    dkvw,
+    dqw,
+):
+    t = pl.program_id(0)
+
+    @pl.when(t == 0)
+    def _():
+        wkt[...] = w_kv[...].T
+        wqt[...] = w_q[...].T
+        dkvw[...] = jnp.zeros_like(dkvw)
+        dqw[...] = jnp.zeros_like(dqw)
+
     acc[...] = jnp.zeros_like(acc)
     for j in range(8):
         acc[grp_ref[j]] += dkv_ref[j].astype(F32)
-    for k in range(4):
-        low = acc[k].astype(BF)
-        dkvp_ref[k] = low
-        part_ref[k] = nt(low, w_ref[...]).astype(BF)
-
-
-def fold_prompts(grp, dkv, w_kv):
-    tile = 128
-    block = pl.BlockSpec((4, tile, D), lambda i, *_: (0, i, 0))
-    shape = jax.ShapeDtypeStruct((4, P_SIZE, D), BF)
+    low = acc[...].astype(BF).reshape(512, D)
+    part_ref[...] = nn(low, wkt[...]).astype(BF).reshape(4, CL, D)
+    dkvo = dkvo_ref[...]
+    dq = dq_ref[...]
+    chip_ref[...] = (nn(dq, wqt[...]) + nn(dkvo, wkt[...])).astype(BF)
+    n1c = n1c_ref[...]
+    rows = jnp.concatenate([n1p_ref[...].reshape(512, D), n1c], axis=0)
+    dkvw[...] += tn(rows, jnp.concatenate([low, dkvo], axis=0))
+    dqw[...] += tn(n1c, dq)
+
+    @pl.when(t == pl.num_programs(0) - 1)
+    def _():
+        for head in range(6):
+            p, b = head // 2, head % 2
+            at_q = 128 * p + (0 if b else 64)
+            at_k = 256 * p + (128 if b else 64)
+            at_v = 256 * p + (192 if b else 0)
+            pieces = (
+                dqw[:, at_q : at_q + HD],
+                dkvw[:, at_k : at_k + HD],
+                dkvw[:, at_v : at_v + HD],
+            )
+            for i, piece in enumerate(pieces):
+                at = (head % 3) * 192 + HD * i
+                dw_ref[head // 3, :, at : at + HD] = piece.astype(BF)
+
+
+def fold_prompts(grp, dkv, dkvo, dq, n1_prompt, n1_chip, w_q, w_kv):
+    tile = CL
+    groups = pl.BlockSpec((4, tile, D), lambda i, *_: (0, i, 0))
     return pl.pallas_call(
         fold_kernel,
         name="fold_prompts",
@@ -592,14 +639,33 @@
             grid=(P_SIZE // tile,),
             in_specs=[
                 pl.BlockSpec((8, tile, D), lambda i, *_: (0, i, 0)),
+                pl.BlockSpec((tile, D), lambda i, *_: (i, 0)),
+                pl.BlockSpec((tile, 384), lambda i, *_: (i, 0)),
+                groups,
+                pl.BlockSpec((tile, D), lambda i, *_: (i, 0)),
+                pl.BlockSpec((D, 384), lambda i, *_: (0, 0)),
                 pl.BlockSpec((D, D), lambda i, *_: (0, 0)),
             ],
-            out_specs=[block, block],
-            scratch_shapes=[pltpu.VMEM((4, tile, D), F32)],
+            out_specs=[
+                groups,
+                pl.BlockSpec((tile, D), lambda i, *_: (i, 0)),
+                pl.BlockSpec((2, D, 576), lambda i, *_: (0, 0, 0)),
+            ],
+            scratch_shapes=[
+                pltpu.VMEM((4, tile, D), F32),
+                pltpu.VMEM((D, D), BF),
+                pltpu.VMEM((384, D), BF),
+                pltpu.VMEM((D, D), F32),
+                pltpu.VMEM((D, 384), F32),
+            ],
         ),
-        out_shape=[shape, shape],
-        compiler_params=pltpu.CompilerParams(vmem_limit_bytes=40 << 20),
-    )(grp, dkv, w_kv)
+        out_shape=[
+            jax.ShapeDtypeStruct((4, P_SIZE, D), BF),
+            jax.ShapeDtypeStruct((2 * QROWS, D), BF),
+            jax.ShapeDtypeStruct((2, D, 576), BF),
+        ],
+        compiler_params=pltpu.CompilerParams(vmem_limit_bytes=48 << 20),
+    )(grp, dkv, dkvo, dq, n1_prompt.reshape(4, P_SIZE, D), n1_chip, w_q, w_kv)
 
 
 def norm_rows(hidden, gain, shift):
@@ -1319,6 +1385,187 @@
     )(part, chip, dw, grad_h2, tokens, vec, sums)
 
 
+GELU_IN = math.sqrt(2.0 / math.pi)
+
+
+def middle_kernel(
+    mixed,
+    w_out_g,
+    w_up,
+    w_down,
+    tokens,
+    teacher,
+    vec,
+    b_up,
+    final_out,
+    grad_h2,
+    dw_up,
+    dw_down,
+    dw_out,
+    gm,
+    sums,
+    wo,
+    wu,
+    wd,
+    h2,
+    n2,
+    n2t,
+    act,
+    slope,
+    gf,
+    gb,
+    gbt,
+    acc,
+    du,
+    dd,
+    l_sems,
+    o_sems,
+):
+    loads_u = [pltpu.make_async_copy(w_up.at[b], wu.at[b], l_sems.at[b]) for b in range(4)]
+    loads_d = [pltpu.make_async_copy(w_down.at[b], wd.at[b], l_sems.at[4 + b]) for b in range(4)]
+    for b in range(4):
+        loads_u[b].start()
+        loads_d[b].start()
+    for k in range(2):
+        for i in range(2):
+            for r in range(4):
+                wo[k, 192 * i : 192 * i + 192, 192 * r : 192 * r + 192] = w_out_g[2 * i + k, r]
+
+    @pl.loop(0, 2)
+    def _(t):
+        r = pl.ds(pl.multiple_of(t * 256, 256), 256)
+        hidden = tokens[r].astype(F32) + vec[0:1]
+        attended = nn(mixed[0, r], wo[0]) + nn(mixed[1, r], wo[1])
+        total = hidden + attended + vec[3:4]
+        h2[r] = total
+        n2[r] = norm_rows(total, vec[4:5], vec[5:6]).astype(BF)
+
+    n2t[...] = n2[...].T
+    acc[...] = jnp.zeros_like(acc)
+    for copy in loads_u + loads_d:
+        copy.wait()
+
+    @pl.loop(0, 4)
+    def _(b):
+        @pl.loop(0, 2)
+        def _(t):
+            r = pl.ds(pl.multiple_of(t * 256, 256), 256)
+            pre = nn(n2[r], wu[b]) + b_up[b, 0:1]
+            square = pre * pre
+            tanh = jnp.tanh(GELU_IN * pre * (1.0 + 0.044715 * square))
+            half = 0.5 * (1.0 + tanh)
+            low = (pre * half).astype(BF)
+            act[b, r] = low
+            slope[b, r] = half + (0.5 * GELU_IN) * pre * (1.0 - tanh * tanh) * (
+                1.0 + (3.0 * 0.044715) * square
+            )
+            acc[r] += nt(low, wd[b])
+
+    sums[...] = jnp.zeros_like(sums)
+
+    @pl.loop(0, 2)
+    def _(t):
+        r = pl.ds(pl.multiple_of(t * 256, 256), 256)
+        final = h2[r] + acc[r] + vec[6:7]
+        final_out[r] = final.astype(BF)
+        diff = final - teacher[r].astype(F32)
+        gf[r] = diff
+        low = diff.astype(BF)
+        gb[r] = low
+        sums[6:7] += jnp.sum(low.astype(F32), axis=0, keepdims=True)
+        sums[11:12] += jnp.sum(diff * diff, axis=0, keepdims=True)
+
+    gbt[...] = gb[...].T
+    acc[...] = jnp.zeros_like(acc)
+
+    @pl.loop(0, 4)
+    def _(b):
+        dd[b] = nn(gbt[...], act[b]).astype(BF)
+        pltpu.make_async_copy(dd.at[b], dw_down.at[b], o_sems.at[b]).start()
+
+        @pl.loop(0, 2)
+        def _(t):
+            r = pl.ds(pl.multiple_of(t * 256, 256), 256)
+            low = (nn(gb[r], wd[b]) * slope[b, r]).astype(BF)
+            act[b, r] = low
+            sums[pl.ds(7 + b, 1)] += jnp.sum(low.astype(F32), axis=0, keepdims=True)
+            acc[r] += nt(low, wu[b])
+
+        du[b] = nn(n2t[...], act[b]).astype(BF)
+        pltpu.make_async_copy(du.at[b], dw_up.at[b], o_sems.at[4 + b]).start()
+
+    @pl.loop(0, 2)
+    def _(t):
+        r = pl.ds(pl.multiple_of(t * 256, 256), 256)
+        hidden = h2[r]
+        center = jnp.mean(hidden, axis=1, keepdims=True)
+        offset = hidden - center
+        factor = lax.rsqrt(jnp.mean(offset * offset, axis=1, keepdims=True) + eps)
+        unit = offset * factor
+        grad = acc[r]
+        scaled = grad * vec[4:5]
+        first = jnp.mean(scaled, axis=1, keepdims=True)
+        second = jnp.mean(scaled * unit, axis=1, keepdims=True)
+        total = gf[r] + factor * (scaled - first - unit * second)
+        grad_h2[r] = total
+        low = total.astype(BF)
+        gb[r] = low
+        sums[3:4] += jnp.sum(grad * unit, axis=0, keepdims=True)
+        sums[4:5] += jnp.sum(grad, axis=0, keepdims=True)
+        sums[5:6] += jnp.sum(low.astype(F32), axis=0, keepdims=True)
+        gm[0, r] = nt(low, wo[0]).astype(BF)
+        gm[1, r] = nt(low, wo[1]).astype(BF)
+
+    for k in range(2):
+        whole = tn(mixed[k], gb[...]).astype(BF)
+        for i in range(2):
+            for r in range(4):
+                dw_out[2 * i + k, r] = whole[192 * i : 192 * i + 192, 192 * r : 192 * r + 192]
+    for b in range(4):
+        pltpu.make_async_copy(dd.at[b], dw_down.at[b], o_sems.at[b]).wait()
+        pltpu.make_async_copy(du.at[b], dw_up.at[b], o_sems.at[4 + b]).wait()
+
+
+def middle(mixed, w_out_g, w_up, w_down, tokens, teacher, vec, b_up):
+    any_space = pl.BlockSpec(memory_space=pl.ANY)
+    vmem = pl.BlockSpec(memory_space=pltpu.VMEM)
+    blocks = (4, D, D)
+    return pl.pallas_call(
+        middle_kernel,
+        name="middle",
+        in_specs=[vmem, vmem, any_space, any_space, vmem, vmem, vmem, vmem],
+        out_specs=[vmem, vmem, any_space, any_space, vmem, vmem, vmem],
+        out_shape=[
+            jax.ShapeDtypeStruct((QROWS, D), BF),
+            jax.ShapeDtypeStruct((QROWS, D), F32),
+            jax.ShapeDtypeStruct(blocks, BF),
+            jax.ShapeDtypeStruct(blocks, BF),
+            jax.ShapeDtypeStruct((4, 4, 192, 192), BF),
+            jax.ShapeDtypeStruct((2, QROWS, 384), BF),
+            jax.ShapeDtypeStruct((16, D), F32),
+        ],
+        scratch_shapes=[
+            pltpu.VMEM((2, 384, D), BF),
+            pltpu.VMEM(blocks, BF),
+            pltpu.VMEM(blocks, BF),
+            pltpu.VMEM((QROWS, D), F32),
+            pltpu.VMEM((QROWS, D), BF),
+            pltpu.VMEM((D, QROWS), BF),
+            pltpu.VMEM((4, QROWS, D), BF),
+            pltpu.VMEM((4, QROWS, D), F32),
+            pltpu.VMEM((QROWS, D), F32),
+            pltpu.VMEM((QROWS, D), BF),
+            pltpu.VMEM((D, QROWS), BF),
+            pltpu.VMEM((QROWS, D), F32),
+            pltpu.VMEM(blocks, BF),
+            pltpu.VMEM(blocks, BF),
+            pltpu.SemaphoreType.DMA((8,)),
+            pltpu.SemaphoreType.DMA((8,)),
+        ],
+        compiler_params=pltpu.CompilerParams(vmem_limit_bytes=60 << 20),
+    )(mixed, w_out_g, w_up, w_down, tokens, teacher, vec, b_up)
+
+
 def norm(hidden, gain, shift):
     center = jnp.mean(hidden, axis=1, keepdims=True)
     offset = hidden - center
@@ -1397,7 +1644,6 @@
         n1_prompt = n1_prompt.reshape(4 * P_SIZE, D)
         n1_chip = n1_chip.reshape(2 * QROWS, D)
         w_qkv = w_pair.reshape(2, D, 576)
-        b_up = b_up[:, 0].reshape(FF)
         owners = owners[:, 0, :8]
     else:
         vectors = lax.all_gather(packed, "gr", axis=1, tiled=True)
@@ -1448,64 +1694,73 @@
         mixed = jnp.where(c == 0, jnp.stack([keep, take]), jnp.stack([take, keep]))
     w_up = w_up.reshape(n_gc, D, FF // n_gc)
     w_down = w_down.reshape(n_gc, D, FF // n_gc)
-    w_out = w_out.reshape(2, 2, n_gr, 192, 192).transpose(1, 0, 3, 2, 4).reshape(2, 384, D)
-
-    attended = lax.dot_general(
-        mixed, w_out, (((0, 2), (0, 1)), ((), ())), preferred_element_type=F32
-    )
-    hidden2 = hidden + attended + b_out
-    normed2, unit2, factor2 = norm(hidden2, gain2, shift2)
-    n2 = normed2.astype(BF)
-    pre = lax.dot_general(n2, w_up, (((1,), (1,)), ((), ())), preferred_element_type=F32)
-    pre = pre.reshape(QROWS, FF) + b_up
-    active, gelu_back = jax.vjp(partial(jax.nn.gelu, approximate=True), pre)
-    act = active.astype(BF)
-    act_blocks = act.reshape(QROWS, n_gc, FF // n_gc)
-    final = (
-        hidden2
-        + lax.dot_general(
-            act_blocks, w_down, (((1, 2), (0, 2)), ((), ())), preferred_element_type=F32
-        )
-        + b_down
-    )
-    grad_final = final - teacher.astype(F32)
-    squared = jnp.sum(grad_final * grad_final)
-    gb = grad_final.astype(BF)
-    grad_b_down = jnp.sum(gb, axis=0, dtype=F32)
-    grad_active = lax.dot_general(
-        gb, w_down, (((1,), (1,)), ((), ())), preferred_element_type=F32
-    ).reshape(QROWS, FF)
-    grad_w_down = jnp.einsum("td,tgf->gdf", gb, act_blocks, preferred_element_type=F32)
-    (grad_pre,) = gelu_back(grad_active)
-    gp = grad_pre.astype(BF)
-    gp_blocks = gp.reshape(QROWS, n_gc, FF // n_gc)
-    grad_b_up = jnp.sum(gp, axis=0, dtype=F32)
-    grad_w_up = jnp.einsum("td,tgf->gdf", n2, gp_blocks, preferred_element_type=F32)
-    grad_n2 = lax.dot_general(
-        gp_blocks, w_up, (((1, 2), (0, 2)), ((), ())), preferred_element_type=F32
-    )
-    back2, grad_gain2, grad_shift2 = norm_back(grad_n2, gain2, unit2, factor2)
-    grad_h2 = grad_final + back2
-    ga = grad_h2.astype(BF)
-    grad_b_out = jnp.sum(ga, axis=0, dtype=F32)
-    grad_w_out = jnp.einsum("ctk,tn->ckn", mixed, ga, preferred_element_type=F32)
-    gm = jnp.einsum("tn,ckn->ctk", ga, w_out, preferred_element_type=F32).astype(BF)
-
+    if n_dp == 2:
+        final, grad_h2, grad_w_up, grad_w_down, grad_w_out, gm, later_sums = middle(
+            mixed, w_out, w_up, w_down, tokens, teacher, vectors, b_up
+        )
+    else:
+        w_out = w_out.reshape(2, 2, n_gr, 192, 192).transpose(1, 0, 3, 2, 4).reshape(2, 384, D)
+
+        attended = lax.dot_general(
+            mixed, w_out, (((0, 2), (0, 1)), ((), ())), preferred_element_type=F32
+        )
+        hidden2 = hidden + attended + b_out
+        normed2, unit2, factor2 = norm(hidden2, gain2, shift2)
+        n2 = normed2.astype(BF)
+        pre = lax.dot_general(n2, w_up, (((1,), (1,)), ((), ())), preferred_element_type=F32)
+        pre = pre.reshape(QROWS, FF) + b_up
+        active, gelu_back = jax.vjp(partial(jax.nn.gelu, approximate=True), pre)
+        act = active.astype(BF)
+        act_blocks = act.reshape(QROWS, n_gc, FF // n_gc)
+        final = (
+            hidden2
+            + lax.dot_general(
+                act_blocks, w_down, (((1, 2), (0, 2)), ((), ())), preferred_element_type=F32
+            )
+            + b_down
+        )
+        grad_final = final - teacher.astype(F32)
+        squared = jnp.sum(grad_final * grad_final, axis=0)
+        gb = grad_final.astype(BF)
+        grad_b_down = jnp.sum(gb, axis=0, dtype=F32)
+        grad_active = lax.dot_general(
+            gb, w_down, (((1,), (1,)), ((), ())), preferred_element_type=F32
+        ).reshape(QROWS, FF)
+        grad_w_down = jnp.einsum("td,tgf->gdf", gb, act_blocks, preferred_element_type=F32)
+        (grad_pre,) = gelu_back(grad_active)
+        gp = grad_pre.astype(BF)
+        gp_blocks = gp.reshape(QROWS, n_gc, FF // n_gc)
+        grad_b_up = jnp.sum(gp, axis=0, dtype=F32)
+        grad_w_up = jnp.einsum("td,tgf->gdf", n2, gp_blocks, preferred_element_type=F32)
+        grad_n2 = lax.dot_general(
+            gp_blocks, w_up, (((1, 2), (0, 2)), ((), ())), preferred_element_type=F32
+        )
+        back2, grad_gain2, grad_shift2 = norm_back(grad_n2, gain2, unit2, factor2)
+        grad_h2 = grad_final + back2
+        ga = grad_h2.astype(BF)
+        grad_b_out = jnp.sum(ga, axis=0, dtype=F32)
+        grad_w_out = jnp.einsum("ctk,tn->ckn", mixed, ga, preferred_element_type=F32)
+        gm = jnp.einsum("tn,ckn->ctk", ga, w_out, preferred_element_type=F32).astype(BF)
+        grad_w_up = grad_w_up.astype(BF)
+        grad_w_down = grad_w_down.astype(BF)
+        grad_w_out = (
+            grad_w_out.astype(BF)
+            .reshape(2, 2, 192, n_gr, 192)
+            .transpose(1, 0, 3, 2, 4)
+            .reshape(n_gc, n_gr, 192, 192)
+        )
     weight_grads = [
-        grad_w_down.astype(BF).reshape(n_gc, n_gr, 192, 768),
-        grad_w_up.astype(BF).reshape(n_gc, n_gr, 192, 768),
-        grad_w_out.astype(BF)
-        .reshape(2, 2, 192, n_gr, 192)
-        .transpose(1, 0, 3, 2, 4)
-        .reshape(n_gc, n_gr, 192, 192),
+        grad_w_down.reshape(n_gc, n_gr, 192, 768),
+        grad_w_up.reshape(n_gc, n_gr, 192, 768),
+        grad_w_out,
     ]
     if n_dp == 2:
         dq, dkvo, dkv, out_w_down, out_w_up, out_w_out = attend_back_scatter(
             grp, q, lse_rows, kvo, kvp, gm, weight_grads, 3
         )
-        dkvp, part_prompt = fold_prompts(grp, dkv, w_kv)
-        dkvp = dkvp.reshape(4 * P_SIZE, D)
-        part_prompt = part_prompt.reshape(4 * P_SIZE, D)
+        part_prompt, part_chip, grad_qkv = fold_prompts(
+            grp, dkv, dkvo, dq, n1_prompt, n1_chip, w_q, w_kv
+        )
     else:
         gm_keep = lax.dynamic_index_in_dim(gm, c, 0, keepdims=False)
         gm_give = lax.dynamic_index_in_dim(gm, 1 - c, 0, keepdims=False)
@@ -1526,33 +1781,34 @@
         dq, dkvo, dkvp = attend_back(grp, z_arr, q, gm_chip, lse_rows, kvo, kvp)
         part_prompt = nt(dkvp, w_kv).astype(BF)
 
-    part_chip = (nt(dq, w_q) + nt(dkvo, w_kv)).reshape(2, QROWS, D)
-    grad_kv = tn(n1_prompt, dkvp) + tn(n1_chip, dkvo)
-    grad_q = tn(n1_chip, dq)
-    grad_qkv = head_layout_back(grad_q, grad_kv)
-    later_sums = jnp.concatenate(
-        [
-            grad_gain2[None],
-            grad_shift2[None],
-            grad_b_out[None],
-            grad_b_down[None],
-            grad_b_up.reshape(4, D),
-            jnp.broadcast_to(squared, (1, D)),
-            jnp.zeros((4, D), F32),
-        ]
-    )
+        part_chip = (nt(dq, w_q) + nt(dkvo, w_kv)).reshape(2, QROWS, D)
+        grad_kv = tn(n1_prompt, dkvp) + tn(n1_chip, dkvo)
+        grad_q = tn(n1_chip, dq)
+        grad_qkv = head_layout_back(grad_q, grad_kv)
+
     if n_dp == 2:
         input_grad, sums, out_w_qkv = tail_exchange(
             part_prompt.reshape(4, 2, QROWS, D),
-            part_chip.astype(BF),
-            grad_qkv.astype(BF).reshape(2, 4, 192, 576),
+            part_chip.reshape(2, QROWS, D),
+            grad_qkv.reshape(2, 4, 192, 576),
             grad_h2,
             tokens,
             vectors,
-            jnp.concatenate([jnp.zeros((3, D), F32), later_sums]),
+            later_sums,
             4,
         )
     else:
+        later_sums = jnp.concatenate(
+            [
+                grad_gain2[None],
+                grad_shift2[None],
+                grad_b_out[None],
+                grad_b_down[None],
+                grad_b_up.reshape(4, D),
+                squared[None],
+                jnp.zeros((4, D), F32),
+            ]
+        )
         back_prompt = lax.psum_scatter(part_prompt, "gc", scatter_dimension=0, tiled=True)
         back_prompt = lax.psum_scatter(
             jnp.concatenate([back_prompt, jnp.zeros_like(back_prompt)]),
@@ -1576,7 +1832,7 @@
         first_sums = jnp.stack([jnp.sum(input_grad, axis=0), grad_gain1, grad_shift1])
         sums = lax.psum(jnp.concatenate([first_sums, later_sums]), ("dp", "gr", "gc"))
     sums = sums[:12].reshape(12 * D)
-    loss = (sums[-1] / (D * token_count[0].astype(F32))).reshape(1)
+    loss = (jnp.sum(sums[11 * D :]) / (D * token_count[0].astype(F32))).reshape(1)
     rows = sums[: 7 * D].reshape(7, n_gr, D // n_gr)
     rows = lax.dynamic_index_in_dim(rows, z, 1, keepdims=False)
     up = lax.dynamic_index_in_dim(

time: 504 us -> 424 us (0.84)
  matrix products: 74.4 us -> 13.8 us
  local copies, waits for them, and re-layouts: 98 us -> 44.2 us
  Pallas kernels: 319 us -> 361 us
    dot_general x14 -> x0, matrix products: 60.3 us -> none  [the longest x3 13.3 us: tn(): lax.dot_general(a, b, (((0,), (0,)), ((), ())), preferred_element_type=F32)]
    reshape x7 -> x0, local copies, waits for them, and re-layouts: 35.9 us -> none  [the longest x1 17.8 us: on_device(): w_up = w_up.reshape(n_gc, D, FF // n_gc)]
    pallas_call x0 -> x1, Pallas kernels: none -> 34.9 us  [middle(): pl.pallas_call(middle_kernel, name='middle', in_specs=[vmem, vmem, any_sp...]
    unnamed x155 -> x85, local copies, waits for them, and re-layouts: 36.2 us -> 27.3 us
    pallas_call x1, Pallas kernels: 18.4 us -> 25.8 us  [fold_prompts(): pl.pallas_call(fold_kernel, name='fold_prompts', grid_spec=pltpu.Prefetch...]
where the time goes in v5:
time: 424 us; the launch traced here: 423 us
  Pallas kernels  361 us (85%)
  local copies, waits for them, and re-layouts  44.2 us (10%)
  matrix products  13.8 us (3%)
    pallas_call x1, Pallas kernels, tail_exchange(): pl.pallas_call(tail_kernel, name='tail_exchange', in_specs=[any_space, an...  84.7 us
    pallas_call x1, Pallas kernels, attend_gather(): pl.pallas_call(partial(att_gather_kernel, count), name='attend_gather', g...  79.9 us
    pallas_call x1, Pallas kernels, attend_back_scatter(): pl.pallas_call(partial(att_scatter_kernel, count), name='attend_back_scat...  77.6 us
    pallas_call x1, Pallas kernels, start_exchange(): pl.pallas_call(body, name='start_exchange', in_specs=[vmem, vmem, vmem, v...  57.7 us
    pallas_call x1, Pallas kernels, middle(): pl.pallas_call(middle_kernel, name='middle', in_specs=[vmem, vmem, any_sp...  34.9 us
    unnamed x85, local copies, waits for them, and re-layouts  27.3 us
    pallas_call x1, Pallas kernels, fold_prompts(): pl.pallas_call(fold_kernel, name='fold_prompts', grid_spec=pltpu.Prefetch...  25.8 us
    dot_general x3, matrix products, nn(): lax.dot_general(a, b, (((1,), (0,)), ((), ())), preferred_element_type=F32)  13.8 us

profile of v5, /device:TPU:0, one launch (start us, length us, event | category | flops | bytes accessed | tf_op | source)
XLA Modules:
  0.0 422.7 jit_solution(13245267108187373147)
XLA Ops:
  0.7 0.7 stack.25
  1.3 0.7 stack.26
  2.0 0.7 stack.27
  2.6 0.7 stack.28
  3.3 0.7 stack.29
  3.9 0.7 stack.30
  4.6 0.7 stack.31
  5.3 0.3 dynamic_update_slice.3.refs_1_
  5.6 0.7 broadcast_in_dim.14.refs_2_
  6.3 0.7 pad.4
  7.0 1.1 copy-done
  8.1 0.9 copy-done.16
  9.0 57.7 %start_exchange.1 = (bf16[4,2,512,768]{3,2,1,0:T(8,128)(2,1)S(1)}, bf16[2,512,768]{2,1,0:T(8,128)(2,1)S(1)}, bf16[2,4,192,576]{3,2,1,0:T(8,128)(2,1)S(1)}, f32[8...) custom-call(bf16[512,768]{1,0:T(8,128)(2,1)S(1)} %copy-done, ...), custom_call_target="tpu_custom_call" | custom-call | tf_op jit(solution)/shard_map/start_exchange/pallas_call | solution.py:879
  66.8 2.6 copy-done.3
  69.4 1.1 copy-done.9
  70.5 2.3 copy.31
  72.8 2.4 fusion.1
  75.2 0.2 copy.56
  75.4 0.2 copy.57
  75.6 0.2 copy.58
  75.7 0.2 copy.59
  75.9 0.2 copy.60
  76.1 0.2 copy.61
  76.2 0.2 copy.62
  76.4 0.2 copy.63
  76.6 0.2 copy.64
  76.8 0.2 copy.65
  76.9 0.2 copy.66
  77.1 0.2 copy.67
  77.3 0.9 concatenate.7.w_kv
  78.2 9.9 %convolution_convert_fusion = bf16[4096,768]{1,0:T(8,128)(2,1)} fusion(bf16[4096,768]{1,0:T(8,128)(2,1)} %bitcast.48, bf16[768,768]{1,0:T(8,128)(2,1)S(1)} %concatenate.7.w_kv), kind=kOutput, calls=%fused_computation | convolution fusion | flops 4834983936 | bytes 13762560 | tf_op jit(solution)/shard_map/dot_general | solution.py:28
  88.1 1.4 convolution_convert_fusion.1.kvo_ref
  89.5 0.2 copy.55
  89.7 0.2 copy.50
  89.9 0.2 copy.51
  90.1 1.1 copy.52
  91.1 1.7 copy.53
  92.8 1.7 copy.54
  94.5 2.0 concatenate.6.w_q
  96.6 2.5 multiply_convert_fusion.q_ref
  99.1 0.7 slice_reduce_fusion.1
  99.8 0.8 reshape_squeeze.3
  100.8 1.0 copy-done.14
  101.8 1.0 copy-done.15
  102.8 0.9 copy-done.17
  103.7 79.9 %attend_gather.1 = (bf16[2,512,384]{2,1,0:T(8,128)(2,1)S(1)}, f32[3,8,2,128]{3,2,1,0:T(2,128)S(1)}, bf16[4,4,192,192]{3,2,1,0:T(8,128)(2,1)S(1)}, bf16[4,4,192,7...) custom-call(s32[8]{0:T(128)S(1)} %broadcast_select_fusion.grp_ref, bf16[1024,384]{1,0:T(8,128)(2,1)S(1)} %multiply_convert_fusion.q_ref, ...), custom_call_target="tpu_custom_call" | custom-call | tf_op jit(solution)/shard_map/attend_gather/pallas_call | solution.py:1117
  183.6 2.2 copy-done.4
  185.8 1.1 copy-done.8
  187.0 0.9 copy-done.12
  187.9 0.6 copy-done.22
  188.5 34.9 %middle.1 = (bf16[512,768]{1,0:T(8,128)(2,1)}, f32[512,768]{1,0:T(8,128)}, bf16[4,768,768]{2,1,0:T(8,128)(2,1)}, bf16[4,768,768]{2,1,0:T(8,128)(2,1)}, bf16[4,4,...) custom-call(bf16[2,512,384]{2,1,0:T(8,128)(2,1)} %copy-done.12, ...), custom_call_target="tpu_custom_call" | custom-call | tf_op jit(solution)/shard_map/middle/pallas_call | solution.py:1533
  223.4 77.6 %attend_back_scatter.1 = (bf16[1024,384]{1,0:T(8,128)(2,1)}, bf16[1024,768]{1,0:T(8,128)(2,1)}, bf16[8,1024,768]{2,1,0:T(8,128)(2,1)}, f32[192,768]{1,0:T(8,128)...) custom-call(s32[8]{0:T(128)} %copy-done.23, bf16[1024,384]{1,0:T(8,128)(2,1)} %copy-done.5, f32[3,8,2,128]{3,2,1,0:T(2,128)} %copy-done.22, ...), custom_call_target="tpu_custom_call" | custom-call | tf_op jit(solution)/shard_map/attend_back_scatter/pallas_call | solution.py:532
  301.0 1.4 copy-done.11
  302.4 1.1 copy-done.13
  303.6 25.8 %fold_prompts.1 = (bf16[4,1024,768]{2,1,0:T(8,128)(2,1)}, bf16[1024,768]{1,0:T(8,128)(2,1)S(1)}, bf16[2,768,576]{2,1,0:T(8,128)(2,1)}) custom-call(s32[8]{0:T(128)S(1)} %copy-done.24, bf16[8,1024,768]{2,1,0:T(8,128)(2,1)} %get-tuple-element.61.dkv_ref, bf16[1024,768]{1,0:T(8,128)(2,1)S(1)} %copy-done.11, bf16[1024,384]{1,0:T(8,128)(2,1)S(1)} %copy-done.13, ...), custom_call_target="tpu_custom_call" | custom-call | tf_op jit(solution)/shard_map/fold_prompts/pallas_call | solution.py:634
  329.4 84.7 %tail_exchange.1 = (f32[512,768]{1,0:T(8,128)S(1)}, f32[16,768]{1,0:T(8,128)S(1)}, f32[192,576]{1,0:T(8,128)S(1)}) custom-call(bf16[4,2,512,768]{3,2,1,0:T(8,128)(2,1)} %bitcast.59, bf16[2,512,768]{2,1,0:T(8,128)(2,1)S(1)} %bitcast.52, bf16[2,4,192,576]{3,2,1,0:T(8,128)(2,1)} %bitcast.63, f32[512,768]{1,0:T(8,128)S(1)} %copy-done.7, ...), custom_call_target="tpu_custom_call" | custom-call | tf_op jit(solution)/shard_map/tail_exchange/pallas_call | solution.py:1352
  414.2 0.6 constant_dynamic-slice_fusion.6
  414.8 0.6 dynamic-slice_reduce_fusion
  415.4 0.6 slice_reduce_fusion
  417.3 1.1 copy.75
  418.5 0.8 copy.76
  419.3 0.7 copy.77
  419.9 0.8 copy.78
  420.8 0.8 copy.79
  (62 shorter events, 0.5 us)
Async XLA Ops:
  7.0 1.1 copy-start
  8.1 0.9 copy-start.16
  66.8 2.6 copy-start.3
  69.4 1.1 copy-start.9
  70.5 2.3 copy-start.18
  70.5 2.3 copy-start.19
  78.2 9.9 %copy-start.10 = (bf16[2,512,768]{2,1,0:T(8,128)(2,1)S(1)}, bf16[2,512,768]{2,1,0:T(8,128)(2,1)}, u32[]{:S(2)}) copy-start(bf16[2,512,768]{2,1,0:T(8,128)(2,1)} %copy-done.9) | copy-start | bytes 4718596
  88.1 1.4 copy-start.29
  88.1 1.6 copy-start.28
  88.1 1.8 copy-start.27
  89.5 11.3 %copy-start.2 = (bf16[1024,768]{1,0:T(8,128)(2,1)}, bf16[1024,768]{1,0:T(8,128)(2,1)S(1)}, u32[]{:S(2)}) copy-start(bf16[1024,768]{1,0:T(8,128)(2,1)S(1)} %convolution_convert_fusion.1.kvo_ref) | copy-start | bytes 4718596
  99.1 84.5 %copy-start.5 = (bf16[1024,384]{1,0:T(8,128)(2,1)}, bf16[1024,384]{1,0:T(8,128)(2,1)S(1)}, u32[]{:S(2)}) copy-start(bf16[1024,384]{1,0:T(8,128)(2,1)S(1)} %multiply_convert_fusion.q_ref) | copy-start | bytes 2359300
  100.8 1.0 copy-start.14
  101.8 1.0 copy-start.15
  102.8 0.9 copy-start.17
  103.7 80.0 %copy-start.23 = (s32[8]{0:T(128)}, s32[8]{0:T(128)S(1)}, u32[]{:S(2)}) copy-start(s32[8]{0:T(128)S(1)} %broadcast_select_fusion.grp_ref) | copy-start | bytes 100
  183.6 2.2 copy-start.4
  185.8 1.1 copy-start.8
  187.0 0.9 copy-start.12
  187.9 0.6 copy-start.22
  223.3 77.7 %copy-start.6 = (bf16[768,384]{1,0:T(8,128)(2,1)S(1)}, bf16[768,384]{1,0:T(8,128)(2,1)}, u32[]{:S(2)}) copy-start(bf16[768,384]{1,0:T(8,128)(2,1)} %concatenate.6.w_q) | copy-start | bytes 1769476
  223.3 77.7 %copy-start.24 = (s32[8]{0:T(128)S(1)}, s32[8]{0:T(128)}, u32[]{:S(2)}) copy-start(s32[8]{0:T(128)} %copy-done.23) | copy-start | bytes 100
  301.0 1.4 copy-start.11
  302.4 1.1 copy-start.13
  303.5 25.8 %copy-start.1 = (bf16[512,768]{1,0:T(8,128)(2,1)S(1)}, bf16[512,768]{1,0:T(8,128)(2,1)}, u32[]{:S(2)}) copy-start(bf16[512,768]{1,0:T(8,128)(2,1)} %tokens.3) | copy-start | bytes 2359300
  303.5 25.8 %copy-start.7 = (f32[512,768]{1,0:T(8,128)S(1)}, f32[512,768]{1,0:T(8,128)}, u32[]{:S(2)}) copy-start(f32[512,768]{1,0:T(8,128)} %get-tuple-element.67.grad_h2) | copy-start | bytes 4718596
  303.5 25.8 %copy-start.20 = (f32[8,768]{1,0:T(8,128)S(1)}, f32[8,768]{1,0:T(8,128)}, u32[]{:S(2)}) copy-start(f32[8,768]{1,0:T(8,128)} %copy-done.19) | copy-start | bytes 73732
  303.6 25.8 %copy-start.21 = (f32[16,768]{1,0:T(8,128)S(1)}, f32[16,768]{1,0:T(8,128)}, u32[]{:S(2)}) copy-start(f32[16,768]{1,0:T(8,128)} %get-tuple-element.68.sums) | copy-start | bytes 147460
  417.3 1.9 copy-start.30
  417.3 2.6 copy-start.26
  418.5 2.3 copy-start.25

commit v6 on v5

--- a/solution.py
+++ b/solution.py
@@ -455,7 +455,7 @@
     group = grp_ref[j]
     low = lax.broadcasted_iota(jnp.int32, (CL, 128), 1) < 64
     zero = jnp.zeros((CL, 128), BF)
-    q = q_ref[...]
+    q = q_ref[0]
     gmix = gmx[p, j // 4, pl.ds(pl.multiple_of((j % 4) * CL, CL), CL)]
     stacks = (
         jnp.concatenate([jnp.where(low, zero, q), jnp.where(low, gmix, zero)], axis=0),
@@ -469,8 +469,8 @@
         dqs = []
         for h in range(2):
             cols = slice(128 * h, 128 * h + 128)
-            kv = kvp_ref[group, :, cols]
-            kvo = kvo_ref[:, cols]
+            kv = kvp_ref[0, group, :, cols]
+            kvo = kvo_ref[0, :, cols]
             lse = lse_ref[0, 0, h : h + 1, :]
             far = nt(kv, stacks[h])
             near = nt(kvo, stacks[h])
@@ -501,7 +501,7 @@
         dqs = []
         for h in range(2):
             cols = slice(128 * h, 128 * h + 128)
-            kv = kvp_ref[group, :, cols]
+            kv = kvp_ref[0, group, :, cols]
             lse = lse_ref[0, 0, h : h + 1, :]
             far = nt(kv, stacks[h])
             pf = jnp.where(allowed, jnp.exp(far[:, :CL] - lse), 0.0)
@@ -522,7 +522,7 @@
 
 
 def attend_back_scatter(grp, q, lse, kvo, kvp, gm, grads, collective_id):
-    rows = q.shape[0]
+    rows = q.shape[1]
     count = len(grads)
     any_space = pl.BlockSpec(memory_space=pl.ANY)
     scratch = []
@@ -536,10 +536,10 @@
             num_scalar_prefetch=1,
             grid=(3, rows // CL),
             in_specs=[
-                pl.BlockSpec((CL, 128), lambda p, j, *_: (j, p)),
+                pl.BlockSpec((1, CL, 128), lambda p, j, *_: (p, j, 0)),
                 pl.BlockSpec((1, 1, 2, 128), lambda p, j, *_: (p, j, 0, 0)),
-                pl.BlockSpec((CL, 256), lambda p, j, *_: (j, p)),
-                pl.BlockSpec((4, P_SIZE, 256), lambda p, j, *_: (0, 0, p)),
+                pl.BlockSpec((1, CL, 256), lambda p, j, *_: (p, j, 0)),
+                pl.BlockSpec((1, 4, P_SIZE, 256), lambda p, j, *_: (p, 0, 0, 0)),
             ]
             + [any_space] * (count + 1),
             out_specs=[
@@ -568,7 +568,7 @@
         compiler_params=pltpu.CompilerParams(
             collective_id=collective_id, has_side_effects=True, vmem_limit_bytes=56 << 20
         ),
-    )(grp, q, lse, kvo, kvp.reshape(4, P_SIZE, kvp.shape[1]), gm, *grads)
+    )(grp, q, lse, kvo, kvp, gm, *grads)
 
 
 def fold_kernel(
@@ -676,387 +676,446 @@
 
 
 CHUNKS = 4
-
-
-def start_kernel(
+FRONT = 13
+GATHER_SLOTS = 40
+SEGMENT = 4
+
+
+def front_kernel(
     tokens,
     vec,
     bup,
     own,
     wq,
-    prompts,
-    chip,
-    wpair,
+    block0,
+    block1,
+    block2,
+    mixed,
+    lse_ref,
+    whole0,
+    whole1,
+    whole2,
+    prompts_out,
+    chip_out,
+    q_out,
+    kvo_out,
+    kvp_out,
+    wq_out,
+    wkv_out,
     vec_out,
     bup_out,
     own_out,
     n1,
     vec_in,
-    z_sems,
-    y_sems,
-    d_sems,
-    w_sems,
-    s_sems,
+    prompts,
+    chip,
+    wpair,
+    q_all,
+    kvo_all,
+    kvp_all,
+    mix,
+    own_scalar,
+    zs,
+    zr,
+    ys,
+    yr,
+    ds,
+    dr,
+    ws,
+    wr,
+    ss,
+    sr,
+    gs,
+    gr_,
+    ms,
+    mr,
     l_sems,
+    o_sems,
 ):
     x, z, g, y, c = places()
     sib, over_y, over_x = {"gc": g ^ 1}, {"gc": g ^ 2}, {"dp": x ^ 1}
-    greet(all_partners() + [{"gc": g ^ 3}])
+    z_sems, y_sems, d_sems, w_sems, s_sems, g_sems = (
+        (zs, zr),
+        (ys, yr),
+        (ds, dr),
+        (ws, wr),
+        (ss, sr),
+        (gs, gr_),
+    )
+    blocks, wholes = (block0, block1, block2), (whole0, whole1, whole2)
     half_rows = wq.shape[0] // 2
     my_half = pl.ds(pl.multiple_of(x * half_rows, 16), half_rows)
-
-    small = []
-    for s in (1, 2, 3):
-        to = {"gr": z ^ s}
-        small.append(send(vec, vec_in.at[s], s_sems, s, to))
-        small.append(send(own, own_out.at[z], s_sems, 3 + s, to))
-        small.append(send(bup, bup_out.at[g], s_sems, 6 + s, {"gc": g ^ s}))
-    for copy in small:
-        copy.start()
-    own_out[z] = own[...]
-    bup_out[g] = bup[...]
-
-    w_local = pltpu.make_async_copy(wq.at[my_half], wpair.at[y, z, my_half], l_sems.at[0])
-    w_local.start()
-    w_gr = [
-        send(wq.at[my_half], wpair.at[y, z, my_half], w_sems, s, {"gr": z ^ s}) for s in (1, 2, 3)
-    ]
-    for copy in w_gr:
-        copy.start()
-
-    def w_step(s):
-        block = z ^ s
-        piece = wpair.at[y, block, my_half]
-        across = wpair.at[1 - y, block, my_half]
+    size = QROWS // CHUNKS
+    first_half = jnp.where(z == 0, 0, 1)
+    order = (z, z ^ 1, jnp.where(z < 2, 2, 1), jnp.where(z < 2, 3, 0))
+    above, below = {"gr": jnp.minimum(z + 1, 3)}, {"gr": jnp.maximum(z - 1, 0)}
+    inner = jnp.logical_and(z > 0, z < 3)
+
+    def line(part, sems, base, b):
         return (
-            send(piece, piece, w_sems, 4 + s, over_y),
-            send(piece, piece, w_sems, 8 + s, over_x),
-            send(across, across, w_sems, 12 + s, over_x),
-        )
-
-    for copy in small[0::3]:
-        copy.wait_recv()
-    total = vec[...]
-    for s in (1, 2, 3):
-        total = total + vec_in[s]
-    vec_out[...] = total
-
-    @pl.loop(0, QROWS // 128)
-    def _(i):
-        rows = pl.ds(pl.multiple_of(i * 128, 128), 128)
-        hidden = tokens[rows].astype(F32) + vec_out[0:1]
-        n1[rows] = norm_rows(hidden, vec_out[1:2], vec_out[2:3]).astype(BF)
-
-    to_chip = pltpu.make_async_copy(n1, chip.at[c], l_sems.at[1])
-    to_chip.start()
-    chip_send = send(n1, chip.at[c], s_sems, 10, sib)
-    chip_send.start()
-    is_prompt = z < 2
-
-    @pl.when(is_prompt)
-    def _():
-        local = pltpu.make_async_copy(n1, prompts.at[g, z], l_sems.at[2])
-        local.start()
-        local.wait()
-
-    w_local.wait()
-    for copy in w_step(0)[:2]:
-        copy.start()
-
-    rows = QROWS // CHUNKS
-
-    def item(column, half, k):
-        return prompts.at[column, half, pl.ds(k * rows, rows)]
-
-    def copies(half, k):
-        mine = item(g, half, k)
-        across = item(g ^ 2, half, k)
-        n = half * CHUNKS + k
-        return {
-            "up": send(mine, mine, z_sems, n, {"gr": jnp.minimum(z + 1, 3)}),
-            "down": send(
-                mine, mine, z_sems, n, {"gr": jnp.maximum(z - 1, 0)}, 2 * CHUNKS + k
+            (jnp.logical_and(z < 3, b <= z), send(part, part, sems, base + b, above)),
+            (
+                jnp.logical_and(z > 0, b >= z),
+                send(part, part, sems, base + b, below, base + 4 + b),
             ),
-            "y": send(mine, mine, y_sems, n, over_y),
-            "core": send(mine, mine, d_sems, n, sib),
-            "core2": send(across, across, d_sems, 2 * CHUNKS + n, sib),
-        }
-
-    first = jnp.where(z == 0, 0, 1)
-
-    def forward(step):
-        half = first if step < CHUNKS else 1 - first
-        k = step % CHUNKS
-        moves = copies(half, k)
-
-        @pl.when(half != z)
+        )
+
+    def pass_on(copies):
+        for goes, copy in copies:
+            pl.when(goes)(copy.start)
+
+    def passed_on(copies):
+        for goes, copy in copies:
+            pl.when(goes)(copy.wait_send)
+
+    local_copy = pltpu.make_async_copy
+
+    def small(kind, s):
+        if kind == 0:
+            return send(vec, vec_in.at[s], s_sems, s, {"gr": z ^ s})
+        if kind == 1:
+            return send(own, own_out.at[z], s_sems, 3 + s, {"gr": z ^ s})
+        return send(bup, bup_out.at[g], s_sems, 6 + s, {"gc": g ^ s})
+
+    def chip_send():
+        return send(n1, chip.at[c], s_sems, 10, sib)
+
+    def w_local():
+        return local_copy(wq.at[my_half], wpair.at[y, z, my_half], l_sems.at[0])
+
+    def w_line(s):
+        return line(wpair.at[y, order[s], my_half], w_sems, 0, order[s])
+
+    def w_gc(s):
+        piece = wpair.at[y, order[s], my_half]
+        return send(piece, piece, w_sems, 8 + s, over_y)
+
+    def w_dp(s):
+        piece = wpair.at[y, order[s], my_half]
+        return send(piece, piece, w_sems, 12 + s, over_x)
+
+    def w_dp_far(s):
+        piece = wpair.at[1 - y, order[s], my_half]
+        return send(piece, piece, w_sems, 16 + s, over_x)
+
+    def chunk(number):
+        return (first_half if number < CHUNKS else 1 - first_half), number % CHUNKS
+
+    def item(column, number):
+        half, k = chunk(number)
+        return prompts.at[column, half, pl.ds(k * size, size)]
+
+    def up(number):
+        half, k = chunk(number)
+        ref = item(g, number)
+        return send(ref, ref, z_sems, half * CHUNKS + k, {"gr": jnp.minimum(z + 1, 3)})
+
+    def down(number):
+        half, k = chunk(number)
+        ref = item(g, number)
+        return send(
+            ref,
+            ref,
+            z_sems,
+            half * CHUNKS + k,
+            {"gr": jnp.maximum(z - 1, 0)},
+            2 * CHUNKS + k,
+        )
+
+    def side(number):
+        half, k = chunk(number)
+        ref = item(g, number)
+        return send(ref, ref, y_sems, half * CHUNKS + k, over_y)
+
+    def core(number, far):
+        half, k = chunk(number)
+        ref = item(g ^ 2 if far else g, number)
+        return send(ref, ref, d_sems, far * 2 * CHUNKS + half * CHUNKS + k, sib)
+
+    def goes_up(number):
+        return jnp.logical_and(z < 3, chunk(number)[0] <= z)
+
+    def goes_down(number):
+        return jnp.logical_and(z == 1, chunk(number)[0] == 1)
+
+    def forward(number):
+        @pl.when(chunk(number)[0] != z)
         def _():
-            moves["up"].wait_recv()
-
-        @pl.when(jnp.logical_and(z < 3, half <= z))
+            up(number).wait_recv()
+
+        @pl.when(goes_up(number))
         def _():
-            moves["up"].start()
-
-        @pl.when(jnp.logical_and(z == 1, half == 1))
+            up(number).start()
+
+        @pl.when(goes_down(number))
         def _():
-            moves["down"].start()
-
-        moves["y"].start()
-        moves["core"].start()
-
-    def across(step):
-        half = first if step < CHUNKS else 1 - first
-        moves = copies(half, step % CHUNKS)
-        moves["y"].wait_recv()
-        moves["core2"].start()
-
-    for step in range(2 * CHUNKS):
-        forward(step)
-        if step >= 2:
-            across(step - 2)
-        if step in (1, 2, 3):
-            w_gr[step - 1].wait_recv()
-            one, two, _ = w_step(step)
-            one.start()
-            two.start()
-        if step in (4, 5, 6, 7):
-            one, _, three = w_step(step - 4)
-            one.wait_recv()
-            three.start()
-    across(2 * CHUNKS - 2)
-    across(2 * CHUNKS - 1)
-
-    for step in range(2 * CHUNKS):
-        half = first if step < CHUNKS else 1 - first
-        moves = copies(half, step % CHUNKS)
-        moves["core"].wait_recv()
-        moves["core2"].wait_recv()
-        moves["y"].wait_send()
-        moves["core"].wait_send()
-        moves["core2"].wait_send()
-
-        @pl.when(jnp.logical_and(z < 3, half <= z))
-        def _():
-            moves["up"].wait_send()
-
-        @pl.when(jnp.logical_and(z == 1, half == 1))
-        def _():
-            moves["down"].wait_send()
-
-    for copy in w_gr:
-        copy.wait_send()
-    for s in range(4):
-        one, two, three = w_step(s)
-        one.wait_send()
-        two.wait()
-        three.wait()
-    for i, copy in enumerate(small):
-        if i % 3 == 0:
-            copy.wait_send()
-        else:
-            copy.wait()
-    to_chip.wait()
-    chip_send.wait()
-
-
-def start_exchange(tokens, vec, bup, own, wq, collective_id):
-    any_space = pl.BlockSpec(memory_space=pl.ANY)
-    vmem = pl.BlockSpec(memory_space=pltpu.VMEM)
-
-    def dma(count):
-        return pltpu.SemaphoreType.DMA((count,))
-
-    def pair(count, extra=0):
-        return dma(count + extra), dma(count)
-
-    z_pair, y_pair, d_pair = pair(2 * CHUNKS, CHUNKS), pair(2 * CHUNKS), pair(4 * CHUNKS)
-    w_pair, s_pair = pair(16), pair(11)
-
-    def body(*refs):
-        main, sems = refs[:13], refs[13:]
-        start_kernel(*main, sems[0:2], sems[2:4], sems[4:6], sems[6:8], sems[8:10], sems[10])
-
-    return pl.pallas_call(
-        body,
-        name="start_exchange",
-        in_specs=[vmem, vmem, vmem, vmem, any_space],
-        out_specs=[any_space, any_space, any_space, vmem, vmem, vmem],
-        out_shape=[
-            jax.ShapeDtypeStruct((4, 2, QROWS, D), BF),
-            jax.ShapeDtypeStruct((2, QROWS, D), BF),
-            jax.ShapeDtypeStruct((2, 4) + wq.shape, BF),
-            jax.ShapeDtypeStruct(vec.shape, F32),
-            jax.ShapeDtypeStruct((4,) + bup.shape, F32),
-            jax.ShapeDtypeStruct((4,) + own.shape, jnp.int32),
-        ],
-        scratch_shapes=[pltpu.VMEM((QROWS, D), BF), pltpu.VMEM((4,) + vec.shape, F32)]
-        + [*z_pair, *y_pair, *d_pair, *w_pair, *s_pair, dma(3)],
-        compiler_params=pltpu.CompilerParams(
-            collective_id=collective_id, has_side_effects=True, vmem_limit_bytes=32 << 20
-        ),
-    )(tokens, vec, bup, own, wq)
-
-
-GATHER_SLOTS = 36
-
-
-def gather_steps(blocks, wholes, sems, l_sems):
-    x, z, g, y, c = places()
-    sib, over_y, over_x = {"gc": g ^ 1}, {"gc": g ^ 2}, {"dp": x ^ 1}
-    steps = []
-
-    def plan(a):
+            down(number).start()
+
+        side(number).start()
+        core(number, 0).start()
+
+    def across(number):
+        side(number).wait_recv()
+        core(number, 1).start()
+
+    def plan(a, s):
         block, whole = blocks[a], wholes[a]
-        rows = block.shape[0]
-        q = rows // 4
+        q = block.shape[0] // 4
         half = pl.ds(pl.multiple_of(x * 2 * q, 16), 2 * q)
         qa = pl.ds(pl.multiple_of(x * 2 * q, 16), q)
         qb = pl.ds(pl.multiple_of(x * 2 * q + q, 16), q)
+        qc = pl.ds(pl.multiple_of((1 - x) * 2 * q + q, 16), q)
         base = a * GATHER_SLOTS
-        local = pltpu.make_async_copy(block.at[half], whole.at[g, z, half], l_sems.at[a])
-        by_gr = [
-            send(block.at[half], whole.at[g, z, half], sems, base + s, {"gr": z ^ s})
-            for s in (1, 2, 3)
+        mine, far = whole.at[g, order[s]], whole.at[g ^ 2, order[s]]
+        o = base + 8 + 8 * s
+
+        def same(part, number, target):
+            return lambda: send(part, part, g_sems, o + number, target)
+
+        return {
+            "line": lambda: line(mine.at[half], g_sems, base, order[s]),
+            "ay": same(mine.at[qa], 0, over_y),
+            "ax": same(mine.at[qa], 1, over_x),
+            "afx": same(far.at[qa], 2, over_x),
+            "bx": same(mine.at[qb], 3, over_x),
+            "by": same(mine.at[qb], 4, over_y),
+            "bfy": same(mine.at[qc], 5, over_y),
+            "c1": same(mine, 6, sib),
+            "c2": same(far, 7, sib),
+        }
+
+    def own_block(a):
+        return local_copy(blocks[a], wholes[a].at[g, z], l_sems.at[4 + a])
+
+    def names(s):
+        return ("ay", "ax", "afx", "bx", "by", "bfy") if s else ("ay", "afx", "by", "bfy")
+
+    def relay(s):
+        @pl.when(inner)
+        def _():
+            for a in range(3):
+                copies = plan(a, s)["line"]()
+                copies[0][1].wait_recv()
+                pass_on(copies)
+
+
+    def gather_first(s):
+        for a in range(3):
+            m = plan(a, s)
+            if s:
+                pl.when(jnp.logical_not(inner))(m["line"]()[0][1].wait_recv)
+                m["bx"]().start()
+                m["ax"]().start()
+            else:
+                m["bfy"]().start()
+            m["ay"]().start()
+            m["by"]().start()
+
+    def gather_second(s):
+        for a in range(3):
+            m = plan(a, s)
+            m["ay"]().wait_recv()
+            m["afx"]().start()
+            if s:
+                m["bx"]().wait_recv()
+                m["bfy"]().start()
+
+    def gather_third(s):
+        for a in range(3):
+            m = plan(a, s)
+            if s:
+                m["ax"]().wait_recv()
+            for name in ("afx", "by", "bfy"):
+                m[name]().wait_recv()
+            m["c1"]().start()
+            m["c2"]().start()
+
+    def out_copies():
+        return [
+            local_copy(prompts, prompts_out, o_sems.at[0]),
+            local_copy(chip, chip_out, o_sems.at[1]),
+            local_copy(q_all, q_out, o_sems.at[2]),
+            local_copy(kvo_all, kvo_out, o_sems.at[3]),
+            local_copy(kvp_all, kvp_out, o_sems.at[4]),
         ]
 
-        def moves(s):
-            o = base + 4 + 8 * s
-            mine, far = whole.at[g, z ^ s], whole.at[g ^ 2, z ^ s]
-            return {
-                "ay": send(mine.at[qa], mine.at[qa], sems, o, over_y),
-                "ax": send(mine.at[qa], mine.at[qa], sems, o + 1, over_x),
-                "afx": send(far.at[qa], far.at[qa], sems, o + 2, over_x),
-                "bx": send(mine.at[qb], mine.at[qb], sems, o + 3, over_x),
-                "by": send(mine.at[qb], mine.at[qb], sems, o + 4, over_y),
-                "bfy": send(
-                    mine.at[pl.ds(pl.multiple_of((1 - x) * 2 * q + q, 16), q)],
-                    mine.at[pl.ds(pl.multiple_of((1 - x) * 2 * q + q, 16), q)],
-                    sems,
-                    o + 5,
-                    over_y,
-                ),
-                "c1": send(mine, mine, sems, o + 6, sib),
-                "c2": send(far, far, sems, o + 7, sib),
-            }
-
-        return local, by_gr, moves
-
-    plans = [plan(a) for a in range(len(blocks))]
+    def exchange(i):
+        cols = pl.ds(128 * i, 128)
+        return (
+            local_copy(mix.at[i, c], mixed.at[c, :, cols], l_sems.at[7 + i]),
+            send(mix.at[i, 1 - c], mixed.at[c, :, cols], (ms, mr), i, sib),
+        )
+
+    hooks = {i: [] for i in range(FRONT)}
 
     def begin():
-        for local, by_gr, _ in plans:
-            local.start()
-            for copy in by_gr:
-                copy.start()
-        for local, _, _ in plans:
-            local.wait()
-
-    def first(a, s):
-        def run():
-            _, by_gr, moves = plans[a]
-            if s:
-                by_gr[s - 1].wait_recv()
-            m = moves(s)
-            for name in ("ay", "bx", "ax", "by"):
-                m[name].start()
-
-        return run
-
-    def second(a, s):
-        def run():
-            m = plans[a][2](s)
-            m["ay"].wait_recv()
-            m["afx"].start()
-            m["bx"].wait_recv()
-            m["bfy"].start()
-
-        return run
-
-    def third(a, s):
-        def run():
-            m = plans[a][2](s)
-            for name in ("ax", "afx", "by", "bfy"):
-                m[name].wait_recv()
-            m["c1"].start()
-            m["c2"].start()
-
-        return run
-
-    def finish():
-        for _, by_gr, moves in plans:
-            for copy in by_gr:
-                copy.wait_send()
-            for s in range(4):
-                m = moves(s)
-                m["c1"].wait_recv()
-                m["c2"].wait_recv()
-                for copy in m.values():
-                    copy.wait_send()
-
-    order = [(a, s) for a in range(len(blocks)) for s in range(4)]
-    steps = [begin]
-    n = len(order)
-    for i in range(n + 4):
-        part = []
-        if i < n:
-            part.append(first(*order[i]))
-        if 2 <= i < n + 2:
-            part.append(second(*order[i - 2]))
-        if i >= 4:
-            part.append(third(*order[i - 4]))
-        steps.append(partial(lambda fs: [f() for f in fs], part))
-    steps.append(finish)
-    return steps
-
-
-def att_gather_kernel(count, grp_ref, q_ref, kvo_ref, kvp_ref, *refs):
-    blocks = refs[:count]
-    mixed, lse_ref = refs[count : count + 2]
-    wholes = refs[count + 2 : 2 * count + 2]
-    mix, sems_s, sems_r, l_sems, m_send, m_recv, m_local = refs[2 * count + 2 :]
-    p, j = pl.program_id(0), pl.program_id(1)
-    step = p * pl.num_programs(1) + j
-    x, z, g, y, c = places()
-
-    hooks = gather_steps(blocks, wholes, (sems_s, sems_r), l_sems)
-
-    @pl.when(step == 0)
-    def _():
-        greet(all_partners())
-
-    last = len(hooks) - 1
-    for i, hook in enumerate(hooks):
-        when = i * 23 // last
-        if i == last:
-            continue
-
-        @pl.when(step == when)
+        greet(all_partners() + [{"gc": g ^ 3}])
+        w_local().start()
+        for s in (1, 2, 3):
+            for kind in range(3):
+                small(kind, s).start()
+        w_local().wait()
+        pass_on(w_line(0))
+        own_out[z] = own[...]
+        bup_out[g] = bup[...]
+        for s in (1, 2, 3):
+            small(0, s).wait_recv()
+        vec_out[...] = (vec[...] + vec_in[1]) + (vec_in[2] + vec_in[3])
+
+        @pl.loop(0, CHUNKS)
+        def _(i):
+            rows = pl.ds(pl.multiple_of(i * size, size), size)
+            hidden = tokens[rows].astype(F32) + vec_out[0:1]
+            n1[rows] = norm_rows(hidden, vec_out[1:2], vec_out[2:3]).astype(BF)
+
+        @pl.when(z < 2)
         def _():
+            to = local_copy(n1, prompts.at[g, jnp.minimum(z, 1)], l_sems.at[2])
+            to.start()
+            to.wait()
+
+    def begin_chip():
+        local_copy(n1, chip.at[c], l_sems.at[1]).start()
+        chip_send().start()
+        w_gc(0).start()
+        w_dp(0).start()
+
+    hooks[0] += [begin, partial(forward, 0), begin_chip]
+    for i in range(1, 8):
+        hooks[i].append(partial(forward, i))
+    for i in range(2, 10):
+        hooks[i].append(partial(across, i - 2))
+
+    def w_pass(s):
+        copies = w_line(s)
+        copies[0][1].wait_recv()
+        pass_on(copies)
+        w_gc(s).start()
+        w_dp(s).start()
+
+    def w_across(s):
+        w_gc(s).wait_recv()
+        w_dp_far(s).start()
+
+    for s in (1, 2, 3):
+        hooks[s].append(partial(w_pass, s))
+    hooks[2].append(partial(w_across, 0))
+    hooks[3] += [partial(w_across, 1)]
+    hooks[4] += [partial(w_across, 2), partial(w_across, 3)]
+
+    def assemble():
+        for s in range(4):
+            w_dp(s).wait_recv()
+            w_dp_far(s).wait_recv()
+        local_copy(n1, chip.at[c], l_sems.at[1]).wait()
+        chip_send().wait_recv()
+        for s in (1, 2, 3):
+            small(1, s).wait_recv()
+        to = local_copy(own_out, own_scalar, l_sems.at[3])
+        to.start()
+        for head in range(6):
+            p, b = head // 2, head % 2
+            at_q = 128 * p + (0 if b else 64)
+            at_k = 256 * p + (128 if b else 64)
+            at_v = 256 * p + (192 if b else 0)
+            start = (head % 3) * 192
+            for r in range(4):
+                rows = slice(192 * r, 192 * r + 192)
+                source = wpair.at[head // 3, r]
+                wq_out[rows, at_q : at_q + HD] = source[:, start : start + HD]
+                wkv_out[rows, at_k : at_k + HD] = source[:, start + HD : start + 2 * HD]
+                wkv_out[rows, at_v : at_v + HD] = source[:, start + 2 * HD : start + 3 * HD]
+        to.wait()
+
+    hooks[5].append(assemble)
+
+    def project(number):
+        core(number, 0).wait_recv()
+        core(number, 1).wait_recv()
+        half, k = chunk(number)
+        w = wkv_out[...]
+        rows = jnp.concatenate(
+            [prompts[i, half, pl.ds(k * size, size)] for i in range(4)], axis=0
+        )
+        kv = nn(rows, w).astype(BF)
+        to = pl.ds(pl.multiple_of(half * QROWS + k * size, size), size)
+        for i in range(4):
+            for p in range(3):
+                kvp_all[p, i, to] = kv[size * i : size * i + size, 256 * p : 256 * p + 256]
+        mine = chip[number // CHUNKS, pl.ds((number % CHUNKS) * size, size)]
+        kvo = nn(mine, w).astype(BF)
+        queries = (nn(mine, wq_out[...]) * 0.125).astype(BF)
+        to = pl.ds(number * size, size)
+        for p in range(3):
+            kvo_all[p, to] = kvo[:, 256 * p : 256 * p + 256]
+            q_all[p, to] = queries[:, 128 * p : 128 * p + 128]
+
+    for i in range(8):
+        hooks[5 + i].append(partial(project, i))
+
+    def begin_gather():
+        for a in range(3):
+            own_block(a).start()
+        for a in range(3):
+            own_block(a).wait()
+            pass_on(plan(a, 0)["line"]())
+
+    hooks[7].insert(1, begin_gather)
+    hooks[8].append(partial(gather_first, 0))
+    hooks[10].append(partial(gather_second, 0))
+    between = [[] for _ in range(24 // SEGMENT + 1)]
+    last = len(between) - 1
+    between[0] += [lambda: [copy.start() for copy in out_copies()], partial(gather_third, 0)]
+    hooks[11].append(partial(relay, 1))
+    for slot, stage, s in (
+        (0, relay, 2),
+        (1, relay, 3),
+        (1, gather_first, 1),
+        (2, gather_first, 2),
+        (2, gather_second, 1),
+        (4, gather_first, 3),
+        (4, gather_second, 2),
+        (4, gather_third, 1),
+        (5, gather_second, 3),
+        (5, gather_third, 2),
+        (6, gather_third, 3),
+    ):
+        between[slot].append(partial(stage, s))
+
+    for number in range(FRONT):
+        for hook in hooks[number]:
             hook()
 
-    group = grp_ref[j]
     low = lax.broadcasted_iota(jnp.int32, (CL, 128), 1) < 64
-    zero = jnp.zeros((CL, 128), BF)
-    q = q_ref[...]
-    q_parts = (jnp.where(low, zero, q), jnp.where(low, q, zero))
-
-    def store(mixes, sums):
+
+    def parts(turn):
+        p, j = turn // 8, turn % 8
+        shard = 2 * y + j // 4
+        group = jnp.where(
+            z < 2, shard, own_scalar[shard, 0, jnp.maximum(z - 2, 0) * 4 + j % 4]
+        )
+        rows_j = pl.ds(pl.multiple_of(j * CL, CL), CL)
+        zero = jnp.zeros((CL, 128), BF)
+        q = q_all[p, rows_j]
+        return p, j, group, rows_j, (jnp.where(low, zero, q), jnp.where(low, q, zero))
+
+    def store(p, j, mixes, sums):
         mix[p, j // 4, pl.ds(pl.multiple_of((j % 4) * CL, CL), CL)] = jnp.where(
             low, mixes[0], mixes[1]
         ).astype(BF)
         flat = jnp.where(low, sums[0], sums[1]).T
-        lse_ref[0, 0, 0:1] = flat[0:1]
-        lse_ref[0, 0, 1:2] = flat[64:65]
-
-    @pl.when(z >= 2)
-    def _():
+        lse_ref[p, j, 0:1] = flat[0:1]
+        lse_ref[p, j, 1:2] = flat[64:65]
+
+    def cont_turn(turn, carried):
+        p, j, group, rows_j, q_parts = parts(turn)
         row = lax.broadcasted_iota(jnp.int32, (CL, CL), 0)
         near_ok = lax.broadcasted_iota(jnp.int32, (CL, CL), 1) <= row
         mixes, sums = [], []
         for h in range(2):
             cols = slice(128 * h, 128 * h + 128)
-            kv = kvp_ref[group, :, cols]
-            kvo = kvo_ref[:, cols]
+            kv = kvp_all[p, group, :, cols]
+            kvo = kvo_all[p, rows_j, cols]
             far = nt(q_parts[h], kv)
             near = jnp.where(near_ok, nt(q_parts[h], kvo), negative)
             top = jnp.maximum(
@@ -1067,10 +1126,11 @@
             total = jnp.sum(far, axis=1, keepdims=True) + jnp.sum(near, axis=1, keepdims=True)
             mixes.append((nn(far.astype(BF), kv) + nn(near.astype(BF), kvo)) / total)
             sums.append(jnp.broadcast_to(top + jnp.log(total), (CL, 128)))
-        store(mixes, sums)
-
-    @pl.when(z < 2)
-    def _():
+        store(p, j, mixes, sums)
+        return carried
+
+    def prompt_turn(turn, carried):
+        p, j, group, rows_j, q_parts = parts(turn)
         limit = z * QROWS + (j % (QROWS // CL)) * CL
         row = lax.broadcasted_iota(jnp.int32, (CL, P_SIZE), 0)
         key = lax.broadcasted_iota(jnp.int32, (CL, P_SIZE), 1)
@@ -1078,75 +1138,139 @@
         mixes, sums = [], []
         for h in range(2):
             cols = slice(128 * h, 128 * h + 128)
-            kv = kvp_ref[group, :, cols]
+            kv = kvp_all[p, group, :, cols]
             far = jnp.where(allowed, nt(q_parts[h], kv), negative)
             top = jnp.max(far, axis=1, keepdims=True)
             far = jnp.exp(far - top)
             total = jnp.sum(far, axis=1, keepdims=True)
             mixes.append(nn(far.astype(BF), kv) / total)
             sums.append(jnp.broadcast_to(top + jnp.log(total), (CL, 128)))
-        store(mixes, sums)
-
-    def exchange(i):
-        cols = pl.ds(128 * i, 128)
-        return (
-            pltpu.make_async_copy(mix.at[i, c], mixed.at[c, :, cols], m_local.at[i]),
-            send(mix.at[i, 1 - c], mixed.at[c, :, cols], (m_send, m_recv), i, {"gc": g ^ 1}),
-        )
-
+        store(p, j, mixes, sums)
+        return carried
+
+    for segment in range(last):
+        for hook in between[segment]:
+            hook()
+        turns = (segment * SEGMENT, segment * SEGMENT + SEGMENT)
+
+        @pl.when(z >= 2)
+        def _():
+            lax.fori_loop(*turns, cont_turn, 0)
+
+        @pl.when(z < 2)
+        def _():
+            lax.fori_loop(*turns, prompt_turn, 0)
+
+        if turns[1] % 8 == 0:
+            for copy in exchange(turns[1] // 8 - 1):
+                copy.start()
+    for hook in between[last]:
+        hook()
+
+    for number in range(8):
+        side(number).wait_send()
+        core(number, 0).wait_send()
+        core(number, 1).wait_send()
+
+        @pl.when(goes_up(number))
+        def _():
+            up(number).wait_send()
+
+        @pl.when(goes_down(number))
+        def _():
+            down(number).wait_send()
+
+    for s in range(4):
+        if s:
+            small(0, s).wait_send()
+            small(1, s).wait_send()
+            small(2, s).wait()
+        passed_on(w_line(s))
+        w_gc(s).wait_send()
+        w_dp(s).wait_send()
+        w_dp_far(s).wait_send()
+    chip_send().wait_send()
+    for s in range(4):
+        for a in range(3):
+            m = plan(a, s)
+            passed_on(m["line"]())
+            for name in names(s):
+                m[name]().wait_send()
+            m["c1"]().wait()
+            m["c2"]().wait()
     for i in range(3):
-
-        @pl.when(step == 8 * i + 7)
-        def _():
-            for copy in exchange(i):
-                copy.start()
-
-    @pl.when(step == 23)
-    def _():
-        hooks[last]()
-        for i in range(3):
-            for copy in exchange(i):
-                copy.wait()
-
-
-def attend_gather(grp, q, kvo, kvp, blocks, collective_id):
-    rows = q.shape[0]
-    count = len(blocks)
+        for copy in exchange(i):
+            copy.wait()
+    for copy in out_copies():
+        copy.wait()
+
+
+def front(tokens, vec, bup, own, wq, blocks, collective_id):
     any_space = pl.BlockSpec(memory_space=pl.ANY)
-    slots = GATHER_SLOTS * count
+    vmem = pl.BlockSpec(memory_space=pltpu.VMEM)
+    rows = 2 * QROWS
+
+    def dma(count):
+        return pltpu.SemaphoreType.DMA((count,))
+
+    slots = 3 * GATHER_SLOTS
+    heads = [(3, rows, 128), (3, rows, 256), (3, 4, P_SIZE, 256)]
     return pl.pallas_call(
-        partial(att_gather_kernel, count),
-        name="attend_gather",
-        grid_spec=pltpu.PrefetchScalarGridSpec(
-            num_scalar_prefetch=1,
-            grid=(3, rows // CL),
-            in_specs=[
-                pl.BlockSpec((CL, 128), lambda p, j, *_: (j, p)),
-                pl.BlockSpec((CL, 256), lambda p, j, *_: (j, p)),
-                pl.BlockSpec((4, P_SIZE, 256), lambda p, j, *_: (0, 0, p)),
-            ]
-            + [any_space] * count,
-            out_specs=[any_space, pl.BlockSpec((1, 1, 2, 128), lambda p, j, *_: (p, j, 0, 0))]
-            + [any_space] * count,
-            scratch_shapes=[
-                pltpu.VMEM((3, 2, QROWS, 128), BF),
-                pltpu.SemaphoreType.DMA((slots,)),
-                pltpu.SemaphoreType.DMA((slots,)),
-                pltpu.SemaphoreType.DMA((count,)),
-                pltpu.SemaphoreType.DMA((3,)),
-                pltpu.SemaphoreType.DMA((3,)),
-                pltpu.SemaphoreType.DMA((3,)),
-            ],
-        ),
+        front_kernel,
+        name="front",
+        in_specs=[vmem, vmem, vmem, vmem] + [any_space] * 4,
+        out_specs=[any_space, vmem]
+        + [any_space] * 8
+        + [vmem] * 5,
         out_shape=[
             jax.ShapeDtypeStruct((2, QROWS, 384), BF),
             jax.ShapeDtypeStruct((3, rows // CL, 2, 128), F32),
         ]
-        + [jax.ShapeDtypeStruct((4, 4) + block.shape, BF) for block in blocks],
+        + [jax.ShapeDtypeStruct((4, 4) + block.shape, BF) for block in blocks]
+        + [
+            jax.ShapeDtypeStruct((4, 2, QROWS, D), BF),
+            jax.ShapeDtypeStruct((2, QROWS, D), BF),
+        ]
+        + [jax.ShapeDtypeStruct(shape, BF) for shape in heads]
+        + [
+            jax.ShapeDtypeStruct((D, 384), BF),
+            jax.ShapeDtypeStruct((D, D), BF),
+            jax.ShapeDtypeStruct(vec.shape, F32),
+            jax.ShapeDtypeStruct((4,) + bup.shape, F32),
+            jax.ShapeDtypeStruct((4,) + own.shape, jnp.int32),
+        ],
+        scratch_shapes=[
+            pltpu.VMEM((QROWS, D), BF),
+            pltpu.VMEM((4,) + vec.shape, F32),
+            pltpu.VMEM((4, 2, QROWS, D), BF),
+            pltpu.VMEM((2, QROWS, D), BF),
+            pltpu.VMEM((2, 4) + wq.shape, BF),
+        ]
+        + [pltpu.VMEM(shape, BF) for shape in heads]
+        + [
+            pltpu.VMEM((3, 2, QROWS, 128), BF),
+            pltpu.SMEM((4,) + own.shape, jnp.int32),
+            dma(3 * CHUNKS),
+            dma(2 * CHUNKS),
+            dma(2 * CHUNKS),
+            dma(2 * CHUNKS),
+            dma(4 * CHUNKS),
+            dma(4 * CHUNKS),
+            dma(20),
+            dma(20),
+            dma(11),
+            dma(11),
+            dma(slots),
+            dma(slots),
+            dma(3),
+            dma(3),
+            dma(10),
+            dma(5),
+        ],
         compiler_params=pltpu.CompilerParams(
-            collective_id=collective_id, has_side_effects=True, vmem_limit_bytes=40 << 20
+            collective_id=collective_id, has_side_effects=True, vmem_limit_bytes=56 << 20
         ),
-    )(grp, q, kvo, kvp.reshape(4, P_SIZE, kvp.shape[1]), *blocks)
+    )(tokens, vec, bup, own, wq, *blocks)
 
 
 def tail_kernel(
@@ -1638,12 +1762,26 @@
         vec = lax.dynamic_update_slice(jnp.zeros((8, D), F32), packed, (0, z * packed.shape[1]))
         bup = jnp.broadcast_to(fc1_bias.astype(F32), (8, fc1_bias.shape[0]))
         own = jnp.broadcast_to(jnp.pad(cont_group, (0, 120)), (8, 128))
-        n1_prompt, n1_chip, w_pair, vectors, b_up, owners = start_exchange(
-            tokens, vec, bup, own, qkv_weight, 1
-        )
-        n1_prompt = n1_prompt.reshape(4 * P_SIZE, D)
+        (
+            mixed,
+            lse_rows,
+            w_out,
+            w_up,
+            w_down,
+            n1_prompt,
+            n1_chip,
+            q,
+            kvo,
+            kvp,
+            w_q,
+            w_kv,
+            vectors,
+            b_up,
+            owners,
+        ) = front(
+            tokens, vec, bup, own, qkv_weight, [out_weight, fc1_weight, fc2_weight], 1
+        )
         n1_chip = n1_chip.reshape(2 * QROWS, D)
-        w_qkv = w_pair.reshape(2, D, 576)
         owners = owners[:, 0, :8]
     else:
         vectors = lax.all_gather(packed, "gr", axis=1, tiled=True)
@@ -1672,16 +1810,10 @@
         )
         n1_col = lax.all_gather(n1, "gr", axis=0, tiled=True)[:P_SIZE]
         n1_prompt = lax.all_gather(n1_col, "gc", axis=0, tiled=True)
-    w_q, w_kv = head_layout(w_qkv)
-
-    kvp = nn(n1_prompt, w_kv).astype(BF)
-    kvo = nn(n1_chip, w_kv).astype(BF)
-    q = (nn(n1_chip, w_q) * 0.125).astype(BF)
-    if n_dp == 2:
-        mixed, lse_rows, w_out, w_up, w_down = attend_gather(
-            grp, q, kvo, kvp, [out_weight, fc1_weight, fc2_weight], 2
-        )
-    else:
+        w_q, w_kv = head_layout(w_qkv)
+        kvp = nn(n1_prompt, w_kv).astype(BF)
+        kvo = nn(n1_chip, w_kv).astype(BF)
+        q = (nn(n1_chip, w_q) * 0.125).astype(BF)
         w_out = lax.all_gather(out_weight, ("gc", "gr"))
         w_up = lax.all_gather(fc1_weight, ("gc", "gr"))
         w_down = lax.all_gather(fc2_weight, ("gc", "gr"))

time: 424 us -> 394 us (0.929)
  local copies, waits for them, and re-layouts: 44.2 us -> 16.7 us
  matrix products: 13.8 us -> 0 us
  Pallas kernels: 361 us -> 368 us
    unnamed x85 -> x31, local copies, waits for them, and re-layouts: 27.3 us -> 6.81 us
    pallas_call x1, Pallas kernels: 77.6 us -> 93.1 us  [attend_back_scatter(): pl.pallas_call(partial(att_scatter_kernel, count), name='attend_back_scat...]
    dot_general x3 -> x0, matrix products: 13.8 us -> none  [nn(): lax.dot_general(a, b, (((1,), (0,)), ((), ())), preferred_element_type=F32)]
    pallas_call x2 -> x1, Pallas kernels: 138 us -> 132 us  [front(): pl.pallas_call(front_kernel, name='front', in_specs=[vmem, vmem, vmem, vm...]
where the time goes in v6:
time: 394 us; the launch traced here: 390 us
  Pallas kernels  368 us (93%)
  local copies, waits for them, and re-layouts  16.7 us (4%)
    pallas_call x1, Pallas kernels, front(): pl.pallas_call(front_kernel, name='front', in_specs=[vmem, vmem, vmem, vm...  132 us
    pallas_call x1, Pallas kernels, attend_back_scatter(): pl.pallas_call(partial(att_scatter_kernel, count), name='attend_back_scat...  93.1 us
    pallas_call x1, Pallas kernels, tail_exchange(): pl.pallas_call(tail_kernel, name='tail_exchange', in_specs=[any_space, an...  83.2 us
    pallas_call x1, Pallas kernels, middle(): pl.pallas_call(middle_kernel, name='middle', in_specs=[vmem, vmem, any_sp...  34.7 us
    pallas_call x1, Pallas kernels, fold_prompts(): pl.pallas_call(fold_kernel, name='fold_prompts', grid_spec=pltpu.Prefetch...  25.7 us

profile of v6, /device:TPU:0, one launch (start us, length us, event | category | flops | bytes accessed | tf_op | source)
XLA Modules:
  0.0 389.8 jit_solution(12663897033619537445)
XLA Ops:
  0.7 0.7 stack.25
  1.3 0.7 stack.26
  2.0 0.7 stack.27
  2.6 0.7 stack.28
  3.3 0.7 stack.29
  3.9 0.7 stack.30
  4.6 0.7 stack.31
  5.3 0.3 dynamic_update_slice.3.vec
  5.6 0.0 copy-start.12
  5.6 1.3 broadcast_in_dim.13.bup
  6.9 0.7 pad.4
  7.6 0.6 broadcast_in_dim.14.own
  8.2 0.0 copy-done.12
  8.2 131.8 %front.1 = (bf16[2,512,384]{2,1,0:T(8,128)(2,1)}, f32[3,8,2,128]{3,2,1,0:T(2,128)}, bf16[4,4,192,192]{3,2,1,0:T(8,128)(2,1)}, bf16[4,4,192,768]{3,2,1,0:T(8,128)...) custom-call(bf16[512,768]{1,0:T(8,128)(2,1)} %tokens.5, ...), custom_call_target="tpu_custom_call" | custom-call | tf_op jit(solution)/shard_map/front/pallas_call | solution.py:1218
  140.0 34.7 %middle.1 = (bf16[512,768]{1,0:T(8,128)(2,1)}, f32[512,768]{1,0:T(8,128)}, bf16[4,768,768]{2,1,0:T(8,128)(2,1)}, bf16[4,768,768]{2,1,0:T(8,128)(2,1)}, bf16[4,4,...) custom-call(bf16[2,512,384]{2,1,0:T(8,128)(2,1)} %get-tuple-element.49.mixed, ...), custom_call_target="tpu_custom_call" | custom-call | tf_op jit(solution)/shard_map/middle/pallas_call | solution.py:1657
  174.7 0.7 slice_reduce_fusion.1
  175.4 0.1 reshape_squeeze.3
  175.5 0.1 reshape.98
  175.6 0.1 broadcast_in_dim.15
  175.7 0.1 reshape.97
  175.8 0.5 broadcast_select_fusion.grp_ref
  176.3 0.0 copy-start.3
  176.3 0.0 copy-start.5
  176.3 0.0 copy-start.8
  176.3 93.1 %attend_back_scatter.1 = (bf16[1024,384]{1,0:T(8,128)(2,1)}, bf16[1024,768]{1,0:T(8,128)(2,1)}, bf16[8,1024,768]{2,1,0:T(8,128)(2,1)}, f32[192,768]{1,0:T(8,128)...) custom-call(s32[8]{0:T(128)} %broadcast_select_fusion.grp_ref, bf16[3,1024,128]{2,1,0:T(8,128)(2,1)} %get-tuple-element.57.q_ref, ...), custom_call_target="tpu_custom_call" | custom-call | tf_op jit(solution)/shard_map/attend_back_scatter/pallas_call | solution.py:532
  269.4 0.0 copy-done.3
  269.4 0.0 copy-done.5
  269.4 0.0 copy-done.8
  269.5 0.0 copy-start.2
  269.5 1.4 copy-done.2
  270.9 0.0 copy-start.4
  270.9 1.1 copy-done.4
  272.0 0.0 copy-start
  272.0 0.0 copy-start.1
  272.0 0.0 copy-start.6
  272.0 0.0 copy-start.7
  272.0 25.7 %fold_prompts.1 = (bf16[4,1024,768]{2,1,0:T(8,128)(2,1)}, bf16[1024,768]{1,0:T(8,128)(2,1)S(1)}, bf16[2,768,576]{2,1,0:T(8,128)(2,1)}) custom-call(s32[8]{0:T(128)S(1)} %copy-done.8, bf16[8,1024,768]{2,1,0:T(8,128)(2,1)} %get-tuple-element.65.dkv_ref, bf16[1024,768]{1,0:T(8,128)(2,1)S(1)} %copy-done.2, bf16[1024,384]{1,0:T(8,128)(2,1)S(1)} %copy-done.4, ...), custom_call_target="tpu_custom_call" | custom-call | tf_op jit(solution)/shard_map/fold_prompts/pallas_call | solution.py:634
  297.7 0.0 copy-done
  297.7 0.0 copy-done.1
  297.7 0.0 copy-done.6
  297.7 0.0 copy-done.7
  297.8 83.2 %tail_exchange.1 = (f32[512,768]{1,0:T(8,128)S(1)}, f32[16,768]{1,0:T(8,128)S(1)}, f32[192,576]{1,0:T(8,128)S(1)}) custom-call(bf16[4,2,512,768]{3,2,1,0:T(8,128)(2,1)} %bitcast.20, bf16[2,512,768]{2,1,0:T(8,128)(2,1)S(1)} %bitcast.18, bf16[2,4,192,576]{3,2,1,0:T(8,128)(2,1)} %bitcast.25, f32[512,768]{1,0:T(8,128)S(1)} %copy-done.1, ...), custom_call_target="tpu_custom_call" | custom-call | tf_op jit(solution)/shard_map/tail_exchange/pallas_call | solution.py:1476
  380.9 0.1 reshape.107
  381.0 0.6 constant_dynamic-slice_fusion.6
  381.6 0.6 dynamic-slice_reduce_fusion
  382.3 0.6 slice_reduce_fusion
  384.2 0.0 copy-start.11
  384.2 0.0 copy-start.10
  384.2 1.1 copy.38
  385.3 0.0 copy-start.9
  385.3 0.8 copy.39
  386.1 0.0 copy-done.11
  386.1 0.7 copy.40
  386.8 0.0 copy-done.10
  386.8 0.8 copy.41
  387.6 0.0 copy-done.9
  387.6 0.8 copy.42
  (7 shorter events, 0.1 us)
Async XLA Ops:
  5.6 2.6 copy-start.12
  176.3 93.1 %copy-start.3 = (bf16[768,768]{1,0:T(8,128)(2,1)S(1)}, bf16[768,768]{1,0:T(8,128)(2,1)}, u32[]{:S(2)}) copy-start(bf16[768,768]{1,0:T(8,128)(2,1)} %get-tuple-element.71.w_kv) | copy-start | bytes 3538948
  176.3 93.2 %copy-start.5 = (bf16[768,384]{1,0:T(8,128)(2,1)S(1)}, bf16[768,384]{1,0:T(8,128)(2,1)}, u32[]{:S(2)}) copy-start(bf16[768,384]{1,0:T(8,128)(2,1)} %get-tuple-element.70.w_q) | copy-start | bytes 1769476
  176.3 93.2 %copy-start.8 = (s32[8]{0:T(128)S(1)}, s32[8]{0:T(128)}, u32[]{:S(2)}) copy-start(s32[8]{0:T(128)} %broadcast_select_fusion.grp_ref) | copy-start | bytes 100
  269.5 1.4 copy-start.2
  270.9 1.1 copy-start.4
  272.0 25.7 %copy-start = (bf16[512,768]{1,0:T(8,128)(2,1)S(1)}, bf16[512,768]{1,0:T(8,128)(2,1)}, u32[]{:S(2)}) copy-start(bf16[512,768]{1,0:T(8,128)(2,1)} %tokens.5) | copy-start | bytes 2359300
  272.0 25.7 %copy-start.1 = (f32[512,768]{1,0:T(8,128)S(1)}, f32[512,768]{1,0:T(8,128)}, u32[]{:S(2)}) copy-start(f32[512,768]{1,0:T(8,128)} %get-tuple-element.75.grad_h2) | copy-start | bytes 4718596
  272.0 25.7 %copy-start.6 = (f32[8,768]{1,0:T(8,128)S(1)}, f32[8,768]{1,0:T(8,128)}, u32[]{:S(2)}) copy-start(f32[8,768]{1,0:T(8,128)} %get-tuple-element.53.vec) | copy-start | bytes 73732
  272.0 25.7 %copy-start.7 = (f32[16,768]{1,0:T(8,128)S(1)}, f32[16,768]{1,0:T(8,128)}, u32[]{:S(2)}) copy-start(f32[16,768]{1,0:T(8,128)} %get-tuple-element.76.sums) | copy-start | bytes 147460
  384.2 1.9 copy-start.11
  384.2 2.6 copy-start.10
  385.3 2.3 copy-start.9

commit v7 on v6

--- a/solution.py
+++ b/solution.py
@@ -569,103 +569,6 @@
             collective_id=collective_id, has_side_effects=True, vmem_limit_bytes=56 << 20
         ),
     )(grp, q, lse, kvo, kvp, gm, *grads)
-
-
-def fold_kernel(
-    grp_ref,
-    dkv_ref,
-    dkvo_ref,
-    dq_ref,
-    n1p_ref,
-    n1c_ref,
-    w_q,
-    w_kv,
-    part_ref,
-    chip_ref,
-    dw_ref,
-    acc,
-    wkt,
-    wqt,
-    dkvw,
-    dqw,
-):
-    t = pl.program_id(0)
-
-    @pl.when(t == 0)
-    def _():
-        wkt[...] = w_kv[...].T
-        wqt[...] = w_q[...].T
-        dkvw[...] = jnp.zeros_like(dkvw)
-        dqw[...] = jnp.zeros_like(dqw)
-
-    acc[...] = jnp.zeros_like(acc)
-    for j in range(8):
-        acc[grp_ref[j]] += dkv_ref[j].astype(F32)
-    low = acc[...].astype(BF).reshape(512, D)
-    part_ref[...] = nn(low, wkt[...]).astype(BF).reshape(4, CL, D)
-    dkvo = dkvo_ref[...]
-    dq = dq_ref[...]
-    chip_ref[...] = (nn(dq, wqt[...]) + nn(dkvo, wkt[...])).astype(BF)
-    n1c = n1c_ref[...]
-    rows = jnp.concatenate([n1p_ref[...].reshape(512, D), n1c], axis=0)
-    dkvw[...] += tn(rows, jnp.concatenate([low, dkvo], axis=0))
-    dqw[...] += tn(n1c, dq)
-
-    @pl.when(t == pl.num_programs(0) - 1)
-    def _():
-        for head in range(6):
-            p, b = head // 2, head % 2
-            at_q = 128 * p + (0 if b else 64)
-            at_k = 256 * p + (128 if b else 64)
-            at_v = 256 * p + (192 if b else 0)
-            pieces = (
-                dqw[:, at_q : at_q + HD],
-                dkvw[:, at_k : at_k + HD],
-                dkvw[:, at_v : at_v + HD],
-            )
-            for i, piece in enumerate(pieces):
-                at = (head % 3) * 192 + HD * i
-                dw_ref[head // 3, :, at : at + HD] = piece.astype(BF)
-
-
-def fold_prompts(grp, dkv, dkvo, dq, n1_prompt, n1_chip, w_q, w_kv):
-    tile = CL
-    groups = pl.BlockSpec((4, tile, D), lambda i, *_: (0, i, 0))
-    return pl.pallas_call(
-        fold_kernel,
-        name="fold_prompts",
-        grid_spec=pltpu.PrefetchScalarGridSpec(
-            num_scalar_prefetch=1,
-            grid=(P_SIZE // tile,),
-            in_specs=[
-                pl.BlockSpec((8, tile, D), lambda i, *_: (0, i, 0)),
-                pl.BlockSpec((tile, D), lambda i, *_: (i, 0)),
-                pl.BlockSpec((tile, 384), lambda i, *_: (i, 0)),
-                groups,
-                pl.BlockSpec((tile, D), lambda i, *_: (i, 0)),
-                pl.BlockSpec((D, 384), lambda i, *_: (0, 0)),
-                pl.BlockSpec((D, D), lambda i, *_: (0, 0)),
-            ],
-            out_specs=[
-                groups,
-                pl.BlockSpec((tile, D), lambda i, *_: (i, 0)),
-                pl.BlockSpec((2, D, 576), lambda i, *_: (0, 0, 0)),
-            ],
-            scratch_shapes=[
-                pltpu.VMEM((4, tile, D), F32),
-                pltpu.VMEM((D, D), BF),
-                pltpu.VMEM((384, D), BF),
-                pltpu.VMEM((D, D), F32),
-                pltpu.VMEM((D, 384), F32),
-            ],
-        ),
-        out_shape=[
-            jax.ShapeDtypeStruct((4, P_SIZE, D), BF),
-            jax.ShapeDtypeStruct((2 * QROWS, D), BF),
-            jax.ShapeDtypeStruct((2, D, 576), BF),
-        ],
-        compiler_params=pltpu.CompilerParams(vmem_limit_bytes=48 << 20),
-    )(grp, dkv, dkvo, dq, n1_prompt.reshape(4, P_SIZE, D), n1_chip, w_q, w_kv)
 
 
 def norm_rows(hidden, gain, shift):
@@ -880,6 +783,7 @@
             "bx": same(mine.at[qb], 3, over_x),
             "by": same(mine.at[qb], 4, over_y),
             "bfy": same(mine.at[qc], 5, over_y),
+            "bfx": same(far.at[qb], 5, over_x),
             "c1": same(mine, 6, sib),
             "c2": same(far, 7, sib),
         }
@@ -888,7 +792,7 @@
         return local_copy(blocks[a], wholes[a].at[g, z], l_sems.at[4 + a])
 
     def names(s):
-        return ("ay", "ax", "afx", "bx", "by", "bfy") if s else ("ay", "afx", "by", "bfy")
+        return ("ay", "ax", "afx", "bx", "by", "bfy") if s else ("ay", "afx", "by", "bfx")
 
     def relay(s):
         @pl.when(inner)
@@ -906,8 +810,6 @@
                 pl.when(jnp.logical_not(inner))(m["line"]()[0][1].wait_recv)
                 m["bx"]().start()
                 m["ax"]().start()
-            else:
-                m["bfy"]().start()
             m["ay"]().start()
             m["by"]().start()
 
@@ -919,13 +821,14 @@
             if s:
                 m["bx"]().wait_recv()
                 m["bfy"]().start()
+            else:
+                m["by"]().wait_recv()
+                m["bfx"]().start()
 
     def gather_third(s):
         for a in range(3):
             m = plan(a, s)
-            if s:
-                m["ax"]().wait_recv()
-            for name in ("afx", "by", "bfy"):
+            for name in ("ax", "afx", "by", "bfy") if s else ("afx", "bfx"):
                 m[name]().wait_recv()
             m["c1"]().start()
             m["c2"]().start()
@@ -1053,31 +956,41 @@
     for i in range(8):
         hooks[5 + i].append(partial(project, i))
 
-    def begin_gather():
+    def own_first():
         for a in range(3):
             own_block(a).start()
+
+    def own_down():
         for a in range(3):
             own_block(a).wait()
-            pass_on(plan(a, 0)["line"]())
-
-    hooks[7].insert(1, begin_gather)
+            goes, copy = plan(a, 0)["line"]()[1]
+            pl.when(goes)(copy.start)
+
+    def own_up():
+        for a in range(3):
+            goes, copy = plan(a, 0)["line"]()[0]
+            pl.when(goes)(copy.start)
+
+    hooks[0].append(own_first)
+    hooks[1].append(own_down)
+    hooks[9].append(own_up)
     hooks[8].append(partial(gather_first, 0))
     hooks[10].append(partial(gather_second, 0))
     between = [[] for _ in range(24 // SEGMENT + 1)]
     last = len(between) - 1
     between[0] += [lambda: [copy.start() for copy in out_copies()], partial(gather_third, 0)]
-    hooks[11].append(partial(relay, 1))
+    hooks[10].append(partial(relay, 1))
+    hooks[12].append(partial(relay, 2))
     for slot, stage, s in (
-        (0, relay, 2),
-        (1, relay, 3),
-        (1, gather_first, 1),
-        (2, gather_first, 2),
-        (2, gather_second, 1),
-        (4, gather_first, 3),
-        (4, gather_second, 2),
-        (4, gather_third, 1),
-        (5, gather_second, 3),
-        (5, gather_third, 2),
+        (0, relay, 3),
+        (0, gather_first, 1),
+        (1, gather_first, 2),
+        (1, gather_second, 1),
+        (2, gather_first, 3),
+        (2, gather_second, 2),
+        (3, gather_third, 1),
+        (3, gather_second, 3),
+        (4, gather_third, 2),
         (6, gather_third, 3),
     ):
         between[slot].append(partial(stage, s))
@@ -1148,22 +1061,32 @@
         store(p, j, mixes, sums)
         return carried
 
-    for segment in range(last):
-        for hook in between[segment]:
-            hook()
-        turns = (segment * SEGMENT, segment * SEGMENT + SEGMENT)
+    def one_turn(turn, carried):
+        for segment in range(last):
+
+            @pl.when(turn == segment * SEGMENT)
+            def _():
+                for hook in between[segment]:
+                    hook()
 
         @pl.when(z >= 2)
         def _():
-            lax.fori_loop(*turns, cont_turn, 0)
+            cont_turn(turn, 0)
 
         @pl.when(z < 2)
         def _():
-            lax.fori_loop(*turns, prompt_turn, 0)
-
-        if turns[1] % 8 == 0:
-            for copy in exchange(turns[1] // 8 - 1):
-                copy.start()
+            prompt_turn(turn, 0)
+
+        for i in range(3):
+
+            @pl.when(turn == 8 * i + 7)
+            def _():
+                for copy in exchange(i):
+                    copy.start()
+
+        return carried
+
+    lax.fori_loop(0, 24, one_turn, 0)
     for hook in between[last]:
         hook()
 
@@ -1274,9 +1197,14 @@
 
 
 def tail_kernel(
-    part,
-    chip,
-    dw,
+    grp,
+    dkv,
+    n1p,
+    n1c,
+    dkvo,
+    dq,
+    w_q,
+    w_kv,
     grad_h2,
     tokens,
     vec,
@@ -1284,11 +1212,19 @@
     out,
     sums_out,
     dw_out,
-    own,
+    part,
+    chip,
+    tiles,
+    rows_p,
+    low,
+    wkt,
+    wqt,
+    dkvw,
+    dqw,
+    dw,
     ra,
     rb,
     rz,
-    keep,
     take,
     gsum,
     cur,
@@ -1301,147 +1237,199 @@
     sib, over_y, over_x = {"gc": g ^ 1}, {"gc": g ^ 2}, {"dp": x ^ 1}
     down = {"gr": jnp.maximum(z - 1, 0)}
     far = z >= 2
+    size = QROWS // CHUNKS
+    count = 2 * CHUNKS
+
+    def fetch(t):
+        rows = pl.ds(pl.multiple_of(t * size, size), size)
+        h, r = t // CHUNKS, pl.ds(pl.multiple_of((t % CHUNKS) * size, size), size)
+        slot = t % 2
+        return (
+            pltpu.make_async_copy(dkv.at[:, rows], tiles.at[slot], l_sems.at[slot]),
+            pltpu.make_async_copy(n1p.at[:, h, r], rows_p.at[slot], l_sems.at[2 + slot]),
+        )
+
+    for copy in fetch(0):
+        copy.start()
     greet(all_partners())
-    hooks = rs_steps([rs_plan(dw, dw_out, bufs, (w_s, w_r), w_l, 0, False)])
-    size = QROWS // CHUNKS
-    chunks = [(h, k) for h in range(2) for k in range(CHUNKS)]
-
-    def rows(k):
-        return pl.ds(k * size, size)
-
-    def index(side):
-        return 1 - y if side == 0 else y
-
-    def load(side, h, k):
-        i = index(side)
-        return pltpu.make_async_copy(
-            part.at[2 * i + c, h, rows(k)],
-            own.at[i, h, rows(k)],
-            l_sems.at[8 * side + CHUNKS * h + k],
-        )
-
-    def hop_a(side, h, k):
-        i = index(side)
-        return send(
-            part.at[2 * i + 1 - c, h, rows(k)],
-            ra.at[i, h, rows(k)],
-            sems,
-            8 * side + CHUNKS * h + k,
-            sib,
-        )
-
-    def hop_y(h, k):
-        return send(
-            own.at[1 - y, h, rows(k)], rb.at[h, rows(k)], sems, 16 + CHUNKS * h + k, over_y
-        )
-
-    def hop_z(h, k):
-        return send(own.at[y, h, rows(k)], rz.at[h, rows(k)], sems, 24 + CHUNKS * h + k, down)
+    wkt[...] = w_kv[...].T
+    wqt[...] = w_q[...].T
+    dkvw[...] = jnp.zeros_like(dkvw)
+    dqw[...] = jnp.zeros_like(dqw)
+
+    def at(t):
+        return t // CHUNKS, pl.ds(pl.multiple_of((t % CHUNKS) * size, size), size)
+
+    def mine(side, t):
+        h, r = at(t)
+        return part.at[2 * (1 - y if side == 0 else y) + c, h, r]
+
+    def hop_a(side, t):
+        h, r = at(t)
+        i = 1 - y if side == 0 else y
+        return send(part.at[2 * i + 1 - c, h, r], ra.at[i, h, r], sems, 8 * side + t, sib)
+
+    def hop_y(t):
+        h, r = at(t)
+        return send(mine(0, t), rb.at[h, r], sems, 16 + t, over_y)
+
+    def hop_z(t):
+        h, r = at(t)
+        return send(mine(1, t), rz.at[h, r], sems, 24 + t, down)
 
     hop_chip = send(chip.at[1 - c], take, sems, 32, sib)
-    load_chip = pltpu.make_async_copy(chip.at[c], keep, l_sems.at[16])
-
-    def fold(h, k, other):
-        add_into(own.at[y, h, rows(k)], own.at[y, h, rows(k)], other.at[rows(k)])
-
-    for h, k in chunks:
+
+    def fold(t, other):
+        h, r = at(t)
+        add_into(mine(1, t), mine(1, t), other.at[r])
+
+    def stage0(t):
+        slot = t % 2
+        for copy in fetch(t):
+            copy.wait()
+
+        @pl.when(t + 1 < count)
+        def _():
+            for copy in fetch(t + 1):
+                copy.start()
+
+        weights = [
+            [jnp.where(grp[j] == i, 1.0, 0.0).astype(F32) for j in range(8)] for i in range(4)
+        ]
+
+        @pl.loop(0, size // 16)
+        def _(q):
+            r = pl.ds(pl.multiple_of(q * 16, 16), 16)
+            pieces = [tiles[slot, j, r].astype(F32) for j in range(8)]
+            for i in range(4):
+                total = weights[i][0] * pieces[0]
+                for j in range(1, 8):
+                    total = total + weights[i][j] * pieces[j]
+                low[i, r] = total.astype(BF)
+
+        whole = low[...].reshape(4 * size, D)
+        grads = nn(whole, wkt[...]).astype(BF)
+        h, r = at(t)
+        for i in range(4):
+            part[i, h, r] = grads[size * i : size * i + size]
 
         @pl.when(far)
         def _():
-            load(0, h, k).start()
-            hop_a(0, h, k).start()
-
-        load(1, h, k).start()
-        hop_a(1, h, k).start()
-    hop_chip.start()
-    load_chip.start()
-    for hook in hooks[0]:
-        hook()
-
-    def stage1(h, k):
+            hop_a(0, t).start()
+
+        hop_a(1, t).start()
+        own = pl.ds(pl.multiple_of(t * size, size), size)
+        near, grad_q, rows_c = dkvo[own], dq[own], n1c[own]
+        chip[h, r] = (nn(grad_q, wqt[...]) + nn(near, wkt[...])).astype(BF)
+        rows = jnp.concatenate([rows_p[slot].reshape(4 * size, D), rows_c], axis=0)
+        dkvw[...] += tn(rows, jnp.concatenate([whole, near], axis=0))
+        dqw[...] += tn(rows_c, grad_q)
+
+    def stage1(t):
+        h, r = at(t)
+
         @pl.when(far)
         def _():
-            load(0, h, k).wait()
-            hop_a(0, h, k).wait()
-            add_into(
-                own.at[1 - y, h, rows(k)], own.at[1 - y, h, rows(k)], ra.at[1 - y, h, rows(k)]
-            )
-            hop_y(h, k).start()
-
-        load(1, h, k).wait()
-        hop_a(1, h, k).wait()
-        fold(h, k, ra.at[y, h])
-
-    def stage2(h, k):
+            hop_a(0, t).wait()
+            add_into(mine(0, t), mine(0, t), ra.at[1 - y, h, r])
+            hop_y(t).start()
+
+        hop_a(1, t).wait()
+        fold(t, ra.at[y, h])
+
+    def stage2(t):
         @pl.when(far)
         def _():
-            hop_y(h, k).wait()
-            fold(h, k, rb.at[h])
+            hop_y(t).wait()
+            fold(t, rb.at[t // CHUNKS])
 
         @pl.when(z == 3)
         def _():
-            hop_z(h, k).start()
-
-    def stage3(h, k):
+            hop_z(t).start()
+
+    def stage3(t):
         @pl.when(z == 2)
         def _():
-            hop_z(h, k).wait_recv()
-            fold(h, k, rz.at[h])
-            hop_z(h, k).start()
-
-    def stage4(h, k):
+            hop_z(t).wait_recv()
+            fold(t, rz.at[t // CHUNKS])
+            hop_z(t).start()
+
+    def stage4(t):
         @pl.when(z == 1)
         def _():
-            hop_z(h, k).wait_recv()
-            fold(h, k, rz.at[h])
-            if h == 0:
-                hop_z(h, k).start()
-
-    def stage5(h, k):
-        if h == 0:
-
-            @pl.when(z == 0)
+            hop_z(t).wait_recv()
+            fold(t, rz.at[t // CHUNKS])
+
+            @pl.when(t < CHUNKS)
             def _():
-                hop_z(h, k).wait_recv()
-                fold(h, k, rz.at[h])
-
-    n = len(chunks)
-    stages = (stage1, stage2, stage3, stage4, stage5)
-    for i in range(max(n + 4, len(hooks) - 1)):
-        for lag, stage in enumerate(stages):
-            if 0 <= i - lag < n:
-                stage(*chunks[i - lag])
-        if i + 1 < len(hooks):
-            for hook in hooks[i + 1]:
-                hook()
-    for h, k in chunks:
-
-        @pl.when(z >= 2 if h else z >= 1)
+                hop_z(t).start()
+
+    def stage5(t):
+        @pl.when(jnp.logical_and(z == 0, t < CHUNKS))
         def _():
-            hop_z(h, k).wait_send()
-
-    load_chip.wait()
+            hop_z(t).wait_recv()
+            fold(t, rz.at[0])
+
+    def stages(t, carried):
+        for lag, stage in zip(
+            (0, 1, 3, 5, 7, 9), (stage0, stage1, stage2, stage3, stage4, stage5)
+        ):
+
+            @pl.when(jnp.logical_and(t >= lag, t < count + lag))
+            def _():
+                stage(t - lag)
+
+        return carried
+
+    lax.fori_loop(0, count, stages, 0)
+    hop_chip.start()
+
+    for head in range(6):
+        p, b = head // 2, head % 2
+        places_in = (
+            dqw[:, 128 * p + (0 if b else 64) : 128 * p + (64 if b else 128)],
+            dkvw[:, 256 * p + (128 if b else 64) : 256 * p + (192 if b else 128)],
+            dkvw[:, 256 * p + (192 if b else 0) : 256 * p + (256 if b else 64)],
+        )
+        for i, piece in enumerate(places_in):
+            at_col = (head % 3) * 192 + HD * i
+            for r in range(4):
+                dw[head // 3, r, :, at_col : at_col + HD] = piece[192 * r : 192 * r + 192].astype(
+                    BF
+                )
+    begin, after_a, after_b, after_c, total, finish = rs_plan(
+        dw, dw_out, bufs, (w_s, w_r), w_l, 0, False
+    )
+    for s in RS_ORDER:
+        begin(s)
+    for s in RS_ORDER:
+        after_a(s)
+    lax.fori_loop(count, count + 3, stages, 0)
+    for s in RS_ORDER:
+        after_b(s)
+    lax.fori_loop(count + 3, count + 9, stages, 0)
+    for s in RS_ORDER:
+        after_c(s)
+
+    @pl.loop(0, count)
+    def _(t):
+        @pl.when(jnp.logical_or(z >= 2, jnp.logical_and(z == 1, t < CHUNKS)))
+        def _():
+            hop_z(t).wait_send()
+
     hop_chip.wait()
+
+    cur[...] = sums[...]
 
     @pl.loop(0, CHUNKS)
     def _(k):
         r = pl.ds(pl.multiple_of(k * size, size), size)
-        gsum[r] = keep[r].astype(F32) + take[r].astype(F32)
-
-    @pl.when(z < 2)
-    def _():
-        place = jnp.minimum(z, 1)
-
-        @pl.loop(0, CHUNKS)
-        def _(k):
-            r = pl.ds(pl.multiple_of(k * size, size), size)
-            gsum[r] += own[y, place, r].astype(F32)
-
-    cur[...] = sums[...]
-
-    @pl.loop(0, CHUNKS)
-    def _(k):
-        r = pl.ds(pl.multiple_of(k * size, size), size)
+        gsum[r] = chip[c, r].astype(F32) + take[r].astype(F32)
+
+        @pl.when(z < 2)
+        def _():
+            gsum[r] += part[2 * y + c, jnp.minimum(z, 1), r].astype(F32)
+
         hidden = tokens[r].astype(F32) + vec[0:1]
         center = jnp.mean(hidden, axis=1, keepdims=True)
         offset = hidden - center
@@ -1451,9 +1439,9 @@
         scaled = grad * vec[1:2]
         first = jnp.mean(scaled, axis=1, keepdims=True)
         second = jnp.mean(scaled * unit, axis=1, keepdims=True)
-        total = grad_h2[r] + factor * (scaled - first - unit * second)
-        out[r] = total
-        cur[0:1] += jnp.sum(total, axis=0, keepdims=True)
+        result = grad_h2[r] + factor * (scaled - first - unit * second)
+        out[r] = result
+        cur[0:1] += jnp.sum(result, axis=0, keepdims=True)
         cur[1:2] += jnp.sum(grad * unit, axis=0, keepdims=True)
         cur[2:3] += jnp.sum(grad, axis=0, keepdims=True)
 
@@ -1462,51 +1450,65 @@
         hop.start()
         hop.wait()
         cur[...] += sb[i]
+        if i == 1:
+            total()
     hops = [send(cur, sb.at[2 + s], sems, 35 + s, {"gr": z ^ s}) for s in (1, 2, 3)]
     for hop in hops:
         hop.start()
+    finish()
     for hop in hops:
         hop.wait()
     sums_out[...] = (cur[...] + sb[3]) + (sb[4] + sb[5])
 
 
-def tail_exchange(part, chip, dw, grad_h2, tokens, vec, sums, collective_id):
+def tail_exchange(
+    grp, dkv, n1p, n1c, dkvo, dq, w_q, w_kv, grad_h2, tokens, vec, sums, collective_id
+):
     any_space = pl.BlockSpec(memory_space=pl.ANY)
     vmem = pl.BlockSpec(memory_space=pltpu.VMEM)
+    block = (2, 4, 192, 576)
     return pl.pallas_call(
         tail_kernel,
         name="tail_exchange",
-        in_specs=[any_space, any_space, any_space, vmem, vmem, vmem, vmem],
+        in_specs=[pl.BlockSpec(memory_space=pltpu.SMEM), any_space, any_space] + [vmem] * 9,
         out_specs=[vmem, vmem, vmem],
         out_shape=[
             jax.ShapeDtypeStruct((QROWS, D), F32),
             jax.ShapeDtypeStruct(sums.shape, F32),
-            jax.ShapeDtypeStruct(dw.shape[2:], F32),
+            jax.ShapeDtypeStruct(block[2:], F32),
         ],
         scratch_shapes=[
-            pltpu.VMEM((2, 2, QROWS, D), BF),
+            pltpu.VMEM((4, 2, QROWS, D), BF),
+            pltpu.VMEM((2, QROWS, D), BF),
+            pltpu.VMEM((2, 8, CL, D), BF),
+            pltpu.VMEM((2, 4, CL, D), BF),
+            pltpu.VMEM((4, CL, D), BF),
+            pltpu.VMEM((D, D), BF),
+            pltpu.VMEM((384, D), BF),
+            pltpu.VMEM((D, D), F32),
+            pltpu.VMEM((D, 384), F32),
+            pltpu.VMEM(block, BF),
             pltpu.VMEM((2, 2, QROWS, D), BF),
             pltpu.VMEM((2, QROWS, D), BF),
             pltpu.VMEM((2, QROWS, D), BF),
-            pltpu.VMEM((QROWS, D), BF),
             pltpu.VMEM((QROWS, D), BF),
             pltpu.VMEM((QROWS, D), F32),
             pltpu.VMEM(sums.shape, F32),
             pltpu.VMEM((6,) + sums.shape, F32),
         ]
-        + rs_scratch(dw.shape[2], dw.shape[3], False)
+        + rs_scratch(block[2], block[3], False)
         + [
             pltpu.SemaphoreType.DMA((39,)),
             pltpu.SemaphoreType.DMA((39,)),
-            pltpu.SemaphoreType.DMA((17,)),
+            pltpu.SemaphoreType.DMA((4,)),
             pltpu.SemaphoreType.DMA((RS_SLOTS,)),
             pltpu.SemaphoreType.DMA((RS_SLOTS,)),
             pltpu.SemaphoreType.DMA((8,)),
         ],
         compiler_params=pltpu.CompilerParams(
-            collective_id=collective_id, has_side_effects=True, vmem_limit_bytes=48 << 20
+            collective_id=collective_id, has_side_effects=True, vmem_limit_bytes=60 << 20
         ),
-    )(part, chip, dw, grad_h2, tokens, vec, sums)
+    )(grp, dkv, n1p, n1c, dkvo, dq, w_q, w_kv, grad_h2, tokens, vec, sums)
 
 
 GELU_IN = math.sqrt(2.0 / math.pi)
@@ -1890,9 +1892,6 @@
         dq, dkvo, dkv, out_w_down, out_w_up, out_w_out = attend_back_scatter(
             grp, q, lse_rows, kvo, kvp, gm, weight_grads, 3
         )
-        part_prompt, part_chip, grad_qkv = fold_prompts(
-            grp, dkv, dkvo, dq, n1_prompt, n1_chip, w_q, w_kv
-        )
     else:
         gm_keep = lax.dynamic_index_in_dim(gm, c, 0, keepdims=False)
         gm_give = lax.dynamic_index_in_dim(gm, 1 - c, 0, keepdims=False)
@@ -1920,9 +1919,14 @@
 
     if n_dp == 2:
         input_grad, sums, out_w_qkv = tail_exchange(
-            part_prompt.reshape(4, 2, QROWS, D),
-            part_chip.reshape(2, QROWS, D),
-            grad_qkv.reshape(2, 4, 192, 576),
+            grp,
+            dkv,
+            n1_prompt,
+            n1_chip,
+            dkvo,
+            dq,
+            w_q,
+            w_kv,
             grad_h2,
             tokens,
             vectors,

time: 394 us -> 376 us (0.954)
  Pallas kernels: 368 us -> 346 us
    pallas_call x1, Pallas kernels: 93.1 us -> 79.7 us  [attend_back_scatter(): pl.pallas_call(partial(att_scatter_kernel, count), name='attend_back_scat...]
    pallas_call x2 -> x1, Pallas kernels: 109 us -> 98.2 us  [tail_exchange(): pl.pallas_call(tail_kernel, name='tail_exchange', in_specs=[pl.BlockSpec(...]
where the time goes in v7:
time: 376 us; the launch traced here: 369 us
  Pallas kernels  346 us (92%)
  local copies, waits for them, and re-layouts  17.3 us (5%)
    pallas_call x1, Pallas kernels, front(): pl.pallas_call(front_kernel, name='front', in_specs=[vmem, vmem, vmem, vm...  133 us
    pallas_call x1, Pallas kernels, tail_exchange(): pl.pallas_call(tail_kernel, name='tail_exchange', in_specs=[pl.BlockSpec(...  98.2 us
    pallas_call x1, Pallas kernels, attend_back_scatter(): pl.pallas_call(partial(att_scatter_kernel, count), name='attend_back_scat...  79.7 us
    pallas_call x1, Pallas kernels, middle(): pl.pallas_call(middle_kernel, name='middle', in_specs=[vmem, vmem, any_sp...  34.7 us

profile of v7, /device:TPU:0, one launch (start us, length us, event | category | flops | bytes accessed | tf_op | source)
XLA Modules:
  0.0 368.7 jit_solution(16719623560449774954)
XLA Ops:
  0.7 0.7 stack.25
  1.3 0.7 stack.26
  2.0 0.7 stack.27
  2.6 0.7 stack.28
  3.3 0.7 stack.29
  3.9 0.7 stack.30
  4.6 0.7 stack.31
  5.3 0.3 dynamic_update_slice.3.vec
  5.6 0.0 copy-start.4
  5.6 1.3 broadcast_in_dim.13.bup
  6.9 0.7 pad.4
  7.6 0.6 broadcast_in_dim.14.own
  8.2 0.0 copy-done.4
  8.2 133.3 %front.1 = (bf16[2,512,384]{2,1,0:T(8,128)(2,1)}, f32[3,8,2,128]{3,2,1,0:T(2,128)}, bf16[4,4,192,192]{3,2,1,0:T(8,128)(2,1)}, bf16[4,4,192,768]{3,2,1,0:T(8,128)...) custom-call(bf16[512,768]{1,0:T(8,128)(2,1)} %tokens.5, ...), custom_call_target="tpu_custom_call" | custom-call | tf_op jit(solution)/shard_map/front/pallas_call | solution.py:1141
  141.5 34.7 %middle.1 = (bf16[512,768]{1,0:T(8,128)(2,1)}, f32[512,768]{1,0:T(8,128)}, bf16[4,768,768]{2,1,0:T(8,128)(2,1)}, bf16[4,768,768]{2,1,0:T(8,128)(2,1)}, bf16[4,4,...) custom-call(bf16[2,512,384]{2,1,0:T(8,128)(2,1)} %get-tuple-element.46.mixed, ...), custom_call_target="tpu_custom_call" | custom-call | tf_op jit(solution)/shard_map/middle/pallas_call | solution.py:1659
  176.2 0.7 slice_reduce_fusion.1
  177.0 0.1 reshape_squeeze.3
  177.1 0.1 reshape.86
  177.2 0.1 broadcast_in_dim.15
  177.2 0.1 reshape.85
  177.3 0.5 broadcast_select_fusion.grp_ref.grp
  177.8 79.7 %attend_back_scatter.1 = (bf16[1024,384]{1,0:T(8,128)(2,1)}, bf16[1024,768]{1,0:T(8,128)(2,1)}, bf16[8,1024,768]{2,1,0:T(8,128)(2,1)}, f32[192,768]{1,0:T(8,128)...) custom-call(s32[8]{0:T(128)} %broadcast_select_fusion.grp_ref.grp, bf16[3,1024,128]{2,1,0:T(8,128)(2,1)} %get-tuple-element.54.q_ref, ...), custom_call_target="tpu_custom_call" | custom-call | tf_op jit(solution)/shard_map/attend_back_scatter/pallas_call | solution.py:532
  257.5 98.2 %tail_exchange.1 = (f32[512,768]{1,0:T(8,128)}, f32[16,768]{1,0:T(8,128)}, f32[192,576]{1,0:T(8,128)}) custom-call(s32[8]{0:T(128)} %broadcast_select_fusion.grp_ref.grp, bf16[8,1024,768]{2,1,0:T(8,128)(2,1)} %get-tuple-element.62.dkv, bf16[4,2,512,768]{3,2,1,0:T(8,128)(2,1)} %get-tuple-element.63.n1p, bf16[1024,768]{1,0:T(8,128)(2,1)} %bitcast.18, ...), custom_call_target="tpu_custom_call" | custom-call | tf_op jit(solution)/shard_map/tail_exchange/pallas_call | solution.py:1470
  355.7 0.7 slice.49
  356.4 0.1 reshape.91
  356.5 0.6 constant_dynamic-slice_fusion.6
  357.1 0.8 slice.56
  358.0 0.6 dynamic-slice_reduce_fusion
  358.6 1.3 slice_reduce_fusion
  361.2 0.0 copy-start.2
  361.2 0.0 copy-start.3
  361.2 0.0 copy-start.1
  361.2 2.7 copy.38
  364.0 0.0 copy-done.2
  364.0 0.0 copy-start
  364.0 0.8 copy.39
  364.8 0.0 copy-done.3
  364.8 0.7 copy.40
  365.5 0.0 copy-done.1
  365.5 0.8 copy.41
  366.3 0.0 copy-done
  366.3 0.8 copy.42
  (5 shorter events, 0.1 us)
Async XLA Ops:
  5.6 2.6 copy-start.4
  361.2 2.8 copy-start.2
  361.2 3.6 copy-start.3
  361.2 4.2 %copy-start.1 = (f32[192,768]{1,0:T(8,128)S(1)}, f32[192,768]{1,0:T(8,128)}, u32[]{:S(2)}) copy-start(f32[192,768]{1,0:T(8,128)} %get-tuple-element.110) | copy-start | bytes 1769476
  364.0 2.3 copy-start

commit v8 on v7

--- a/solution.py
+++ b/solution.py
@@ -269,7 +269,13 @@
 
 
 def add_into(dst, left, right):
-    dst[...] = (left[...].astype(F32) + right[...].astype(F32)).astype(dst.dtype)
+    rows = dst.shape[0]
+    size = 48 if rows % 48 == 0 else 64
+
+    @pl.loop(0, rows // size)
+    def _(i):
+        r = pl.ds(pl.multiple_of(i * size, 16), size)
+        dst[r] = (left[r].astype(F32) + right[r].astype(F32)).astype(dst.dtype)
 
 
 RS_SLOTS = 28
@@ -702,11 +708,11 @@
         return send(piece, piece, w_sems, 16 + s, over_x)
 
     def chunk(number):
-        return (first_half if number < CHUNKS else 1 - first_half), number % CHUNKS
+        return jnp.where(number < CHUNKS, first_half, 1 - first_half), number % CHUNKS
 
     def item(column, number):
         half, k = chunk(number)
-        return prompts.at[column, half, pl.ds(k * size, size)]
+        return prompts.at[column, half, pl.ds(pl.multiple_of(k * size, size), size)]
 
     def up(number):
         half, k = chunk(number)
@@ -938,23 +944,25 @@
         half, k = chunk(number)
         w = wkv_out[...]
         rows = jnp.concatenate(
-            [prompts[i, half, pl.ds(k * size, size)] for i in range(4)], axis=0
+            [
+                prompts[i, half, pl.ds(pl.multiple_of(k * size, size), size)]
+                for i in range(4)
+            ],
+            axis=0,
         )
         kv = nn(rows, w).astype(BF)
         to = pl.ds(pl.multiple_of(half * QROWS + k * size, size), size)
         for i in range(4):
             for p in range(3):
                 kvp_all[p, i, to] = kv[size * i : size * i + size, 256 * p : 256 * p + 256]
-        mine = chip[number // CHUNKS, pl.ds((number % CHUNKS) * size, size)]
+        mine = chip[number // CHUNKS, pl.ds(pl.multiple_of(k * size, size), size)]
         kvo = nn(mine, w).astype(BF)
         queries = (nn(mine, wq_out[...]) * 0.125).astype(BF)
-        to = pl.ds(number * size, size)
+        to = pl.ds(pl.multiple_of(number * size, size), size)
         for p in range(3):
             kvo_all[p, to] = kvo[:, 256 * p : 256 * p + 256]
             q_all[p, to] = queries[:, 128 * p : 128 * p + 128]
 
-    for i in range(8):
-        hooks[5 + i].append(partial(project, i))
 
     def own_first():
         for a in range(3):
@@ -995,9 +1003,23 @@
     ):
         between[slot].append(partial(stage, s))
 
-    for number in range(FRONT):
+    for number in range(FRONT - 8):
         for hook in hooks[number]:
             hook()
+
+    def one_piece(number, carried):
+        for i in range(FRONT - 8, FRONT):
+            if hooks[i]:
+
+                @pl.when(number == i)
+                def _():
+                    for hook in hooks[i]:
+                        hook()
+
+        project(number - (FRONT - 8))
+        return carried
+
+    lax.fori_loop(FRONT - 8, FRONT, one_piece, 0)
 
     low = lax.broadcasted_iota(jnp.int32, (CL, 128), 1) < 64
 
@@ -1370,10 +1392,9 @@
             hop_z(t).wait_recv()
             fold(t, rz.at[0])
 
-    def stages(t, carried):
-        for lag, stage in zip(
-            (0, 1, 3, 5, 7, 9), (stage0, stage1, stage2, stage3, stage4, stage5)
-        ):
+    def stages(t, carried, skip=0):
+        todo = list(zip((0, 1, 3, 5, 7, 9), (stage0, stage1, stage2, stage3, stage4, stage5)))
+        for lag, stage in todo[skip:]:
 
             @pl.when(jnp.logical_and(t >= lag, t < count + lag))
             def _():
@@ -1404,10 +1425,10 @@
         begin(s)
     for s in RS_ORDER:
         after_a(s)
-    lax.fori_loop(count, count + 3, stages, 0)
+    lax.fori_loop(count, count + 3, partial(stages, skip=1), 0)
     for s in RS_ORDER:
         after_b(s)
-    lax.fori_loop(count + 3, count + 9, stages, 0)
+    lax.fori_loop(count + 3, count + 9, partial(stages, skip=2), 0)
     for s in RS_ORDER:
         after_c(s)
 
@@ -1757,9 +1778,11 @@
     swap_core = [(i, i ^ 1) for i in range(n_gc)]
     swap_y = [(i, i ^ 2) for i in range(n_gc)]
 
-    packed = jnp.stack(
-        [pass_embed, ln1_gain, ln1_bias, out_bias, ln2_gain, ln2_bias, fc2_bias, fc2_bias]
-    ).astype(F32)
+    parts = [pass_embed, ln1_gain, ln1_bias, out_bias, ln2_gain, ln2_bias, fc2_bias]
+    row = lax.broadcasted_iota(jnp.int32, (8, pass_embed.shape[0]), 0)
+    packed = jnp.zeros(row.shape, F32)
+    for i, values in enumerate(parts):
+        packed = jnp.where(row == i, values.astype(F32)[None], packed)
     if n_dp == 2:
         vec = lax.dynamic_update_slice(jnp.zeros((8, D), F32), packed, (0, z * packed.shape[1]))
         bup = jnp.broadcast_to(fc1_bias.astype(F32), (8, fc1_bias.shape[0]))

time: 376 us -> 368 us (0.979); the launches traced: 369 us -> 367 us
  local copies, waits for them, and re-layouts: 17.3 us -> 12.6 us
  other arithmetic: 1.87 us -> 6.57 us
    another operation x8 -> x0, local copies, waits for them, and re-layouts: 4.64 us -> none  [on_device(): jnp.stack([pass_embed, ln1_gain, ln1_bias, out_bias, ln2_gain, ln2_bias,...]
    convert_element_type x1 -> x7, other arithmetic: 0.01 us -> 4.6 us  [on_device(): packed = jnp.where(row == i, values.astype(F32)[None], packed)]
where the time goes in v8:
time: 368 us; the launch traced here: 367 us
  Pallas kernels  345 us (94%)
  local copies, waits for them, and re-layouts  12.6 us (3%)
  other arithmetic  6.57 us (2%)
    pallas_call x1, Pallas kernels, front(): pl.pallas_call(front_kernel, name='front', in_specs=[vmem, vmem, vmem, vm...  133 us
    pallas_call x1, Pallas kernels, tail_exchange(): pl.pallas_call(tail_kernel, name='tail_exchange', in_specs=[pl.BlockSpec(...  97.9 us
    pallas_call x1, Pallas kernels, attend_back_scatter(): pl.pallas_call(partial(att_scatter_kernel, count), name='attend_back_scat...  79.5 us
    pallas_call x1, Pallas kernels, middle(): pl.pallas_call(middle_kernel, name='middle', in_specs=[vmem, vmem, any_sp...  34.9 us

profile of v8, /device:TPU:0, one launch (start us, length us, event | category | flops | bytes accessed | tf_op | source)
XLA Modules:
  0.0 367.2 jit_solution(10220233979809457962)
XLA Ops:
  0.7 0.7 convert_element_type.28
  1.3 0.7 convert_element_type.29
  2.0 0.7 convert_element_type.30
  2.7 0.7 convert_element_type.31
  3.3 0.7 convert_element_type.32
  4.0 0.7 convert_element_type.33
  4.6 0.7 convert_element_type.34
  5.3 0.1 select_select_fusion
  5.4 0.3 dynamic_update_slice.3.vec
  5.7 0.0 copy-start.4
  5.7 1.3 broadcast_in_dim.69.bup
  7.0 0.7 pad.4
  7.6 0.6 broadcast_in_dim.70.own
  8.2 0.0 copy-done.4
  8.2 132.5 %front.1 = (bf16[2,512,384]{2,1,0:T(8,128)(2,1)}, f32[3,8,2,128]{3,2,1,0:T(2,128)}, bf16[4,4,192,192]{3,2,1,0:T(8,128)(2,1)}, bf16[4,4,192,768]{3,2,1,0:T(8,128)...) custom-call(bf16[512,768]{1,0:T(8,128)(2,1)} %tokens.5, ...), custom_call_target="tpu_custom_call" | custom-call | tf_op jit(solution)/shard_map/front/pallas_call | solution.py:1163
  140.8 34.9 %middle.1 = (bf16[512,768]{1,0:T(8,128)(2,1)}, f32[512,768]{1,0:T(8,128)}, bf16[4,768,768]{2,1,0:T(8,128)(2,1)}, bf16[4,768,768]{2,1,0:T(8,128)(2,1)}, bf16[4,4,...) custom-call(bf16[2,512,384]{2,1,0:T(8,128)(2,1)} %get-tuple-element.46.mixed, ...), custom_call_target="tpu_custom_call" | custom-call | tf_op jit(solution)/shard_map/middle/pallas_call | solution.py:1680
  175.7 0.7 slice_reduce_fusion.1
  176.4 0.1 reshape_squeeze.3
  176.5 0.1 reshape.93
  176.6 0.1 broadcast_in_dim.71
  176.7 0.1 reshape.92
  176.8 0.5 broadcast_select_fusion.grp_ref.grp
  177.3 79.5 %attend_back_scatter.1 = (bf16[1024,384]{1,0:T(8,128)(2,1)}, bf16[1024,768]{1,0:T(8,128)(2,1)}, bf16[8,1024,768]{2,1,0:T(8,128)(2,1)}, f32[192,768]{1,0:T(8,128)...) custom-call(s32[8]{0:T(128)} %broadcast_select_fusion.grp_ref.grp, bf16[3,1024,128]{2,1,0:T(8,128)(2,1)} %get-tuple-element.54.q_ref, ...), custom_call_target="tpu_custom_call" | custom-call | tf_op jit(solution)/shard_map/attend_back_scatter/pallas_call | solution.py:538
  256.9 97.9 %tail_exchange.1 = (f32[512,768]{1,0:T(8,128)}, f32[16,768]{1,0:T(8,128)}, f32[192,576]{1,0:T(8,128)}) custom-call(s32[8]{0:T(128)} %broadcast_select_fusion.grp_ref.grp, bf16[8,1024,768]{2,1,0:T(8,128)(2,1)} %get-tuple-element.62.dkv, bf16[4,2,512,768]{3,2,1,0:T(8,128)(2,1)} %get-tuple-element.63.n1p, bf16[1024,768]{1,0:T(8,128)(2,1)} %bitcast.18, ...), custom_call_target="tpu_custom_call" | custom-call | tf_op jit(solution)/shard_map/tail_exchange/pallas_call | solution.py:1491
  354.7 0.7 slice.49
  355.5 0.1 reshape.98
  355.6 0.6 constant_dynamic-slice_fusion.6
  356.2 0.8 slice.56
  357.0 0.6 dynamic-slice_reduce_fusion
  357.6 1.3 slice_reduce_fusion
  360.2 0.0 copy-start.2
  360.2 0.0 copy-start.3
  360.3 0.0 copy-start.1
  360.3 2.7 copy.38
  363.0 0.0 copy-done.2
  363.0 0.0 copy-start
  363.0 0.8 copy.39
  363.8 0.0 copy-done.3
  363.8 0.7 copy.40
  364.5 0.0 copy-done.1
  364.5 0.8 copy.41
  365.3 0.0 copy-done
  365.3 0.8 copy.42
  (7 shorter events, 0.1 us)
Async XLA Ops:
  5.7 2.6 copy-start.4
  360.2 2.8 copy-start.2
  360.2 3.6 copy-start.3
  360.3 4.2 %copy-start.1 = (f32[192,768]{1,0:T(8,128)S(1)}, f32[192,768]{1,0:T(8,128)}, u32[]{:S(2)}) copy-start(f32[192,768]{1,0:T(8,128)} %get-tuple-element.116) | copy-start | bytes 1769476
  363.0 2.3 copy-start

commit v9 on v8

--- a/solution.py
+++ b/solution.py
@@ -280,6 +280,7 @@
 
 RS_SLOTS = 28
 RS_ORDER = (3, 2, 1, 0)
+PACE = 26
 
 
 def rs_plan(grads, outs, bufs, sems, l_sems, base, paired):
@@ -450,7 +451,7 @@
 
     last = len(hooks) - 1
     for when in range(1, 23):
-        parts = [h for i in range(1, last) if i * 22 // (last - 1) == when for h in hooks[i]]
+        parts = [h for i in range(1, last) if max(1, i * PACE // (last - 1)) == when for h in hooks[i]]
         if parts:
 
             @pl.when(step == when)
@@ -523,8 +524,10 @@
 
     @pl.when(step == 23)
     def _():
-        for hook in hooks[last]:
-            hook()
+        for i in range(1, last + 1):
+            if i == last or i * PACE // (last - 1) > 22:
+                for hook in hooks[i]:
+                    hook()
 
 
 def attend_back_scatter(grp, q, lse, kvo, kvp, gm, grads, collective_id):
@@ -1150,7 +1153,25 @@
         copy.wait()
 
 
-def front(tokens, vec, bup, own, wq, blocks, collective_id):
+def front(tokens, vectors, bias, own, wq, blocks, collective_id):
+    def body(tokens_ref, *refs):
+        parts, bias_ref = refs[:7], refs[7]
+        rest, vec, bup = refs[8:-2], refs[-2], refs[-1]
+        z = lax.axis_index("gr")
+        width = bias_ref.shape[0] // 4
+        vec[...] = jnp.zeros_like(vec)
+        for k in range(4):
+
+            @pl.when(z == k)
+            def _():
+                for i, part in enumerate(parts):
+                    vec[i : i + 1, width * k : width * k + width] = (
+                        part[...].astype(F32).reshape(1, width)
+                    )
+
+        bup[0:1] = bias_ref[...].astype(F32).reshape(1, 4 * width)
+        front_kernel(tokens_ref, vec, bup, *rest)
+
     any_space = pl.BlockSpec(memory_space=pl.ANY)
     vmem = pl.BlockSpec(memory_space=pltpu.VMEM)
     rows = 2 * QROWS
@@ -1161,9 +1182,9 @@
     slots = 3 * GATHER_SLOTS
     heads = [(3, rows, 128), (3, rows, 256), (3, 4, P_SIZE, 256)]
     return pl.pallas_call(
-        front_kernel,
+        body,
         name="front",
-        in_specs=[vmem, vmem, vmem, vmem] + [any_space] * 4,
+        in_specs=[vmem] * 10 + [any_space] * 4,
         out_specs=[any_space, vmem]
         + [any_space] * 8
         + [vmem] * 5,
@@ -1180,13 +1201,13 @@
         + [
             jax.ShapeDtypeStruct((D, 384), BF),
             jax.ShapeDtypeStruct((D, D), BF),
-            jax.ShapeDtypeStruct(vec.shape, F32),
-            jax.ShapeDtypeStruct((4,) + bup.shape, F32),
+            jax.ShapeDtypeStruct((8, D), F32),
+            jax.ShapeDtypeStruct((4, 8, D), F32),
             jax.ShapeDtypeStruct((4,) + own.shape, jnp.int32),
         ],
         scratch_shapes=[
             pltpu.VMEM((QROWS, D), BF),
-            pltpu.VMEM((4,) + vec.shape, F32),
+            pltpu.VMEM((4, 8, D), F32),
             pltpu.VMEM((4, 2, QROWS, D), BF),
             pltpu.VMEM((2, QROWS, D), BF),
             pltpu.VMEM((2, 4) + wq.shape, BF),
@@ -1211,11 +1232,13 @@
             dma(3),
             dma(10),
             dma(5),
+            pltpu.VMEM((8, D), F32),
+            pltpu.VMEM((8, D), F32),
         ],
         compiler_params=pltpu.CompilerParams(
             collective_id=collective_id, has_side_effects=True, vmem_limit_bytes=56 << 20
         ),
-    )(tokens, vec, bup, own, wq, *blocks)
+    )(tokens, *vectors, bias, own, wq, *blocks)
 
 
 def tail_kernel(
@@ -1594,9 +1617,9 @@
 
     @pl.loop(0, 4)
     def _(b):
-        @pl.loop(0, 2)
+        @pl.loop(0, 1)
         def _(t):
-            r = pl.ds(pl.multiple_of(t * 256, 256), 256)
+            r = pl.ds(pl.multiple_of(t * QROWS, QROWS), QROWS)
             pre = nn(n2[r], wu[b]) + b_up[b, 0:1]
             square = pre * pre
             tanh = jnp.tanh(GELU_IN * pre * (1.0 + 0.044715 * square))
@@ -1630,9 +1653,9 @@
         dd[b] = nn(gbt[...], act[b]).astype(BF)
         pltpu.make_async_copy(dd.at[b], dw_down.at[b], o_sems.at[b]).start()
 
-        @pl.loop(0, 2)
+        @pl.loop(0, 1)
         def _(t):
-            r = pl.ds(pl.multiple_of(t * 256, 256), 256)
+            r = pl.ds(pl.multiple_of(t * QROWS, QROWS), QROWS)
             low = (nn(gb[r], wd[b]) * slope[b, r]).astype(BF)
             act[b, r] = low
             sums[pl.ds(7 + b, 1)] += jnp.sum(low.astype(F32), axis=0, keepdims=True)
@@ -1779,13 +1802,7 @@
     swap_y = [(i, i ^ 2) for i in range(n_gc)]
 
     parts = [pass_embed, ln1_gain, ln1_bias, out_bias, ln2_gain, ln2_bias, fc2_bias]
-    row = lax.broadcasted_iota(jnp.int32, (8, pass_embed.shape[0]), 0)
-    packed = jnp.zeros(row.shape, F32)
-    for i, values in enumerate(parts):
-        packed = jnp.where(row == i, values.astype(F32)[None], packed)
     if n_dp == 2:
-        vec = lax.dynamic_update_slice(jnp.zeros((8, D), F32), packed, (0, z * packed.shape[1]))
-        bup = jnp.broadcast_to(fc1_bias.astype(F32), (8, fc1_bias.shape[0]))
         own = jnp.broadcast_to(jnp.pad(cont_group, (0, 120)), (8, 128))
         (
             mixed,
@@ -1804,12 +1821,12 @@
             b_up,
             owners,
         ) = front(
-            tokens, vec, bup, own, qkv_weight, [out_weight, fc1_weight, fc2_weight], 1
+            tokens, parts, fc1_bias, own, qkv_weight, [out_weight, fc1_weight, fc2_weight], 1
         )
         n1_chip = n1_chip.reshape(2 * QROWS, D)
         owners = owners[:, 0, :8]
     else:
-        vectors = lax.all_gather(packed, "gr", axis=1, tiled=True)
+        vectors = lax.all_gather(jnp.stack(parts).astype(F32), "gr", axis=1, tiled=True)
         b_up = lax.all_gather(fc1_bias, "gc", axis=0, tiled=True).astype(F32)
         owners = lax.all_gather(cont_group, "gr", axis=0, tiled=True)
     embed, gain1, shift1, b_out, gain2, shift2, b_down = [vectors[i] for i in range(7)]

time: 368 us -> 354 us (0.962)
  Pallas kernels: 345 us -> 338 us
  other arithmetic: 6.57 us -> 1.87 us
    convert_element_type x7 -> x0, other arithmetic: 4.6 us -> none  [on_device(): packed = jnp.where(row == i, values.astype(F32)[None], packed)]
    pallas_call x1, Pallas kernels: 34.9 us -> 30.9 us  [middle(): pl.pallas_call(middle_kernel, name='middle', in_specs=[vmem, vmem, any_sp...]
where the time goes in v9:
time: 354 us
  Pallas kernels  338 us (95%)
  local copies, waits for them, and re-layouts  11 us (3%)
    pallas_call x1, Pallas kernels, front(): pl.pallas_call(body, name='front', in_specs=[vmem] * 10 + [any_space] * 4...  133 us
    pallas_call x1, Pallas kernels, tail_exchange(): pl.pallas_call(tail_kernel, name='tail_exchange', in_specs=[pl.BlockSpec(...  98.2 us
    pallas_call x1, Pallas kernels, attend_back_scatter(): pl.pallas_call(partial(att_scatter_kernel, count), name='attend_back_scat...  76.1 us
    pallas_call x1, Pallas kernels, middle(): pl.pallas_call(middle_kernel, name='middle', in_specs=[vmem, vmem, any_sp...  30.9 us

profile of v9, /device:TPU:0, one launch (start us, length us, event | category | flops | bytes accessed | tf_op | source)
XLA Modules:
  0.0 353.8 jit_solution(14068849118456551942)
XLA Ops:
  0.7 0.7 pad.4
  1.3 0.6 broadcast_in_dim.6.refs_8_
  1.9 132.6 %front.1 = (bf16[2,512,384]{2,1,0:T(8,128)(2,1)}, f32[3,8,2,128]{3,2,1,0:T(2,128)}, bf16[4,4,192,192]{3,2,1,0:T(8,128)(2,1)}, bf16[4,4,192,768]{3,2,1,0:T(8,128)...) custom-call(bf16[512,768]{1,0:T(8,128)(2,1)} %tokens.3, ...), custom_call_target="tpu_custom_call" | custom-call | tf_op jit(solution)/shard_map/front/pallas_call | solution.py:1184
  134.6 0.7 slice_reduce_fusion.1
  135.3 0.1 reshape_squeeze.3
  135.4 0.1 reshape.86
  135.5 0.1 broadcast_in_dim.7
  135.6 0.1 reshape.85
  135.6 0.5 broadcast_select_fusion.grp_ref.grp
  136.2 30.9 %middle.1 = (bf16[512,768]{1,0:T(8,128)(2,1)}, f32[512,768]{1,0:T(8,128)}, bf16[4,768,768]{2,1,0:T(8,128)(2,1)}, bf16[4,768,768]{2,1,0:T(8,128)(2,1)}, bf16[4,4,...) custom-call(bf16[2,512,384]{2,1,0:T(8,128)(2,1)} %get-tuple-element.46.mixed, ...), custom_call_target="tpu_custom_call" | custom-call | tf_op jit(solution)/shard_map/middle/pallas_call | solution.py:1703
  167.0 76.1 %attend_back_scatter.1 = (bf16[1024,384]{1,0:T(8,128)(2,1)}, bf16[1024,768]{1,0:T(8,128)(2,1)}, bf16[8,1024,768]{2,1,0:T(8,128)(2,1)}, f32[192,768]{1,0:T(8,128)...) custom-call(s32[8]{0:T(128)} %broadcast_select_fusion.grp_ref.grp, bf16[3,1024,128]{2,1,0:T(8,128)(2,1)} %get-tuple-element.54.q_ref, ...), custom_call_target="tpu_custom_call" | custom-call | tf_op jit(solution)/shard_map/attend_back_scatter/pallas_call | solution.py:541
  243.1 98.2 %tail_exchange.1 = (f32[512,768]{1,0:T(8,128)}, f32[16,768]{1,0:T(8,128)}, f32[192,576]{1,0:T(8,128)}) custom-call(s32[8]{0:T(128)} %broadcast_select_fusion.grp_ref.grp, bf16[8,1024,768]{2,1,0:T(8,128)(2,1)} %get-tuple-element.62.dkv, bf16[4,2,512,768]{3,2,1,0:T(8,128)(2,1)} %get-tuple-element.63.n1p, bf16[1024,768]{1,0:T(8,128)(2,1)} %bitcast.18, ...), custom_call_target="tpu_custom_call" | custom-call | tf_op jit(solution)/shard_map/tail_exchange/pallas_call | solution.py:1514
  341.3 0.7 slice.49
  342.0 0.1 reshape.91
  342.1 0.6 constant_dynamic-slice_fusion.6
  342.7 0.8 slice.56
  343.5 0.6 dynamic-slice_reduce_fusion
  344.2 1.3 slice_reduce_fusion
  346.8 0.0 copy-start.2
  346.8 0.0 copy-start.3
  346.8 0.0 copy-start.1
  346.8 2.7 copy.37
  349.6 0.0 copy-done.2
  349.6 0.0 copy-start
  349.6 0.8 copy.38
  350.4 0.0 copy-done.3
  350.4 0.7 copy.39
  351.1 0.0 copy-done.1
  351.1 0.8 copy.40
  351.9 0.0 copy-done
  351.9 0.8 copy.41
  (2 shorter events, 0.0 us)
Async XLA Ops:
  346.8 2.8 copy-start.2
  346.8 3.6 %copy-start.3 = (f32[192,192]{1,0:T(8,128)S(1)}, f32[192,192]{1,0:T(8,128)}, u32[]{:S(2)}) copy-start(f32[192,192]{1,0:T(8,128)} %get-tuple-element.106) | copy-start | bytes 442372
  346.8 4.2 %copy-start.1 = (f32[192,768]{1,0:T(8,128)S(1)}, f32[192,768]{1,0:T(8,128)}, u32[]{:S(2)}) copy-start(f32[192,768]{1,0:T(8,128)} %get-tuple-element.110) | copy-start | bytes 1769476
  349.6 2.3 copy-start

commit v10 on v9

--- a/solution.py
+++ b/solution.py
@@ -588,7 +588,8 @@
 
 
 CHUNKS = 4
-FRONT = 13
+PIECES = 4
+FRONT = 5 + 2 * PIECES
 GATHER_SLOTS = 40
 SEGMENT = 4
 
@@ -657,7 +658,7 @@
     blocks, wholes = (block0, block1, block2), (whole0, whole1, whole2)
     half_rows = wq.shape[0] // 2
     my_half = pl.ds(pl.multiple_of(x * half_rows, 16), half_rows)
-    size = QROWS // CHUNKS
+    size = QROWS // PIECES
     first_half = jnp.where(z == 0, 0, 1)
     order = (z, z ^ 1, jnp.where(z < 2, 2, 1), jnp.where(z < 2, 3, 0))
     above, below = {"gr": jnp.minimum(z + 1, 3)}, {"gr": jnp.maximum(z - 1, 0)}
@@ -711,7 +712,7 @@
         return send(piece, piece, w_sems, 16 + s, over_x)
 
     def chunk(number):
-        return jnp.where(number < CHUNKS, first_half, 1 - first_half), number % CHUNKS
+        return jnp.where(number < PIECES, first_half, 1 - first_half), number % PIECES
 
     def item(column, number):
         half, k = chunk(number)
@@ -720,7 +721,7 @@
     def up(number):
         half, k = chunk(number)
         ref = item(g, number)
-        return send(ref, ref, z_sems, half * CHUNKS + k, {"gr": jnp.minimum(z + 1, 3)})
+        return send(ref, ref, z_sems, half * PIECES + k, {"gr": jnp.minimum(z + 1, 3)})
 
     def down(number):
         half, k = chunk(number)
@@ -729,20 +730,20 @@
             ref,
             ref,
             z_sems,
-            half * CHUNKS + k,
+            half * PIECES + k,
             {"gr": jnp.maximum(z - 1, 0)},
-            2 * CHUNKS + k,
+            2 * PIECES + k,
         )
 
     def side(number):
         half, k = chunk(number)
         ref = item(g, number)
-        return send(ref, ref, y_sems, half * CHUNKS + k, over_y)
+        return send(ref, ref, y_sems, half * PIECES + k, over_y)
 
     def core(number, far):
         half, k = chunk(number)
         ref = item(g ^ 2 if far else g, number)
-        return send(ref, ref, d_sems, far * 2 * CHUNKS + half * CHUNKS + k, sib)
+        return send(ref, ref, d_sems, far * 2 * PIECES + half * PIECES + k, sib)
 
     def goes_up(number):
         return jnp.logical_and(z < 3, chunk(number)[0] <= z)
@@ -874,7 +875,7 @@
             small(0, s).wait_recv()
         vec_out[...] = (vec[...] + vec_in[1]) + (vec_in[2] + vec_in[3])
 
-        @pl.loop(0, CHUNKS)
+        @pl.loop(0, PIECES)
         def _(i):
             rows = pl.ds(pl.multiple_of(i * size, size), size)
             hidden = tokens[rows].astype(F32) + vec_out[0:1]
@@ -893,9 +894,9 @@
         w_dp(0).start()
 
     hooks[0] += [begin, partial(forward, 0), begin_chip]
-    for i in range(1, 8):
+    for i in range(1, 2 * PIECES):
         hooks[i].append(partial(forward, i))
-    for i in range(2, 10):
+    for i in range(2, 2 * PIECES + 2):
         hooks[i].append(partial(across, i - 2))
 
     def w_pass(s):
@@ -958,7 +959,7 @@
         for i in range(4):
             for p in range(3):
                 kvp_all[p, i, to] = kv[size * i : size * i + size, 256 * p : 256 * p + 256]
-        mine = chip[number // CHUNKS, pl.ds(pl.multiple_of(k * size, size), size)]
+        mine = chip[number // PIECES, pl.ds(pl.multiple_of(k * size, size), size)]
         kvo = nn(mine, w).astype(BF)
         queries = (nn(mine, wq_out[...]) * 0.125).astype(BF)
         to = pl.ds(pl.multiple_of(number * size, size), size)
@@ -984,14 +985,14 @@
 
     hooks[0].append(own_first)
     hooks[1].append(own_down)
-    hooks[9].append(own_up)
-    hooks[8].append(partial(gather_first, 0))
-    hooks[10].append(partial(gather_second, 0))
+    hooks[8].append(own_up)
+    hooks[7].append(partial(gather_first, 0))
+    hooks[9].append(partial(gather_second, 0))
     between = [[] for _ in range(24 // SEGMENT + 1)]
     last = len(between) - 1
     between[0] += [lambda: [copy.start() for copy in out_copies()], partial(gather_third, 0)]
-    hooks[10].append(partial(relay, 1))
-    hooks[12].append(partial(relay, 2))
+    hooks[9].append(partial(relay, 1))
+    hooks[11].append(partial(relay, 2))
     for slot, stage, s in (
         (0, relay, 3),
         (0, gather_first, 1),
@@ -1006,12 +1007,12 @@
     ):
         between[slot].append(partial(stage, s))
 
-    for number in range(FRONT - 8):
+    for number in range(FRONT - 2 * PIECES):
         for hook in hooks[number]:
             hook()
 
     def one_piece(number, carried):
-        for i in range(FRONT - 8, FRONT):
+        for i in range(FRONT - 2 * PIECES, FRONT):
             if hooks[i]:
 
                 @pl.when(number == i)
@@ -1019,10 +1020,10 @@
                     for hook in hooks[i]:
                         hook()
 
-        project(number - (FRONT - 8))
+        project(number - (FRONT - 2 * PIECES))
         return carried
 
-    lax.fori_loop(FRONT - 8, FRONT, one_piece, 0)
+    lax.fori_loop(FRONT - 2 * PIECES, FRONT, one_piece, 0)
 
     low = lax.broadcasted_iota(jnp.int32, (CL, 128), 1) < 64
 
@@ -1115,7 +1116,7 @@
     for hook in between[last]:
         hook()
 
-    for number in range(8):
+    for number in range(2 * PIECES):
         side(number).wait_send()
         core(number, 0).wait_send()
         core(number, 1).wait_send()
@@ -1216,12 +1217,12 @@
         + [
             pltpu.VMEM((3, 2, QROWS, 128), BF),
             pltpu.SMEM((4,) + own.shape, jnp.int32),
-            dma(3 * CHUNKS),
-            dma(2 * CHUNKS),
-            dma(2 * CHUNKS),
-            dma(2 * CHUNKS),
-            dma(4 * CHUNKS),
-            dma(4 * CHUNKS),
+            dma(3 * PIECES),
+            dma(2 * PIECES),
+            dma(2 * PIECES),
+            dma(2 * PIECES),
+            dma(4 * PIECES),
+            dma(4 * PIECES),
             dma(20),
             dma(20),
             dma(11),
@@ -1448,12 +1449,14 @@
         begin(s)
     for s in RS_ORDER:
         after_a(s)
-    lax.fori_loop(count, count + 3, partial(stages, skip=1), 0)
+    lax.fori_loop(count, count + 2, partial(stages, skip=1), 0)
     for s in RS_ORDER:
         after_b(s)
-    lax.fori_loop(count + 3, count + 9, partial(stages, skip=2), 0)
+    lax.fori_loop(count + 2, count + 3, partial(stages, skip=2), 0)
+    lax.fori_loop(count + 3, count + 6, partial(stages, skip=2), 0)
     for s in RS_ORDER:
         after_c(s)
+    lax.fori_loop(count + 6, count + 9, partial(stages, skip=3), 0)
 
     @pl.loop(0, count)
     def _(t):
@@ -1601,9 +1604,9 @@
             for r in range(4):
                 wo[k, 192 * i : 192 * i + 192, 192 * r : 192 * r + 192] = w_out_g[2 * i + k, r]
 
-    @pl.loop(0, 2)
+    @pl.loop(0, 1)
     def _(t):
-        r = pl.ds(pl.multiple_of(t * 256, 256), 256)
+        r = pl.ds(pl.multiple_of(t * QROWS, QROWS), QROWS)
         hidden = tokens[r].astype(F32) + vec[0:1]
         attended = nn(mixed[0, r], wo[0]) + nn(mixed[1, r], wo[1])
         total = hidden + attended + vec[3:4]
@@ -1633,9 +1636,9 @@
 
     sums[...] = jnp.zeros_like(sums)
 
-    @pl.loop(0, 2)
+    @pl.loop(0, 1)
     def _(t):
-        r = pl.ds(pl.multiple_of(t * 256, 256), 256)
+        r = pl.ds(pl.multiple_of(t * QROWS, QROWS), QROWS)
         final = h2[r] + acc[r] + vec[6:7]
         final_out[r] = final.astype(BF)
         diff = final - teacher[r].astype(F32)
@@ -1664,9 +1667,9 @@
         du[b] = nn(n2t[...], act[b]).astype(BF)
         pltpu.make_async_copy(du.at[b], dw_up.at[b], o_sems.at[4 + b]).start()
 
-    @pl.loop(0, 2)
+    @pl.loop(0, 1)
     def _(t):
-        r = pl.ds(pl.multiple_of(t * 256, 256), 256)
+        r = pl.ds(pl.multiple_of(t * QROWS, QROWS), QROWS)
         hidden = h2[r]
         center = jnp.mean(hidden, axis=1, keepdims=True)
         offset = hidden - center

time: 354 us -> 353 us (level)
  no operation moved by 1% of the time
where the time goes in v10:
time: 353 us
  Pallas kernels  337 us (95%)
  local copies, waits for them, and re-layouts  11 us (3%)
    pallas_call x1, Pallas kernels, front(): pl.pallas_call(body, name='front', in_specs=[vmem] * 10 + [any_space] * 4...  133 us
    pallas_call x1, Pallas kernels, tail_exchange(): pl.pallas_call(tail_kernel, name='tail_exchange', in_specs=[pl.BlockSpec(...  97.6 us
    pallas_call x1, Pallas kernels, attend_back_scatter(): pl.pallas_call(partial(att_scatter_kernel, count), name='attend_back_scat...  76.3 us
    pallas_call x1, Pallas kernels, middle(): pl.pallas_call(middle_kernel, name='middle', in_specs=[vmem, vmem, any_sp...  30.3 us

profile of v10, /device:TPU:0, one launch (start us, length us, event | category | flops | bytes accessed | tf_op | source)
XLA Modules:
  0.0 353.0 jit_solution(14920011596341356382)
XLA Ops:
  0.7 0.7 pad.4
  1.3 0.6 broadcast_in_dim.6.refs_8_
  1.9 132.7 %front.1 = (bf16[2,512,384]{2,1,0:T(8,128)(2,1)}, f32[3,8,2,128]{3,2,1,0:T(2,128)}, bf16[4,4,192,192]{3,2,1,0:T(8,128)(2,1)}, bf16[4,4,192,768]{3,2,1,0:T(8,128)...) custom-call(bf16[512,768]{1,0:T(8,128)(2,1)} %tokens.3, ...), custom_call_target="tpu_custom_call" | custom-call | tf_op jit(solution)/shard_map/front/pallas_call | solution.py:1185
  134.6 0.7 slice_reduce_fusion.1
  135.3 0.1 reshape_squeeze.3
  135.4 0.1 reshape.86
  135.5 0.1 broadcast_in_dim.7
  135.6 0.1 reshape.85
  135.7 0.5 broadcast_select_fusion.grp_ref.grp
  136.2 30.3 %middle.1 = (bf16[512,768]{1,0:T(8,128)(2,1)}, f32[512,768]{1,0:T(8,128)}, bf16[4,768,768]{2,1,0:T(8,128)(2,1)}, bf16[4,768,768]{2,1,0:T(8,128)(2,1)}, bf16[4,4,...) custom-call(bf16[2,512,384]{2,1,0:T(8,128)(2,1)} %get-tuple-element.46.mixed, ...), custom_call_target="tpu_custom_call" | custom-call | tf_op jit(solution)/shard_map/middle/pallas_call | solution.py:1706
  166.5 76.3 %attend_back_scatter.1 = (bf16[1024,384]{1,0:T(8,128)(2,1)}, bf16[1024,768]{1,0:T(8,128)(2,1)}, bf16[8,1024,768]{2,1,0:T(8,128)(2,1)}, f32[192,768]{1,0:T(8,128)...) custom-call(s32[8]{0:T(128)} %broadcast_select_fusion.grp_ref.grp, bf16[3,1024,128]{2,1,0:T(8,128)(2,1)} %get-tuple-element.54.q_ref, ...), custom_call_target="tpu_custom_call" | custom-call | tf_op jit(solution)/shard_map/attend_back_scatter/pallas_call | solution.py:541
  242.8 97.6 %tail_exchange.1 = (f32[512,768]{1,0:T(8,128)}, f32[16,768]{1,0:T(8,128)}, f32[192,576]{1,0:T(8,128)}) custom-call(s32[8]{0:T(128)} %broadcast_select_fusion.grp_ref.grp, bf16[8,1024,768]{2,1,0:T(8,128)(2,1)} %get-tuple-element.62.dkv, bf16[4,2,512,768]{3,2,1,0:T(8,128)(2,1)} %get-tuple-element.63.n1p, bf16[1024,768]{1,0:T(8,128)(2,1)} %bitcast.18, ...), custom_call_target="tpu_custom_call" | custom-call | tf_op jit(solution)/shard_map/tail_exchange/pallas_call | solution.py:1517
  340.4 0.7 slice.49
  341.2 0.1 reshape.91
  341.3 0.6 constant_dynamic-slice_fusion.6
  341.9 0.8 slice.56
  342.7 0.6 dynamic-slice_reduce_fusion
  343.3 1.3 slice_reduce_fusion
  345.9 0.0 copy-start.2
  346.0 0.0 copy-start.3
  346.0 0.0 copy-start.1
  346.0 2.7 copy.37
  348.7 0.0 copy-done.2
  348.7 0.0 copy-start
  348.7 0.8 copy.38
  349.5 0.0 copy-done.3
  349.5 0.7 copy.39
  350.2 0.0 copy-done.1
  350.2 0.8 copy.40
  351.0 0.0 copy-done
  351.0 0.8 copy.41
  (2 shorter events, 0.0 us)
Async XLA Ops:
  345.9 2.8 copy-start.2
  346.0 3.6 %copy-start.3 = (f32[192,192]{1,0:T(8,128)S(1)}, f32[192,192]{1,0:T(8,128)}, u32[]{:S(2)}) copy-start(f32[192,192]{1,0:T(8,128)} %get-tuple-element.106) | copy-start | bytes 442372
  346.0 4.2 %copy-start.1 = (f32[192,768]{1,0:T(8,128)S(1)}, f32[192,768]{1,0:T(8,128)}, u32[]{:S(2)}) copy-start(f32[192,768]{1,0:T(8,128)} %get-tuple-element.110) | copy-start | bytes 1769476
  348.7 2.3 copy-start

commit v11 on v10

--- a/solution.py
+++ b/solution.py
@@ -244,10 +244,12 @@
     return x, z, g, g // 2, g % 2
 
 
-def greet(partners):
+def greet(partners, meanwhile=None):
     barrier = pltpu.get_barrier_semaphore()
     for partner in partners:
         pl.semaphore_signal(barrier, inc=1, device_id=partner, device_id_type=MESH)
+    if meanwhile is not None:
+        meanwhile()
     pl.semaphore_wait(barrier, len(partners))
 
 
@@ -1297,11 +1299,14 @@
 
     for copy in fetch(0):
         copy.start()
-    greet(all_partners())
-    wkt[...] = w_kv[...].T
-    wqt[...] = w_q[...].T
-    dkvw[...] = jnp.zeros_like(dkvw)
-    dqw[...] = jnp.zeros_like(dqw)
+
+    def prepare():
+        wkt[...] = w_kv[...].T
+        wqt[...] = w_q[...].T
+        dkvw[...] = jnp.zeros_like(dkvw)
+        dqw[...] = jnp.zeros_like(dqw)
+
+    greet(all_partners(), prepare)
 
     def at(t):
         return t // CHUNKS, pl.ds(pl.multiple_of((t % CHUNKS) * size, size), size)

time: 353 us -> 353 us (level)
  no operation moved by 1% of the time
where the time goes in v11:
time: 353 us; the launch traced here: 352 us
  Pallas kernels  336 us (95%)
  local copies, waits for them, and re-layouts  11 us (3%)
    pallas_call x1, Pallas kernels, front(): pl.pallas_call(body, name='front', in_specs=[vmem] * 10 + [any_space] * 4...  133 us
    pallas_call x1, Pallas kernels, tail_exchange(): pl.pallas_call(tail_kernel, name='tail_exchange', in_specs=[pl.BlockSpec(...  97.1 us
    pallas_call x1, Pallas kernels, attend_back_scatter(): pl.pallas_call(partial(att_scatter_kernel, count), name='attend_back_scat...  76.3 us
    pallas_call x1, Pallas kernels, middle(): pl.pallas_call(middle_kernel, name='middle', in_specs=[vmem, vmem, any_sp...  30.3 us

profile of v11, /device:TPU:0, one launch (start us, length us, event | category | flops | bytes accessed | tf_op | source)
XLA Modules:
  0.0 352.4 jit_solution(11783927790458873440)
XLA Ops:
  0.7 0.7 pad.4
  1.3 0.6 broadcast_in_dim.6.refs_8_
  1.9 132.7 %front.1 = (bf16[2,512,384]{2,1,0:T(8,128)(2,1)}, f32[3,8,2,128]{3,2,1,0:T(2,128)}, bf16[4,4,192,192]{3,2,1,0:T(8,128)(2,1)}, bf16[4,4,192,768]{3,2,1,0:T(8,128)...) custom-call(bf16[512,768]{1,0:T(8,128)(2,1)} %tokens.3, ...), custom_call_target="tpu_custom_call" | custom-call | tf_op jit(solution)/shard_map/front/pallas_call | solution.py:1187
  134.6 0.7 slice_reduce_fusion.1
  135.3 0.1 reshape_squeeze.3
  135.4 0.1 reshape.86
  135.5 0.1 broadcast_in_dim.7
  135.6 0.1 reshape.85
  135.7 0.5 broadcast_select_fusion.grp_ref.grp
  136.2 30.3 %middle.1 = (bf16[512,768]{1,0:T(8,128)(2,1)}, f32[512,768]{1,0:T(8,128)}, bf16[4,768,768]{2,1,0:T(8,128)(2,1)}, bf16[4,768,768]{2,1,0:T(8,128)(2,1)}, bf16[4,4,...) custom-call(bf16[2,512,384]{2,1,0:T(8,128)(2,1)} %get-tuple-element.46.mixed, ...), custom_call_target="tpu_custom_call" | custom-call | tf_op jit(solution)/shard_map/middle/pallas_call | solution.py:1711
  166.5 76.3 %attend_back_scatter.1 = (bf16[1024,384]{1,0:T(8,128)(2,1)}, bf16[1024,768]{1,0:T(8,128)(2,1)}, bf16[8,1024,768]{2,1,0:T(8,128)(2,1)}, f32[192,768]{1,0:T(8,128)...) custom-call(s32[8]{0:T(128)} %broadcast_select_fusion.grp_ref.grp, bf16[3,1024,128]{2,1,0:T(8,128)(2,1)} %get-tuple-element.54.q_ref, ...), custom_call_target="tpu_custom_call" | custom-call | tf_op jit(solution)/shard_map/attend_back_scatter/pallas_call | solution.py:543
  242.8 97.1 %tail_exchange.1 = (f32[512,768]{1,0:T(8,128)}, f32[16,768]{1,0:T(8,128)}, f32[192,576]{1,0:T(8,128)}) custom-call(s32[8]{0:T(128)} %broadcast_select_fusion.grp_ref.grp, bf16[8,1024,768]{2,1,0:T(8,128)(2,1)} %get-tuple-element.62.dkv, bf16[4,2,512,768]{3,2,1,0:T(8,128)(2,1)} %get-tuple-element.63.n1p, bf16[1024,768]{1,0:T(8,128)(2,1)} %bitcast.18, ...), custom_call_target="tpu_custom_call" | custom-call | tf_op jit(solution)/shard_map/tail_exchange/pallas_call | solution.py:1522
  339.9 0.7 slice.49
  340.6 0.1 reshape.91
  340.7 0.6 constant_dynamic-slice_fusion.6
  341.3 0.8 slice.56
  342.1 0.6 dynamic-slice_reduce_fusion
  342.7 1.3 slice_reduce_fusion
  345.4 0.0 copy-start.2
  345.4 0.0 copy-start.3
  345.4 0.0 copy-start.1
  345.4 2.7 copy.37
  348.2 0.0 copy-done.2
  348.2 0.0 copy-start
  348.2 0.8 copy.38
  349.0 0.0 copy-done.3
  349.0 0.7 copy.39
  349.6 0.0 copy-done.1
  349.6 0.8 copy.40
  350.5 0.0 copy-done
  350.5 0.8 copy.41
  (2 shorter events, 0.0 us)
Async XLA Ops:
  345.4 2.8 copy-start.2
  345.4 3.6 %copy-start.3 = (f32[192,192]{1,0:T(8,128)S(1)}, f32[192,192]{1,0:T(8,128)}, u32[]{:S(2)}) copy-start(f32[192,192]{1,0:T(8,128)} %get-tuple-element.106) | copy-start | bytes 442372
  345.4 4.2 %copy-start.1 = (f32[192,768]{1,0:T(8,128)S(1)}, f32[192,768]{1,0:T(8,128)}, u32[]{:S(2)}) copy-start(f32[192,768]{1,0:T(8,128)} %get-tuple-element.110) | copy-start | bytes 1769476
  348.2 2.3 copy-start
